TPU v7x, 32 devices: a whole 2x2x4 slice. The times are simulated.
32 devices in a mesh: grp: 2 (over y), row: 4 (over x, core), col: 4 (over z).
Axes of the slice: x: 2, y: 2, z: 4, core: 2. Of those that a mesh axis runs over, the one named last changes fastest.
Arguments:
- level_one: bfloat16 [128, 256, 192], P(('grp', 'row'), 'col'), parts along dimension 0, may hold values from -6 to 6
- level_two: bfloat16 [64, 128, 384], P(('grp', 'row'), 'col'), parts along dimension 0, may hold values from -6 to 6
- level_three: bfloat16 [32, 64, 768], P(('grp', 'row'), None, 'col'), parts along dimension 0, may hold values from -6 to 6
- level_four: bfloat16 [16, 32, 1536], P(('grp', 'row'), None, 'col'), parts along dimension 0, may hold values from -10.5 to 10.5
- bin_weight: bfloat16 [4, 1536, 256], P(None, 'col'), may hold values from -0.21875 to 0.21875
- neck_feature: bfloat16 [3, 3, 1536, 256], P(None, None, 'col'), may hold values from -0.0546875 to 0.0546875
- neck_pooled: bfloat16 [3, 3, 1024, 256], P(None, None, 'col'), may hold values from -0.0546875 to 0.0546875
- lateral_one: bfloat16 [192, 256], replicated, may hold values from -0.625 to 0.625
- lateral_two: bfloat16 [384, 256], replicated, may hold values from -0.4375 to 0.4375
- lateral_three: bfloat16 [768, 256], replicated, may hold values from -0.3125 to 0.3125
- smooth_weight: bfloat16 [3, 3, 3, 256, 256], replicated, may hold values from -0.1875 to 0.1875
- join_weight: bfloat16 [3, 3, 1024, 256], replicated, may hold values from -0.09375 to 0.09375
- biases: float32 [12, 256], replicated, may hold values from -2 to 2
Outputs:
- joined: bfloat16 [128, 256, 256], P(('grp', 'row'), 'col'), parts along dimension 0
There are 2 independent parts, one for each index of `grp`. A program takes and returns all parts, laid end to end along the dimension named above; an argument that names none is the same for every part. Nothing has to cross between parts.
All inputs are finite; a program needn't handle non-finite values.
Results may differ from a plain program's by a relative error of at most 0.015.
Values may be sent and summed in bfloat16 or wider, within the bound.
No kernel may reach another device: no remote copies, remote signals or barrier semaphores. Data moves between devices by JAX's collectives and lax.ppermute only.
A program may use at most 64 MiB of HBM per device.

v0:
```python
import jax
import jax.numpy as jnp
from jax import lax
from jax.sharding import PartitionSpec as P

highest = lax.Precision.HIGHEST
bin_sides = (1, 2, 3, 6)


def with_halo(block, sides, width):
    for axis, dim in sides:
        count = lax.axis_size(axis)
        forward = [(i, i + 1) for i in range(count - 1)]
        backward = [(target, source) for source, target in forward]
        low = lax.ppermute(
            lax.slice_in_dim(block, block.shape[dim] - width, None, axis=dim), axis, forward
        )
        high = lax.ppermute(lax.slice_in_dim(block, 0, width, axis=dim), axis, backward)
        block = jnp.concatenate([low, block, high], axis=dim)
    return block


def pool_matrix(bin_side, extent, first, length):
    cell_index = jnp.arange(bin_side, dtype=jnp.int32)[:, None]
    position = first + jnp.arange(length, dtype=jnp.int32)[None, :]
    cell_first = cell_index * extent // bin_side
    cell_end = ((cell_index + 1) * extent + bin_side - 1) // bin_side
    inside = (position >= cell_first) & (position < cell_end)
    return inside.astype(jnp.float32) / (cell_end - cell_first).astype(jnp.float32)


def stretch_rows(position, bin_side, extent):
    source = jnp.clip((position + 0.5) * bin_side / extent - 0.5, 0.0, bin_side - 1.0)
    targets = jnp.arange(bin_side, dtype=jnp.float32)[None, :]
    return jnp.maximum(0.0, 1.0 - jnp.abs(source[:, None] - targets))


def tile_rim(feature):
    return with_halo(feature, (("row", 0), ("col", 1)), 1)


def clamp_edges(padded):
    row_here = lax.axis_index("row")
    row_last = lax.axis_size("row") - 1
    top_edge = jnp.where(row_here == 0, padded[1:2], padded[0:1])
    bottom_edge = jnp.where(row_here == row_last, padded[-2:-1], padded[-1:])
    padded = jnp.concatenate([top_edge, padded[1:-1], bottom_edge], axis=0)
    col_here = lax.axis_index("col")
    col_last = lax.axis_size("col") - 1
    left_edge = jnp.where(col_here == 0, padded[:, 1:2], padded[:, 0:1])
    right_edge = jnp.where(col_here == col_last, padded[:, -2:-1], padded[:, -1:])
    return jnp.concatenate([left_edge, padded[:, 1:-1], right_edge], axis=1)


def local_stretch(length, factor, border):
    output = jnp.arange(length * factor + 2 * border, dtype=jnp.float32) - border
    position = (output + 0.5) / factor + 0.5
    targets = jnp.arange(length + 2, dtype=jnp.float32)[None, :]
    return jnp.maximum(0.0, 1.0 - jnp.abs(position[:, None] - targets))


def upscale_rimmed(padded, factor, border):
    height = padded.shape[0] - 2
    breadth = padded.shape[1] - 2
    clamped = clamp_edges(padded).astype(jnp.float32)
    result = jnp.einsum(
        "oh,hwc->owc", local_stretch(height, factor, border), clamped, precision=highest
    )
    return jnp.einsum(
        "pw,owc->opc", local_stretch(breadth, factor, border), result, precision=highest
    )


def taps_sum(padded, weight):
    height = padded.shape[0] - 2
    breadth = padded.shape[1] - 2
    channels = padded.shape[2]
    summed = jnp.zeros((height * breadth, weight.shape[-1]), jnp.float32)
    for row_tap in range(3):
        for col_tap in range(3):
            window = padded[row_tap : row_tap + height, col_tap : col_tap + breadth].reshape(
                height * breadth, channels
            )
            summed = summed + jnp.dot(
                window, weight[row_tap, col_tap], preferred_element_type=jnp.float32
            )
    return summed.reshape(height, breadth, -1)


def project(feature, weight):
    height, breadth, channels = feature.shape
    result = jnp.dot(
        feature.reshape(height * breadth, channels), weight, preferred_element_type=jnp.float32
    )
    return result.reshape(height, breadth, -1)


def local(
    level_one,
    level_two,
    level_three,
    level_four,
    bin_weight,
    neck_feature,
    neck_pooled,
    lateral_one,
    lateral_two,
    lateral_three,
    smooth_weight,
    join_weight,
    biases,
):
    row_here = lax.axis_index("row")
    col_here = lax.axis_index("col")
    strip_rows, grid_cols, part_four = level_four.shape
    grid_rows = strip_rows * lax.axis_size("row")
    first_row = row_here * strip_rows
    out_channels = bin_weight.shape[2]
    coarse = level_four.astype(jnp.float32)
    pooled_parts = []
    cell_offsets = [0]
    for bin_side in bin_sides:
        pool_down = pool_matrix(bin_side, grid_rows, first_row, strip_rows)
        pool_across = pool_matrix(bin_side, grid_cols, 0, grid_cols)
        pooled = jnp.einsum("ih,hwc->iwc", pool_down, coarse, precision=highest)
        pooled = jnp.einsum("jw,iwc->ijc", pool_across, pooled, precision=highest)
        pooled_parts.append(pooled.reshape(bin_side * bin_side, part_four))
        cell_offsets.append(cell_offsets[-1] + bin_side * bin_side)
    bin_local = bin_weight.astype(jnp.float32)

    def bin_terms(pooled_list):
        return jnp.concatenate(
            [
                jnp.dot(pooled_list[number], bin_local[number], precision=highest)
                for number in range(len(bin_sides))
            ],
            axis=0,
        )

    pooled_whole = lax.psum(
        jnp.concatenate(pooled_parts, axis=0).astype(jnp.bfloat16), "row"
    ).astype(jnp.float32)
    pooled_split = [
        pooled_whole[cell_offsets[number] : cell_offsets[number + 1]]
        for number in range(len(bin_sides))
    ]
    bin_total = lax.psum(bin_terms(pooled_split).astype(jnp.bfloat16), "col").astype(jnp.float32)
    down_place = (first_row - 1 + jnp.arange(strip_rows + 2, dtype=jnp.int32)).astype(jnp.float32)
    inside_grid = ((down_place >= 0.0) & (down_place < grid_rows)).astype(jnp.float32)
    across_place = jnp.arange(grid_cols, dtype=jnp.float32)
    bin_maps = []
    for number, bin_side in enumerate(bin_sides):
        cell_values = bin_total[cell_offsets[number] : cell_offsets[number + 1]].reshape(
            bin_side, bin_side, out_channels
        )
        binned = jax.nn.relu(cell_values + biases[number])
        stretch_down = stretch_rows(down_place, bin_side, grid_rows) * inside_grid[:, None]
        stretch_across = stretch_rows(across_place, bin_side, grid_cols)
        spread = jnp.einsum("hi,ijd->hjd", stretch_down, binned, precision=highest)
        spread = jnp.einsum("wj,hjd->hwd", stretch_across, spread, precision=highest)
        bin_maps.append(spread)
    ppm_maps = jnp.concatenate(bin_maps, axis=2).astype(jnp.bfloat16)
    share_ppm = neck_pooled.shape[2]
    ppm_maps = lax.dynamic_slice_in_dim(ppm_maps, col_here * share_ppm, share_ppm, 2)
    feature_rim = with_halo(level_four, (("row", 0),), 1)
    stacked = jnp.concatenate([feature_rim, ppm_maps], axis=2)
    stacked = jnp.pad(stacked, ((0, 0), (1, 1), (0, 0)))
    neck_weight = jnp.concatenate([neck_feature, neck_pooled], axis=2)
    neck_term = taps_sum(stacked, neck_weight)
    share_three = level_three.shape[2]
    weight_three = lax.dynamic_slice_in_dim(lateral_three, col_here * share_three, share_three, 0)
    three_term = project(level_three, weight_three)
    three_sum, top_sum = (
        lax.psum_scatter(
            three_term.astype(jnp.bfloat16), "col", scatter_dimension=1, tiled=True
        ).astype(jnp.float32),
        lax.psum_scatter(
            neck_term.astype(jnp.bfloat16), "col", scatter_dimension=1, tiled=True
        ).astype(jnp.float32),
    )
    pyramid_four = jax.nn.relu(top_sum + biases[4]).astype(jnp.bfloat16)
    rimmed_four = tile_rim(pyramid_four)
    pyramid_three = (jax.nn.relu(three_sum + biases[7]) + upscale_rimmed(rimmed_four, 2, 0)).astype(
        jnp.bfloat16
    )
    rimmed_three = tile_rim(pyramid_three)
    pyramid_two = (
        jax.nn.relu(project(level_two, lateral_two) + biases[6])
        + upscale_rimmed(rimmed_three, 2, 0)
    ).astype(jnp.bfloat16)
    rimmed_two = tile_rim(pyramid_two)
    pyramid_one = (
        jax.nn.relu(project(level_one, lateral_one) + biases[5]) + upscale_rimmed(rimmed_two, 2, 0)
    ).astype(jnp.bfloat16)
    smooth_one = jax.nn.relu(taps_sum(tile_rim(pyramid_one), smooth_weight[0]) + biases[8]).astype(
        jnp.bfloat16
    )
    smooth_two = jax.nn.relu(taps_sum(rimmed_two, smooth_weight[1]) + biases[9]).astype(
        jnp.bfloat16
    )
    smooth_three = jax.nn.relu(taps_sum(rimmed_three, smooth_weight[2]) + biases[10]).astype(
        jnp.bfloat16
    )
    stacked_top = jnp.concatenate(
        [
            smooth_one,
            upscale_rimmed(tile_rim(smooth_two), 2, 0).astype(jnp.bfloat16),
            upscale_rimmed(tile_rim(smooth_three), 4, 0).astype(jnp.bfloat16),
            upscale_rimmed(rimmed_four, 8, 0).astype(jnp.bfloat16),
        ],
        axis=2,
    )
    framed = tile_rim(stacked_top)
    return jax.nn.relu(taps_sum(framed, join_weight) + biases[11]).astype(jnp.bfloat16)


def solution(mesh):
    placed = (
        P(("grp", "row"), "col", None),
        P(("grp", "row"), "col", None),
        P(("grp", "row"), None, "col"),
        P(("grp", "row"), None, "col"),
        P(None, "col", None),
        P(None, None, "col", None),
        P(None, None, "col", None),
        P(),
        P(),
        P(),
        P(),
        P(),
        P(),
    )
    return jax.shard_map(
        local, mesh=mesh, in_specs=placed, out_specs=P(("grp", "row"), "col", None), check_vma=False
    )
```

profile of v0, /device:TPU:1, one launch (start us, length us, event | category | flops | bytes accessed | tf_op | source)
XLA Modules:
  0.0 225.7 jit_solution(17948178878431407120)
XLA Ops:
  6.5 1.5 fusion.376
  8.0 4.5 %collective-permute-start = (bf16[1,32,384]{2,1,0:T(8,128)(2,1)}, bf16[1,32,384]{2,1,0:T(8,128)(2,1)}, u32[]{:S(2)}, u32[]{:S(2)}) collective-permute-start(bf16[1,32,384]{2,1,0:T(8,128)(2,1)} %get-tuple-element.83), channel_id=1, source_target_pairs={{0,4},{4,8},{8,12},{1,5},{5,9},{9,13},{2,6},{6,10},{10,14},{3,7},{... | collective-permute-start | bytes 73736 | tf_op jit(solution)/shard_map/ppermute | solution.py:15
  12.5 1.9 collective-permute-start.1
  21.9 10.5 %psum.14 = bf16[50,384]{1,0:T(8,128)(2,1)S(1)} all-reduce(bf16[50,384]{1,0:T(8,128)(2,1)S(1)} %pad_maximum_fusion.36), channel_id=1, replica_groups=mesh['grp'=2,'row'=4,'col'=4] {'row'}, use_global_device_ids=true, to_apply=%region_1.2 | all-reduce | flops 19200 | bytes 76800 | tf_op jit(solution)/shard_map/psum | solution.py:140
  33.2 15.5 %psum.15 = bf16[50,256]{1,0:T(8,128)(2,1)S(1)} all-reduce(bf16[50,256]{1,0:T(8,128)(2,1)S(1)} %pad_maximum_fusion.42), channel_id=1, replica_groups=mesh['grp'=2,'row'=4,'col'=4] {'col'}, use_global_device_ids=true, to_apply=%region_2.3 | all-reduce | flops 12800 | bytes 51200 | tf_op jit(solution)/shard_map/psum | solution.py:147
  50.0 1.6 constant_dynamic-update-slice_fusion.1
  51.6 1.3 fusion.379
  60.7 1.4 constant_dynamic-update-slice_fusion
  66.2 1.8 convolution_convert_fusion.3
  68.2 3.3 %slice_bitcast_fusion.2 = (bf16[3,3,256,256]{3,2,1,0:T(8,128)(2,1)}, bf16[3,3,256,256]{3,2,1,0:T(8,128)(2,1)S(1)}, bf16[3,3,256,256]{3,2,1,0:T(8,128)(2,1)S(1)}) fusion(bf16[3,3,3,256,256]{4,3,2,1,0:T(8,128)(2,1)} %param.23), kind=kLoop, calls=%fused_computation.40 | loop fusion | bytes 7077888 | tf_op jit(solution)/shard_map/squeeze | solution.py:195
  72.8 12.5 %reduce-scatter.7.cloned.1.call-done = bf16[8,512]{1,0:T(8,128)(2,1)} async-done(((bf16[32,512]{1,0:T(8,128)(2,1)}), bf16[8,512]{1,0:T(8,128)(2,1)}) %reduce-scatter.7.cloned.1.call-update) | async-done | bytes 8208
  86.0 5.9 %collective-permute-start.2 = (bf16[1,8,256]{2,1,0:T(8,128)(2,1)S(1)}, bf16[1,8,256]{2,1,0:T(8,128)(2,1)S(1)}, u32[]{:S(2)}, u32[]{:S(2)}) collective-permute-start(bf16[1,8,256]{2,1,0:T(8,128)(2,1)S(1)} %get-tuple-element.109), channel_id=1, source_target_pairs={{0,4},{4,8},{8,12},{1,5},{5,9},{9,13},{2,6},{6,10},{10,14},{3,7},{... | collective-permute-start | bytes 12296 | tf_op jit(solution)/shard_map/ppermute | solution.py:15
  91.9 1.9 collective-permute-start.3
  93.9 3.1 %collective-permute-done.3 = bf16[1,8,256]{2,1,0:T(8,128)(2,1)S(1)} collective-permute-done((bf16[1,8,256]{2,1,0:T(8,128)(2,1)S(1)}, bf16[1,8,256]{2,1,0:T(8,128)(2,1)S(1)}, u32[]{:S(2)}, u32[]{:S(2)}) %collective-permute-start.3) | collective-permute-done | bytes 4128 | tf_op jit(solution)/shard_map/ppermute | solution.py:18
  98.3 1.3 collective-permute-start.5
  99.6 3.0 %collective-permute-done.5 = bf16[4,1,256]{2,1,0:T(2,128)(2,1)S(1)} collective-permute-done((bf16[4,1,256]{2,1,0:T(2,128)(2,1)S(1)}, bf16[4,1,256]{2,1,0:T(2,128)(2,1)S(1)}, u32[]{:S(2)}, u32[]{:S(2)}) %collective-permute-start.5) | collective-permute-done | bytes 2080 | tf_op jit(solution)/shard_map/ppermute | solution.py:18
  103.3 1.7 reduce-scatter.5.cloned.1.call-done
  106.1 6.1 %collective-permute-start.6 = (bf16[1,16,256]{2,1,0:T(8,128)(2,1)S(1)}, bf16[1,16,256]{2,1,0:T(8,128)(2,1)S(1)}, u32[]{:S(2)}, u32[]{:S(2)}) collective-permute-start(bf16[1,16,256]{2,1,0:T(8,128)(2,1)S(1)} %get-tuple-element.89), channel_id=1, source_target_pairs={{0,4},{4,8},{8,12},{1,5},{5,9},{9,13},{2,6},{6,10},{10,14},{3,7},{... | collective-permute-start | bytes 24584 | tf_op jit(solution)/shard_map/ppermute | solution.py:15
  112.1 1.9 collective-permute-start.7
  115.1 2.0 collective-permute-done.7
  119.9 2.9 %collective-permute-done.9 = bf16[6,1,256]{2,1,0:T(2,128)(2,1)S(1)} collective-permute-done((bf16[6,1,256]{2,1,0:T(2,128)(2,1)S(1)}, bf16[6,1,256]{2,1,0:T(2,128)(2,1)S(1)}, u32[]{:S(2)}, u32[]{:S(2)}) %collective-permute-start.9) | collective-permute-done | bytes 3104 | tf_op jit(solution)/shard_map/ppermute | solution.py:18
  124.4 3.1 %collective-permute-start.22 = (bf16[1,16,256]{2,1,0:T(8,128)(2,1)S(1)}, bf16[1,16,256]{2,1,0:T(8,128)(2,1)S(1)}, u32[]{:S(2)}, u32[]{:S(2)}) collective-permute-start(bf16[1,16,256]{2,1,0:T(8,128)(2,1)S(1)} %get-tuple-element.85), channel_id=1, source_target_pairs={{0,4},{4,8},{8,12},{1,5},{5,9},{9,13},{2,6},{6,10},{10,14},{3,7},{... | collective-permute-start | bytes 24584 | tf_op jit(solution)/shard_map/ppermute | solution.py:15
  127.5 1.9 collective-permute-start.23
  130.4 2.0 collective-permute-done.23
  132.5 3.4 %collective-permute-start.24 = (bf16[6,1,256]{2,1,0:T(2,128)(2,1)S(1)}, bf16[6,1,256]{2,1,0:T(2,128)(2,1)S(1)}, u32[]{:S(2)}, u32[]{:S(2)}) collective-permute-start(bf16[6,1,256]{2,1,0:T(2,128)(2,1)S(1)} %get-tuple-element.77), channel_id=1, source_target_pairs={{0,1},{1,2},{2,3},{4,5},{5,6},{6,7},{8,9},{9,10},{10,11},{12,13},{... | collective-permute-start | bytes 9224 | tf_op jit(solution)/shard_map/ppermute | solution.py:15
  137.2 2.2 collective-permute-start.10
  139.4 2.1 collective-permute-start.11
  144.5 4.3 %collective-permute-start.12 = (bf16[10,1,256]{2,1,0:T(2,128)(2,1)S(1)}, bf16[10,1,256]{2,1,0:T(2,128)(2,1)S(1)}, u32[]{:S(2)}, u32[]{:S(2)}) collective-permute-start(bf16[10,1,256]{2,1,0:T(2,128)(2,1)S(1)} %get-tuple-element.50), channel_id=1, source_target_pairs={{0,1},{1,2},{2,3},{4,5},{5,6},{6,7},{8,9},{9,10},{10,11},{12,13},{... | collective-permute-start | bytes 15368 | tf_op jit(solution)/shard_map/ppermute | solution.py:15
  148.8 1.5 collective-permute-start.13
  150.5 2.7 %collective-permute-done.13 = bf16[10,1,256]{2,1,0:T(2,128)(2,1)S(1)} collective-permute-done((bf16[10,1,256]{2,1,0:T(2,128)(2,1)S(1)}, bf16[10,1,256]{2,1,0:T(2,128)(2,1)S(1)}, u32[]{:S(2)}, u32[]{:S(2)}) %collective-permute-start.13) | collective-permute-done | bytes 5152 | tf_op jit(solution)/shard_map/ppermute | solution.py:18
  155.8 3.7 %collective-permute-start.18 = (bf16[1,32,256]{2,1,0:T(8,128)(2,1)S(1)}, bf16[1,32,256]{2,1,0:T(8,128)(2,1)S(1)}, u32[]{:S(2)}, u32[]{:S(2)}) collective-permute-start(bf16[1,32,256]{2,1,0:T(8,128)(2,1)S(1)} %get-tuple-element.61), channel_id=1, source_target_pairs={{0,4},{4,8},{8,12},{1,5},{5,9},{9,13},{2,6},{6,10},{10,14},{3,7},{... | collective-permute-start | bytes 49160 | tf_op jit(solution)/shard_map/ppermute | solution.py:15
  159.5 1.9 collective-permute-start.19
  161.4 1.4 fusion.9
  162.8 1.7 collective-permute-done.19
  164.6 2.1 collective-permute-start.20
  168.0 2.2 collective-permute-start.14
  170.2 2.1 collective-permute-start.15
  173.2 1.3 fusion.12
  175.5 4.3 %collective-permute-start.16 = (bf16[18,1,256]{2,1,0:T(2,128)(2,1)S(1)}, bf16[18,1,256]{2,1,0:T(2,128)(2,1)S(1)}, u32[]{:S(2)}, u32[]{:S(2)}) collective-permute-start(bf16[18,1,256]{2,1,0:T(2,128)(2,1)S(1)} %get-tuple-element.30), channel_id=1, source_target_pairs={{0,1},{1,2},{2,3},{4,5},{5,6},{6,7},{8,9},{9,10},{10,11},{12,13},{... | collective-permute-start | bytes 27656 | tf_op jit(solution)/shard_map/ppermute | solution.py:15
  181.5 2.8 %collective-permute-done.17 = bf16[18,1,256]{2,1,0:T(2,128)(2,1)S(1)} collective-permute-done((bf16[18,1,256]{2,1,0:T(2,128)(2,1)S(1)}, bf16[18,1,256]{2,1,0:T(2,128)(2,1)S(1)}, u32[]{:S(2)}, u32[]{:S(2)}) %collective-permute-start.17) | collective-permute-done | bytes 9248 | tf_op jit(solution)/shard_map/ppermute | solution.py:18
  188.5 4.0 %collective-permute-start.26 = (bf16[1,64,1024]{2,1,0:T(8,128)(2,1)S(1)}, bf16[1,64,1024]{2,1,0:T(8,128)(2,1)S(1)}, u32[]{:S(2)}, u32[]{:S(2)}) collective-permute-start(bf16[1,64,1024]{2,1,0:T(8,128)(2,1)S(1)} %get-tuple-element.20), channel_id=1, source_target_pairs={{0,4},{4,8},{8,12},{1,5},{5,9},{9,13},{2,6},{6,10},{10,14},{3,7},{... | collective-permute-start | bytes 393224 | tf_op jit(solution)/shard_map/ppermute | solution.py:15
  192.5 1.9 collective-permute-start.27
  195.2 3.6 %collective-permute-done.27 = bf16[1,64,1024]{2,1,0:T(8,128)(2,1)S(1)} collective-permute-done((bf16[1,64,1024]{2,1,0:T(8,128)(2,1)S(1)}, bf16[1,64,1024]{2,1,0:T(8,128)(2,1)S(1)}, u32[]{:S(2)}, u32[]{:S(2)}) %collective-permute-start.27) | collective-permute-done | bytes 131104 | tf_op jit(solution)/shard_map/ppermute | solution.py:18
  198.9 1.6 collective-permute-start.28
  200.6 1.5 collective-permute-start.29
  204.1 1.5 collective-permute-done.29
  205.7 5.5 %maximum_maximum_fusion = (bf16[18,65,1024]{2,1,0:T(8,128)(2,1)S(1)}, bf16[18,65,1024]{2,1,0:T(8,128)(2,1)S(1)}) fusion(bf16[1,64,1024]{2,1,0:T(8,128)(2,1)S(1)} %collective-permute-done.27, bf16[16,64,256]{2,1,0:T(8,128)(2,1)S(1)} %fusion.10, bf16[16,64,256]{2,1,0:T(8,128)(2,1)S(1)} %fusion.11, bf16[16,64,256]{2,1,0:T(8,128)(2,1)S(1)} %fusion.12, ...), kind=kLoop, calls=%fused_computation | loop fusion | flops 33546240 | bytes 7225344 | tf_op jit(solution)/shard_map/concatenate | solution.py:19
  213.5 1.5 fusion.364
  (272 shorter events, 56.9 us)
Async XLA Ops:
  6.5 64.9 %copy-start = (bf16[16,64,192]{2,1,0:T(8,128)(2,1)S(1)}, bf16[16,64,192]{2,1,0:T(8,128)(2,1)}, u32[]{:S(2)}) copy-start(bf16[16,64,192]{2,1,0:T(8,128)(2,1)} %param.13) | copy-start | bytes 1179652
  6.5 25.9 %copy-start.5 = (bf16[4,384,256]{2,1,0:T(8,128)(2,1)S(1)}, bf16[4,384,256]{2,1,0:T(8,128)(2,1)}, u32[]{:S(2)}) copy-start(bf16[4,384,256]{2,1,0:T(8,128)(2,1)} %param.17) | copy-start | bytes 2359300
  6.5 78.7 %reduce-scatter.7.cloned.1.call-start = ((), (), s32[]{:S(2)}) async-start(), calls=%async_computation.3 | async-start | bytes 40960
  8.0 54.8 %collective-permute-start = (bf16[1,32,384]{2,1,0:T(8,128)(2,1)}, bf16[1,32,384]{2,1,0:T(8,128)(2,1)}, u32[]{:S(2)}, u32[]{:S(2)}) collective-permute-start(bf16[1,32,384]{2,1,0:T(8,128)(2,1)} %get-tuple-element.83), channel_id=1, source_target_pairs={{0,4},{4,8},{8,12},{1,5},{5,9},{9,13},{2,6},{6,10},{10,14},{3,7},{... | collective-permute-start | bytes 73736 | tf_op jit(solution)/shard_map/ppermute | solution.py:15
  12.5 50.3 %collective-permute-start.1 = (bf16[1,32,384]{2,1,0:T(8,128)(2,1)}, bf16[1,32,384]{2,1,0:T(8,128)(2,1)}, u32[]{:S(2)}, u32[]{:S(2)}) collective-permute-start(bf16[1,32,384]{2,1,0:T(8,128)(2,1)} %get-tuple-element.84), channel_id=1, source_target_pairs={{4,0},{8,4},{12,8},{5,1},{9,5},{13,9},{6,2},{10,6},{14,10},{7,3},{... | collective-permute-start | bytes 73736 | tf_op jit(solution)/shard_map/ppermute | solution.py:18
  32.9 18.6 %copy-start.9 = (f32[12,256]{1,0:T(8,128)S(1)}, f32[12,256]{1,0:T(8,128)}, u32[]{:S(2)}) copy-start(f32[12,256]{1,0:T(8,128)} %param.25) | copy-start | bytes 36868
  51.6 11.2 %copy-start.4 = (bf16[2,32,384]{2,1,0:T(8,128)(2,1)S(1)}, bf16[2,32,384]{2,1,0:T(8,128)(2,1)}, u32[]{:S(2)}) copy-start(bf16[2,32,384]{2,1,0:T(8,128)(2,1)} %param.16) | copy-start | bytes 147460
  66.2 38.9 %reduce-scatter.5.cloned.1.call-start = ((), (), s32[]{:S(2)}) async-start(), calls=%async_computation.2 | async-start | bytes 163840 | tf_op jit(solution)/shard_map/reduce_scatter | solution.py:174
  68.1 3.4 %copy-start.8 = (bf16[192,256]{1,0:T(8,128)(2,1)S(1)}, bf16[192,256]{1,0:T(8,128)(2,1)}, u32[]{:S(2)}) copy-start(bf16[192,256]{1,0:T(8,128)(2,1)} %param.20) | copy-start | bytes 294916
  68.1 3.3 %copy-start.17 = (f32[1,256]{1,0:T(1,128)S(1)}, f32[1,256]{1,0:T(1,128)}, u32[]{:S(2)}) copy-start(f32[1,256]{1,0:T(1,128)} %get-tuple-element.105) | copy-start | bytes 3076
  68.2 17.8 %copy-start.14 = (f32[1,256]{1,0:T(1,128)S(1)}, f32[1,256]{1,0:T(1,128)}, u32[]{:S(2)}) copy-start(f32[1,256]{1,0:T(1,128)} %get-tuple-element.98) | copy-start | bytes 3076
  71.5 33.5 %copy-start.13 = (f32[1,256]{1,0:T(1,128)S(1)}, f32[1,256]{1,0:T(1,128)}, u32[]{:S(2)}) copy-start(f32[1,256]{1,0:T(1,128)} %get-tuple-element.103) | copy-start | bytes 3076
  86.0 7.9 %collective-permute-start.2 = (bf16[1,8,256]{2,1,0:T(8,128)(2,1)S(1)}, bf16[1,8,256]{2,1,0:T(8,128)(2,1)S(1)}, u32[]{:S(2)}, u32[]{:S(2)}) collective-permute-start(bf16[1,8,256]{2,1,0:T(8,128)(2,1)S(1)} %get-tuple-element.109), channel_id=1, source_target_pairs={{0,4},{4,8},{8,12},{1,5},{5,9},{9,13},{2,6},{6,10},{10,14},{3,7},{... | collective-permute-start | bytes 12296 | tf_op jit(solution)/shard_map/ppermute | solution.py:15
  91.9 5.1 %collective-permute-start.3 = (bf16[1,8,256]{2,1,0:T(8,128)(2,1)S(1)}, bf16[1,8,256]{2,1,0:T(8,128)(2,1)S(1)}, u32[]{:S(2)}, u32[]{:S(2)}) collective-permute-start(bf16[1,8,256]{2,1,0:T(8,128)(2,1)S(1)} %get-tuple-element.110), channel_id=1, source_target_pairs={{4,0},{8,4},{12,8},{5,1},{9,5},{13,9},{6,2},{10,6},{14,10},{7,3},{... | collective-permute-start | bytes 12296 | tf_op jit(solution)/shard_map/ppermute | solution.py:18
  97.0 2.6 %collective-permute-start.4 = (bf16[4,1,256]{2,1,0:T(2,128)(2,1)S(1)}, bf16[4,1,256]{2,1,0:T(2,128)(2,1)S(1)}, u32[]{:S(2)}, u32[]{:S(2)}) collective-permute-start(bf16[4,1,256]{2,1,0:T(2,128)(2,1)S(1)} %get-tuple-element.107), channel_id=1, source_target_pairs={{0,1},{1,2},{2,3},{4,5},{5,6},{6,7},{8,9},{9,10},{10,11},{12,13},{... | collective-permute-start | bytes 6152 | tf_op jit(solution)/shard_map/ppermute | solution.py:15
  98.3 4.4 %collective-permute-start.5 = (bf16[4,1,256]{2,1,0:T(2,128)(2,1)S(1)}, bf16[4,1,256]{2,1,0:T(2,128)(2,1)S(1)}, u32[]{:S(2)}, u32[]{:S(2)}) collective-permute-start(bf16[4,1,256]{2,1,0:T(2,128)(2,1)S(1)} %get-tuple-element.108), channel_id=1, source_target_pairs={{1,0},{2,1},{3,2},{5,4},{6,5},{7,6},{9,8},{10,9},{11,10},{13,12},{... | collective-permute-start | bytes 6152 | tf_op jit(solution)/shard_map/ppermute | solution.py:18
  106.1 9.1 %collective-permute-start.6 = (bf16[1,16,256]{2,1,0:T(8,128)(2,1)S(1)}, bf16[1,16,256]{2,1,0:T(8,128)(2,1)S(1)}, u32[]{:S(2)}, u32[]{:S(2)}) collective-permute-start(bf16[1,16,256]{2,1,0:T(8,128)(2,1)S(1)} %get-tuple-element.89), channel_id=1, source_target_pairs={{0,4},{4,8},{8,12},{1,5},{5,9},{9,13},{2,6},{6,10},{10,14},{3,7},{... | collective-permute-start | bytes 24584 | tf_op jit(solution)/shard_map/ppermute | solution.py:15
  112.1 5.0 %collective-permute-start.7 = (bf16[1,16,256]{2,1,0:T(8,128)(2,1)S(1)}, bf16[1,16,256]{2,1,0:T(8,128)(2,1)S(1)}, u32[]{:S(2)}, u32[]{:S(2)}) collective-permute-start(bf16[1,16,256]{2,1,0:T(8,128)(2,1)S(1)} %get-tuple-element.90), channel_id=1, source_target_pairs={{4,0},{8,4},{12,8},{5,1},{9,5},{13,9},{6,2},{10,6},{14,10},{7,3},{... | collective-permute-start | bytes 24584 | tf_op jit(solution)/shard_map/ppermute | solution.py:18
  115.1 9.2 %copy-start.12 = (f32[1,256]{1,0:T(1,128)S(1)}, f32[1,256]{1,0:T(1,128)}, u32[]{:S(2)}) copy-start(f32[1,256]{1,0:T(1,128)} %get-tuple-element.106) | copy-start | bytes 3076
  117.1 2.8 %collective-permute-start.8 = (bf16[6,1,256]{2,1,0:T(2,128)(2,1)S(1)}, bf16[6,1,256]{2,1,0:T(2,128)(2,1)S(1)}, u32[]{:S(2)}, u32[]{:S(2)}) collective-permute-start(bf16[6,1,256]{2,1,0:T(2,128)(2,1)S(1)} %get-tuple-element.81), channel_id=1, source_target_pairs={{0,1},{1,2},{2,3},{4,5},{5,6},{6,7},{8,9},{9,10},{10,11},{12,13},{... | collective-permute-start | bytes 9224 | tf_op jit(solution)/shard_map/ppermute | solution.py:15
  118.4 4.4 %collective-permute-start.9 = (bf16[6,1,256]{2,1,0:T(2,128)(2,1)S(1)}, bf16[6,1,256]{2,1,0:T(2,128)(2,1)S(1)}, u32[]{:S(2)}, u32[]{:S(2)}) collective-permute-start(bf16[6,1,256]{2,1,0:T(2,128)(2,1)S(1)} %get-tuple-element.82), channel_id=1, source_target_pairs={{1,0},{2,1},{3,2},{5,4},{6,5},{7,6},{9,8},{10,9},{11,10},{13,12},{... | collective-permute-start | bytes 9224 | tf_op jit(solution)/shard_map/ppermute | solution.py:18
  122.9 7.2 %copy-start.6 = (bf16[8,32,384]{2,1,0:T(8,128)(2,1)S(1)}, bf16[8,32,384]{2,1,0:T(8,128)(2,1)}, u32[]{:S(2)}) copy-start(bf16[8,32,384]{2,1,0:T(8,128)(2,1)} %param.14) | copy-start | bytes 589828
  122.9 7.2 %copy-start.7 = (bf16[384,256]{1,0:T(8,128)(2,1)S(1)}, bf16[384,256]{1,0:T(8,128)(2,1)}, u32[]{:S(2)}) copy-start(bf16[384,256]{1,0:T(8,128)(2,1)} %param.21) | copy-start | bytes 589828
  122.9 7.2 %copy-start.11 = (f32[1,256]{1,0:T(1,128)S(1)}, f32[1,256]{1,0:T(1,128)}, u32[]{:S(2)}) copy-start(f32[1,256]{1,0:T(1,128)} %get-tuple-element.104) | copy-start | bytes 3076
  124.4 6.0 %collective-permute-start.22 = (bf16[1,16,256]{2,1,0:T(8,128)(2,1)S(1)}, bf16[1,16,256]{2,1,0:T(8,128)(2,1)S(1)}, u32[]{:S(2)}, u32[]{:S(2)}) collective-permute-start(bf16[1,16,256]{2,1,0:T(8,128)(2,1)S(1)} %get-tuple-element.85), channel_id=1, source_target_pairs={{0,4},{4,8},{8,12},{1,5},{5,9},{9,13},{2,6},{6,10},{10,14},{3,7},{... | collective-permute-start | bytes 24584 | tf_op jit(solution)/shard_map/ppermute | solution.py:15
  127.5 5.0 %collective-permute-start.23 = (bf16[1,16,256]{2,1,0:T(8,128)(2,1)S(1)}, bf16[1,16,256]{2,1,0:T(8,128)(2,1)S(1)}, u32[]{:S(2)}, u32[]{:S(2)}) collective-permute-start(bf16[1,16,256]{2,1,0:T(8,128)(2,1)S(1)} %get-tuple-element.86), channel_id=1, source_target_pairs={{4,0},{8,4},{12,8},{5,1},{9,5},{13,9},{6,2},{10,6},{14,10},{7,3},{... | collective-permute-start | bytes 24584 | tf_op jit(solution)/shard_map/ppermute | solution.py:18
  132.5 9.0 %collective-permute-start.24 = (bf16[6,1,256]{2,1,0:T(2,128)(2,1)S(1)}, bf16[6,1,256]{2,1,0:T(2,128)(2,1)S(1)}, u32[]{:S(2)}, u32[]{:S(2)}) collective-permute-start(bf16[6,1,256]{2,1,0:T(2,128)(2,1)S(1)} %get-tuple-element.77), channel_id=1, source_target_pairs={{0,1},{1,2},{2,3},{4,5},{5,6},{6,7},{8,9},{9,10},{10,11},{12,13},{... | collective-permute-start | bytes 9224 | tf_op jit(solution)/shard_map/ppermute | solution.py:15
  135.9 5.7 %collective-permute-start.25 = (bf16[6,1,256]{2,1,0:T(2,128)(2,1)S(1)}, bf16[6,1,256]{2,1,0:T(2,128)(2,1)S(1)}, u32[]{:S(2)}, u32[]{:S(2)}) collective-permute-start(bf16[6,1,256]{2,1,0:T(2,128)(2,1)S(1)} %get-tuple-element.78), channel_id=1, source_target_pairs={{1,0},{2,1},{3,2},{5,4},{6,5},{7,6},{9,8},{10,9},{11,10},{13,12},{... | collective-permute-start | bytes 9224 | tf_op jit(solution)/shard_map/ppermute | solution.py:18
  137.2 6.0 %collective-permute-start.10 = (bf16[1,32,256]{2,1,0:T(8,128)(2,1)S(1)}, bf16[1,32,256]{2,1,0:T(8,128)(2,1)S(1)}, u32[]{:S(2)}, u32[]{:S(2)}) collective-permute-start(bf16[1,32,256]{2,1,0:T(8,128)(2,1)S(1)} %get-tuple-element.65), channel_id=1, source_target_pairs={{0,4},{4,8},{8,12},{1,5},{5,9},{9,13},{2,6},{6,10},{10,14},{3,7},{... | collective-permute-start | bytes 49160 | tf_op jit(solution)/shard_map/ppermute | solution.py:15
  139.4 5.1 %collective-permute-start.11 = (bf16[1,32,256]{2,1,0:T(8,128)(2,1)S(1)}, bf16[1,32,256]{2,1,0:T(8,128)(2,1)S(1)}, u32[]{:S(2)}, u32[]{:S(2)}) collective-permute-start(bf16[1,32,256]{2,1,0:T(8,128)(2,1)S(1)} %get-tuple-element.66), channel_id=1, source_target_pairs={{4,0},{8,4},{12,8},{5,1},{9,5},{13,9},{6,2},{10,6},{14,10},{7,3},{... | collective-permute-start | bytes 49160 | tf_op jit(solution)/shard_map/ppermute | solution.py:18
  144.5 6.0 %collective-permute-start.12 = (bf16[10,1,256]{2,1,0:T(2,128)(2,1)S(1)}, bf16[10,1,256]{2,1,0:T(2,128)(2,1)S(1)}, u32[]{:S(2)}, u32[]{:S(2)}) collective-permute-start(bf16[10,1,256]{2,1,0:T(2,128)(2,1)S(1)} %get-tuple-element.50), channel_id=1, source_target_pairs={{0,1},{1,2},{2,3},{4,5},{5,6},{6,7},{8,9},{9,10},{10,11},{12,13},{... | collective-permute-start | bytes 15368 | tf_op jit(solution)/shard_map/ppermute | solution.py:15
  148.8 4.4 %collective-permute-start.13 = (bf16[10,1,256]{2,1,0:T(2,128)(2,1)S(1)}, bf16[10,1,256]{2,1,0:T(2,128)(2,1)S(1)}, u32[]{:S(2)}, u32[]{:S(2)}) collective-permute-start(bf16[10,1,256]{2,1,0:T(2,128)(2,1)S(1)} %get-tuple-element.51), channel_id=1, source_target_pairs={{1,0},{2,1},{3,2},{5,4},{6,5},{7,6},{9,8},{10,9},{11,10},{13,12},{... | collective-permute-start | bytes 15368 | tf_op jit(solution)/shard_map/ppermute | solution.py:18
  155.0 6.4 %copy-start.3 = (f32[16,64,256]{2,1,0:T(8,128)S(1)}, f32[16,64,256]{2,1,0:T(8,128)}, u32[]{:S(2)}) copy-start(f32[16,64,256]{2,1,0:T(8,128)} %fusion.8) | copy-start | bytes 3145732
  155.8 7.0 %collective-permute-start.18 = (bf16[1,32,256]{2,1,0:T(8,128)(2,1)S(1)}, bf16[1,32,256]{2,1,0:T(8,128)(2,1)S(1)}, u32[]{:S(2)}, u32[]{:S(2)}) collective-permute-start(bf16[1,32,256]{2,1,0:T(8,128)(2,1)S(1)} %get-tuple-element.61), channel_id=1, source_target_pairs={{0,4},{4,8},{8,12},{1,5},{5,9},{9,13},{2,6},{6,10},{10,14},{3,7},{... | collective-permute-start | bytes 49160 | tf_op jit(solution)/shard_map/ppermute | solution.py:15
  159.5 5.1 %collective-permute-start.19 = (bf16[1,32,256]{2,1,0:T(8,128)(2,1)S(1)}, bf16[1,32,256]{2,1,0:T(8,128)(2,1)S(1)}, u32[]{:S(2)}, u32[]{:S(2)}) collective-permute-start(bf16[1,32,256]{2,1,0:T(8,128)(2,1)S(1)} %get-tuple-element.62), channel_id=1, source_target_pairs={{4,0},{8,4},{12,8},{5,1},{9,5},{13,9},{6,2},{10,6},{14,10},{7,3},{... | collective-permute-start | bytes 49160 | tf_op jit(solution)/shard_map/ppermute | solution.py:18
  164.6 7.8 %collective-permute-start.20 = (bf16[10,1,256]{2,1,0:T(2,128)(2,1)S(1)}, bf16[10,1,256]{2,1,0:T(2,128)(2,1)S(1)}, u32[]{:S(2)}, u32[]{:S(2)}) collective-permute-start(bf16[10,1,256]{2,1,0:T(2,128)(2,1)S(1)} %get-tuple-element.46), channel_id=1, source_target_pairs={{0,1},{1,2},{2,3},{4,5},{5,6},{6,7},{8,9},{9,10},{10,11},{12,13},{... | collective-permute-start | bytes 15368 | tf_op jit(solution)/shard_map/ppermute | solution.py:15
  166.7 5.7 %collective-permute-start.21 = (bf16[10,1,256]{2,1,0:T(2,128)(2,1)S(1)}, bf16[10,1,256]{2,1,0:T(2,128)(2,1)S(1)}, u32[]{:S(2)}, u32[]{:S(2)}) collective-permute-start(bf16[10,1,256]{2,1,0:T(2,128)(2,1)S(1)} %get-tuple-element.47), channel_id=1, source_target_pairs={{1,0},{2,1},{3,2},{5,4},{6,5},{7,6},{9,8},{10,9},{11,10},{13,12},{... | collective-permute-start | bytes 15368 | tf_op jit(solution)/shard_map/ppermute | solution.py:18
  168.0 6.5 %collective-permute-start.14 = (bf16[1,64,256]{2,1,0:T(8,128)(2,1)S(1)}, bf16[1,64,256]{2,1,0:T(8,128)(2,1)S(1)}, u32[]{:S(2)}, u32[]{:S(2)}) collective-permute-start(bf16[1,64,256]{2,1,0:T(8,128)(2,1)S(1)} %get-tuple-element.34), channel_id=1, source_target_pairs={{0,4},{4,8},{8,12},{1,5},{5,9},{9,13},{2,6},{6,10},{10,14},{3,7},{... | collective-permute-start | bytes 98312 | tf_op jit(solution)/shard_map/ppermute | solution.py:15
  170.2 5.2 %collective-permute-start.15 = (bf16[1,64,256]{2,1,0:T(8,128)(2,1)S(1)}, bf16[1,64,256]{2,1,0:T(8,128)(2,1)S(1)}, u32[]{:S(2)}, u32[]{:S(2)}) collective-permute-start(bf16[1,64,256]{2,1,0:T(8,128)(2,1)S(1)} %get-tuple-element.35), channel_id=1, source_target_pairs={{4,0},{8,4},{12,8},{5,1},{9,5},{13,9},{6,2},{10,6},{14,10},{7,3},{... | collective-permute-start | bytes 98312 | tf_op jit(solution)/shard_map/ppermute | solution.py:18
  172.8 8.4 %copy-start.2 = (bf16[3,3,256,256]{3,2,1,0:T(8,128)(2,1)S(1)}, bf16[3,3,256,256]{3,2,1,0:T(8,128)(2,1)}, u32[]{:S(2)}) copy-start(bf16[3,3,256,256]{3,2,1,0:T(8,128)(2,1)} %get-tuple-element.5) | copy-start | bytes 3538948
  175.5 6.0 %collective-permute-start.16 = (bf16[18,1,256]{2,1,0:T(2,128)(2,1)S(1)}, bf16[18,1,256]{2,1,0:T(2,128)(2,1)S(1)}, u32[]{:S(2)}, u32[]{:S(2)}) collective-permute-start(bf16[18,1,256]{2,1,0:T(2,128)(2,1)S(1)} %get-tuple-element.30), channel_id=1, source_target_pairs={{0,1},{1,2},{2,3},{4,5},{5,6},{6,7},{8,9},{9,10},{10,11},{12,13},{... | collective-permute-start | bytes 27656 | tf_op jit(solution)/shard_map/ppermute | solution.py:15
  179.8 4.5 %collective-permute-start.17 = (bf16[18,1,256]{2,1,0:T(2,128)(2,1)S(1)}, bf16[18,1,256]{2,1,0:T(2,128)(2,1)S(1)}, u32[]{:S(2)}, u32[]{:S(2)}) collective-permute-start(bf16[18,1,256]{2,1,0:T(2,128)(2,1)S(1)} %get-tuple-element.31), channel_id=1, source_target_pairs={{1,0},{2,1},{3,2},{5,4},{6,5},{7,6},{9,8},{10,9},{11,10},{13,12},{... | collective-permute-start | bytes 27656 | tf_op jit(solution)/shard_map/ppermute | solution.py:18
  187.0 7.4 %slice-start = ((s8[4718592]{0:T(1024)(128)(4,1)}), s8[4194304]{0:T(1024)(128)(4,1)S(1)}, s32[]{:S(2)}) async-start(s8[4718592]{0:T(1024)(128)(4,1)} %bitcast.439), calls=%async_computation.4 | async-start | bytes 8388608
  187.3 7.1 %slice-start.1 = ((s8[4718592]{0:T(1024)(128)(4,1)}), s8[524288]{0:T(1024)(128)(4,1)S(1)}, s32[]{:S(2)}) async-start(s8[4718592]{0:T(1024)(128)(4,1)} %bitcast.439), calls=%async_computation.5 | async-start | bytes 1048576
  188.5 6.7 %collective-permute-start.26 = (bf16[1,64,1024]{2,1,0:T(8,128)(2,1)S(1)}, bf16[1,64,1024]{2,1,0:T(8,128)(2,1)S(1)}, u32[]{:S(2)}, u32[]{:S(2)}) collective-permute-start(bf16[1,64,1024]{2,1,0:T(8,128)(2,1)S(1)} %get-tuple-element.20), channel_id=1, source_target_pairs={{0,4},{4,8},{8,12},{1,5},{5,9},{9,13},{2,6},{6,10},{10,14},{3,7},{... | collective-permute-start | bytes 393224 | tf_op jit(solution)/shard_map/ppermute | solution.py:15
  192.5 6.3 %collective-permute-start.27 = (bf16[1,64,1024]{2,1,0:T(8,128)(2,1)S(1)}, bf16[1,64,1024]{2,1,0:T(8,128)(2,1)S(1)}, u32[]{:S(2)}, u32[]{:S(2)}) collective-permute-start(bf16[1,64,1024]{2,1,0:T(8,128)(2,1)S(1)} %get-tuple-element.21), channel_id=1, source_target_pairs={{4,0},{8,4},{12,8},{5,1},{9,5},{13,9},{6,2},{10,6},{14,10},{7,3},{... | collective-permute-start | bytes 393224 | tf_op jit(solution)/shard_map/ppermute | solution.py:18
  198.9 5.2 %collective-permute-start.28 = (bf16[18,1,1024]{2,1,0:T(2,128)(2,1)S(1)}, bf16[18,1,1024]{2,1,0:T(2,128)(2,1)S(1)}, u32[]{:S(2)}, u32[]{:S(2)}) collective-permute-start(bf16[18,1,1024]{2,1,0:T(2,128)(2,1)S(1)} %get-tuple-element.16), channel_id=1, source_target_pairs={{0,1},{1,2},{2,3},{4,5},{5,6},{6,7},{8,9},{9,10},{10,11},{12,13},{... | collective-permute-start | bytes 110600 | tf_op jit(solution)/shard_map/ppermute | solution.py:15
  200.6 5.1 %collective-permute-start.29 = (bf16[18,1,1024]{2,1,0:T(2,128)(2,1)S(1)}, bf16[18,1,1024]{2,1,0:T(2,128)(2,1)S(1)}, u32[]{:S(2)}, u32[]{:S(2)}) collective-permute-start(bf16[18,1,1024]{2,1,0:T(2,128)(2,1)S(1)} %get-tuple-element.17), channel_id=1, source_target_pairs={{1,0},{2,1},{3,2},{5,4},{6,5},{7,6},{9,8},{10,9},{11,10},{13,12},{... | collective-permute-start | bytes 110600 | tf_op jit(solution)/shard_map/ppermute | solution.py:18
  (4 other events, 4.2 us)
Sparse Core Ops, SparseCore 0:
  66.3 18.9 reduce-scatter.6
  87.5 17.4 reduce-scatter.4
where the time goes:
time: 227 us; the launch traced here: 226 us
  starting transfers between devices  75.2 us (33%)
  waiting for transfers between devices  41.8 us (18%)
  matrix products  33.9 us (15%)
  blocking collectives  26 us (11%)
  other arithmetic  19.2 us (8%)
  between operations  15.2 us (7%)
  local copies, waits for them, and re-layouts  14.4 us (6%)
    ppermute x15, starting transfers between devices, with_halo(): lax.ppermute(lax.slice_in_dim(block, block.shape[dim] - width, None, axis...  50 us
    ppermute x15, waiting for transfers between devices, with_halo(): lax.ppermute(lax.slice_in_dim(block, 0, width, axis=dim), axis, backward)  27.5 us
    ppermute x15, starting transfers between devices, with_halo(): lax.ppermute(lax.slice_in_dim(block, 0, width, axis=dim), axis, backward)  25.2 us
    psum x1, blocking collectives, local(): lax.psum(bin_terms(pooled_split).astype(jnp.bfloat16), 'col')  15.5 us
    dot_general x45, matrix products, taps_sum(): jnp.dot(window, weight[row_tap, col_tap], preferred_element_type=jnp.floa...  13.8 us
    unnamed x3, waiting for transfers between devices  12.5 us
    psum x1, blocking collectives, local(): lax.psum(jnp.concatenate(pooled_parts, axis=0).astype(jnp.bfloat16), 'row')  10.5 us
    concatenate x13, other arithmetic, with_halo(): block = jnp.concatenate([low, block, high], axis=dim)  6.99 us
  transfers between devices with their start and end apart: 32, of which 14 were waited for; matrix products, arithmetic and copies ran while one was open for 18% of the time, Pallas kernels for 0%

commit v1 on v0

v1 whole, which is shorter than its diff:
```python
import jax
import jax.numpy as jnp
from jax import lax
from jax.sharding import PartitionSpec as P

highest = lax.Precision.HIGHEST
bin_sides = (1, 2, 3, 6)
rim = 2
f32 = jnp.float32
bf16 = jnp.bfloat16


def others(value, axis):
    count = lax.axis_size(axis)
    for shift in range(1, count):
        yield lax.ppermute(value, axis, [(i, (i + shift) % count) for i in range(count)])


def windows_sum(padded, axis, dim, pitch, width, join):
    count = lax.axis_size(axis)
    here = lax.axis_index(axis)

    def window_for(target):
        return lax.dynamic_slice_in_dim(padded, target * pitch, width, dim)

    pieces = [window_for(here)]
    for shift in range(1, count):
        target = lax.rem(here + shift, count)
        pieces.append(
            lax.ppermute(window_for(target), axis, [(i, (i + shift) % count) for i in range(count)])
        )
    return join(pieces)


def edge_swap(low_out, high_out, axis):
    count = lax.axis_size(axis)
    forward = [(i, i + 1) for i in range(count - 1)]
    backward = [(target, source) for source, target in forward]
    return lax.ppermute(high_out, axis, forward), lax.ppermute(low_out, axis, backward)


def cell_table(size):
    branch, row, col = [], [], []
    for number, side in enumerate(bin_sides):
        for i in range(side):
            for j in range(side):
                branch.append(number)
                row.append(i)
                col.append(j)
    return (
        jnp.array(branch, jnp.int32),
        jnp.array(row, jnp.int32),
        jnp.array(col, jnp.int32),
        jnp.array([bin_sides[b] for b in branch], jnp.int32),
    )


def pool_inside(index, side, extent):
    position = jnp.arange(extent, dtype=jnp.int32)[None, :]
    first = (index * extent // side)[:, None]
    end = (((index + 1) * extent + side - 1) // side)[:, None]
    inside = ((position >= first) & (position < end)).astype(f32)
    return inside, (end - first).astype(f32)


def spread_weights(position, index, side, extent):
    sides = side.astype(f32)[None, :]
    source = (position.astype(f32)[:, None] + 0.5) * sides / extent - 0.5
    source = jnp.minimum(jnp.maximum(source, 0.0), sides - 1.0)
    return jnp.maximum(0.0, 1.0 - jnp.abs(source - index.astype(f32)[None, :]))


def stretch(first_out, length_out, first_in, length_in, factor, extent):
    output = (first_out + jnp.arange(length_out, dtype=jnp.int32)).astype(f32)
    source = jnp.clip((output + 0.5) / factor - 0.5, 0.0, extent - 1.0)
    targets = (first_in + jnp.arange(length_in, dtype=jnp.int32)).astype(f32)
    inside = ((output >= 0.0) & (output < extent * factor)).astype(f32)
    return jnp.maximum(0.0, 1.0 - jnp.abs(source[:, None] - targets[None, :])) * inside[:, None]


def conv(feature, weight, padding):
    return lax.conv_general_dilated(
        feature[None],
        weight,
        (1, 1),
        padding,
        dimension_numbers=("NHWC", "HWIO", "NHWC"),
        preferred_element_type=f32,
    )[0]


def project(feature, weight):
    height, breadth, channels = feature.shape
    result = jnp.dot(
        feature.reshape(height * breadth, channels), weight, preferred_element_type=f32
    )
    return result.reshape(height, breadth, -1)


def local(
    level_one,
    level_two,
    level_three,
    level_four,
    bin_weight,
    neck_feature,
    neck_pooled,
    lateral_one,
    lateral_two,
    lateral_three,
    smooth_weight,
    join_weight,
    biases,
):
    row_here = lax.axis_index("row")
    col_here = lax.axis_index("col")
    row_count = lax.axis_size("row")
    col_count = lax.axis_size("col")
    rows4, grid_cols, part_four = level_four.shape
    grid_rows = rows4 * row_count
    cols4 = grid_cols // col_count
    channels = bin_weight.shape[2]

    four = lax.all_gather(level_four, "row", axis=0, tiled=True)
    branch, cell_row, cell_col, cell_side = cell_table(None)
    cells = branch.shape[0]
    in_rows, row_size = pool_inside(cell_row, cell_side, grid_rows)
    in_cols, col_size = pool_inside(cell_col, cell_side, grid_cols)
    inside = (in_rows[:, :, None] * in_cols[:, None, :]).reshape(cells, -1).astype(bf16)
    pooled = jnp.dot(inside, four.reshape(-1, part_four), preferred_element_type=f32)
    pooled = (pooled / (row_size * col_size)).astype(bf16)
    terms = []
    offset = 0
    for number, side in enumerate(bin_sides):
        terms.append(
            jnp.dot(
                pooled[offset : offset + side * side],
                bin_weight[number],
                preferred_element_type=f32,
            )
        )
        offset += side * side
    bin_term = jnp.concatenate(terms, axis=0).astype(bf16)
    bin_total = bin_term.astype(f32)
    for other in others(bin_term, "col"):
        bin_total = bin_total + other.astype(f32)

    lat_one = jax.nn.relu(project(level_one, lateral_one) + biases[5]).astype(bf16)
    lat_two = jax.nn.relu(project(level_two, lateral_two) + biases[6]).astype(bf16)
    cols3 = level_three.shape[1] // col_count
    three_wide = windows_sum(
        jnp.pad(level_three, ((0, 0), (rim, rim), (0, 0))),
        "col",
        1,
        cols3,
        cols3 + 2 * rim,
        lambda pieces: pieces,
    )
    share_three = level_three.shape[2]
    three_sum = jnp.zeros((), f32)
    for shift, piece in enumerate(three_wide):
        source = lax.rem(col_here - shift + col_count, col_count)
        weight = lax.dynamic_slice_in_dim(lateral_three, source * share_three, share_three, 0)
        three_sum = three_sum + project(piece, weight)
    lat_three = jax.nn.relu(three_sum + biases[7])
    rows3 = level_three.shape[0]
    first_col3 = col_here * cols3 - rim
    place = first_col3 + jnp.arange(cols3 + 2 * rim, dtype=jnp.int32)
    in_three = ((place >= 0) & (place < cols3 * col_count))[None, :, None]
    lat_three = jnp.where(in_three, lat_three, 0.0).astype(bf16)

    levels = [lat_one, lat_two, lat_three]

    def pack(parts):
        return jnp.concatenate([p.reshape(-1, channels) for p in parts], axis=0)

    def unpack(packed, shapes):
        result, start = [], 0
        for shape in shapes:
            size = shape[0] * shape[1]
            result.append(packed[start : start + size].reshape(shape + (channels,)))
            start += size
        return result

    shapes = [(rim, level.shape[1]) for level in levels]
    above, below = edge_swap(
        pack([level[:rim] for level in levels]), pack([level[-rim:] for level in levels]), "row"
    )
    levels = [
        jnp.concatenate([a, level, b], axis=0)
        for a, level, b in zip(unpack(above, shapes), levels, unpack(below, shapes))
    ]
    sided = levels[:2]
    shapes = [(level.shape[0], rim) for level in sided]
    before, after = edge_swap(
        pack([level[:, :rim] for level in sided]), pack([level[:, -rim:] for level in sided]), "col"
    )
    wide_one, wide_two = [
        jnp.concatenate([a, level, b], axis=1)
        for a, level, b in zip(unpack(before, shapes), sided, unpack(after, shapes))
    ]
    wide_three = levels[2]

    first_row = row_here * rows4
    span = rows4 + 2 * rim + 2
    place_rows = first_row - rim - 1 + jnp.arange(span, dtype=jnp.int32)
    in_grid = ((place_rows >= 0) & (place_rows < grid_rows)).astype(f32)
    four_span = lax.dynamic_slice_in_dim(
        jnp.pad(four, ((rim + 1, rim + 1), (0, 0), (0, 0))), first_row, span, 0
    )
    binned = jax.nn.relu(bin_total + biases[branch])
    spread_rows = spread_weights(place_rows, cell_row, cell_side, grid_rows) * in_grid[:, None]
    spread_cols = spread_weights(
        jnp.arange(grid_cols, dtype=jnp.int32), cell_col, cell_side, grid_cols
    )
    spread = (spread_rows[:, None, :] * spread_cols[None, :, :]).reshape(-1, cells)
    share_ppm = neck_pooled.shape[2]
    branches = len(bin_sides)
    lane_branch = jnp.arange(branches * channels, dtype=jnp.int32) // channels
    sorted_bins = jnp.where(
        branch[:, None] == lane_branch[None, :], jnp.tile(binned, (1, branches)), 0.0
    )
    sorted_bins = lax.dynamic_slice_in_dim(sorted_bins, col_here * share_ppm, share_ppm, 1)
    ppm = jnp.dot(spread, sorted_bins, precision=highest).astype(bf16)
    ppm = ppm.reshape(span, grid_cols, share_ppm)
    around = ((0, 0), (1, 1))
    neck_term = conv(four_span, neck_feature, around) + conv(ppm, neck_pooled, around)
    neck_pad = jnp.pad(neck_term.astype(bf16), ((0, 0), (rim, rim), (0, 0)))
    top_sum = windows_sum(
        neck_pad,
        "col",
        1,
        cols4,
        cols4 + 2 * rim,
        lambda pieces: sum(p.astype(f32) for p in pieces),
    )
    top = jax.nn.relu(top_sum + biases[4]).astype(bf16)

    def upscale(source, level_rows, level_cols, factor, border_in, border_out):
        high, wide = source.shape[0], source.shape[1]
        out_high = level_rows * factor + 2 * border_out
        out_wide = level_cols * factor + 2 * border_out
        down = stretch(
            row_here * level_rows * factor - border_out,
            out_high,
            row_here * level_rows - border_in,
            high,
            factor,
            level_rows * row_count,
        )
        across = stretch(
            col_here * level_cols * factor - border_out,
            out_wide,
            col_here * level_cols - border_in,
            wide,
            factor,
            level_cols * col_count,
        )
        matrix = (down[:, None, :, None] * across[None, :, None, :]).reshape(
            out_high * out_wide, high * wide
        )
        result = jnp.dot(
            matrix.astype(bf16), source.reshape(high * wide, -1), preferred_element_type=f32
        )
        return result.reshape(out_high, out_wide, -1)

    rows2, cols2 = level_two.shape[0], level_two.shape[1]
    rows1, cols1 = level_one.shape[0], level_one.shape[1]
    pyr_three = (wide_three.astype(f32) + upscale(top, rows4, cols4, 2, rim, rim)).astype(bf16)
    pyr_two = (wide_two.astype(f32) + upscale(pyr_three, rows3, cols3, 2, rim, rim)).astype(bf16)
    pyr_one = (wide_one.astype(f32) + upscale(pyr_two, rows2, cols2, 2, rim, rim)).astype(bf16)
    valid = ((0, 0), (0, 0))
    smooth_one = jax.nn.relu(conv(pyr_one, smooth_weight[0], valid) + biases[8])
    smooth_two = jax.nn.relu(conv(pyr_two, smooth_weight[1], valid) + biases[9]).astype(bf16)
    smooth_three = jax.nn.relu(conv(pyr_three, smooth_weight[2], valid) + biases[10]).astype(bf16)

    def in_image(length, here, count):
        place = here * length - 1 + jnp.arange(length + 2, dtype=jnp.int32)
        return (place >= 0) & (place < length * count)

    mask = (
        in_image(rows1, row_here, row_count)[:, None] & in_image(cols1, col_here, col_count)[None, :]
    )
    smooth_one = jnp.where(mask[:, :, None], smooth_one, 0.0).astype(bf16)
    stacked_top = jnp.concatenate(
        [
            smooth_one,
            upscale(smooth_two, rows2, cols2, 2, 1, 1).astype(bf16),
            upscale(smooth_three, rows3, cols3, 4, 1, 1).astype(bf16),
            upscale(top, rows4, cols4, 8, rim, 1).astype(bf16),
        ],
        axis=2,
    )
    return jax.nn.relu(conv(stacked_top, join_weight, valid) + biases[11]).astype(bf16)


def solution(mesh):
    placed = (
        P(("grp", "row"), "col", None),
        P(("grp", "row"), "col", None),
        P(("grp", "row"), None, "col"),
        P(("grp", "row"), None, "col"),
        P(None, "col", None),
        P(None, None, "col", None),
        P(None, None, "col", None),
        P(),
        P(),
        P(),
        P(),
        P(),
        P(),
    )
    return jax.shard_map(
        local, mesh=mesh, in_specs=placed, out_specs=P(("grp", "row"), "col", None), check_vma=False
    )
```

time: 227 us -> 113 us (0.50)
  starting transfers between devices: 75.2 us -> 25.4 us
  waiting for transfers between devices: 41.8 us -> 0.77 us
  blocking collectives: 26 us -> 7.06 us
  between operations: 15.2 us -> 1.36 us
  local copies, waits for them, and re-layouts: 14.4 us -> 25.5 us
    ppermute x30 -> x13, starting transfers between devices: 75.2 us -> 25.4 us  [the longest x2 7.6 us: edge_swap(): lax.ppermute(high_out, axis, forward)]
    ppermute x30 -> x13, waiting for transfers between devices: 27.6 us -> 0.77 us  [the longest x2 0.73 us: edge_swap(): lax.ppermute(high_out, axis, forward)]
    psum x2 -> x0, blocking collectives: 26 us -> none  [the longest x1 15.5 us: local(): lax.psum(bin_terms(pooled_split).astype(jnp.bfloat16), 'col')]
    dot_general x75 -> x12, matrix products: 30.6 us -> 12.3 us  [the longest x6 6.07 us: upscale(): jnp.dot(matrix.astype(bf16), source.reshape(high * wide, -1), preferred_e...]
    conv_general_dilated x0 -> x6, matrix products: none -> 15.8 us  [conv(): lax.conv_general_dilated(feature[None], weight, (1, 1), padding, dimensio...]
    unnamed x3 -> x0, waiting for transfers between devices: 12.5 us -> none
    all_gather x0 -> x1, blocking collectives: none -> 7.06 us  [local(): four = lax.all_gather(level_four, 'row', axis=0, tiled=True)]
    concatenate x28 -> x5, other arithmetic: 9.23 us -> 2.52 us  [the longest x4 1.9 us: pack(): return jnp.concatenate([p.reshape(-1, channels) for p in parts], axis=0)]
  transfers between devices with their start and end apart: 32 -> 13, of which waited for: 14 -> 1; matrix products, arithmetic and copies ran while one was open for 18% -> 33% of each run, Pallas kernels for 0% -> 0%
where the time goes in v1:
time: 113 us; the launch traced here: 111 us
  matrix products  32 us (28%)
  local copies, waits for them, and re-layouts  25.5 us (23%)
  starting transfers between devices  25.4 us (22%)
  other arithmetic  19.2 us (17%)
  blocking collectives  7.06 us (6%)
  between operations  1.36 us (1%)
    conv_general_dilated x6, matrix products, conv(): lax.conv_general_dilated(feature[None], weight, (1, 1), padding, dimensio...  15.8 us
    ppermute x2, starting transfers between devices, edge_swap(): lax.ppermute(high_out, axis, forward)  7.6 us
    all_gather x1, blocking collectives, local(): four = lax.all_gather(level_four, 'row', axis=0, tiled=True)  7.06 us
    ppermute x6, starting transfers between devices, windows_sum(): lax.ppermute(window_for(target), axis, [(i, (i + shift) % count) for i in...  6.53 us
    dot_general x6, matrix products, upscale(): jnp.dot(matrix.astype(bf16), source.reshape(high * wide, -1), preferred_e...  6.07 us
    ppermute x3, starting transfers between devices, others(): lax.ppermute(value, axis, [(i, (i + shift) % count) for i in range(count)])  5.78 us
    ppermute x2, starting transfers between devices, edge_swap(): lax.ppermute(low_out, axis, backward)  5.54 us
    slice x10, local copies, waits for them, and re-layouts, unpack(): result.append(packed[start:start + size].reshape(shape + (channels,)))  5.34 us
  transfers between devices with their start and end apart: 13, of which 1 were waited for; matrix products, arithmetic and copies ran while one was open for 33% of the time, Pallas kernels for 0%

profile of v1, /device:TPU:1, one launch (start us, length us, event | category | flops | bytes accessed | tf_op | source)
XLA Modules:
  0.0 111.3 jit_solution(11040737455989784107)
XLA Ops:
  0.0 7.1 %all_gather.3 = bf16[8,32,384]{2,1,0:T(8,128)(2,1)S(1)} all-gather(bf16[2,32,384]{2,1,0:T(8,128)(2,1)} %param.20), channel_id=1, replica_groups=mesh['grp'=2,'row'=4,'col'=4] {'row'}, dimensions={0}, use_global_device_ids=true | all-gather | bytes 245760 | tf_op jit(solution)/shard_map/all_gather | solution.py:124
  8.4 0.8 fusion.56
  9.3 1.1 fusion.105
  10.3 1.1 convolution_convert_fusion.5
  11.4 1.1 convolution_convert_fusion.4
  12.5 1.1 %convolution_convert_fusion.3 = bf16[36,256]{1,0:T(8,128)(2,1)S(1)} fusion(bf16[4,384,256]{2,1,0:T(8,128)(2,1)} %param.21, bf16[50,384]{1,0:T(8,128)(2,1)S(1)} %fusion.56), kind=kOutput, calls=%fused_computation.70 | convolution fusion | flops 7087104 | bytes 245760 | tf_op jit(solution)/shard_map/dot_general | solution.py:136
  14.3 2.5 %collective-permute-start.8 = (bf16[50,256]{1,0:T(8,128)(2,1)}, bf16[50,256]{1,0:T(8,128)(2,1)}, u32[]{:S(2)}, u32[]{:S(2)}) collective-permute-start(bf16[50,256]{1,0:T(8,128)(2,1)} %pad_maximum_fusion.4), channel_id=1, source_target_pairs={{0,2},{1,3},{2,0},{3,1},{4,6},{5,7},{6,4},{7,5},{8,10},{9,11},{10,... | collective-permute-start | bytes 76808 | tf_op jit(solution)/shard_map/ppermute | solution.py:16
  16.8 1.3 %collective-permute-start.7 = (bf16[50,256]{1,0:T(8,128)(2,1)}, bf16[50,256]{1,0:T(8,128)(2,1)}, u32[]{:S(2)}, u32[]{:S(2)}) collective-permute-start(bf16[50,256]{1,0:T(8,128)(2,1)} %pad_maximum_fusion.4), channel_id=1, source_target_pairs={{0,1},{1,2},{2,3},{3,0},{4,5},{5,6},{6,7},{7,4},{8,9},{9,10},{10,1... | collective-permute-start | bytes 76808 | tf_op jit(solution)/shard_map/ppermute | solution.py:16
  18.1 2.0 %collective-permute-start.9 = (bf16[50,256]{1,0:T(8,128)(2,1)}, bf16[50,256]{1,0:T(8,128)(2,1)}, u32[]{:S(2)}, u32[]{:S(2)}) collective-permute-start(bf16[50,256]{1,0:T(8,128)(2,1)} %pad_maximum_fusion.4), channel_id=1, source_target_pairs={{0,3},{1,0},{2,1},{3,2},{4,7},{5,4},{6,5},{7,6},{8,11},{9,8},{10,9... | collective-permute-start | bytes 76808 | tf_op jit(solution)/shard_map/ppermute | solution.py:16
  20.1 1.7 %pad_dynamic-slice_fusion.6 = (bf16[4,20,192]{2,1,0:T(8,128)(2,1)}, bf16[4,20,192]{2,1,0:T(8,128)(2,1)}, bf16[4,20,192]{2,1,0:T(8,128)(2,1)}) fusion(s32[]{:T(128)S(6)} %select_n.84, bf16[4,64,192]{2,1,0:T(8,128)(2,1)} %param.19, s32[]{:T(128)S(6)} %select_n.82, s32[]{:T(128)S(6)} %select_n.86), kind=kLoop, calls=%fused_computation.149 | loop fusion | bytes 190476 | tf_op jit(solution)/shard_map/dynamic_slice | solution.py:24
  31.4 1.3 %fusion.23 = bf16[16,64,256]{2,1,0:T(8,128)(2,1)S(1)} fusion(bf16[16,64,192]{2,1,0:T(8,128)(2,1)} %param.17, f32[256]{0:T(256)S(1)} %bitcast.234, bf16[192,256]{1,0:T(8,128)(2,1)S(1)} %copy-done.44), kind=kOutput, calls=%fused_computation.33 | convolution fusion | flops 101449728 | bytes 1016832 | tf_op jit(solution)/shard_map/dot_general | solution.py:94
  36.3 1.1 fusion.130
  37.4 2.0 %convolution_select_fusion.3 = f32[6,8,5,256]{3,1,2,0:T(8,128)} fusion(bf16[3,3,384,256]{3,2,1,0:T(8,128)(2,1)S(1)} %copy-done, bf16[8,1,7,2,384]{4,2,3,0,1:T(8,128)(2,1)S(1)} %slice.185, bf16[8,1,8,5,384]{4,2,3,0,1:T(8,128)(2,1)S(1)} %copy.121, pred[8,5]{0,1:T(8,128)(4,1)} %constant.322), kind=kOutput, calls=%fused_computation.51 | convolution fusion | flops 425766912 | bytes 2347048 | tf_op jit(solution)/shard_map/conv_general_dilated | solution.py:82
  43.1 0.7 mul.504
  43.9 0.8 copy.132
  44.6 0.9 dynamic-slice
  45.5 2.9 %collective-permute-start.2 = (bf16[4,20,192]{2,1,0:T(8,128)(2,1)}, bf16[4,20,192]{2,1,0:T(8,128)(2,1)S(1)}, u32[]{:S(2)}, u32[]{:S(2)}) collective-permute-start(bf16[4,20,192]{2,1,0:T(8,128)(2,1)} %get-tuple-element.15), channel_id=1, source_target_pairs={{0,3},{1,0},{2,1},{3,2},{4,7},{5,4},{6,5},{7,6},{8,11},{9,8},{10,9... | collective-permute-start | bytes 92168 | tf_op jit(solution)/shard_map/ppermute | solution.py:30
  48.4 0.8 add_maximum_fusion
  49.4 1.1 convolution_convert_fusion.2
  50.7 1.2 %fusion.37 = bf16[6,8,5,256]{3,1,2,0:T(8,128)(2,1)S(1)} fusion(f32[6,8,5,256]{3,1,2,0:T(8,128)S(1)} %copy-done.49, bf16[3,3,256,256]{3,2,1,0:T(8,128)(2,1)S(1)} %copy-done.43, bf16[8,1,7,2,256]{4,2,3,0,1:T(8,128)(2,1)S(1)} %slice.190, bf16[8,1,8,5,256]{4,2,3,0,1:T(8,128)(2,1)S(1)} %copy.124, pred[8,5]{0,1:T(8,128)(4,1)} %constant.322), kind=kOutput, calls=%fused_computation.55 | convolution fusion | flops 283987968 | bytes 1769512 | tf_op jit(solution)/shard_map/conv_general_dilated | solution.py:82
  53.2 2.7 %collective-permute-start.12 = (bf16[6,12,256]{2,0,1:T(8,128)(2,1)S(1)}, bf16[6,12,256]{2,0,1:T(8,128)(2,1)S(1)}, u32[]{:S(2)}, u32[]{:S(2)}) collective-permute-start(bf16[6,12,256]{2,0,1:T(8,128)(2,1)S(1)} %get-tuple-element.18), channel_id=1, source_target_pairs={{0,3},{1,0},{2,1},{3,2},{4,7},{5,4},{6,5},{7,6},{8,11},{9,8},{10,9... | collective-permute-start | bytes 110600 | tf_op jit(solution)/shard_map/ppermute | solution.py:30
  55.9 1.0 convolution_add_fusion.3
  57.3 4.3 %collective-permute-start.4 = (bf16[232,256]{1,0:T(8,128)(2,1)S(1)}, bf16[232,256]{1,0:T(8,128)(2,1)S(1)}, u32[]{:S(2)}, u32[]{:S(2)}) collective-permute-start(bf16[232,256]{1,0:T(8,128)(2,1)S(1)} %pad_maximum_fusion.1), channel_id=1, source_target_pairs={{4,0},{8,4},{12,8},{5,1},{9,5},{13,9},{6,2},{10,6},{14,10},{7,3},{... | collective-permute-start | bytes 356360 | tf_op jit(solution)/shard_map/ppermute | solution.py:39
  62.2 3.0 %collective-permute-start.3 = (bf16[232,256]{1,0:T(8,128)(2,1)}, bf16[232,256]{1,0:T(8,128)(2,1)S(1)}, u32[]{:S(2)}, u32[]{:S(2)}) collective-permute-start(bf16[232,256]{1,0:T(8,128)(2,1)} %pad_maximum_fusion), channel_id=1, source_target_pairs={{0,4},{4,8},{8,12},{1,5},{5,9},{9,13},{2,6},{6,10},{10,14},{3,7},{... | collective-permute-start | bytes 356360 | tf_op jit(solution)/shard_map/ppermute | solution.py:39
  66.7 0.7 collective-permute-done.3
  68.1 0.8 slice.178
  68.9 0.8 slice.176
  69.7 0.8 slice.172
  71.3 1.3 %collective-permute-start.6 = (bf16[64,256]{1,0:T(8,128)(2,1)}, bf16[64,256]{1,0:T(8,128)(2,1)}, u32[]{:S(2)}, u32[]{:S(2)}) collective-permute-start(bf16[64,256]{1,0:T(8,128)(2,1)} %pad_maximum_fusion.3), channel_id=1, source_target_pairs={{1,0},{2,1},{3,2},{5,4},{6,5},{7,6},{9,8},{10,9},{11,10},{13,12},{... | collective-permute-start | bytes 98312 | tf_op jit(solution)/shard_map/ppermute | solution.py:39
  73.2 4.6 %collective-permute-start.5 = (bf16[64,256]{1,0:T(8,128)(2,1)}, bf16[64,256]{1,0:T(8,128)(2,1)}, u32[]{:S(2)}, u32[]{:S(2)}) collective-permute-start(bf16[64,256]{1,0:T(8,128)(2,1)} %pad_maximum_fusion.2), channel_id=1, source_target_pairs={{0,1},{1,2},{2,3},{4,5},{5,6},{6,7},{8,9},{9,10},{10,11},{12,13},{... | collective-permute-start | bytes 98312 | tf_op jit(solution)/shard_map/ppermute | solution.py:39
  77.8 1.0 add_convert_fusion.1
  79.6 1.6 %fusion.47 = bf16[6,8,3,256]{3,1,2,0:T(8,128)(2,1)S(1)} fusion(bf16[3,3,3,256,256]{4,3,2,1,0:T(8,128)(2,1)} %param.27, bf16[8,1,7,2,256]{4,2,3,0,1:T(8,128)(2,1)S(1)} %slice.196, bf16[8,1,8,3,256]{4,2,3,0,1:T(8,128)(2,1)S(1)} %copy.141, f32[256]{0:T(256)S(1)} %bitcast.233, pred[8,3]{0,1:T(4,128)(4,1)S(1)} %copy-done.48), kind=kOutput, calls=%fused_computation.59 | convolution fusion | flops 170508288 | bytes 1410072 | tf_op jit(solution)/shard_map/conv_general_dilated | solution.py:82
  81.7 0.7 slice.180
  82.4 0.7 slice.182
  83.2 0.7 slice.179
  83.9 0.7 slice.181
  84.7 1.4 %add_convert_fusion = bf16[12,36,256]{2,1,0:T(8,128)(2,1)S(1)} fusion(bf16[12,2,256]{2,1,0:T(2,128)(2,1)S(1)} %reshape.1210, bf16[2,32,256]{2,1,0:T(8,128)(2,1)S(1)} %bitcast.220, bf16[8,32,256]{2,1,0:T(8,128)(2,1)S(1)} %fusion.36, bf16[2,32,256]{2,1,0:T(8,128)(2,1)S(1)} %bitcast.222, bf16[12,2,256]{2,1,0:T(2,128)(2,1)S(1)} %reshape.1209, ...), kind=kOutput, calls=%fused_computation.93 | convolution fusion | flops 36854784 | bytes 527552 | tf_op jit(solution)/shard_map/dot_general | solution.py:262
  86.1 2.2 %fusion.68 = bf16[20,1,68,256]{3,2,0,1:T(8,128)(2,1)S(1)} fusion(bf16[20,2,256]{2,1,0:T(2,128)(2,1)S(1)} %reshape.1208, bf16[2,64,256]{2,1,0:T(8,128)(2,1)S(1)} %bitcast.215, bf16[16,64,256]{2,1,0:T(8,128)(2,1)} %copy-done.3, bf16[2,64,256]{2,1,0:T(8,128)(2,1)S(1)} %bitcast.217, bf16[20,2,256]{2,1,0:T(2,128)(2,1)S(1)} %reshape.1205, ...), kind=kOutput, calls=%fused_computation.85 | convolution fusion | flops 306163200 | bytes 1624576 | tf_op jit(solution)/shard_map/dot_general | solution.py:262
  88.7 0.8 slice.192
  89.7 1.9 %fusion.26 = bf16[10,8,5,256]{3,1,2,0:T(8,128)(2,1)S(1)} fusion(bf16[3,3,3,256,256]{4,3,2,1,0:T(8,128)(2,1)} %param.27, bf16[12,1,7,2,256]{4,2,3,0,1:T(8,128)(2,1)S(1)} %slice.194, bf16[12,1,8,5,256]{4,2,3,0,1:T(8,128)(2,1)S(1)} %copy.135, f32[256]{0:T(256)S(1)} %bitcast.232, pred[8,5]{0,1:T(8,128)(4,1)S(1)} %copy-done.47), kind=kOutput, calls=%fused_computation.38 | convolution fusion | flops 473300992 | bytes 1717288 | tf_op jit(solution)/shard_map/conv_general_dilated | solution.py:82
  91.8 0.8 reshape.1239
  92.5 1.0 reshape.1316
  93.5 3.4 %convolution_select_fusion = f32[18,8,9,256]{3,1,2,0:T(8,128)S(1)} fusion(bf16[3,3,3,256,256]{4,3,2,1,0:T(8,128)(2,1)} %param.27, bf16[20,1,7,2,256]{4,2,3,0,1:T(8,128)(2,1)} %slice.192, bf16[20,1,8,9,256]{4,2,3,0,1:T(8,128)(2,1)} %copy-done.2, pred[8,9]{0,1:T(8,128)(4,1)S(1)} %copy-done.46), kind=kOutput, calls=%fused_computation.23 | convolution fusion | flops 1531858944 | bytes 3407944 | tf_op jit(solution)/shard_map/conv_general_dilated | solution.py:82
  97.5 0.8 copy-done.10
  99.9 1.4 %copy.160 = bf16[18,1,66,1024]{3,0,2,1:T(8,128)(2,1)S(1)} copy(bf16[18,1,66,1024]{3,2,0,1:T(8,128)(2,1)S(1)} %maximum_bitcast_fusion) | data formatting | bytes 4866048
  102.0 1.5 %copy.147 = bf16[18,1,8,9,1024]{4,2,3,0,1:T(8,128)(2,1)S(1)} copy(bf16[18,1,8,9,1024]{4,0,3,2,1:T(8,128)(2,1)S(1)} %bitcast.197) | data formatting | bytes 5308416 | tf_op jit(solution)/shard_map/conv_general_dilated | solution.py:82
  103.6 5.7 %fusion.16 = f32[16,8,9,256]{3,1,2,0:T(8,128)S(1)} fusion(bf16[3,3,1024,256]{3,2,1,0:T(8,128)(2,1)S(1)} %bitcast.236, bf16[18,1,7,2,1024]{4,2,3,0,1:T(8,128)(2,1)S(1)} %slice.198, bf16[18,1,8,9,1024]{4,2,3,0,1:T(8,128)(2,1)S(1)} %copy.147, pred[8,9]{0,1:T(8,128)(4,1)S(1)} %copy-done.45), kind=kOutput, calls=%fused_computation.27 | convolution fusion | flops 5445844992 | bytes 9068616 | tf_op jit(solution)/shard_map/conv_general_dilated | solution.py:82
  110.0 1.4 %fusion.59 = bf16[16,64,256]{2,1,0:T(8,128)(2,1)} fusion(f32[16,1,64,256]{3,0,2,1:T(8,128)S(1)} %slice.199, f32[256]{0:T(256)S(1)} %bitcast.230), kind=kLoop, calls=%fused_computation.76 | loop fusion | flops 786432 | bytes 1573888 | tf_op jit(solution)/shard_map/convert_element_type | solution.py:294
  (258 shorter events, 29.9 us)
Async XLA Ops:
  0.0 37.4 %copy-start = (bf16[3,3,384,256]{3,2,1,0:T(8,128)(2,1)S(1)}, bf16[3,3,384,256]{3,2,1,0:T(8,128)(2,1)}, u32[]{:S(2)}) copy-start(bf16[3,3,384,256]{3,2,1,0:T(8,128)(2,1)} %param.22) | copy-start | bytes 5308420
  0.0 30.0 %copy-start.21 = (s32[50]{0:T(128)S(1)}, s32[50]{0:T(128)}, u32[]{:S(2)}) copy-start(s32[50]{0:T(128)} %constant.284.clone) | copy-start | bytes 604
  0.0 30.1 %copy-start.1 = (f32[12,256]{1,0:T(8,128)S(1)}, f32[12,256]{1,0:T(8,128)}, u32[]{:S(2)}) copy-start(f32[12,256]{1,0:T(8,128)} %param.29) | copy-start | bytes 36868
  0.0 30.7 %copy-start.7 = (bf16[384,256]{1,0:T(8,128)(2,1)S(1)}, bf16[384,256]{1,0:T(8,128)(2,1)}, u32[]{:S(2)}) copy-start(bf16[384,256]{1,0:T(8,128)(2,1)} %param.25) | copy-start | bytes 589828
  0.0 30.7 %copy-start.6 = (bf16[8,32,384]{2,1,0:T(8,128)(2,1)S(1)}, bf16[8,32,384]{2,1,0:T(8,128)(2,1)}, u32[]{:S(2)}) copy-start(bf16[8,32,384]{2,1,0:T(8,128)(2,1)} %param.18) | copy-start | bytes 589828
  12.5 18.9 %copy-start.44 = (bf16[192,256]{1,0:T(8,128)(2,1)S(1)}, bf16[192,256]{1,0:T(8,128)(2,1)}, u32[]{:S(2)}) copy-start(bf16[192,256]{1,0:T(8,128)(2,1)} %param.24) | copy-start | bytes 294916
  13.7 11.7 %copy-start.16 = (bf16[1,256]{1,0:T(2,128)(2,1)}, bf16[1,256]{1,0:T(2,128)(2,1)S(1)}, u32[]{:S(2)}) copy-start(bf16[1,256]{1,0:T(2,128)(2,1)S(1)} %dot_general.64) | copy-start | bytes 1540
  14.3 31.2 %collective-permute-start.8 = (bf16[50,256]{1,0:T(8,128)(2,1)}, bf16[50,256]{1,0:T(8,128)(2,1)}, u32[]{:S(2)}, u32[]{:S(2)}) collective-permute-start(bf16[50,256]{1,0:T(8,128)(2,1)} %pad_maximum_fusion.4), channel_id=1, source_target_pairs={{0,2},{1,3},{2,0},{3,1},{4,6},{5,7},{6,4},{7,5},{8,10},{9,11},{10,... | collective-permute-start | bytes 76808 | tf_op jit(solution)/shard_map/ppermute | solution.py:16
  16.8 31.6 %collective-permute-start.7 = (bf16[50,256]{1,0:T(8,128)(2,1)}, bf16[50,256]{1,0:T(8,128)(2,1)}, u32[]{:S(2)}, u32[]{:S(2)}) collective-permute-start(bf16[50,256]{1,0:T(8,128)(2,1)} %pad_maximum_fusion.4), channel_id=1, source_target_pairs={{0,1},{1,2},{2,3},{3,0},{4,5},{5,6},{6,7},{7,4},{8,9},{9,10},{10,1... | collective-permute-start | bytes 76808 | tf_op jit(solution)/shard_map/ppermute | solution.py:16
  18.1 30.3 %collective-permute-start.9 = (bf16[50,256]{1,0:T(8,128)(2,1)}, bf16[50,256]{1,0:T(8,128)(2,1)}, u32[]{:S(2)}, u32[]{:S(2)}) collective-permute-start(bf16[50,256]{1,0:T(8,128)(2,1)} %pad_maximum_fusion.4), channel_id=1, source_target_pairs={{0,3},{1,0},{2,1},{3,2},{4,7},{5,4},{6,5},{7,6},{8,11},{9,8},{10,9... | collective-permute-start | bytes 76808 | tf_op jit(solution)/shard_map/ppermute | solution.py:16
  21.7 35.3 %collective-permute-start.1 = (bf16[4,20,192]{2,1,0:T(8,128)(2,1)}, bf16[4,20,192]{2,1,0:T(8,128)(2,1)S(1)}, u32[]{:S(2)}, u32[]{:S(2)}) collective-permute-start(bf16[4,20,192]{2,1,0:T(8,128)(2,1)} %get-tuple-element.13), channel_id=1, source_target_pairs={{0,2},{1,3},{2,0},{3,1},{4,6},{5,7},{6,4},{7,5},{8,10},{9,11},{10,... | collective-permute-start | bytes 92168 | tf_op jit(solution)/shard_map/ppermute | solution.py:30
  21.7 31.5 %collective-permute-start = (bf16[4,20,192]{2,1,0:T(8,128)(2,1)}, bf16[4,20,192]{2,1,0:T(8,128)(2,1)}, u32[]{:S(2)}, u32[]{:S(2)}) collective-permute-start(bf16[4,20,192]{2,1,0:T(8,128)(2,1)} %get-tuple-element.14), channel_id=1, source_target_pairs={{0,1},{1,2},{2,3},{3,0},{4,5},{5,6},{6,7},{7,4},{8,9},{9,10},{10,1... | collective-permute-start | bytes 92168 | tf_op jit(solution)/shard_map/ppermute | solution.py:30
  31.0 2.9 %copy-start.32 = (f32[50]{0:T(128)S(1)}, f32[50]{0:T(128)}, u32[]{:S(2)}) copy-start(f32[50]{0:T(128)} %constant.383) | copy-start | bytes 604
  31.0 2.9 %copy-start.38 = (f32[8]{0:T(128)S(1)}, f32[8]{0:T(128)}, u32[]{:S(2)}) copy-start(f32[8]{0:T(128)} %and_convert_fusion.2) | copy-start | bytes 100
  31.0 2.8 %copy-start.39 = (f32[8]{0:T(128)S(1)}, f32[8]{0:T(128)}, u32[]{:S(2)}) copy-start(f32[8]{0:T(128)} %convert_add_fusion.3) | copy-start | bytes 100
  31.0 3.0 %copy-start.33 = (f32[12]{0:T(128)S(1)}, f32[12]{0:T(128)}, u32[]{:S(2)}) copy-start(f32[12]{0:T(128)} %add_clamp_fusion.9) | copy-start | bytes 148
  31.0 3.0 %copy-start.34 = (f32[12]{0:T(128)S(1)}, f32[12]{0:T(128)}, u32[]{:S(2)}) copy-start(f32[12]{0:T(128)} %and_convert_fusion.6) | copy-start | bytes 148
  31.0 3.0 %copy-start.37 = (f32[8]{0:T(128)S(1)}, f32[8]{0:T(128)}, u32[]{:S(2)}) copy-start(f32[8]{0:T(128)} %add_convert_fusion.8) | copy-start | bytes 100
  31.1 3.0 %copy-start.35 = (f32[8]{0:T(128)S(1)}, f32[8]{0:T(128)}, u32[]{:S(2)}) copy-start(f32[8]{0:T(128)} %add_clamp_fusion.7) | copy-start | bytes 100
  31.1 3.0 %copy-start.36 = (f32[8]{0:T(128)S(1)}, f32[8]{0:T(128)}, u32[]{:S(2)}) copy-start(f32[8]{0:T(128)} %and_convert_fusion.4) | copy-start | bytes 100
  31.1 3.7 %copy-start.40 = (f32[18]{0:T(128)S(1)}, f32[18]{0:T(128)}, u32[]{:S(2)}) copy-start(f32[18]{0:T(128)} %get-tuple-element.35) | copy-start | bytes 220
  31.1 3.7 %copy-start.41 = (f32[18]{0:T(128)S(1)}, f32[18]{0:T(128)}, u32[]{:S(2)}) copy-start(f32[18]{0:T(128)} %get-tuple-element.36) | copy-start | bytes 220
  31.1 3.7 %copy-start.42 = (f32[6]{0:T(128)S(1)}, f32[6]{0:T(128)}, u32[]{:S(2)}) copy-start(f32[6]{0:T(128)} %add_convert_fusion.3) | copy-start | bytes 76
  31.1 4.6 %copy-start.28 = (f32[68]{0:T(128)S(1)}, f32[68]{0:T(128)}, u32[]{:S(2)}) copy-start(f32[68]{0:T(128)} %add_clamp_fusion.10) | copy-start | bytes 820
  31.1 4.6 %copy-start.29 = (f32[36]{0:T(128)S(1)}, f32[36]{0:T(128)}, u32[]{:S(2)}) copy-start(f32[36]{0:T(128)} %add_convert_fusion.9) | copy-start | bytes 436
  31.2 5.2 %copy-start.4 = (bf16[4,64,192]{2,1,0:T(8,128)(2,1)S(1)}, bf16[4,64,192]{2,1,0:T(8,128)(2,1)}, u32[]{:S(2)}) copy-start(bf16[4,64,192]{2,1,0:T(8,128)(2,1)} %param.19) | copy-start | bytes 294916
  32.7 37.9 %copy-start.3 = (bf16[16,64,256]{2,1,0:T(8,128)(2,1)}, bf16[16,64,256]{2,1,0:T(8,128)(2,1)S(1)}, u32[]{:S(2)}) copy-start(bf16[16,64,256]{2,1,0:T(8,128)(2,1)S(1)} %fusion.23) | copy-start | bytes 1572868
  44.6 6.0 %copy-start.49 = (f32[6,8,5,256]{3,1,2,0:T(8,128)S(1)}, f32[6,8,5,256]{3,1,2,0:T(8,128)}, u32[]{:S(2)}) copy-start(f32[6,8,5,256]{3,1,2,0:T(8,128)} %convolution_select_fusion.3) | copy-start | bytes 737284
  44.6 6.0 %copy-start.43 = (bf16[3,3,256,256]{3,2,1,0:T(8,128)(2,1)S(1)}, bf16[3,3,256,256]{3,2,1,0:T(8,128)(2,1)}, u32[]{:S(2)}) copy-start(bf16[3,3,256,256]{3,2,1,0:T(8,128)(2,1)} %param.23) | copy-start | bytes 3538948
  45.5 11.4 %collective-permute-start.2 = (bf16[4,20,192]{2,1,0:T(8,128)(2,1)}, bf16[4,20,192]{2,1,0:T(8,128)(2,1)S(1)}, u32[]{:S(2)}, u32[]{:S(2)}) collective-permute-start(bf16[4,20,192]{2,1,0:T(8,128)(2,1)} %get-tuple-element.15), channel_id=1, source_target_pairs={{0,3},{1,0},{2,1},{3,2},{4,7},{5,4},{6,5},{7,6},{8,11},{9,8},{10,9... | collective-permute-start | bytes 92168 | tf_op jit(solution)/shard_map/ppermute | solution.py:30
  50.7 5.2 %copy-start.5 = (bf16[768,256]{1,0:T(8,128)(2,1)S(1)}, bf16[768,256]{1,0:T(8,128)(2,1)}, u32[]{:S(2)}) copy-start(bf16[768,256]{1,0:T(8,128)(2,1)} %param.26) | copy-start | bytes 1179652
  50.7 6.4 %copy-start.19 = (f32[1,256]{1,0:T(1,128)S(1)}, f32[1,256]{1,0:T(1,128)}, u32[]{:S(2)}) copy-start(f32[1,256]{1,0:T(1,128)} %get-tuple-element.25) | copy-start | bytes 3076
  50.7 6.4 %copy-start.26 = (pred[20]{0:T(512)(128)(4,1)S(1)}, pred[20]{0:T(512)(128)(4,1)}, u32[]{:S(2)}) copy-start(pred[20]{0:T(512)(128)(4,1)} %compare_and_fusion) | copy-start | bytes 64
  51.9 13.4 %copy-start.18 = (f32[1,256]{1,0:T(1,128)S(1)}, f32[1,256]{1,0:T(1,128)}, u32[]{:S(2)}) copy-start(f32[1,256]{1,0:T(1,128)} %get-tuple-element.24) | copy-start | bytes 3076
  52.6 12.6 %collective-permute-start.10 = (bf16[6,12,256]{2,0,1:T(8,128)(2,1)}, bf16[6,12,256]{2,0,1:T(8,128)(2,1)S(1)}, u32[]{:S(2)}, u32[]{:S(2)}) collective-permute-start(bf16[6,12,256]{2,0,1:T(8,128)(2,1)} %get-tuple-element.16), channel_id=1, source_target_pairs={{0,1},{1,2},{2,3},{3,0},{4,5},{5,6},{6,7},{7,4},{8,9},{9,10},{10,1... | collective-permute-start | bytes 110600 | tf_op jit(solution)/shard_map/ppermute | solution.py:30
  52.6 12.6 %collective-permute-start.11 = (bf16[6,12,256]{2,0,1:T(8,128)(2,1)S(1)}, bf16[6,12,256]{2,0,1:T(8,128)(2,1)S(1)}, u32[]{:S(2)}, u32[]{:S(2)}) collective-permute-start(bf16[6,12,256]{2,0,1:T(8,128)(2,1)S(1)} %get-tuple-element.17), channel_id=1, source_target_pairs={{0,2},{1,3},{2,0},{3,1},{4,6},{5,7},{6,4},{7,5},{8,10},{9,11},{10,... | collective-permute-start | bytes 110600 | tf_op jit(solution)/shard_map/ppermute | solution.py:30
  53.2 12.1 %collective-permute-start.12 = (bf16[6,12,256]{2,0,1:T(8,128)(2,1)S(1)}, bf16[6,12,256]{2,0,1:T(8,128)(2,1)S(1)}, u32[]{:S(2)}, u32[]{:S(2)}) collective-permute-start(bf16[6,12,256]{2,0,1:T(8,128)(2,1)S(1)} %get-tuple-element.18), channel_id=1, source_target_pairs={{0,3},{1,0},{2,1},{3,2},{4,7},{5,4},{6,5},{7,6},{8,11},{9,8},{10,9... | collective-permute-start | bytes 110600 | tf_op jit(solution)/shard_map/ppermute | solution.py:30
  57.2 20.5 %copy-start.15 = (f32[20,12]{0,1:T(8,128)S(1)}, f32[20,12]{0,1:T(8,128)}, u32[]{:S(2)}) copy-start(f32[20,12]{0,1:T(8,128)} %maximum_multiply_fusion.6) | copy-start | bytes 2884
  57.3 8.7 %collective-permute-start.4 = (bf16[232,256]{1,0:T(8,128)(2,1)S(1)}, bf16[232,256]{1,0:T(8,128)(2,1)S(1)}, u32[]{:S(2)}, u32[]{:S(2)}) collective-permute-start(bf16[232,256]{1,0:T(8,128)(2,1)S(1)} %pad_maximum_fusion.1), channel_id=1, source_target_pairs={{4,0},{8,4},{12,8},{5,1},{9,5},{13,9},{6,2},{10,6},{14,10},{7,3},{... | collective-permute-start | bytes 356360 | tf_op jit(solution)/shard_map/ppermute | solution.py:39
  62.2 5.1 %collective-permute-start.3 = (bf16[232,256]{1,0:T(8,128)(2,1)}, bf16[232,256]{1,0:T(8,128)(2,1)S(1)}, u32[]{:S(2)}, u32[]{:S(2)}) collective-permute-start(bf16[232,256]{1,0:T(8,128)(2,1)} %pad_maximum_fusion), channel_id=1, source_target_pairs={{0,4},{4,8},{8,12},{1,5},{5,9},{9,13},{2,6},{6,10},{10,14},{3,7},{... | collective-permute-start | bytes 356360 | tf_op jit(solution)/shard_map/ppermute | solution.py:39
  65.4 14.2 %copy-start.25 = (f32[1,256]{1,0:T(1,128)S(1)}, f32[1,256]{1,0:T(1,128)}, u32[]{:S(2)}) copy-start(f32[1,256]{1,0:T(1,128)} %get-tuple-element.28) | copy-start | bytes 3076
  66.0 13.6 %copy-start.48 = (pred[8,3]{0,1:T(4,128)(4,1)S(1)}, pred[8,3]{0,1:T(4,128)(4,1)}, u32[]{:S(2)}) copy-start(pred[8,3]{0,1:T(4,128)(4,1)} %constant.381) | copy-start | bytes 76
  71.3 10.4 %collective-permute-start.6 = (bf16[64,256]{1,0:T(8,128)(2,1)}, bf16[64,256]{1,0:T(8,128)(2,1)}, u32[]{:S(2)}, u32[]{:S(2)}) collective-permute-start(bf16[64,256]{1,0:T(8,128)(2,1)} %pad_maximum_fusion.3), channel_id=1, source_target_pairs={{1,0},{2,1},{3,2},{5,4},{6,5},{7,6},{9,8},{10,9},{11,10},{13,12},{... | collective-permute-start | bytes 98312 | tf_op jit(solution)/shard_map/ppermute | solution.py:39
  73.2 10.0 %collective-permute-start.5 = (bf16[64,256]{1,0:T(8,128)(2,1)}, bf16[64,256]{1,0:T(8,128)(2,1)}, u32[]{:S(2)}, u32[]{:S(2)}) collective-permute-start(bf16[64,256]{1,0:T(8,128)(2,1)} %pad_maximum_fusion.2), channel_id=1, source_target_pairs={{0,1},{1,2},{2,3},{4,5},{5,6},{6,7},{8,9},{9,10},{10,11},{12,13},{... | collective-permute-start | bytes 98312 | tf_op jit(solution)/shard_map/ppermute | solution.py:39
  81.2 4.9 %copy-start.14 = (f32[68,36]{0,1:T(8,128)S(1)}, f32[68,36]{0,1:T(8,128)}, u32[]{:S(2)}) copy-start(f32[68,36]{0,1:T(8,128)} %maximum_multiply_fusion.1) | copy-start | bytes 29380
  88.7 3.0 %copy-start.2 = (bf16[20,1,8,9,256]{4,2,3,0,1:T(8,128)(2,1)}, bf16[20,1,8,9,256]{4,2,3,0,1:T(8,128)(2,1)S(1)}, u32[]{:S(2)}) copy-start(bf16[20,1,8,9,256]{4,2,3,0,1:T(8,128)(2,1)S(1)} %copy.129) | copy-start | bytes 2211844
  89.7 3.8 %copy-start.46 = (pred[8,9]{0,1:T(8,128)(4,1)S(1)}, pred[8,9]{0,1:T(8,128)(4,1)}, u32[]{:S(2)}) copy-start(pred[8,9]{0,1:T(8,128)(4,1)} %constant.321) | copy-start | bytes 220
  99.9 3.7 %slice-start = ((s8[4718592]{0:T(1024)(128)(4,1)}), s8[4194304]{0:T(1024)(128)(4,1)S(1)}, s32[]{:S(2)}) async-start(s8[4718592]{0:T(1024)(128)(4,1)} %bitcast.235), calls=%async_computation | async-start | bytes 8388608
  (17 other events, 29.2 us)

commit v2 on v1

--- a/solution.py
+++ b/solution.py
@@ -1,6 +1,10 @@
+import functools
+
 import jax
 import jax.numpy as jnp
 from jax import lax
+from jax.experimental import pallas as pl
+from jax.experimental.pallas import tpu as pltpu
 from jax.sharding import PartitionSpec as P
 
 highest = lax.Precision.HIGHEST
@@ -70,14 +74,6 @@
     return jnp.maximum(0.0, 1.0 - jnp.abs(source - index.astype(f32)[None, :]))
 
 
-def stretch(first_out, length_out, first_in, length_in, factor, extent):
-    output = (first_out + jnp.arange(length_out, dtype=jnp.int32)).astype(f32)
-    source = jnp.clip((output + 0.5) / factor - 0.5, 0.0, extent - 1.0)
-    targets = (first_in + jnp.arange(length_in, dtype=jnp.int32)).astype(f32)
-    inside = ((output >= 0.0) & (output < extent * factor)).astype(f32)
-    return jnp.maximum(0.0, 1.0 - jnp.abs(source[:, None] - targets[None, :])) * inside[:, None]
-
-
 def conv(feature, weight, padding):
     return lax.conv_general_dilated(
         feature[None],
@@ -95,6 +91,254 @@
         feature.reshape(height * breadth, channels), weight, preferred_element_type=f32
     )
     return result.reshape(height, breadth, -1)
+
+
+def floor_div(value, step):
+    return jnp.floor((value + 0.5) / step)
+
+
+def stretch_matrix(out_shape, out_first, in_shape, in_first, factor, extent):
+    out_rows, out_pitch = out_shape
+    in_rows, in_pitch = in_shape
+    place = lax.broadcasted_iota(jnp.int32, (1, in_rows * in_pitch), 1).astype(f32)
+    place_row = floor_div(place, in_pitch)
+    place_col = place - place_row * in_pitch
+
+    def weights(length, first_out, first_in, targets, whole):
+        output = first_out + lax.broadcasted_iota(jnp.int32, (length, 1), 0).astype(f32)
+        source = (output + 0.5) * (1.0 / factor) - 0.5
+        source = jnp.minimum(jnp.maximum(source, 0.0), whole - 1.0)
+        inside = jnp.where((output >= 0.0) & (output < whole * factor), 1.0, 0.0)
+        return jnp.maximum(0.0, 1.0 - jnp.abs(source - (first_in + targets))) * inside
+
+    down = weights(out_rows, out_first[0], in_first[0], place_row, extent[0])
+    across = weights(out_pitch, out_first[1], in_first[1], place_col, extent[1])
+    matrix = down[:, None, :] * across[None, :, :]
+    return matrix.astype(bf16).reshape(out_rows * out_pitch, in_rows * in_pitch)
+
+
+def tail_kernel(
+    sizes,
+    top_count,
+    here_ref,
+    *refs,
+):
+    (high1, wide1), (high2, wide2), (high3, wide3), (high4, wide4), (row_count, col_count) = sizes
+    top_refs, refs = refs[:top_count], refs[top_count:]
+    (
+        lat1_ref,
+        lat2_ref,
+        lat3_ref,
+        above_ref,
+        below_ref,
+        before_ref,
+        after_ref,
+        bias_ref,
+        smooth_hbm,
+        join_hbm,
+        out_ref,
+        top_buf,
+        lat1_buf,
+        lat2_buf,
+        lat3_buf,
+        pyr1_buf,
+        pyr2_buf,
+        pyr3_buf,
+        acc_buf,
+        sums_buf,
+        stack_buf,
+        smooth_w,
+        join_w,
+        sems,
+    ) = refs
+    smooth_copy = pltpu.make_async_copy(smooth_hbm, smooth_w, sems.at[0])
+    join_copy = pltpu.make_async_copy(join_hbm, join_w, sems.at[1])
+    smooth_copy.start()
+    join_copy.start()
+    row_here = here_ref[0].astype(f32)
+    col_here = here_ref[1].astype(f32)
+    channels = bias_ref.shape[1]
+
+    def firsts(high, wide, border):
+        return row_here * high - border, col_here * wide - border
+
+    def extent(high, wide):
+        return float(high * row_count), float(wide * col_count)
+
+    start = 0
+    for ref, buf, high, wide in (
+        (lat1_ref, lat1_buf, high1, wide1),
+        (lat2_ref, lat2_buf, high2, wide2),
+    ):
+        buf[...] = jnp.zeros_like(buf)
+        buf[rim : rim + high, rim : rim + wide, :] = ref[...].astype(f32)
+        for source, row in ((above_ref, 0), (below_ref, rim + high)):
+            for step in range(rim):
+                at = start + step * wide
+                buf[row + step, rim : rim + wide, :] = source[at : at + wide, :].astype(f32)
+        start += rim * wide
+    lat3_buf[...] = jnp.zeros_like(lat3_buf)
+    whole3 = wide3 + 2 * rim
+    lat3_buf[rim : rim + high3, :whole3, :] = lat3_ref[...].astype(f32)
+    for source, row in ((above_ref, 0), (below_ref, rim + high3)):
+        both = source[start : start + rim * whole3, :].astype(f32)
+        for step in range(rim):
+            lat3_buf[row + step, :whole3, :] = both[step * whole3 : (step + 1) * whole3]
+    start = 0
+    for buf, high, wide in ((lat1_buf, high1, wide1), (lat2_buf, high2, wide2)):
+        tall = high + 2 * rim
+        for source, col in ((before_ref, 0), (after_ref, rim + wide)):
+            sides = source[start : start + rim * tall, :].astype(f32)
+            for row in range(tall):
+                buf[row, col : col + rim, :] = sides[rim * row : rim * row + rim]
+        start += rim * tall
+
+    tall4, whole4 = high4 + 2 * rim, wide4 + 2 * rim
+    top_sum = top_refs[0][...].astype(f32)
+    for ref in top_refs[1:]:
+        top_sum = top_sum + ref[...].astype(f32)
+    top_buf[...] = jnp.zeros_like(top_buf)
+    top_buf[:, :whole4, :] = jnp.maximum(top_sum + bias_ref[4:5, :][None], 0.0)
+    pitch4 = top_buf.shape[1]
+    top = top_buf[...].astype(bf16).reshape(tall4 * pitch4, channels)
+
+    def dot(a, b):
+        return jnp.dot(a, b, preferred_element_type=f32)
+
+    def pyramid(lat_buf, high, wide, source, source_shape, source_first, source_size):
+        rows, pitch = lat_buf.shape[:2]
+        matrix = stretch_matrix(
+            (rows, pitch), firsts(high, wide, rim), source_shape, source_first, 2, extent(*source_size)
+        )
+        total = lat_buf[...].reshape(rows * pitch, channels) + dot(matrix, source)
+        return total.astype(bf16)
+
+    first4 = firsts(high4, wide4, rim)
+    pyr3_buf[...] = pyramid(lat3_buf, high3, wide3, top, (tall4, pitch4), first4, (high4, wide4))
+    shape3 = lat3_buf.shape[:2]
+    pyr2_buf[...] = pyramid(
+        lat2_buf, high2, wide2, pyr3_buf[...], shape3, firsts(high3, wide3, rim), (high3, wide3)
+    )
+    shape2 = lat2_buf.shape[:2]
+    pyr1_buf[...] = pyramid(
+        lat1_buf, high1, wide1, pyr2_buf[...], shape2, firsts(high2, wide2, rim), (high2, wide2)
+    )
+    shape1 = lat1_buf.shape[:2]
+    smooth_copy.wait()
+
+    def conv(source, shape, weight_at, rows):
+        pitch = shape[1]
+        span = rows * pitch
+        for col_tap in range(3):
+            total = dot(source[0:span, :], weight_at(0, col_tap))
+            for row_tap in (1, 2):
+                total = total + dot(
+                    source[row_tap * pitch : row_tap * pitch + span, :], weight_at(row_tap, col_tap)
+                )
+            yield col_tap, total.reshape(rows, pitch, channels)
+
+    def smooth(number, source, shape, wide):
+        rows, pitch = shape[0] - 2, shape[1]
+        for col_tap, total in conv(
+            source, shape, lambda i, j: smooth_w[number, i, j], rows
+        ):
+            acc_buf[col_tap, :rows, :pitch, :] = total
+        whole = wide + 2
+        total = (
+            acc_buf[0, :rows, 0:whole, :]
+            + acc_buf[1, :rows, 1 : whole + 1, :]
+            + acc_buf[2, :rows, 2 : whole + 2, :]
+        )
+        return jnp.maximum(total + bias_ref[8 + number : 9 + number, :][None], 0.0)
+
+    def smooth_flat(number, source, shape, wide):
+        rows, pitch = shape[0] - 2, shape[1]
+        value = smooth(number, source, shape, wide)
+        sums_buf[:rows, :pitch, :] = jnp.zeros((rows, pitch, channels), f32)
+        sums_buf[:rows, : wide + 2, :] = value
+        return sums_buf[:rows, :pitch, :].astype(bf16).reshape(rows * pitch, channels)
+
+    rows1, pitch1 = shape1[0] - 2, shape1[1]
+    out_first = firsts(high1, wide1, 1)
+
+    def raise_to_one(source, source_shape, source_first, factor, source_size):
+        matrix = stretch_matrix(
+            (rows1, pitch1), out_first, source_shape, source_first, factor, extent(*source_size)
+        )
+        return dot(matrix, source).astype(bf16)
+
+    stack_buf[:, 3 * channels : 4 * channels] = raise_to_one(
+        top, (tall4, pitch4), first4, 8, (high4, wide4)
+    )
+    smooth3 = smooth_flat(2, pyr3_buf, shape3, wide3)
+    stack_buf[:, 2 * channels : 3 * channels] = raise_to_one(
+        smooth3, (shape3[0] - 2, shape3[1]), firsts(high3, wide3, 1), 4, (high3, wide3)
+    )
+    smooth2 = smooth_flat(1, pyr2_buf, shape2, wide2)
+    stack_buf[:, channels : 2 * channels] = raise_to_one(
+        smooth2, (shape2[0] - 2, shape2[1]), firsts(high2, wide2, 1), 2, (high2, wide2)
+    )
+    value = smooth(0, pyr1_buf, shape1, wide1)
+    down = out_first[0] + lax.broadcasted_iota(jnp.int32, (rows1, 1, 1), 0).astype(f32)
+    across = out_first[1] + lax.broadcasted_iota(jnp.int32, (1, wide1 + 2, 1), 1).astype(f32)
+    tall, broad = extent(high1, wide1)
+    inside = (down >= 0.0) & (down < tall) & (across >= 0.0) & (across < broad)
+    sums_buf[:rows1, : wide1 + 2, :] = jnp.where(inside, value, 0.0)
+    stack_buf[:, 0:channels] = sums_buf[...].astype(bf16).reshape(rows1 * pitch1, channels)
+    join_copy.wait()
+    shape_join = (rows1, pitch1)
+    for col_tap, total in conv(stack_buf, shape_join, lambda i, j: join_w[i, j], high1):
+        acc_buf[col_tap, :high1] = total
+    total = (
+        acc_buf[0, :high1, 0:wide1, :]
+        + acc_buf[1, :high1, 1 : wide1 + 1, :]
+        + acc_buf[2, :high1, 2 : wide1 + 2, :]
+    )
+    out_ref[...] = jnp.maximum(total + bias_ref[11:12, :][None], 0.0).astype(bf16)
+
+
+def pitch_of(width):
+    return (width + 15) // 16 * 16
+
+
+def tail(here, tops, lats, above, below, before, after, biases, smooth_weight, join_weight, sizes):
+    (high1, wide1), (high2, wide2), (high3, wide3), (high4, wide4), _ = sizes
+    channels = biases.shape[1]
+
+    def window(high, wide):
+        return high + 2 * rim, pitch_of(wide + 2 * rim)
+
+    shapes = [window(high, wide) for high, wide in sizes[:4]]
+    (rows1, pitch1), (rows2, pitch2), (rows3, pitch3), (rows4, pitch4) = shapes
+    vmem = pl.BlockSpec(memory_space=pltpu.VMEM)
+    anywhere = pl.BlockSpec(memory_space=pl.ANY)
+    return pl.pallas_call(
+        functools.partial(tail_kernel, sizes, len(tops)),
+        out_shape=jax.ShapeDtypeStruct((high1, wide1, channels), bf16),
+        in_specs=[pl.BlockSpec(memory_space=pltpu.SMEM)]
+        + [vmem] * (len(tops) + 8)
+        + [anywhere] * 2,
+        out_specs=vmem,
+        scratch_shapes=[
+            pltpu.VMEM((rows4, pitch4, channels), f32),
+            pltpu.VMEM((rows1, pitch1, channels), f32),
+            pltpu.VMEM((rows2, pitch2, channels), f32),
+            pltpu.VMEM((rows3, pitch3, channels), f32),
+            pltpu.VMEM((rows1 * pitch1, channels), bf16),
+            pltpu.VMEM((rows2 * pitch2, channels), bf16),
+            pltpu.VMEM((rows3 * pitch3, channels), bf16),
+            pltpu.VMEM((3, rows1 - 2, pitch1, channels), f32),
+            pltpu.VMEM((rows1 - 2, pitch1, channels), f32),
+            pltpu.VMEM(((rows1 - 2) * pitch1, 4 * channels), bf16),
+            pltpu.VMEM(smooth_weight.shape, bf16),
+            pltpu.VMEM(join_weight.shape, bf16),
+            pltpu.SemaphoreType.DMA((2,)),
+        ],
+        compiler_params=pltpu.CompilerParams(vmem_limit_bytes=60 * 1024 * 1024),
+        cost_estimate=pl.CostEstimate(
+            flops=10_000_000_000, bytes_accessed=12_000_000, transcendentals=0
+        ),
+    )(here, *tops, *lats, above, below, before, after, biases, smooth_weight, join_weight)
 
 
 def local(
@@ -186,20 +430,18 @@
     above, below = edge_swap(
         pack([level[:rim] for level in levels]), pack([level[-rim:] for level in levels]), "row"
     )
-    levels = [
-        jnp.concatenate([a, level, b], axis=0)
-        for a, level, b in zip(unpack(above, shapes), levels, unpack(below, shapes))
+    shapes = [(rim, level.shape[1]) for level in levels]
+
+    def sides(value):
+        return jnp.concatenate([value[:, :rim], value[:, -rim:]], axis=1)
+
+    sided = [
+        jnp.concatenate([sides(a), sides(level), sides(b)], axis=0)
+        for a, level, b in zip(unpack(above, shapes)[:2], levels[:2], unpack(below, shapes)[:2])
     ]
-    sided = levels[:2]
-    shapes = [(level.shape[0], rim) for level in sided]
     before, after = edge_swap(
         pack([level[:, :rim] for level in sided]), pack([level[:, -rim:] for level in sided]), "col"
     )
-    wide_one, wide_two = [
-        jnp.concatenate([a, level, b], axis=1)
-        for a, level, b in zip(unpack(before, shapes), sided, unpack(after, shapes))
-    ]
-    wide_three = levels[2]
 
     first_row = row_here * rows4
     span = rows4 + 2 * rim + 2
@@ -226,72 +468,35 @@
     around = ((0, 0), (1, 1))
     neck_term = conv(four_span, neck_feature, around) + conv(ppm, neck_pooled, around)
     neck_pad = jnp.pad(neck_term.astype(bf16), ((0, 0), (rim, rim), (0, 0)))
-    top_sum = windows_sum(
+    tops = windows_sum(
         neck_pad,
         "col",
         1,
         cols4,
         cols4 + 2 * rim,
-        lambda pieces: sum(p.astype(f32) for p in pieces),
-    )
-    top = jax.nn.relu(top_sum + biases[4]).astype(bf16)
-
-    def upscale(source, level_rows, level_cols, factor, border_in, border_out):
-        high, wide = source.shape[0], source.shape[1]
-        out_high = level_rows * factor + 2 * border_out
-        out_wide = level_cols * factor + 2 * border_out
-        down = stretch(
-            row_here * level_rows * factor - border_out,
-            out_high,
-            row_here * level_rows - border_in,
-            high,
-            factor,
-            level_rows * row_count,
-        )
-        across = stretch(
-            col_here * level_cols * factor - border_out,
-            out_wide,
-            col_here * level_cols - border_in,
-            wide,
-            factor,
-            level_cols * col_count,
-        )
-        matrix = (down[:, None, :, None] * across[None, :, None, :]).reshape(
-            out_high * out_wide, high * wide
-        )
-        result = jnp.dot(
-            matrix.astype(bf16), source.reshape(high * wide, -1), preferred_element_type=f32
-        )
-        return result.reshape(out_high, out_wide, -1)
-
-    rows2, cols2 = level_two.shape[0], level_two.shape[1]
-    rows1, cols1 = level_one.shape[0], level_one.shape[1]
-    pyr_three = (wide_three.astype(f32) + upscale(top, rows4, cols4, 2, rim, rim)).astype(bf16)
-    pyr_two = (wide_two.astype(f32) + upscale(pyr_three, rows3, cols3, 2, rim, rim)).astype(bf16)
-    pyr_one = (wide_one.astype(f32) + upscale(pyr_two, rows2, cols2, 2, rim, rim)).astype(bf16)
-    valid = ((0, 0), (0, 0))
-    smooth_one = jax.nn.relu(conv(pyr_one, smooth_weight[0], valid) + biases[8])
-    smooth_two = jax.nn.relu(conv(pyr_two, smooth_weight[1], valid) + biases[9]).astype(bf16)
-    smooth_three = jax.nn.relu(conv(pyr_three, smooth_weight[2], valid) + biases[10]).astype(bf16)
-
-    def in_image(length, here, count):
-        place = here * length - 1 + jnp.arange(length + 2, dtype=jnp.int32)
-        return (place >= 0) & (place < length * count)
-
-    mask = (
-        in_image(rows1, row_here, row_count)[:, None] & in_image(cols1, col_here, col_count)[None, :]
-    )
-    smooth_one = jnp.where(mask[:, :, None], smooth_one, 0.0).astype(bf16)
-    stacked_top = jnp.concatenate(
-        [
-            smooth_one,
-            upscale(smooth_two, rows2, cols2, 2, 1, 1).astype(bf16),
-            upscale(smooth_three, rows3, cols3, 4, 1, 1).astype(bf16),
-            upscale(top, rows4, cols4, 8, rim, 1).astype(bf16),
-        ],
-        axis=2,
-    )
-    return jax.nn.relu(conv(stacked_top, join_weight, valid) + biases[11]).astype(bf16)
+        lambda pieces: pieces,
+    )
+    sizes = (
+        level_one.shape[:2],
+        level_two.shape[:2],
+        (rows3, cols3),
+        (rows4, cols4),
+        (row_count, col_count),
+    )
+    here = jnp.stack([row_here, col_here]).astype(jnp.int32)
+    return tail(
+        here,
+        tops,
+        levels,
+        above,
+        below,
+        before,
+        after,
+        biases,
+        smooth_weight,
+        join_weight,
+        sizes,
+    )
 
 
 def solution(mesh):

time: 113 us -> 75.8 us (0.67)
  the two profiles are of different devices: /device:TPU:1 before, /device:TPU:6 now
where the time goes in v2:
time: 75.8 us; the launch traced here: 75.3 us
  starting transfers between devices  26 us (34%)
  Pallas kernels  17.8 us (23%)
  matrix products  12.5 us (16%)
  blocking collectives  5.94 us (8%)
  local copies, waits for them, and re-layouts  4.9 us (6%)
  waiting for transfers between devices  3.75 us (5%)
  other arithmetic  3.5 us (5%)
  between operations  0.93 us (1%)
    pallas_call x1, Pallas kernels, tail(): pl.pallas_call(functools.partial(tail_kernel, sizes, len(tops)), out_shap...  17.8 us
    ppermute x2, starting transfers between devices, edge_swap(): lax.ppermute(high_out, axis, forward)  7.42 us
    ppermute x6, starting transfers between devices, windows_sum(): lax.ppermute(window_for(target), axis, [(i, (i + shift) % count) for i in...  7.04 us
    ppermute x3, starting transfers between devices, others(): lax.ppermute(value, axis, [(i, (i + shift) % count) for i in range(count)])  6.41 us
    all_gather x1, blocking collectives, local(): four = lax.all_gather(level_four, 'row', axis=0, tiled=True)  5.94 us
    ppermute x2, starting transfers between devices, edge_swap(): lax.ppermute(low_out, axis, backward)  5.11 us
    conv_general_dilated x2, matrix products, conv(): lax.conv_general_dilated(feature[None], weight, (1, 1), padding, dimensio...  4.73 us
    dot_general x4, matrix products, local(): jnp.dot(pooled[offset:offset + side * side], bin_weight[number], preferre...  4.35 us
  transfers between devices with their start and end apart: 13, of which 1 were waited for; matrix products, arithmetic and copies ran while one was open for 16% of the time, Pallas kernels for 0%

profile of v2, /device:TPU:6, one launch (start us, length us, event | category | flops | bytes accessed | tf_op | source)
XLA Modules:
  0.0 75.3 jit_solution(11297093321512668964)
XLA Ops:
  0.0 5.9 %all_gather.3 = bf16[8,32,384]{2,1,0:T(8,128)(2,1)S(1)} all-gather(bf16[2,32,384]{2,1,0:T(8,128)(2,1)} %param.20), channel_id=1, replica_groups=mesh['grp'=2,'row'=4,'col'=4] {'row'}, dimensions={0}, use_global_device_ids=true | all-gather | bytes 245760 | tf_op jit(solution)/shard_map/all_gather | solution.py:368
  6.0 0.7 fusion.57
  6.6 0.7 fusion.49
  7.3 0.8 %fusion.10 = bf16[50,384]{1,0:T(8,128)(2,1)S(1)} fusion(bf16[8,32,384]{2,1,0:T(8,128)(2,1)S(1)} %all_gather.3, f32[50,32]{0,1:T(8,128)S(1)} %fusion.49, f32[50,8]{0,1:T(8,128)S(1)} %fusion.57, f32[50]{0:T(128)} %constant.213), kind=kOutput, calls=%fused_computation.17 | convolution fusion | flops 9894400 | bytes 243208 | tf_op jit(solution)/shard_map/dot_general | solution.py:374
  8.2 1.1 %fusion.20 = f32[1,256]{1,0:T(1,128)S(1)} fusion(bf16[4,384,256]{2,1,0:T(8,128)(2,1)} %param.21, bf16[50,384]{1,0:T(8,128)(2,1)S(1)} %fusion.10), kind=kOutput, calls=%fused_computation.31 | convolution fusion | flops 196608 | bytes 199168 | tf_op jit(solution)/shard_map/dot_general | solution.py:380
  9.2 1.1 %convolution_convert_fusion.3 = bf16[4,256]{1,0:T(4,128)(2,1)S(1)} fusion(bf16[4,384,256]{2,1,0:T(8,128)(2,1)} %param.21, bf16[50,384]{1,0:T(8,128)(2,1)S(1)} %fusion.10), kind=kOutput, calls=%fused_computation.20 | convolution fusion | flops 787456 | bytes 201728 | tf_op jit(solution)/shard_map/dot_general | solution.py:380
  10.3 1.1 %convolution_convert_fusion.2 = bf16[9,256]{1,0:T(8,128)(2,1)S(1)} fusion(bf16[4,384,256]{2,1,0:T(8,128)(2,1)} %param.21, bf16[50,384]{1,0:T(8,128)(2,1)S(1)} %fusion.10), kind=kOutput, calls=%fused_computation.19 | convolution fusion | flops 1771776 | bytes 213504 | tf_op jit(solution)/shard_map/dot_general | solution.py:380
  11.4 0.0 copy-start.15
  11.4 0.0 copy-start.17
  11.4 0.0 copy-start.18
  11.4 1.1 %convolution_convert_fusion.1 = bf16[36,256]{1,0:T(8,128)(2,1)S(1)} fusion(bf16[4,384,256]{2,1,0:T(8,128)(2,1)} %param.21, bf16[50,384]{1,0:T(8,128)(2,1)S(1)} %fusion.10), kind=kOutput, calls=%fused_computation.18 | convolution fusion | flops 7087104 | bytes 245760 | tf_op jit(solution)/shard_map/dot_general | solution.py:380
  12.6 0.6 pad_maximum_fusion.4
  13.2 2.6 %collective-permute-start.1 = (bf16[50,256]{1,0:T(8,128)(2,1)}, bf16[50,256]{1,0:T(8,128)(2,1)S(1)}, u32[]{:S(2)}, u32[]{:S(2)}) collective-permute-start(bf16[50,256]{1,0:T(8,128)(2,1)} %pad_maximum_fusion.4), channel_id=1, source_target_pairs={{0,2},{1,3},{2,0},{3,1},{4,6},{5,7},{6,4},{7,5},{8,10},{9,11},{10,... | collective-permute-start | bytes 76808 | tf_op jit(solution)/shard_map/ppermute | solution.py:20
  15.8 1.6 %collective-permute-start = (bf16[50,256]{1,0:T(8,128)(2,1)}, bf16[50,256]{1,0:T(8,128)(2,1)S(1)}, u32[]{:S(2)}, u32[]{:S(2)}) collective-permute-start(bf16[50,256]{1,0:T(8,128)(2,1)} %pad_maximum_fusion.4), channel_id=1, source_target_pairs={{0,1},{1,2},{2,3},{3,0},{4,5},{5,6},{6,7},{7,4},{8,9},{9,10},{10,1... | collective-permute-start | bytes 76808 | tf_op jit(solution)/shard_map/ppermute | solution.py:20
  17.4 2.3 %collective-permute-start.2 = (bf16[50,256]{1,0:T(8,128)(2,1)}, bf16[50,256]{1,0:T(8,128)(2,1)S(1)}, u32[]{:S(2)}, u32[]{:S(2)}) collective-permute-start(bf16[50,256]{1,0:T(8,128)(2,1)} %pad_maximum_fusion.4), channel_id=1, source_target_pairs={{0,3},{1,0},{2,1},{3,2},{4,7},{5,4},{6,5},{7,6},{8,11},{9,8},{10,9... | collective-permute-start | bytes 76808 | tf_op jit(solution)/shard_map/ppermute | solution.py:20
  19.6 1.0 %pad_dynamic-slice_fusion.2 = (bf16[4,20,192]{2,1,0:T(8,128)(2,1)S(1)}, bf16[4,20,192]{2,1,0:T(8,128)(2,1)S(1)}, bf16[4,20,192]{2,1,0:T(8,128)(2,1)S(1)}) fusion(s32[]{:T(128)S(6)} %select_n.93, bf16[4,64,192]{2,1,0:T(8,128)(2,1)} %param.19, s32[]{:T(128)S(6)} %select_n.91, s32[]{:T(128)S(6)} %select_n.95), kind=kLoop, calls=%fused_computation.41 | loop fusion | bytes 190476 | tf_op jit(solution)/shard_map/dynamic_slice | solution.py:28
  20.7 0.1 collective-permute-start.7
  20.7 0.6 collective-permute-start.6
  21.4 0.6 fusion.78
  22.0 0.2 fusion.3.refs_5_
  22.3 1.3 %fusion.1.refs_4_ = bf16[16,64,256]{2,1,0:T(8,128)(2,1)S(1)} fusion(bf16[16,64,192]{2,1,0:T(8,128)(2,1)} %param.17, f32[256]{0:T(256)S(1)} %bitcast.86, bf16[192,256]{1,0:T(8,128)(2,1)S(1)} %copy-done.19), kind=kOutput, calls=%fused_computation.3 | convolution fusion | flops 101449728 | bytes 1016832 | tf_op jit(solution)/shard_map/dot_general | solution.py:90
  23.6 0.8 %copy-done.10 = bf16[16,64,256]{2,1,0:T(8,128)(2,1)} copy-done((bf16[16,64,256]{2,1,0:T(8,128)(2,1)}, bf16[16,64,256]{2,1,0:T(8,128)(2,1)S(1)}, u32[]{:S(2)}) %copy-start.10) | copy-done | bytes 524312
  24.5 0.1 fusion.47
  24.6 0.1 fusion.55
  24.8 2.0 %fusion.11 = f32[1,6,32,256]{3,0,2,1:T(1,128)S(1)} fusion(bf16[3,3,384,256]{3,2,1,0:T(8,128)(2,1)S(1)} %copy-done, bf16[1,8,32,384]{3,2,1,0:T(8,128)(2,1)S(1)} %fusion.15), kind=kOutput, calls=%fused_computation.21 | convolution fusion | flops 332660736 | bytes 2162688 | tf_op jit(solution)/shard_map/conv_general_dilated | solution.py:78
  26.8 0.2 fusion.32
  27.0 0.6 compare_and_fusion
  27.5 0.6 gather_fusion
  28.2 0.1 dynamic-slice
  28.3 3.3 %collective-permute-start.8 = (bf16[4,20,192]{2,1,0:T(8,128)(2,1)S(1)}, bf16[4,20,192]{2,1,0:T(8,128)(2,1)S(1)}, u32[]{:S(2)}, u32[]{:S(2)}) collective-permute-start(bf16[4,20,192]{2,1,0:T(8,128)(2,1)S(1)} %get-tuple-element.15), channel_id=1, source_target_pairs={{0,3},{1,0},{2,1},{3,2},{4,7},{5,4},{6,5},{7,6},{8,11},{9,8},{10,9... | collective-permute-start | bytes 92168 | tf_op jit(solution)/shard_map/ppermute | solution.py:34
  31.8 0.4 convolution_convert_fusion
  32.2 2.7 %fusion.13 = f32[1,6,32,256]{3,0,2,1:T(1,128)S(1)} fusion(bf16[3,3,256,256]{3,2,1,0:T(8,128)(2,1)} %param.23, bf16[1,8,32,256]{3,2,1,0:T(8,128)(2,1)S(1)} %bitcast.76), kind=kOutput, calls=%fused_computation.24 | convolution fusion | flops 221773824 | bytes 1507328 | tf_op jit(solution)/shard_map/conv_general_dilated | solution.py:78
  35.0 0.2 convolution_add_fusion.3
  35.2 0.1 fusion.28
  35.3 0.0 collective-permute-done.7
  35.4 0.2 fusion.9.refs_6_
  35.6 1.9 %collective-permute-start.9 = (bf16[232,256]{1,0:T(8,128)(2,1)S(1)}, bf16[232,256]{1,0:T(8,128)(2,1)S(1)}, u32[]{:S(2)}, u32[]{:S(2)}) collective-permute-start(bf16[232,256]{1,0:T(8,128)(2,1)S(1)} %pad_maximum_fusion), channel_id=1, source_target_pairs={{0,4},{4,8},{8,12},{1,5},{5,9},{9,13},{2,6},{6,10},{10,14},{3,7},{... | collective-permute-start | bytes 356360 | tf_op jit(solution)/shard_map/ppermute | solution.py:43
  37.6 3.6 %collective-permute-start.10 = (bf16[232,256]{1,0:T(8,128)(2,1)S(1)}, bf16[232,256]{1,0:T(8,128)(2,1)S(1)}, u32[]{:S(2)}, u32[]{:S(2)}) collective-permute-start(bf16[232,256]{1,0:T(8,128)(2,1)S(1)} %pad_maximum_fusion.1), channel_id=1, source_target_pairs={{4,0},{8,4},{12,8},{5,1},{9,5},{13,9},{6,2},{10,6},{14,10},{7,3},{... | collective-permute-start | bytes 356360 | tf_op jit(solution)/shard_map/ppermute | solution.py:43
  41.3 0.7 pad_dynamic-slice_fusion.5
  42.0 2.3 %collective-permute-start.5 = (bf16[6,12,256]{2,1,0:T(8,128)(2,1)S(1)}, bf16[6,12,256]{2,1,0:T(8,128)(2,1)S(1)}, u32[]{:S(2)}, u32[]{:S(2)}) collective-permute-start(bf16[6,12,256]{2,1,0:T(8,128)(2,1)S(1)} %get-tuple-element.16), channel_id=1, source_target_pairs={{0,3},{1,0},{2,1},{3,2},{4,7},{5,4},{6,5},{7,6},{8,11},{9,8},{10,9... | collective-permute-start | bytes 110600 | tf_op jit(solution)/shard_map/ppermute | solution.py:34
  44.3 0.8 %collective-permute-start.4 = (bf16[6,12,256]{2,1,0:T(8,128)(2,1)S(1)}, bf16[6,12,256]{2,1,0:T(8,128)(2,1)S(1)}, u32[]{:S(2)}, u32[]{:S(2)}) collective-permute-start(bf16[6,12,256]{2,1,0:T(8,128)(2,1)S(1)} %get-tuple-element.18), channel_id=1, source_target_pairs={{0,2},{1,3},{2,0},{3,1},{4,6},{5,7},{6,4},{7,5},{8,10},{9,11},{10,... | collective-permute-start | bytes 110600 | tf_op jit(solution)/shard_map/ppermute | solution.py:34
  45.3 0.1 maximum_maximum_fusion
  45.4 5.5 %collective-permute-start.11 = (bf16[64,256]{1,0:T(8,128)(2,1)S(1)}, bf16[64,256]{1,0:T(8,128)(2,1)S(1)}, u32[]{:S(2)}, u32[]{:S(2)}) collective-permute-start(bf16[64,256]{1,0:T(8,128)(2,1)S(1)} %pad_maximum_fusion.2), channel_id=1, source_target_pairs={{0,1},{1,2},{2,3},{4,5},{5,6},{6,7},{8,9},{9,10},{10,11},{12,13},{... | collective-permute-start | bytes 98312 | tf_op jit(solution)/shard_map/ppermute | solution.py:43
  51.0 1.5 %collective-permute-start.12 = (bf16[64,256]{1,0:T(8,128)(2,1)S(1)}, bf16[64,256]{1,0:T(8,128)(2,1)S(1)}, u32[]{:S(2)}, u32[]{:S(2)}) collective-permute-start(bf16[64,256]{1,0:T(8,128)(2,1)S(1)} %pad_maximum_fusion.3), channel_id=1, source_target_pairs={{1,0},{2,1},{3,2},{5,4},{6,5},{7,6},{9,8},{10,9},{11,10},{13,12},{... | collective-permute-start | bytes 98312 | tf_op jit(solution)/shard_map/ppermute | solution.py:43
  52.4 0.6 pad_add_fusion.here_ref
  53.1 3.7 %collective-permute-done.12.refs_10_ = bf16[64,256]{1,0:T(8,128)(2,1)S(1)} collective-permute-done((bf16[64,256]{1,0:T(8,128)(2,1)S(1)}, bf16[64,256]{1,0:T(8,128)(2,1)S(1)}, u32[]{:S(2)}, u32[]{:S(2)}) %collective-permute-start.12) | collective-permute-done | bytes 32800 | tf_op jit(solution)/shard_map/ppermute | solution.py:43
  56.8 0.6 copy-done.24
  57.4 17.8 %shard_map.163 = bf16[16,64,256]{2,1,0:T(8,128)(2,1)} custom-call(s32[2]{0:T(128)} %pad_add_fusion.here_ref, bf16[6,12,256]{2,1,0:T(8,128)(2,1)} %get-tuple-element.19.refs_0_, bf16[6,12,256]{2,1,0:T(8,128)(2,1)} %copy-done.21, bf16[6,12,256]{2,1,0:T(8,128)(2,1)} %copy-done.22, bf16[6,12,256]{2,1,0:T(8,128)(2,1)} %copy-done.20, ...), custom_call_target="tpu_custom_call" | custom-call | flops 10000000000 | bytes 12000000 | tf_op jit(solution)/shard_map/pallas_call | solution.py:315
  (95 shorter events, 0.7 us)
Async XLA Ops:
  0.0 24.7 %copy-start = (bf16[3,3,384,256]{3,2,1,0:T(8,128)(2,1)S(1)}, bf16[3,3,384,256]{3,2,1,0:T(8,128)(2,1)}, u32[]{:S(2)}) copy-start(bf16[3,3,384,256]{3,2,1,0:T(8,128)(2,1)} %param.22) | copy-start | bytes 5308420
  0.0 21.4 %copy-start.1 = (f32[12,256]{1,0:T(8,128)S(1)}, f32[12,256]{1,0:T(8,128)}, u32[]{:S(2)}) copy-start(f32[12,256]{1,0:T(8,128)} %refs_11_.1) | copy-start | bytes 36868
  0.0 22.0 %copy-start.7 = (bf16[384,256]{1,0:T(8,128)(2,1)S(1)}, bf16[384,256]{1,0:T(8,128)(2,1)}, u32[]{:S(2)}) copy-start(bf16[384,256]{1,0:T(8,128)(2,1)} %param.25) | copy-start | bytes 589828
  0.0 22.0 %copy-start.6 = (bf16[8,32,384]{2,1,0:T(8,128)(2,1)S(1)}, bf16[8,32,384]{2,1,0:T(8,128)(2,1)}, u32[]{:S(2)}) copy-start(bf16[8,32,384]{2,1,0:T(8,128)(2,1)} %param.18) | copy-start | bytes 589828
  0.0 22.2 %copy-start.19 = (bf16[192,256]{1,0:T(8,128)(2,1)S(1)}, bf16[192,256]{1,0:T(8,128)(2,1)}, u32[]{:S(2)}) copy-start(bf16[192,256]{1,0:T(8,128)(2,1)} %param.24) | copy-start | bytes 294916
  9.2 15.2 %copy-start.12 = (s32[50]{0:T(128)S(1)}, s32[50]{0:T(128)}, u32[]{:S(2)}) copy-start(s32[50]{0:T(128)} %constant.145.clone) | copy-start | bytes 604
  11.4 13.1 %copy-start.14 = (f32[50]{0:T(128)S(1)}, f32[50]{0:T(128)}, u32[]{:S(2)}) copy-start(f32[50]{0:T(128)} %constant.158) | copy-start | bytes 604
  11.4 13.1 %copy-start.15 = (f32[50]{0:T(128)S(1)}, f32[50]{0:T(128)}, u32[]{:S(2)}) copy-start(f32[50]{0:T(128)} %constant.157) | copy-start | bytes 604
  11.4 13.1 %copy-start.17 = (f32[50]{0:T(128)S(1)}, f32[50]{0:T(128)}, u32[]{:S(2)}) copy-start(f32[50]{0:T(128)} %constant.215) | copy-start | bytes 604
  11.4 13.2 %copy-start.18 = (f32[50]{0:T(128)S(1)}, f32[50]{0:T(128)}, u32[]{:S(2)}) copy-start(f32[50]{0:T(128)} %constant.214) | copy-start | bytes 604
  13.2 15.1 %collective-permute-start.1 = (bf16[50,256]{1,0:T(8,128)(2,1)}, bf16[50,256]{1,0:T(8,128)(2,1)S(1)}, u32[]{:S(2)}, u32[]{:S(2)}) collective-permute-start(bf16[50,256]{1,0:T(8,128)(2,1)} %pad_maximum_fusion.4), channel_id=1, source_target_pairs={{0,2},{1,3},{2,0},{3,1},{4,6},{5,7},{6,4},{7,5},{8,10},{9,11},{10,... | collective-permute-start | bytes 76808 | tf_op jit(solution)/shard_map/ppermute | solution.py:20
  15.8 15.8 %collective-permute-start = (bf16[50,256]{1,0:T(8,128)(2,1)}, bf16[50,256]{1,0:T(8,128)(2,1)S(1)}, u32[]{:S(2)}, u32[]{:S(2)}) collective-permute-start(bf16[50,256]{1,0:T(8,128)(2,1)} %pad_maximum_fusion.4), channel_id=1, source_target_pairs={{0,1},{1,2},{2,3},{3,0},{4,5},{5,6},{6,7},{7,4},{8,9},{9,10},{10,1... | collective-permute-start | bytes 76808 | tf_op jit(solution)/shard_map/ppermute | solution.py:20
  17.4 14.2 %collective-permute-start.2 = (bf16[50,256]{1,0:T(8,128)(2,1)}, bf16[50,256]{1,0:T(8,128)(2,1)S(1)}, u32[]{:S(2)}, u32[]{:S(2)}) collective-permute-start(bf16[50,256]{1,0:T(8,128)(2,1)} %pad_maximum_fusion.4), channel_id=1, source_target_pairs={{0,3},{1,0},{2,1},{3,2},{4,7},{5,4},{6,5},{7,6},{8,11},{9,8},{10,9... | collective-permute-start | bytes 76808 | tf_op jit(solution)/shard_map/ppermute | solution.py:20
  20.7 14.7 %collective-permute-start.7 = (bf16[4,20,192]{2,1,0:T(8,128)(2,1)S(1)}, bf16[4,20,192]{2,1,0:T(8,128)(2,1)S(1)}, u32[]{:S(2)}, u32[]{:S(2)}) collective-permute-start(bf16[4,20,192]{2,1,0:T(8,128)(2,1)S(1)} %get-tuple-element.13), channel_id=1, source_target_pairs={{0,2},{1,3},{2,0},{3,1},{4,6},{5,7},{6,4},{7,5},{8,10},{9,11},{10,... | collective-permute-start | bytes 92168 | tf_op jit(solution)/shard_map/ppermute | solution.py:34
  20.7 14.3 %collective-permute-start.6 = (bf16[4,20,192]{2,1,0:T(8,128)(2,1)S(1)}, bf16[4,20,192]{2,1,0:T(8,128)(2,1)S(1)}, u32[]{:S(2)}, u32[]{:S(2)}) collective-permute-start(bf16[4,20,192]{2,1,0:T(8,128)(2,1)S(1)} %get-tuple-element.14), channel_id=1, source_target_pairs={{0,1},{1,2},{2,3},{3,0},{4,5},{5,6},{6,7},{7,4},{8,9},{9,10},{10,1... | collective-permute-start | bytes 92168 | tf_op jit(solution)/shard_map/ppermute | solution.py:34
  22.2 4.6 %copy-start.4 = (bf16[8,32,256]{2,1,0:T(8,128)(2,1)}, bf16[8,32,256]{2,1,0:T(8,128)(2,1)S(1)}, u32[]{:S(2)}) copy-start(bf16[8,32,256]{2,1,0:T(8,128)(2,1)S(1)} %fusion.3.refs_5_) | copy-start | bytes 393220
  23.6 0.8 %copy-start.10 = (bf16[16,64,256]{2,1,0:T(8,128)(2,1)}, bf16[16,64,256]{2,1,0:T(8,128)(2,1)S(1)}, u32[]{:S(2)}) copy-start(bf16[16,64,256]{2,1,0:T(8,128)(2,1)S(1)} %fusion.1.refs_4_) | copy-start | bytes 1572868
  24.7 2.0 %copy-start.2 = (bf16[4,64,192]{2,1,0:T(8,128)(2,1)S(1)}, bf16[4,64,192]{2,1,0:T(8,128)(2,1)}, u32[]{:S(2)}) copy-start(bf16[4,64,192]{2,1,0:T(8,128)(2,1)} %param.19) | copy-start | bytes 294916
  24.7 2.0 %copy-start.3 = (bf16[768,256]{1,0:T(8,128)(2,1)S(1)}, bf16[768,256]{1,0:T(8,128)(2,1)}, u32[]{:S(2)}) copy-start(bf16[768,256]{1,0:T(8,128)(2,1)} %param.26) | copy-start | bytes 1179652
  26.8 5.0 %copy-start.13 = (s32[50]{0:T(128)S(1)}, s32[50]{0:T(128)}, u32[]{:S(2)}) copy-start(s32[50]{0:T(128)} %constant.145.clone) | copy-start | bytes 604
  28.3 6.9 %collective-permute-start.8 = (bf16[4,20,192]{2,1,0:T(8,128)(2,1)S(1)}, bf16[4,20,192]{2,1,0:T(8,128)(2,1)S(1)}, u32[]{:S(2)}, u32[]{:S(2)}) collective-permute-start(bf16[4,20,192]{2,1,0:T(8,128)(2,1)S(1)} %get-tuple-element.15), channel_id=1, source_target_pairs={{0,3},{1,0},{2,1},{3,2},{4,7},{5,4},{6,5},{7,6},{8,11},{9,8},{10,9... | collective-permute-start | bytes 92168 | tf_op jit(solution)/shard_map/ppermute | solution.py:34
  32.2 3.1 %copy-start.11 = (f32[1,256]{1,0:T(1,128)S(1)}, f32[1,256]{1,0:T(1,128)}, u32[]{:S(2)}) copy-start(f32[1,256]{1,0:T(1,128)} %get-tuple-element.34) | copy-start | bytes 3076
  32.2 3.1 %copy-start.16 = (pred[20]{0:T(512)(128)(4,1)S(1)}, pred[20]{0:T(512)(128)(4,1)}, u32[]{:S(2)}) copy-start(pred[20]{0:T(512)(128)(4,1)} %compare_and_fusion) | copy-start | bytes 64
  35.6 21.2 %copy-start.5 = (bf16[4,20,256]{2,1,0:T(8,128)(2,1)}, bf16[4,20,256]{2,1,0:T(8,128)(2,1)S(1)}, u32[]{:S(2)}) copy-start(bf16[4,20,256]{2,1,0:T(8,128)(2,1)S(1)} %fusion.9.refs_6_) | copy-start | bytes 122884
  35.6 9.4 %collective-permute-start.9 = (bf16[232,256]{1,0:T(8,128)(2,1)S(1)}, bf16[232,256]{1,0:T(8,128)(2,1)S(1)}, u32[]{:S(2)}, u32[]{:S(2)}) collective-permute-start(bf16[232,256]{1,0:T(8,128)(2,1)S(1)} %pad_maximum_fusion), channel_id=1, source_target_pairs={{0,4},{4,8},{8,12},{1,5},{5,9},{9,13},{2,6},{6,10},{10,14},{3,7},{... | collective-permute-start | bytes 356360 | tf_op jit(solution)/shard_map/ppermute | solution.py:43
  37.6 7.5 %collective-permute-start.10 = (bf16[232,256]{1,0:T(8,128)(2,1)S(1)}, bf16[232,256]{1,0:T(8,128)(2,1)S(1)}, u32[]{:S(2)}, u32[]{:S(2)}) collective-permute-start(bf16[232,256]{1,0:T(8,128)(2,1)S(1)} %pad_maximum_fusion.1), channel_id=1, source_target_pairs={{4,0},{8,4},{12,8},{5,1},{9,5},{13,9},{6,2},{10,6},{14,10},{7,3},{... | collective-permute-start | bytes 356360 | tf_op jit(solution)/shard_map/ppermute | solution.py:43
  42.0 11.0 %collective-permute-start.5 = (bf16[6,12,256]{2,1,0:T(8,128)(2,1)S(1)}, bf16[6,12,256]{2,1,0:T(8,128)(2,1)S(1)}, u32[]{:S(2)}, u32[]{:S(2)}) collective-permute-start(bf16[6,12,256]{2,1,0:T(8,128)(2,1)S(1)} %get-tuple-element.16), channel_id=1, source_target_pairs={{0,3},{1,0},{2,1},{3,2},{4,7},{5,4},{6,5},{7,6},{8,11},{9,8},{10,9... | collective-permute-start | bytes 110600 | tf_op jit(solution)/shard_map/ppermute | solution.py:34
  44.3 8.7 %collective-permute-start.3 = (bf16[6,12,256]{2,1,0:T(8,128)(2,1)S(1)}, bf16[6,12,256]{2,1,0:T(8,128)(2,1)S(1)}, u32[]{:S(2)}, u32[]{:S(2)}) collective-permute-start(bf16[6,12,256]{2,1,0:T(8,128)(2,1)S(1)} %get-tuple-element.17), channel_id=1, source_target_pairs={{0,1},{1,2},{2,3},{3,0},{4,5},{5,6},{6,7},{7,4},{8,9},{9,10},{10,1... | collective-permute-start | bytes 110600 | tf_op jit(solution)/shard_map/ppermute | solution.py:34
  44.3 8.7 %collective-permute-start.4 = (bf16[6,12,256]{2,1,0:T(8,128)(2,1)S(1)}, bf16[6,12,256]{2,1,0:T(8,128)(2,1)S(1)}, u32[]{:S(2)}, u32[]{:S(2)}) collective-permute-start(bf16[6,12,256]{2,1,0:T(8,128)(2,1)S(1)} %get-tuple-element.18), channel_id=1, source_target_pairs={{0,2},{1,3},{2,0},{3,1},{4,6},{5,7},{6,4},{7,5},{8,10},{9,11},{10,... | collective-permute-start | bytes 110600 | tf_op jit(solution)/shard_map/ppermute | solution.py:34
  45.1 11.7 %copy-start.8 = (bf16[232,256]{1,0:T(8,128)(2,1)}, bf16[232,256]{1,0:T(8,128)(2,1)S(1)}, u32[]{:S(2)}) copy-start(bf16[232,256]{1,0:T(8,128)(2,1)S(1)} %collective-permute-done.9.refs_7_) | copy-start | bytes 356356
  45.1 11.7 %copy-start.9 = (bf16[232,256]{1,0:T(8,128)(2,1)}, bf16[232,256]{1,0:T(8,128)(2,1)S(1)}, u32[]{:S(2)}) copy-start(bf16[232,256]{1,0:T(8,128)(2,1)S(1)} %collective-permute-done.10.refs_8_) | copy-start | bytes 356356
  45.4 7.6 %collective-permute-start.11 = (bf16[64,256]{1,0:T(8,128)(2,1)S(1)}, bf16[64,256]{1,0:T(8,128)(2,1)S(1)}, u32[]{:S(2)}, u32[]{:S(2)}) collective-permute-start(bf16[64,256]{1,0:T(8,128)(2,1)S(1)} %pad_maximum_fusion.2), channel_id=1, source_target_pairs={{0,1},{1,2},{2,3},{4,5},{5,6},{6,7},{8,9},{9,10},{10,11},{12,13},{... | collective-permute-start | bytes 98312 | tf_op jit(solution)/shard_map/ppermute | solution.py:43
  51.0 5.8 %collective-permute-start.12 = (bf16[64,256]{1,0:T(8,128)(2,1)S(1)}, bf16[64,256]{1,0:T(8,128)(2,1)S(1)}, u32[]{:S(2)}, u32[]{:S(2)}) collective-permute-start(bf16[64,256]{1,0:T(8,128)(2,1)S(1)} %pad_maximum_fusion.3), channel_id=1, source_target_pairs={{1,0},{2,1},{3,2},{5,4},{6,5},{7,6},{9,8},{10,9},{11,10},{13,12},{... | collective-permute-start | bytes 98312 | tf_op jit(solution)/shard_map/ppermute | solution.py:43
  53.0 3.8 %copy-start.20 = (bf16[6,12,256]{2,1,0:T(8,128)(2,1)}, bf16[6,12,256]{2,1,0:T(8,128)(2,1)S(1)}, u32[]{:S(2)}) copy-start(bf16[6,12,256]{2,1,0:T(8,128)(2,1)S(1)} %collective-permute-done.5.refs_3_) | copy-start | bytes 110596
  53.0 3.8 %copy-start.21 = (bf16[6,12,256]{2,1,0:T(8,128)(2,1)}, bf16[6,12,256]{2,1,0:T(8,128)(2,1)S(1)}, u32[]{:S(2)}) copy-start(bf16[6,12,256]{2,1,0:T(8,128)(2,1)S(1)} %collective-permute-done.3.refs_1_) | copy-start | bytes 110596
  53.0 3.8 %copy-start.22 = (bf16[6,12,256]{2,1,0:T(8,128)(2,1)}, bf16[6,12,256]{2,1,0:T(8,128)(2,1)S(1)}, u32[]{:S(2)}) copy-start(bf16[6,12,256]{2,1,0:T(8,128)(2,1)S(1)} %collective-permute-done.4.refs_2_) | copy-start | bytes 110596
  53.0 3.8 %copy-start.23 = (bf16[64,256]{1,0:T(8,128)(2,1)}, bf16[64,256]{1,0:T(8,128)(2,1)S(1)}, u32[]{:S(2)}) copy-start(bf16[64,256]{1,0:T(8,128)(2,1)S(1)} %collective-permute-done.11.refs_9_) | copy-start | bytes 98308
  56.8 0.6 copy-start.24

commit v3 on v2

v3 whole, which is shorter than its diff:
```python
import functools

import jax
import jax.numpy as jnp
import numpy as np
from jax import lax
from jax.experimental import pallas as pl
from jax.experimental.pallas import tpu as pltpu
from jax.sharding import PartitionSpec as P

highest = lax.Precision.HIGHEST
bin_sides = (1, 2, 3, 6)
rim = 2
f32 = jnp.float32
bf16 = jnp.bfloat16
vmem_spec = pl.BlockSpec(memory_space=pltpu.VMEM)
smem_spec = pl.BlockSpec(memory_space=pltpu.SMEM)
params = pltpu.CompilerParams(vmem_limit_bytes=24 * 1024 * 1024)


def shifted(value, axis, shift):
    count = lax.axis_size(axis)
    return lax.ppermute(value, axis, [(i, (i + shift) % count) for i in range(count)])


def edge_swap(low_out, high_out, axis):
    count = lax.axis_size(axis)
    forward = [(i, i + 1) for i in range(count - 1)]
    backward = [(target, source) for source, target in forward]
    return lax.ppermute(high_out, axis, forward), lax.ppermute(low_out, axis, backward)


def cell_table(extent_rows, extent_cols):
    rows = []
    for number, side in enumerate(bin_sides):
        for i in range(side):
            for j in range(side):
                top, low = i * extent_rows // side, -(-(i + 1) * extent_rows // side)
                left, right = j * extent_cols // side, -(-(j + 1) * extent_cols // side)
                rows.append([number, side, i, j, top, low, left, right, (low - top) * (right - left)])
    padded = (len(rows) + 15) // 16 * 16
    table = np.zeros((padded, 16), np.float32)
    table[:, 0] = -1.0
    table[:, 1] = 1.0
    table[:, 8] = 1.0
    table[: len(rows), :9] = np.array(rows, np.float32)
    return table


def dot(a, b):
    return jnp.dot(a, b, preferred_element_type=f32)


def call(kernel, outs, specs, scratch, flops, moved):
    return pl.pallas_call(
        kernel,
        out_shape=outs,
        in_specs=specs,
        out_specs=jax.tree.map(lambda _: vmem_spec, outs),
        scratch_shapes=scratch,
        compiler_params=params,
        cost_estimate=pl.CostEstimate(flops=flops, bytes_accessed=moved, transcendentals=0),
    )


def wrap(value, count):
    return lax.rem(value + count, count)


def floor_div(value, step):
    return jnp.floor((value + 0.5) / step)


def lateral_kernel(col_count, here_ref, one_ref, two_ref, three_ref, w1_ref, w2_ref, w3_ref, bias_ref, *refs):
    (lat1_ref, lat2_ref), pieces, (wide_buf, one_buf, two_buf, piece_buf) = (
        refs[:2],
        refs[2 : 2 + col_count],
        refs[2 + col_count :],
    )
    channels = w1_ref.shape[1]
    for source, weight, row, buf, out in (
        (one_ref, w1_ref, 5, one_buf, lat1_ref),
        (two_ref, w2_ref, 6, two_buf, lat2_ref),
    ):
        high, wide, depth = source.shape
        value = dot(source[...].reshape(high * wide, depth), weight[...])
        value = jnp.maximum(value + bias_ref[row : row + 1, :], 0.0).reshape(high, wide, channels)
        buf[...] = value
        out[...] = value.astype(bf16)
    high3, whole3, share = three_ref.shape
    wide3 = whole3 // col_count
    col_here = here_ref[1]
    weight = w3_ref[pl.ds(pl.multiple_of(col_here * share, 16), share), :]
    value = dot(three_ref[...].reshape(high3 * whole3, share), weight)
    wide_buf[...] = jnp.zeros_like(wide_buf)
    wide_buf[:, rim : rim + whole3, :] = value.reshape(high3, whole3, channels)
    span = wide3 + 2 * rim
    for shift, piece in enumerate(pieces):
        target = wrap(col_here + shift, col_count)
        for row in range(high3):
            piece_buf[row * span : (row + 1) * span, :] = wide_buf[
                row, pl.ds(pl.multiple_of(target * wide3, 8), span), :
            ]
        start = high3 * span
        for buf in (one_buf, two_buf):
            high, wide = buf.shape[:2]
            first = wide - rim if shift == 1 else 0
            for row in range(high):
                piece_buf[start : start + rim, :] = buf[row, first : first + rim, :]
                start += rim
        piece[...] = piece_buf[...].astype(bf16)


def bins_kernel(row_count, col_count, window_rows, here_ref, table_ref, weight_ref, *refs):
    blocks, pieces, messages = (
        refs[:row_count],
        refs[row_count : row_count + col_count],
        refs[row_count + col_count :],
    )
    table = table_ref[...]
    high, wide, depth = blocks[0].shape
    place = lax.broadcasted_iota(jnp.int32, (1, high * wide), 1).astype(f32)
    place_row = floor_div(place, wide)
    place_col = place - place_row * wide
    in_cols = (place_col >= table[:, 6:7]) & (place_col < table[:, 7:8])
    pooled = None
    for shift, block in enumerate(blocks):
        row = place_row + (wrap(here_ref[0] - shift, row_count) * high).astype(f32)
        inside = in_cols & (row >= table[:, 4:5]) & (row < table[:, 5:6])
        inside = jnp.where(inside, 1.0, 0.0).astype(bf16)
        term = dot(inside, block[...].reshape(high * wide, depth))
        pooled = term if pooled is None else pooled + term
    pooled = (pooled / table[:, 8:9]).astype(bf16)
    bins = None
    for number in range(len(bin_sides)):
        term = jnp.where(table[:, 0:1] == number, dot(pooled, weight_ref[number]), 0.0)
        bins = term if bins is None else bins + term
    bins = bins.astype(bf16)
    cells = bins.shape[0]
    for piece, message in zip(pieces, messages):
        message[0:window_rows, :] = piece[0:window_rows, :]
        message[window_rows : window_rows + cells, :] = bins
        if message.shape[0] > window_rows + cells:
            message[window_rows + cells :, :] = piece[window_rows:, :]


def feature_kernel(row_count, here_ref, weight_ref, *refs):
    blocks, (out_ref, grid_buf) = refs[:row_count], refs[row_count:]
    high, wide, depth = blocks[0].shape
    grid_buf[...] = jnp.zeros_like(grid_buf)
    for shift, block in enumerate(blocks):
        row = wrap(here_ref[0] - shift, row_count) * high + rim + 1
        grid_buf[pl.ds(row, high)] = block[...]
    rows = out_ref.shape[1] // wide
    window = grid_buf[pl.ds(here_ref[0] * high, rows + 2)].reshape((rows + 2) * wide, depth)
    for col_tap in range(3):
        total = dot(window[0 : rows * wide], weight_ref[0, col_tap])
        for row_tap in (1, 2):
            total = total + dot(
                window[row_tap * wide : (row_tap + rows) * wide], weight_ref[row_tap, col_tap]
            )
        out_ref[col_tap] = total


def neck_kernel(
    row_count, col_count, high, window_rows, here_ref, table_ref, turned_ref, weight_ref, bias_ref, taps_ref, *refs
):
    messages, refs = refs[:col_count], refs[col_count:]
    windows, (bins_buf, acc_buf, term_buf) = refs[:col_count], refs[col_count:]
    rows, span, channels = windows[0].shape
    wide = taps_ref.shape[1] // rows
    width4 = span - 2 * rim
    table = table_ref[...]
    cells = table.shape[0]
    bins = messages[0][window_rows : window_rows + cells, :].astype(f32)
    for message in messages[1:]:
        bins = bins + message[window_rows : window_rows + cells, :].astype(f32)
    bias = jnp.zeros((cells, channels), f32)
    for number in range(len(bin_sides)):
        bias = jnp.where(table[:, 0:1] == number, bias_ref[number : number + 1, :], bias)
    share = weight_ref.shape[2]
    first = here_ref[1] * share
    mine = table[:, 0:1] == (first // channels).astype(f32)
    bins_buf[...] = jnp.where(mine, jnp.maximum(bins + bias, 0.0), 0.0)
    if share == channels:
        binned = bins_buf[...]
    else:
        binned = bins_buf[:, pl.ds(pl.multiple_of(lax.rem(first, channels), 128), share)]
    place = lax.broadcasted_iota(jnp.int32, ((rows + 2) * wide, 1), 0).astype(f32)
    place_row = floor_div(place, wide)
    place_col = place - place_row * wide
    place_row = place_row + (here_ref[0] * high - rim - 1).astype(f32)
    grid_rows = float(high * row_count)
    sides = turned_ref[1:2, :]

    def weights(position, extent, index):
        source = (position + 0.5) * sides / extent - 0.5
        source = jnp.minimum(jnp.maximum(source, 0.0), sides - 1.0)
        return jnp.maximum(0.0, 1.0 - jnp.abs(source - index))

    spread = weights(place_row, grid_rows, turned_ref[2:3, :])
    spread = spread * weights(place_col, float(wide), turned_ref[3:4, :])
    spread = jnp.where((place_row >= 0.0) & (place_row < grid_rows), spread, 0.0)
    ppm = jnp.dot(spread, binned, precision=highest, preferred_element_type=f32).astype(bf16)
    size = rows * wide
    for col_tap in range(3):
        total = taps_ref[col_tap]
        for row_tap in range(3):
            total = total + dot(
                ppm[row_tap * wide : row_tap * wide + size], weight_ref[row_tap, col_tap]
            )
        acc_buf[col_tap, 8 : 8 + size, :] = total
    col = place_col[0:size]
    total = (
        acc_buf[1, 8 : 8 + size, :]
        + jnp.where(col > 0.0, acc_buf[0, 7 : 7 + size, :], 0.0)
        + jnp.where(col < wide - 1.0, acc_buf[2, 9 : 9 + size, :], 0.0)
    )
    term_buf[...] = jnp.zeros_like(term_buf)
    term_buf[:, rim : rim + wide, :] = total.reshape(rows, wide, channels)
    for shift, window in enumerate(windows):
        target = wrap(here_ref[1] + shift, col_count)
        window[...] = term_buf[:, pl.ds(pl.multiple_of(target * width4, 8), span), :].astype(bf16)


def rows_kernel(col_count, high3, wide3, here_ref, bias_ref, lat1_ref, lat2_ref, *refs):
    messages, (lat3_ref, low_ref, high_ref, three_buf, pack_buf) = refs[:col_count], refs[col_count:]
    span = wide3 + 2 * rim
    total = messages[0][0 : high3 * span, :].astype(f32)
    for message in messages[1:]:
        total = total + message[0 : high3 * span, :].astype(f32)
    total = jnp.maximum(total + bias_ref[7:8, :], 0.0)
    col_here = here_ref[1]
    place = lax.broadcasted_iota(jnp.int32, (span, 1), 0) + col_here * wide3 - rim
    inside = (place >= 0) & (place < wide3 * col_count)
    for row in range(high3):
        three_buf[row, :span, :] = jnp.where(inside, total[row * span : (row + 1) * span], 0.0)
    lat3_ref[...] = three_buf[:, :span, :].astype(bf16)
    high1, wide1 = lat1_ref.shape[:2]
    high2, wide2 = lat2_ref.shape[:2]
    before, after = messages[1], messages[col_count - 1]
    sides_at = before.shape[0] - rim * (high1 + high2)
    for out, last in ((low_ref, False), (high_ref, True)):
        start, at = 0, sides_at
        for lat, high, wide in ((lat1_ref, high1, wide1), (lat2_ref, high2, wide2)):
            whole = wide + 2 * rim
            first = high - rim if last else 0
            left = before[at + rim * first : at + rim * (first + rim), :].astype(f32)
            right = after[at + rim * first : at + rim * (first + rim), :].astype(f32)
            left = jnp.where(col_here > 0, left, 0.0)
            right = jnp.where(col_here < col_count - 1, right, 0.0)
            for step in range(rim):
                pack_buf[start : start + rim, :] = left[rim * step : rim * (step + 1)]
                pack_buf[start + rim : start + rim + wide, :] = lat[first + step].astype(f32)
                pack_buf[start + rim + wide : start + whole, :] = right[rim * step : rim * (step + 1)]
                start += whole
            at += rim * high
        for step in range(rim):
            row = high3 - rim + step if last else step
            pack_buf[start : start + span, :] = three_buf[row, :span, :]
            start += span
        out[...] = pack_buf[...].astype(bf16)


def stretch_matrix(out_shape, out_first, in_shape, in_first, factor, extent):
    out_rows, out_pitch = out_shape
    in_rows, in_pitch = in_shape
    place = lax.broadcasted_iota(jnp.int32, (1, in_rows * in_pitch), 1).astype(f32)
    place_row = floor_div(place, in_pitch)
    place_col = place - place_row * in_pitch

    def weights(length, first_out, first_in, targets, whole):
        output = first_out + lax.broadcasted_iota(jnp.int32, (length, 1), 0).astype(f32)
        source = (output + 0.5) * (1.0 / factor) - 0.5
        source = jnp.minimum(jnp.maximum(source, 0.0), whole - 1.0)
        inside = jnp.where((output >= 0.0) & (output < whole * factor), 1.0, 0.0)
        return jnp.maximum(0.0, 1.0 - jnp.abs(source - (first_in + targets))) * inside

    down = weights(out_rows, out_first[0], in_first[0], place_row, extent[0])
    across = weights(out_pitch, out_first[1], in_first[1], place_col, extent[1])
    matrix = down[:, None, :] * across[None, :, :]
    return matrix.astype(bf16).reshape(out_rows * out_pitch, in_rows * in_pitch)


def tail_kernel(
    sizes,
    top_count,
    here_ref,
    *refs,
):
    (high1, wide1), (high2, wide2), (high3, wide3), (high4, wide4), (row_count, col_count) = sizes
    top_refs, refs = refs[:top_count], refs[top_count:]
    (
        lat1_ref,
        lat2_ref,
        lat3_ref,
        above_ref,
        below_ref,
        before_ref,
        after_ref,
        bias_ref,
        smooth_hbm,
        join_hbm,
        out_ref,
        top_buf,
        lat1_buf,
        lat2_buf,
        lat3_buf,
        pyr1_buf,
        pyr2_buf,
        pyr3_buf,
        acc_buf,
        sums_buf,
        stack_buf,
        smooth_w,
        join_w,
        sems,
    ) = refs
    smooth_copy = pltpu.make_async_copy(smooth_hbm, smooth_w, sems.at[0])
    join_copy = pltpu.make_async_copy(join_hbm, join_w, sems.at[1])
    smooth_copy.start()
    join_copy.start()
    row_here = here_ref[0].astype(f32)
    col_here = here_ref[1].astype(f32)
    channels = bias_ref.shape[1]

    def firsts(high, wide, border):
        return row_here * high - border, col_here * wide - border

    def extent(high, wide):
        return float(high * row_count), float(wide * col_count)

    side_start = before_ref.shape[0] - rim * (high1 + high2)
    row_start = 0
    for ref, buf, high, wide in (
        (lat1_ref, lat1_buf, high1, wide1),
        (lat2_ref, lat2_buf, high2, wide2),
        (lat3_ref, lat3_buf, high3, wide3 + 2 * rim),
    ):
        buf[...] = jnp.zeros_like(buf)
        whole = wide
        if buf is lat3_buf:
            buf[rim : rim + high, :wide, :] = ref[...].astype(f32)
        else:
            whole = wide + 2 * rim
            buf[rim : rim + high, rim : rim + wide, :] = ref[...].astype(f32)
            for source, col, keep in (
                (before_ref, 0, here_ref[1] > 0),
                (after_ref, rim + wide, here_ref[1] < col_count - 1),
            ):
                sides = source[side_start : side_start + rim * high, :].astype(f32)
                sides = jnp.where(keep, sides, 0.0)
                for row in range(high):
                    buf[rim + row, col : col + rim, :] = sides[rim * row : rim * row + rim]
            side_start += rim * high
        for source, row in ((above_ref, 0), (below_ref, rim + high)):
            both = source[row_start : row_start + rim * whole, :].astype(f32)
            for step in range(rim):
                buf[row + step, :whole, :] = both[step * whole : (step + 1) * whole]
        row_start += rim * whole

    tall4, whole4 = high4 + 2 * rim, wide4 + 2 * rim
    top_sum = top_refs[0][...].astype(f32)
    for ref in top_refs[1:]:
        top_sum = top_sum + ref[...].astype(f32)
    top_buf[...] = jnp.zeros_like(top_buf)
    top_buf[:, :whole4, :] = jnp.maximum(top_sum + bias_ref[4:5, :][None], 0.0)
    pitch4 = top_buf.shape[1]
    top = top_buf[...].astype(bf16).reshape(tall4 * pitch4, channels)

    def pyramid(lat_buf, high, wide, source, source_shape, source_first, source_size):
        rows, pitch = lat_buf.shape[:2]
        matrix = stretch_matrix(
            (rows, pitch), firsts(high, wide, rim), source_shape, source_first, 2, extent(*source_size)
        )
        total = lat_buf[...].reshape(rows * pitch, channels) + dot(matrix, source)
        return total.astype(bf16)

    first4 = firsts(high4, wide4, rim)
    pyr3_buf[...] = pyramid(lat3_buf, high3, wide3, top, (tall4, pitch4), first4, (high4, wide4))
    shape3 = lat3_buf.shape[:2]
    pyr2_buf[...] = pyramid(
        lat2_buf, high2, wide2, pyr3_buf[...], shape3, firsts(high3, wide3, rim), (high3, wide3)
    )
    shape2 = lat2_buf.shape[:2]
    pyr1_buf[...] = pyramid(
        lat1_buf, high1, wide1, pyr2_buf[...], shape2, firsts(high2, wide2, rim), (high2, wide2)
    )
    shape1 = lat1_buf.shape[:2]
    smooth_copy.wait()

    def conv(source, shape, weight_at, rows):
        pitch = shape[1]
        span = rows * pitch
        for col_tap in range(3):
            total = dot(source[0:span, :], weight_at(0, col_tap))
            for row_tap in (1, 2):
                total = total + dot(
                    source[row_tap * pitch : row_tap * pitch + span, :], weight_at(row_tap, col_tap)
                )
            yield col_tap, total.reshape(rows, pitch, channels)

    def smooth(number, source, shape, wide):
        rows, pitch = shape[0] - 2, shape[1]
        for col_tap, total in conv(
            source, shape, lambda i, j: smooth_w[number, i, j], rows
        ):
            acc_buf[col_tap, :rows, :pitch, :] = total
        whole = wide + 2
        total = (
            acc_buf[0, :rows, 0:whole, :]
            + acc_buf[1, :rows, 1 : whole + 1, :]
            + acc_buf[2, :rows, 2 : whole + 2, :]
        )
        return jnp.maximum(total + bias_ref[8 + number : 9 + number, :][None], 0.0)

    def smooth_flat(number, source, shape, wide):
        rows, pitch = shape[0] - 2, shape[1]
        value = smooth(number, source, shape, wide)
        sums_buf[:rows, :pitch, :] = jnp.zeros((rows, pitch, channels), f32)
        sums_buf[:rows, : wide + 2, :] = value
        return sums_buf[:rows, :pitch, :].astype(bf16).reshape(rows * pitch, channels)

    rows1, pitch1 = shape1[0] - 2, shape1[1]
    out_first = firsts(high1, wide1, 1)

    def raise_to_one(source, source_shape, source_first, factor, source_size):
        matrix = stretch_matrix(
            (rows1, pitch1), out_first, source_shape, source_first, factor, extent(*source_size)
        )
        return dot(matrix, source).astype(bf16)

    stack_buf[:, 3 * channels : 4 * channels] = raise_to_one(
        top, (tall4, pitch4), first4, 8, (high4, wide4)
    )
    smooth3 = smooth_flat(2, pyr3_buf, shape3, wide3)
    stack_buf[:, 2 * channels : 3 * channels] = raise_to_one(
        smooth3, (shape3[0] - 2, shape3[1]), firsts(high3, wide3, 1), 4, (high3, wide3)
    )
    smooth2 = smooth_flat(1, pyr2_buf, shape2, wide2)
    stack_buf[:, channels : 2 * channels] = raise_to_one(
        smooth2, (shape2[0] - 2, shape2[1]), firsts(high2, wide2, 1), 2, (high2, wide2)
    )
    value = smooth(0, pyr1_buf, shape1, wide1)
    down = out_first[0] + lax.broadcasted_iota(jnp.int32, (rows1, 1, 1), 0).astype(f32)
    across = out_first[1] + lax.broadcasted_iota(jnp.int32, (1, wide1 + 2, 1), 1).astype(f32)
    tall, broad = extent(high1, wide1)
    inside = (down >= 0.0) & (down < tall) & (across >= 0.0) & (across < broad)
    sums_buf[:rows1, : wide1 + 2, :] = jnp.where(inside, value, 0.0)
    stack_buf[:, 0:channels] = sums_buf[...].astype(bf16).reshape(rows1 * pitch1, channels)
    join_copy.wait()
    shape_join = (rows1, pitch1)
    for col_tap, total in conv(stack_buf, shape_join, lambda i, j: join_w[i, j], high1):
        acc_buf[col_tap, :high1] = total
    total = (
        acc_buf[0, :high1, 0:wide1, :]
        + acc_buf[1, :high1, 1 : wide1 + 1, :]
        + acc_buf[2, :high1, 2 : wide1 + 2, :]
    )
    out_ref[...] = jnp.maximum(total + bias_ref[11:12, :][None], 0.0).astype(bf16)


def pitch_of(width):
    return (width + 15) // 16 * 16


def tail(here, tops, lats, above, below, before, after, biases, smooth_weight, join_weight, sizes):
    (high1, wide1), (high2, wide2), (high3, wide3), (high4, wide4), _ = sizes
    channels = biases.shape[1]

    def window(high, wide):
        return high + 2 * rim, pitch_of(wide + 2 * rim)

    shapes = [window(high, wide) for high, wide in sizes[:4]]
    (rows1, pitch1), (rows2, pitch2), (rows3, pitch3), (rows4, pitch4) = shapes
    vmem = pl.BlockSpec(memory_space=pltpu.VMEM)
    anywhere = pl.BlockSpec(memory_space=pl.ANY)
    return pl.pallas_call(
        functools.partial(tail_kernel, sizes, len(tops)),
        out_shape=jax.ShapeDtypeStruct((high1, wide1, channels), bf16),
        in_specs=[pl.BlockSpec(memory_space=pltpu.SMEM)]
        + [vmem] * (len(tops) + 8)
        + [anywhere] * 2,
        out_specs=vmem,
        scratch_shapes=[
            pltpu.VMEM((rows4, pitch4, channels), f32),
            pltpu.VMEM((rows1, pitch1, channels), f32),
            pltpu.VMEM((rows2, pitch2, channels), f32),
            pltpu.VMEM((rows3, pitch3, channels), f32),
            pltpu.VMEM((rows1 * pitch1, channels), bf16),
            pltpu.VMEM((rows2 * pitch2, channels), bf16),
            pltpu.VMEM((rows3 * pitch3, channels), bf16),
            pltpu.VMEM((3, rows1 - 2, pitch1, channels), f32),
            pltpu.VMEM((rows1 - 2, pitch1, channels), f32),
            pltpu.VMEM(((rows1 - 2) * pitch1, 4 * channels), bf16),
            pltpu.VMEM(smooth_weight.shape, bf16),
            pltpu.VMEM(join_weight.shape, bf16),
            pltpu.SemaphoreType.DMA((2,)),
        ],
        compiler_params=pltpu.CompilerParams(vmem_limit_bytes=44 * 1024 * 1024),
        cost_estimate=pl.CostEstimate(
            flops=10_000_000_000, bytes_accessed=12_000_000, transcendentals=0
        ),
    )(here, *tops, *lats, above, below, before, after, biases, smooth_weight, join_weight)


def local(
    level_one,
    level_two,
    level_three,
    level_four,
    bin_weight,
    neck_feature,
    neck_pooled,
    lateral_one,
    lateral_two,
    lateral_three,
    smooth_weight,
    join_weight,
    biases,
):
    row_count = lax.axis_size("row")
    col_count = lax.axis_size("col")
    here = jnp.stack([lax.axis_index("row"), lax.axis_index("col")]).astype(jnp.int32)
    high1, wide1 = level_one.shape[:2]
    high2, wide2 = level_two.shape[:2]
    high3, wide3 = level_three.shape[0], level_three.shape[1] // col_count
    high4, grid_cols, part_four = level_four.shape
    wide4 = grid_cols // col_count
    channels = bin_weight.shape[2]
    grid_rows = high4 * row_count
    table = cell_table(grid_rows, grid_cols)
    cells = table.shape[0]
    turned = jnp.asarray(np.ascontiguousarray(table.T))
    table = jnp.asarray(table)

    def shape(dims, kind=bf16):
        return jax.ShapeDtypeStruct(dims, kind)

    blocks = [level_four] + [shifted(level_four, "row", shift) for shift in range(1, row_count)]
    window_rows = high3 * (wide3 + 2 * rim)
    side_rows = rim * (high1 + high2)
    lat1, lat2, *pieces = call(
        functools.partial(lateral_kernel, col_count),
        [shape((high1, wide1, channels)), shape((high2, wide2, channels))]
        + [shape((window_rows + side_rows, channels))] * col_count,
        [smem_spec] + [vmem_spec] * 7,
        [
            pltpu.VMEM((high3, level_three.shape[1] + 8, channels), f32),
            pltpu.VMEM((high1, wide1, channels), f32),
            pltpu.VMEM((high2, wide2, channels), f32),
            pltpu.VMEM((window_rows + side_rows, channels), f32),
        ],
        300_000_000,
        2_000_000,
    )(here, level_one, level_two, level_three, lateral_one, lateral_two, lateral_three, biases)
    near = (1, col_count - 1)
    messages = call(
        functools.partial(bins_kernel, row_count, col_count, window_rows),
        [
            shape((window_rows + cells + (side_rows if shift in near else 0), channels))
            for shift in range(col_count)
        ],
        [smem_spec] + [vmem_spec] * (2 + row_count + col_count),
        [],
        100_000_000,
        1_000_000,
    )(here, table, bin_weight, *blocks, *pieces)

    received = [messages[0]] + [
        shifted(messages[shift], "col", shift) for shift in range(1, col_count)
    ]
    rows = high4 + 2 * rim
    taps = call(
        functools.partial(feature_kernel, row_count),
        shape((3, rows * grid_cols, channels), f32),
        [smem_spec] + [vmem_spec] * (1 + row_count),
        [pltpu.VMEM((grid_rows + 2 * rim + 2, grid_cols, part_four), bf16)],
        700_000_000,
        3_000_000,
    )(here, neck_feature, *blocks)
    span4 = wide4 + 2 * rim
    windows = call(
        functools.partial(neck_kernel, row_count, col_count, high4, window_rows),
        [shape((rows, span4, channels))] * col_count,
        [smem_spec] + [vmem_spec] * (5 + col_count),
        [
            pltpu.VMEM((cells, channels), f32),
            pltpu.VMEM((3, rows * grid_cols + 16, channels), f32),
            pltpu.VMEM((rows, grid_cols + 16, channels), f32),
        ],
        300_000_000,
        3_000_000,
    )(here, table, turned, neck_pooled, biases, taps, *received)

    tops = [windows[0]] + [shifted(windows[shift], "col", shift) for shift in range(1, col_count)]
    span3 = wide3 + 2 * rim
    packed = rim * (wide1 + wide2 + wide3 + 6 * rim)
    lat3, low_rows, high_rows = call(
        functools.partial(rows_kernel, col_count, high3, wide3),
        [shape((high3, span3, channels))] + [shape((packed, channels))] * 2,
        [smem_spec] + [vmem_spec] * (3 + col_count),
        [
            pltpu.VMEM((high3, (span3 + 7) // 8 * 8, channels), f32),
            pltpu.VMEM((packed, channels), f32),
        ],
        1_000_000,
        1_000_000,
    )(here, biases, lat1, lat2, *received)
    above, below = edge_swap(low_rows, high_rows, "row")
    sizes = (
        (high1, wide1),
        (high2, wide2),
        (high3, wide3),
        (high4, wide4),
        (row_count, col_count),
    )
    return tail(
        here,
        tops,
        (lat1, lat2, lat3),
        above,
        below,
        received[1],
        received[-1],
        biases,
        smooth_weight,
        join_weight,
        sizes,
    )


def solution(mesh):
    placed = (
        P(("grp", "row"), "col", None),
        P(("grp", "row"), "col", None),
        P(("grp", "row"), None, "col"),
        P(("grp", "row"), None, "col"),
        P(None, "col", None),
        P(None, None, "col", None),
        P(None, None, "col", None),
        P(),
        P(),
        P(),
        P(),
        P(),
        P(),
    )
    return jax.shard_map(
        local, mesh=mesh, in_specs=placed, out_specs=P(("grp", "row"), "col", None), check_vma=False
    )
```

time: 75.8 us -> 64.8 us (0.85)
  the two profiles are of different devices: /device:TPU:6 before, /device:TPU:1 now
where the time goes in v3:
time: 64.8 us; the launch traced here: 63.8 us
  Pallas kernels  23.4 us (36%)
  starting transfers between devices  16.2 us (25%)
  local copies, waits for them, and re-layouts  13.3 us (21%)
  waiting for transfers between devices  10.5 us (16%)
    pallas_call x1, Pallas kernels, tail(): pl.pallas_call(functools.partial(tail_kernel, sizes, len(tops)), out_shap...  17.7 us
    unnamed x38, local copies, waits for them, and re-layouts  13.3 us
    ppermute x9, starting transfers between devices, shifted(): lax.ppermute(value, axis, [(i, (i + shift) % count) for i in range(count)])  11.2 us
    ppermute x9, waiting for transfers between devices, shifted(): lax.ppermute(value, axis, [(i, (i + shift) % count) for i in range(count)])  10.5 us
    ppermute x1, starting transfers between devices, edge_swap(): lax.ppermute(high_out, axis, forward)  3.12 us
    ppermute x1, starting transfers between devices, edge_swap(): lax.ppermute(low_out, axis, backward)  1.92 us
    pallas_call x1, Pallas kernels, local(): call(functools.partial(neck_kernel, row_count, col_count, high4, window_r...  1.78 us
  transfers between devices with their start and end apart: 11, of which 4 were waited for; matrix products, arithmetic and copies ran while one was open for 0% of the time, Pallas kernels for 6%

profile of v3, /device:TPU:1, one launch (start us, length us, event | category | flops | bytes accessed | tf_op | source)
XLA Modules:
  0.0 63.8 jit_solution(10778878872062353531)
XLA Ops:
  0.0 0.0 collective-permute-start.2
  0.0 2.7 %collective-permute-start.1 = (bf16[2,32,384]{2,1,0:T(8,128)(2,1)}, bf16[2,32,384]{2,1,0:T(8,128)(2,1)S(1)}, u32[]{:S(2)}, u32[]{:S(2)}) collective-permute-start(bf16[2,32,384]{2,1,0:T(8,128)(2,1)} %refs_0_.3), channel_id=1, source_target_pairs={{0,8},{4,12},{8,0},{12,4},{1,9},{5,13},{9,1},{13,5},{2,10},{6,14},... | collective-permute-start | bytes 147464 | tf_op jit(solution)/shard_map/ppermute | solution.py:23
  2.7 1.4 %collective-permute-start = (bf16[2,32,384]{2,1,0:T(8,128)(2,1)}, bf16[2,32,384]{2,1,0:T(8,128)(2,1)S(1)}, u32[]{:S(2)}, u32[]{:S(2)}) collective-permute-start(bf16[2,32,384]{2,1,0:T(8,128)(2,1)} %refs_0_.3), channel_id=1, source_target_pairs={{0,4},{4,8},{8,12},{12,0},{1,5},{5,9},{9,13},{13,1},{2,6},{6,10},{... | collective-permute-start | bytes 147464 | tf_op jit(solution)/shard_map/ppermute | solution.py:23
  4.1 0.1 pad_add_fusion.here_ref
  4.1 1.0 %copy-done.2 = bf16[16,64,192]{2,1,0:T(8,128)(2,1)S(1)} copy-done((bf16[16,64,192]{2,1,0:T(8,128)(2,1)S(1)}, bf16[16,64,192]{2,1,0:T(8,128)(2,1)}, u32[]{:S(2)}) %copy-start.2) | copy-done | bytes 393240
  5.2 1.0 %copy-done.3 = bf16[768,256]{1,0:T(8,128)(2,1)S(1)} copy-done((bf16[768,256]{1,0:T(8,128)(2,1)S(1)}, bf16[768,256]{1,0:T(8,128)(2,1)}, u32[]{:S(2)}) %copy-start.3) | copy-done | bytes 393240
  6.2 0.9 %copy-done.4 = bf16[8,32,384]{2,1,0:T(8,128)(2,1)S(1)} copy-done((bf16[8,32,384]{2,1,0:T(8,128)(2,1)S(1)}, bf16[8,32,384]{2,1,0:T(8,128)(2,1)}, u32[]{:S(2)}) %copy-start.4) | copy-done | bytes 196632
  7.1 0.9 %copy-done.5 = bf16[384,256]{1,0:T(8,128)(2,1)S(1)} copy-done((bf16[384,256]{1,0:T(8,128)(2,1)S(1)}, bf16[384,256]{1,0:T(8,128)(2,1)}, u32[]{:S(2)}) %copy-start.5) | copy-done | bytes 196632
  8.0 0.7 %copy-done.6 = f32[12,256]{1,0:T(8,128)S(1)} copy-done((f32[12,256]{1,0:T(8,128)S(1)}, f32[12,256]{1,0:T(8,128)}, u32[]{:S(2)}) %copy-start.6) | copy-done | bytes 12312
  8.7 0.9 %copy-done.11 = bf16[4,64,192]{2,1,0:T(8,128)(2,1)S(1)} copy-done((bf16[4,64,192]{2,1,0:T(8,128)(2,1)S(1)}, bf16[4,64,192]{2,1,0:T(8,128)(2,1)}, u32[]{:S(2)}) %copy-start.11) | copy-done | bytes 98328
  9.7 0.9 %copy-done.12 = bf16[192,256]{1,0:T(8,128)(2,1)S(1)} copy-done((bf16[192,256]{1,0:T(8,128)(2,1)S(1)}, bf16[192,256]{1,0:T(8,128)(2,1)}, u32[]{:S(2)}) %copy-start.12) | copy-done | bytes 98328
  10.6 1.1 %shard_map.146 = (bf16[16,64,256]{2,1,0:T(8,128)(2,1)S(1)}, bf16[8,32,256]{2,1,0:T(8,128)(2,1)S(1)}, bf16[128,256]{1,0:T(8,128)(2,1)S(1)}, bf16[128,256]{1,0:T(8...) custom-call(s32[2]{0:T(128)S(1)} %pad_add_fusion.here_ref, ...), custom_call_target="tpu_custom_call" | custom-call | flops 300000000 | bytes 2000000 | tf_op jit(solution)/shard_map/pallas_call | solution.py:543
  11.6 0.0 collective-permute-done.2.refs_3_
  11.6 0.0 collective-permute-done.1.refs_2_
  11.7 0.0 collective-permute-done.refs_1_
  11.7 0.0 copy-start.1
  11.7 1.1 %copy-done.1 = bf16[4,384,256]{2,1,0:T(8,128)(2,1)S(1)} copy-done((bf16[4,384,256]{2,1,0:T(8,128)(2,1)S(1)}, bf16[4,384,256]{2,1,0:T(8,128)(2,1)}, u32[]{:S(2)}) %copy-start.1) | copy-done | bytes 786456
  12.8 0.8 %copy-done.9 = f32[64,16]{1,0:T(8,128)S(1)} copy-done((f32[64,16]{1,0:T(8,128)S(1)}, f32[64,16]{1,0:T(8,128)}, u32[]{:S(2)}) %copy-start.9) | copy-done | bytes 4120
  13.6 0.8 %copy-done.13 = bf16[2,32,384]{2,1,0:T(8,128)(2,1)S(1)} copy-done((bf16[2,32,384]{2,1,0:T(8,128)(2,1)S(1)}, bf16[2,32,384]{2,1,0:T(8,128)(2,1)}, u32[]{:S(2)}) %copy-start.13) | copy-done | bytes 49176
  14.4 1.1 %shard_map.147 = (bf16[144,256]{1,0:T(8,128)(2,1)S(1)}, bf16[192,256]{1,0:T(8,128)(2,1)S(1)}, bf16[144,256]{1,0:T(8,128)(2,1)S(1)}, bf16[192,256]{1,0:T(8,128)(2,1)S(1)}) custom-call(s32[2]{0:T(128)S(1)} %pad_add_fusion.here_ref, f32[64,16]{1,0:T(8,128)S(1)} %copy-done.9, bf16[4,384,256]{2,1,0:T(8,128)(2,1)S(1)} %copy-done.1, ...), custom_call_target="tpu_custom_call" | custom-call | flops 100000000 | bytes 1000000 | tf_op jit(solution)/shard_map/pallas_call | solution.py:558
  15.4 1.3 %collective-permute-start.3 = (bf16[192,256]{1,0:T(8,128)(2,1)S(1)}, bf16[192,256]{1,0:T(8,128)(2,1)S(1)}, u32[]{:S(2)}, u32[]{:S(2)}) collective-permute-start(bf16[192,256]{1,0:T(8,128)(2,1)S(1)} %get-tuple-element.27), channel_id=1, source_target_pairs={{0,1},{1,2},{2,3},{3,0},{4,5},{5,6},{6,7},{7,4},{8,9},{9,10},{10,1... | collective-permute-start | bytes 294920 | tf_op jit(solution)/shard_map/ppermute | solution.py:23
  16.8 2.1 %collective-permute-start.5 = (bf16[192,256]{1,0:T(8,128)(2,1)S(1)}, bf16[192,256]{1,0:T(8,128)(2,1)S(1)}, u32[]{:S(2)}, u32[]{:S(2)}) collective-permute-start(bf16[192,256]{1,0:T(8,128)(2,1)S(1)} %get-tuple-element.29), channel_id=1, source_target_pairs={{0,3},{1,0},{2,1},{3,2},{4,7},{5,4},{6,5},{7,6},{8,11},{9,8},{10,9... | collective-permute-start | bytes 294920 | tf_op jit(solution)/shard_map/ppermute | solution.py:23
  18.9 0.4 collective-permute-start.4
  19.3 7.7 %collective-permute-done.4.refs_2_ = bf16[144,256]{1,0:T(8,128)(2,1)S(1)} collective-permute-done((bf16[144,256]{1,0:T(8,128)(2,1)S(1)}, bf16[144,256]{1,0:T(8,128)(2,1)S(1)}, u32[]{:S(2)}, u32[]{:S(2)}) %collective-permute-start.4) | collective-permute-done | bytes 73760 | tf_op jit(solution)/shard_map/ppermute | solution.py:23
  27.0 0.0 collective-permute-done.3.refs_1_.refs_9_
  27.0 0.0 collective-permute-done.5.refs_3_.refs_10_
  27.0 0.7 %copy-done.7 = f32[12,256]{1,0:T(8,128)S(1)} copy-done((f32[12,256]{1,0:T(8,128)S(1)}, f32[12,256]{1,0:T(8,128)}, u32[]{:S(2)}) %copy-start.7) | copy-done | bytes 12312
  27.7 0.6 %shard_map.149 = (bf16[4,20,256]{2,1,0:T(8,128)(2,1)S(1)}, bf16[248,256]{1,0:T(8,128)(2,1)S(1)}, bf16[248,256]{1,0:T(8,128)(2,1)S(1)}) custom-call(s32[2]{0:T(128)S(1)} %pad_add_fusion.here_ref, f32[12,256]{1,0:T(8,128)S(1)} %copy-done.7, bf16[16,64,256]{2,1,0:T(8,128)(2,1)S(1)} %get-tuple-element.34.lat1_ref.refs_4_, ...), custom_call_target="tpu_custom_call" | custom-call | flops 1000000 | bytes 1000000 | tf_op jit(solution)/shard_map/pallas_call | solution.py:599
  28.3 3.1 %collective-permute-start.9 = (bf16[248,256]{1,0:T(8,128)(2,1)S(1)}, bf16[248,256]{1,0:T(8,128)(2,1)S(1)}, u32[]{:S(2)}, u32[]{:S(2)}) collective-permute-start(bf16[248,256]{1,0:T(8,128)(2,1)S(1)} %get-tuple-element.37), channel_id=1, source_target_pairs={{0,4},{4,8},{8,12},{1,5},{5,9},{9,13},{2,6},{6,10},{10,14},{3,7},{... | collective-permute-start | bytes 380936 | tf_op jit(solution)/shard_map/ppermute | solution.py:30
  31.5 1.9 %collective-permute-start.10 = (bf16[248,256]{1,0:T(8,128)(2,1)S(1)}, bf16[248,256]{1,0:T(8,128)(2,1)S(1)}, u32[]{:S(2)}, u32[]{:S(2)}) collective-permute-start(bf16[248,256]{1,0:T(8,128)(2,1)S(1)} %get-tuple-element.38), channel_id=1, source_target_pairs={{4,0},{8,4},{12,8},{5,1},{9,5},{13,9},{6,2},{10,6},{14,10},{7,3},{... | collective-permute-start | bytes 380936 | tf_op jit(solution)/shard_map/ppermute | solution.py:30
  33.4 0.0 copy-done.14
  33.4 0.0 copy-start.18
  33.4 1.5 %copy-done.18 = bf16[3,3,384,256]{3,2,1,0:T(8,128)(2,1)S(1)} copy-done((bf16[3,3,384,256]{3,2,1,0:T(8,128)(2,1)S(1)}, bf16[3,3,384,256]{3,2,1,0:T(8,128)(2,1)}, u32[]{:S(2)}) %copy-start.18) | copy-done | bytes 1769496
  34.9 1.2 %shard_map.145.taps_ref = f32[3,192,256]{2,1,0:T(8,128)S(1)} custom-call(s32[2]{0:T(128)S(1)} %pad_add_fusion.here_ref, bf16[3,3,384,256]{3,2,1,0:T(8,128)(2,1)S(1)} %copy-done.18, bf16[2,32,384]{2,1,0:T(8,128)(2,1)S(1)} %copy-done.14, bf16[2,32,384]{2,1,0:T(8,128)(2,1)S(1)} %collective-permute-done.refs_1_, ...), custom_call_target="tpu_custom_call" | custom-call | flops 700000000 | bytes 3000000 | tf_op jit(solution)/shard_map/pallas_call | solution.py:574
  36.1 0.0 copy-done
  36.1 0.0 copy-done.8
  36.1 1.8 %shard_map.148 = (bf16[6,12,256]{2,1,0:T(8,128)(2,1)S(1)}, bf16[6,12,256]{2,1,0:T(8,128)(2,1)S(1)}, bf16[6,12,256]{2,1,0:T(8,128)(2,1)S(1)}, bf16[6,12,256]{2,1,0:T(8,128)(2,1)S(1)}) custom-call(s32[2]{0:T(128)S(1)} %pad_add_fusion.here_ref, f32[64,16]{1,0:T(8,128)S(1)} %copy-done.10, f32[16,64]{1,0:T(8,128)S(1)} %copy-done.15, ...), custom_call_target="tpu_custom_call" | custom-call | flops 300000000 | bytes 3000000 | tf_op jit(solution)/shard_map/pallas_call | solution.py:583
  37.9 0.1 collective-permute-start.6
  38.0 1.6 %collective-permute-start.7 = (bf16[6,12,256]{2,1,0:T(8,128)(2,1)S(1)}, bf16[6,12,256]{2,1,0:T(8,128)(2,1)S(1)}, u32[]{:S(2)}, u32[]{:S(2)}) collective-permute-start(bf16[6,12,256]{2,1,0:T(8,128)(2,1)S(1)} %get-tuple-element.32), channel_id=1, source_target_pairs={{0,2},{1,3},{2,0},{3,1},{4,6},{5,7},{6,4},{7,5},{8,10},{9,11},{10,... | collective-permute-start | bytes 110600 | tf_op jit(solution)/shard_map/ppermute | solution.py:23
  39.6 1.6 %collective-permute-start.8 = (bf16[6,12,256]{2,1,0:T(8,128)(2,1)S(1)}, bf16[6,12,256]{2,1,0:T(8,128)(2,1)S(1)}, u32[]{:S(2)}, u32[]{:S(2)}) collective-permute-start(bf16[6,12,256]{2,1,0:T(8,128)(2,1)S(1)} %get-tuple-element.33), channel_id=1, source_target_pairs={{0,3},{1,0},{2,1},{3,2},{4,7},{5,4},{6,5},{7,6},{8,11},{9,8},{10,9... | collective-permute-start | bytes 110600 | tf_op jit(solution)/shard_map/ppermute | solution.py:23
  41.2 2.0 %collective-permute-done.6.refs_1_ = bf16[6,12,256]{2,1,0:T(8,128)(2,1)S(1)} collective-permute-done((bf16[6,12,256]{2,1,0:T(8,128)(2,1)S(1)}, bf16[6,12,256]{2,1,0:T(8,128)(2,1)S(1)}, u32[]{:S(2)}, u32[]{:S(2)}) %collective-permute-start.6) | collective-permute-done | bytes 36896 | tf_op jit(solution)/shard_map/ppermute | solution.py:23
  43.3 0.6 collective-permute-done.7.refs_2_
  43.8 0.2 collective-permute-done.8.refs_3_
  44.0 0.0 collective-permute-done.9.refs_7_
  44.0 0.0 collective-permute-done.10.refs_8_
  44.0 0.0 copy-start.17
  44.0 2.0 %copy-done.17 = bf16[3,3,3,256,256]{4,3,2,1,0:T(8,128)(2,1)S(1)} copy-done((bf16[3,3,3,256,256]{4,3,2,1,0:T(8,128)(2,1)S(1)}, bf16[3,3,3,256,256]{4,3,2,1,0:T(8,128)(2,1)}, u32[]{:S(2)}) %copy-start.17) | copy-done | bytes 3538968
  46.0 17.7 %shard_map.150 = bf16[16,64,256]{2,1,0:T(8,128)(2,1)} custom-call(s32[2]{0:T(128)S(1)} %pad_add_fusion.here_ref, bf16[6,12,256]{2,1,0:T(8,128)(2,1)S(1)} %get-tuple-element.30.refs_0_, bf16[6,12,256]{2,1,0:T(8,128)(2,1)S(1)} %collective-permute-done.6.refs_1_, bf16[6,12,256]{2,1,0:T(8,128)(2,1)S(1)} %collective-permute-done.7.refs_2_, ...), custom_call_target="tpu_custom_call" | custom-call | flops 10000000000 | bytes 12000000 | tf_op jit(solution)/shard_map/pallas_call | solution.py:478
  (19 shorter events, 0.0 us)
Async XLA Ops:
  0.0 36.1 %copy-start = (bf16[3,3,256,256]{3,2,1,0:T(8,128)(2,1)S(1)}, bf16[3,3,256,256]{3,2,1,0:T(8,128)(2,1)}, u32[]{:S(2)}) copy-start(bf16[3,3,256,256]{3,2,1,0:T(8,128)(2,1)} %weight_ref.5) | copy-start | bytes 3538948
  0.0 11.6 %collective-permute-start.2 = (bf16[2,32,384]{2,1,0:T(8,128)(2,1)}, bf16[2,32,384]{2,1,0:T(8,128)(2,1)S(1)}, u32[]{:S(2)}, u32[]{:S(2)}) collective-permute-start(bf16[2,32,384]{2,1,0:T(8,128)(2,1)} %refs_0_.3), channel_id=1, source_target_pairs={{0,12},{4,0},{8,4},{12,8},{1,13},{5,1},{9,5},{13,9},{2,14},{6,2},{... | collective-permute-start | bytes 147464 | tf_op jit(solution)/shard_map/ppermute | solution.py:23
  0.0 11.6 %collective-permute-start.1 = (bf16[2,32,384]{2,1,0:T(8,128)(2,1)}, bf16[2,32,384]{2,1,0:T(8,128)(2,1)S(1)}, u32[]{:S(2)}, u32[]{:S(2)}) collective-permute-start(bf16[2,32,384]{2,1,0:T(8,128)(2,1)} %refs_0_.3), channel_id=1, source_target_pairs={{0,8},{4,12},{8,0},{12,4},{1,9},{5,13},{9,1},{13,5},{2,10},{6,14},... | collective-permute-start | bytes 147464 | tf_op jit(solution)/shard_map/ppermute | solution.py:23
  2.7 8.9 %collective-permute-start = (bf16[2,32,384]{2,1,0:T(8,128)(2,1)}, bf16[2,32,384]{2,1,0:T(8,128)(2,1)S(1)}, u32[]{:S(2)}, u32[]{:S(2)}) collective-permute-start(bf16[2,32,384]{2,1,0:T(8,128)(2,1)} %refs_0_.3), channel_id=1, source_target_pairs={{0,4},{4,8},{8,12},{12,0},{1,5},{5,9},{9,13},{13,1},{2,6},{6,10},{... | collective-permute-start | bytes 147464 | tf_op jit(solution)/shard_map/ppermute | solution.py:23
  4.1 1.0 %copy-start.2 = (bf16[16,64,192]{2,1,0:T(8,128)(2,1)S(1)}, bf16[16,64,192]{2,1,0:T(8,128)(2,1)}, u32[]{:S(2)}) copy-start(bf16[16,64,192]{2,1,0:T(8,128)(2,1)} %one_ref.1) | copy-start | bytes 1179652
  5.2 1.0 %copy-start.3 = (bf16[768,256]{1,0:T(8,128)(2,1)S(1)}, bf16[768,256]{1,0:T(8,128)(2,1)}, u32[]{:S(2)}) copy-start(bf16[768,256]{1,0:T(8,128)(2,1)} %w3_ref.1) | copy-start | bytes 1179652
  6.2 0.9 %copy-start.4 = (bf16[8,32,384]{2,1,0:T(8,128)(2,1)S(1)}, bf16[8,32,384]{2,1,0:T(8,128)(2,1)}, u32[]{:S(2)}) copy-start(bf16[8,32,384]{2,1,0:T(8,128)(2,1)} %two_ref.1) | copy-start | bytes 589828
  7.1 0.9 %copy-start.5 = (bf16[384,256]{1,0:T(8,128)(2,1)S(1)}, bf16[384,256]{1,0:T(8,128)(2,1)}, u32[]{:S(2)}) copy-start(bf16[384,256]{1,0:T(8,128)(2,1)} %w2_ref.1) | copy-start | bytes 589828
  8.0 0.7 %copy-start.6 = (f32[12,256]{1,0:T(8,128)S(1)}, f32[12,256]{1,0:T(8,128)}, u32[]{:S(2)}) copy-start(f32[12,256]{1,0:T(8,128)} %refs_11_.1) | copy-start | bytes 36868
  8.7 0.9 %copy-start.11 = (bf16[4,64,192]{2,1,0:T(8,128)(2,1)S(1)}, bf16[4,64,192]{2,1,0:T(8,128)(2,1)}, u32[]{:S(2)}) copy-start(bf16[4,64,192]{2,1,0:T(8,128)(2,1)} %three_ref.1) | copy-start | bytes 294916
  9.7 0.9 %copy-start.12 = (bf16[192,256]{1,0:T(8,128)(2,1)S(1)}, bf16[192,256]{1,0:T(8,128)(2,1)}, u32[]{:S(2)}) copy-start(bf16[192,256]{1,0:T(8,128)(2,1)} %w1_ref.1) | copy-start | bytes 294916
  10.5 22.9 %copy-start.14 = (bf16[2,32,384]{2,1,0:T(8,128)(2,1)S(1)}, bf16[2,32,384]{2,1,0:T(8,128)(2,1)}, u32[]{:S(2)}) copy-start(bf16[2,32,384]{2,1,0:T(8,128)(2,1)} %refs_0_.3) | copy-start | bytes 147460
  10.5 25.6 %copy-start.8 = (f32[12,256]{1,0:T(8,128)S(1)}, f32[12,256]{1,0:T(8,128)}, u32[]{:S(2)}) copy-start(f32[12,256]{1,0:T(8,128)} %refs_11_.1) | copy-start | bytes 36868
  10.5 25.6 %copy-start.10 = (f32[64,16]{1,0:T(8,128)S(1)}, f32[64,16]{1,0:T(8,128)}, u32[]{:S(2)}) copy-start(f32[64,16]{1,0:T(8,128)} %constant.12.clone.table_ref) | copy-start | bytes 12292
  10.5 25.6 %copy-start.15 = (f32[16,64]{1,0:T(8,128)S(1)}, f32[16,64]{1,0:T(8,128)}, u32[]{:S(2)}) copy-start(f32[16,64]{1,0:T(8,128)} %constant.11.clone.turned_ref) | copy-start | bytes 12292
  11.7 1.1 %copy-start.1 = (bf16[4,384,256]{2,1,0:T(8,128)(2,1)S(1)}, bf16[4,384,256]{2,1,0:T(8,128)(2,1)}, u32[]{:S(2)}) copy-start(bf16[4,384,256]{2,1,0:T(8,128)(2,1)} %weight_ref.4) | copy-start | bytes 2359300
  12.8 0.8 %copy-start.9 = (f32[64,16]{1,0:T(8,128)S(1)}, f32[64,16]{1,0:T(8,128)}, u32[]{:S(2)}) copy-start(f32[64,16]{1,0:T(8,128)} %constant.12.clone.table_ref) | copy-start | bytes 12292
  13.6 0.8 %copy-start.13 = (bf16[2,32,384]{2,1,0:T(8,128)(2,1)S(1)}, bf16[2,32,384]{2,1,0:T(8,128)(2,1)}, u32[]{:S(2)}) copy-start(bf16[2,32,384]{2,1,0:T(8,128)(2,1)} %refs_0_.3) | copy-start | bytes 147460
  15.4 11.5 %collective-permute-start.3 = (bf16[192,256]{1,0:T(8,128)(2,1)S(1)}, bf16[192,256]{1,0:T(8,128)(2,1)S(1)}, u32[]{:S(2)}, u32[]{:S(2)}) collective-permute-start(bf16[192,256]{1,0:T(8,128)(2,1)S(1)} %get-tuple-element.27), channel_id=1, source_target_pairs={{0,1},{1,2},{2,3},{3,0},{4,5},{5,6},{6,7},{7,4},{8,9},{9,10},{10,1... | collective-permute-start | bytes 294920 | tf_op jit(solution)/shard_map/ppermute | solution.py:23
  16.8 10.2 %collective-permute-start.5 = (bf16[192,256]{1,0:T(8,128)(2,1)S(1)}, bf16[192,256]{1,0:T(8,128)(2,1)S(1)}, u32[]{:S(2)}, u32[]{:S(2)}) collective-permute-start(bf16[192,256]{1,0:T(8,128)(2,1)S(1)} %get-tuple-element.29), channel_id=1, source_target_pairs={{0,3},{1,0},{2,1},{3,2},{4,7},{5,4},{6,5},{7,6},{8,11},{9,8},{10,9... | collective-permute-start | bytes 294920 | tf_op jit(solution)/shard_map/ppermute | solution.py:23
  18.9 8.1 %collective-permute-start.4 = (bf16[144,256]{1,0:T(8,128)(2,1)S(1)}, bf16[144,256]{1,0:T(8,128)(2,1)S(1)}, u32[]{:S(2)}, u32[]{:S(2)}) collective-permute-start(bf16[144,256]{1,0:T(8,128)(2,1)S(1)} %get-tuple-element.28), channel_id=1, source_target_pairs={{0,2},{1,3},{2,0},{3,1},{4,6},{5,7},{6,4},{7,5},{8,10},{9,11},{10,... | collective-permute-start | bytes 221192 | tf_op jit(solution)/shard_map/ppermute | solution.py:23
  27.0 0.7 %copy-start.7 = (f32[12,256]{1,0:T(8,128)S(1)}, f32[12,256]{1,0:T(8,128)}, u32[]{:S(2)}) copy-start(f32[12,256]{1,0:T(8,128)} %refs_11_.1) | copy-start | bytes 36868
  27.7 16.3 %copy-start.16 = (bf16[3,3,1024,256]{3,2,1,0:T(8,128)(2,1)S(1)}, bf16[3,3,1024,256]{3,2,1,0:T(8,128)(2,1)}, u32[]{:S(2)}) copy-start(bf16[3,3,1024,256]{3,2,1,0:T(8,128)(2,1)} %refs_13_.1) | copy-start | bytes 14155780
  28.3 15.7 %collective-permute-start.9 = (bf16[248,256]{1,0:T(8,128)(2,1)S(1)}, bf16[248,256]{1,0:T(8,128)(2,1)S(1)}, u32[]{:S(2)}, u32[]{:S(2)}) collective-permute-start(bf16[248,256]{1,0:T(8,128)(2,1)S(1)} %get-tuple-element.37), channel_id=1, source_target_pairs={{0,4},{4,8},{8,12},{1,5},{5,9},{9,13},{2,6},{6,10},{10,14},{3,7},{... | collective-permute-start | bytes 380936 | tf_op jit(solution)/shard_map/ppermute | solution.py:30
  31.5 12.5 %collective-permute-start.10 = (bf16[248,256]{1,0:T(8,128)(2,1)S(1)}, bf16[248,256]{1,0:T(8,128)(2,1)S(1)}, u32[]{:S(2)}, u32[]{:S(2)}) collective-permute-start(bf16[248,256]{1,0:T(8,128)(2,1)S(1)} %get-tuple-element.38), channel_id=1, source_target_pairs={{4,0},{8,4},{12,8},{5,1},{9,5},{13,9},{6,2},{10,6},{14,10},{7,3},{... | collective-permute-start | bytes 380936 | tf_op jit(solution)/shard_map/ppermute | solution.py:30
  33.4 1.5 %copy-start.18 = (bf16[3,3,384,256]{3,2,1,0:T(8,128)(2,1)S(1)}, bf16[3,3,384,256]{3,2,1,0:T(8,128)(2,1)}, u32[]{:S(2)}) copy-start(bf16[3,3,384,256]{3,2,1,0:T(8,128)(2,1)} %weight_ref.3) | copy-start | bytes 5308420
  37.9 5.4 %collective-permute-start.6 = (bf16[6,12,256]{2,1,0:T(8,128)(2,1)S(1)}, bf16[6,12,256]{2,1,0:T(8,128)(2,1)S(1)}, u32[]{:S(2)}, u32[]{:S(2)}) collective-permute-start(bf16[6,12,256]{2,1,0:T(8,128)(2,1)S(1)} %get-tuple-element.31), channel_id=1, source_target_pairs={{0,1},{1,2},{2,3},{3,0},{4,5},{5,6},{6,7},{7,4},{8,9},{9,10},{10,1... | collective-permute-start | bytes 110600 | tf_op jit(solution)/shard_map/ppermute | solution.py:23
  38.0 5.8 %collective-permute-start.7 = (bf16[6,12,256]{2,1,0:T(8,128)(2,1)S(1)}, bf16[6,12,256]{2,1,0:T(8,128)(2,1)S(1)}, u32[]{:S(2)}, u32[]{:S(2)}) collective-permute-start(bf16[6,12,256]{2,1,0:T(8,128)(2,1)S(1)} %get-tuple-element.32), channel_id=1, source_target_pairs={{0,2},{1,3},{2,0},{3,1},{4,6},{5,7},{6,4},{7,5},{8,10},{9,11},{10,... | collective-permute-start | bytes 110600 | tf_op jit(solution)/shard_map/ppermute | solution.py:23
  39.6 4.4 %collective-permute-start.8 = (bf16[6,12,256]{2,1,0:T(8,128)(2,1)S(1)}, bf16[6,12,256]{2,1,0:T(8,128)(2,1)S(1)}, u32[]{:S(2)}, u32[]{:S(2)}) collective-permute-start(bf16[6,12,256]{2,1,0:T(8,128)(2,1)S(1)} %get-tuple-element.33), channel_id=1, source_target_pairs={{0,3},{1,0},{2,1},{3,2},{4,7},{5,4},{6,5},{7,6},{8,11},{9,8},{10,9... | collective-permute-start | bytes 110600 | tf_op jit(solution)/shard_map/ppermute | solution.py:23
  44.0 2.0 %copy-start.17 = (bf16[3,3,3,256,256]{4,3,2,1,0:T(8,128)(2,1)S(1)}, bf16[3,3,3,256,256]{4,3,2,1,0:T(8,128)(2,1)}, u32[]{:S(2)}) copy-start(bf16[3,3,3,256,256]{4,3,2,1,0:T(8,128)(2,1)} %refs_12_.1) | copy-start | bytes 10616836

commit v4 on v3

--- a/solution.py
+++ b/solution.py
@@ -14,6 +14,7 @@
 f32 = jnp.float32
 bf16 = jnp.bfloat16
 vmem_spec = pl.BlockSpec(memory_space=pltpu.VMEM)
+hbm_spec = pl.BlockSpec(memory_space=pltpu.HBM)
 smem_spec = pl.BlockSpec(memory_space=pltpu.SMEM)
 params = pltpu.CompilerParams(vmem_limit_bytes=24 * 1024 * 1024)
 
@@ -51,6 +52,10 @@
     return jnp.dot(a, b, preferred_element_type=f32)
 
 
+def in_hbm(value):
+    return pltpu.with_memory_space_constraint(value, pltpu.HBM)
+
+
 def call(kernel, outs, specs, scratch, flops, moved):
     return pl.pallas_call(
         kernel,
@@ -71,17 +76,30 @@
     return jnp.floor((value + 0.5) / step)
 
 
-def lateral_kernel(col_count, here_ref, one_ref, two_ref, three_ref, w1_ref, w2_ref, w3_ref, bias_ref, *refs):
-    (lat1_ref, lat2_ref), pieces, (wide_buf, one_buf, two_buf, piece_buf) = (
-        refs[:2],
-        refs[2 : 2 + col_count],
-        refs[2 + col_count :],
-    )
+def lateral_kernel(col_count, kept_count, here_ref, *refs):
+    sources, refs = refs[: 6 + kept_count], refs[6 + kept_count :]
+    (lat1_ref, lat2_ref), refs = refs[:2], refs[2:]
+    pieces, refs = refs[:col_count], refs[col_count:]
+    kept, refs = refs[:kept_count], refs[kept_count:]
+    fetched, (wide_buf, one_buf, two_buf, piece_buf, sems) = refs[:6], refs[6:]
+    copies = [
+        pltpu.make_async_copy(source, target, sems.at[number])
+        for number, (source, target) in enumerate(zip(sources, (*fetched, *kept)))
+    ]
+    for copy in copies:
+        copy.start()
+    one_ref, w1_ref, two_ref, w2_ref, three_ref, w3_ref = fetched
+    bias_ref = kept[0]
+    copies[6].wait()
     channels = w1_ref.shape[1]
-    for source, weight, row, buf, out in (
-        (one_ref, w1_ref, 5, one_buf, lat1_ref),
-        (two_ref, w2_ref, 6, two_buf, lat2_ref),
+    for number, (source, weight, row, buf, out) in enumerate(
+        (
+            (one_ref, w1_ref, 5, one_buf, lat1_ref),
+            (two_ref, w2_ref, 6, two_buf, lat2_ref),
+        )
     ):
+        copies[2 * number].wait()
+        copies[2 * number + 1].wait()
         high, wide, depth = source.shape
         value = dot(source[...].reshape(high * wide, depth), weight[...])
         value = jnp.maximum(value + bias_ref[row : row + 1, :], 0.0).reshape(high, wide, channels)
@@ -90,6 +108,8 @@
     high3, whole3, share = three_ref.shape
     wide3 = whole3 // col_count
     col_here = here_ref[1]
+    copies[4].wait()
+    copies[5].wait()
     weight = w3_ref[pl.ds(pl.multiple_of(col_here * share, 16), share), :]
     value = dot(three_ref[...].reshape(high3 * whole3, share), weight)
     wide_buf[...] = jnp.zeros_like(wide_buf)
@@ -109,6 +129,8 @@
                 piece_buf[start : start + rim, :] = buf[row, first : first + rim, :]
                 start += rim
         piece[...] = piece_buf[...].astype(bf16)
+    for copy in copies[7:]:
+        copy.wait()
 
 
 def bins_kernel(row_count, col_count, window_rows, here_ref, table_ref, weight_ref, *refs):
@@ -473,15 +495,13 @@
 
     shapes = [window(high, wide) for high, wide in sizes[:4]]
     (rows1, pitch1), (rows2, pitch2), (rows3, pitch3), (rows4, pitch4) = shapes
-    vmem = pl.BlockSpec(memory_space=pltpu.VMEM)
-    anywhere = pl.BlockSpec(memory_space=pl.ANY)
     return pl.pallas_call(
         functools.partial(tail_kernel, sizes, len(tops)),
         out_shape=jax.ShapeDtypeStruct((high1, wide1, channels), bf16),
-        in_specs=[pl.BlockSpec(memory_space=pltpu.SMEM)]
-        + [vmem] * (len(tops) + 8)
-        + [anywhere] * 2,
-        out_specs=vmem,
+        in_specs=[smem_spec]
+        + [vmem_spec] * (len(tops) + 8)
+        + [hbm_spec] * 2,
+        out_specs=vmem_spec,
         scratch_shapes=[
             pltpu.VMEM((rows4, pitch4, channels), f32),
             pltpu.VMEM((rows1, pitch1, channels), f32),
@@ -501,7 +521,18 @@
         cost_estimate=pl.CostEstimate(
             flops=10_000_000_000, bytes_accessed=12_000_000, transcendentals=0
         ),
-    )(here, *tops, *lats, above, below, before, after, biases, smooth_weight, join_weight)
+    )(
+        here,
+        *tops,
+        *lats,
+        above,
+        below,
+        before,
+        after,
+        biases,
+        in_hbm(smooth_weight),
+        in_hbm(join_weight),
+    )
 
 
 def local(
@@ -537,23 +568,31 @@
     def shape(dims, kind=bf16):
         return jax.ShapeDtypeStruct(dims, kind)
 
-    blocks = [level_four] + [shifted(level_four, "row", shift) for shift in range(1, row_count)]
+    others = [shifted(level_four, "row", shift) for shift in range(1, row_count)]
     window_rows = high3 * (wide3 + 2 * rim)
     side_rows = rim * (high1 + high2)
-    lat1, lat2, *pieces = call(
-        functools.partial(lateral_kernel, col_count),
+    used = (level_one, lateral_one, level_two, lateral_two, level_three, lateral_three)
+    kept = (biases, level_four, table, bin_weight, turned, neck_feature, neck_pooled)
+    lat1, lat2, *rest = call(
+        functools.partial(lateral_kernel, col_count, len(kept)),
         [shape((high1, wide1, channels)), shape((high2, wide2, channels))]
-        + [shape((window_rows + side_rows, channels))] * col_count,
-        [smem_spec] + [vmem_spec] * 7,
-        [
+        + [shape((window_rows + side_rows, channels))] * col_count
+        + [shape(value.shape, value.dtype) for value in kept],
+        [smem_spec] + [hbm_spec] * (len(used) + len(kept)),
+        [pltpu.VMEM(value.shape, value.dtype) for value in used]
+        + [
             pltpu.VMEM((high3, level_three.shape[1] + 8, channels), f32),
             pltpu.VMEM((high1, wide1, channels), f32),
             pltpu.VMEM((high2, wide2, channels), f32),
             pltpu.VMEM((window_rows + side_rows, channels), f32),
+            pltpu.SemaphoreType.DMA((len(used) + len(kept),)),
         ],
         300_000_000,
-        2_000_000,
-    )(here, level_one, level_two, level_three, lateral_one, lateral_two, lateral_three, biases)
+        8_000_000,
+    )(here, *(in_hbm(value) for value in (*used, *kept)))
+    pieces = rest[:col_count]
+    bias_table, level_four, table, bin_weight, turned, neck_feature, neck_pooled = rest[col_count:]
+    blocks = [level_four] + others
     near = (1, col_count - 1)
     messages = call(
         functools.partial(bins_kernel, row_count, col_count, window_rows),
@@ -591,7 +630,7 @@
         ],
         300_000_000,
         3_000_000,
-    )(here, table, turned, neck_pooled, biases, taps, *received)
+    )(here, table, turned, neck_pooled, bias_table, taps, *received)
 
     tops = [windows[0]] + [shifted(windows[shift], "col", shift) for shift in range(1, col_count)]
     span3 = wide3 + 2 * rim
@@ -606,7 +645,7 @@
         ],
         1_000_000,
         1_000_000,
-    )(here, biases, lat1, lat2, *received)
+    )(here, bias_table, lat1, lat2, *received)
     above, below = edge_swap(low_rows, high_rows, "row")
     sizes = (
         (high1, wide1),
@@ -623,7 +662,7 @@
         below,
         received[1],
         received[-1],
-        biases,
+        bias_table,
         smooth_weight,
         join_weight,
         sizes,

time: 64.8 us -> 53.9 us (0.83)
  local copies, waits for them, and re-layouts: 13.3 us -> 0 us
  Pallas kernels: 23.4 us -> 26.8 us
  waiting for transfers between devices: 10.5 us -> 8.98 us
  starting transfers between devices: 16.2 us -> 17.3 us
    unnamed x38 -> x0, local copies, waits for them, and re-layouts: 13.3 us -> none
    ppermute x1, starting transfers between devices: 3.12 us -> 5.5 us  [edge_swap(): lax.ppermute(high_out, axis, forward)]
    pallas_call x1, Pallas kernels: 1.07 us -> 3.22 us  [local(): call(functools.partial(lateral_kernel, col_count, len(kept)), [shape((hig...]
    ppermute x9, waiting for transfers between devices: 10.5 us -> 8.98 us  [shifted(): lax.ppermute(value, axis, [(i, (i + shift) % count) for i in range(count)])]
    ppermute x9, starting transfers between devices: 11.2 us -> 9.84 us  [shifted(): lax.ppermute(value, axis, [(i, (i + shift) % count) for i in range(count)])]
    pallas_call x1, Pallas kernels: 17.7 us -> 18.9 us  [tail(): pl.pallas_call(functools.partial(tail_kernel, sizes, len(tops)), out_shap...]
  transfers between devices with their start and end apart: 11 -> 11, of which waited for: 4 -> 4; matrix products, arithmetic and copies ran while one was open for 0% -> 0% of each run, Pallas kernels for 6% -> 12%
where the time goes in v4:
time: 53.9 us; the launch traced here: 53.3 us
  Pallas kernels  26.8 us (50%)
  starting transfers between devices  17.3 us (32%)
  waiting for transfers between devices  8.98 us (17%)
    pallas_call x1, Pallas kernels, tail(): pl.pallas_call(functools.partial(tail_kernel, sizes, len(tops)), out_shap...  18.9 us
    ppermute x9, starting transfers between devices, shifted(): lax.ppermute(value, axis, [(i, (i + shift) % count) for i in range(count)])  9.84 us
    ppermute x9, waiting for transfers between devices, shifted(): lax.ppermute(value, axis, [(i, (i + shift) % count) for i in range(count)])  8.98 us
    ppermute x1, starting transfers between devices, edge_swap(): lax.ppermute(high_out, axis, forward)  5.5 us
    pallas_call x1, Pallas kernels, local(): call(functools.partial(lateral_kernel, col_count, len(kept)), [shape((hig...  3.22 us
    ppermute x1, starting transfers between devices, edge_swap(): lax.ppermute(low_out, axis, backward)  1.92 us
    pallas_call x1, Pallas kernels, local(): call(functools.partial(neck_kernel, row_count, col_count, high4, window_r...  1.78 us
    pallas_call x1, Pallas kernels, local(): call(functools.partial(feature_kernel, row_count), shape((3, rows * grid_...  1.19 us
  transfers between devices with their start and end apart: 11, of which 4 were waited for; matrix products, arithmetic and copies ran while one was open for 0% of the time, Pallas kernels for 12%

profile of v4, /device:TPU:1, one launch (start us, length us, event | category | flops | bytes accessed | tf_op | source)
XLA Modules:
  0.0 53.3 jit_solution(16536730491534232622)
XLA Ops:
  0.0 2.6 %collective-permute-start = (bf16[2,32,384]{2,1,0:T(8,128)(2,1)}, bf16[2,32,384]{2,1,0:T(8,128)(2,1)S(1)}, u32[]{:S(2)}, u32[]{:S(2)}) collective-permute-start(bf16[2,32,384]{2,1,0:T(8,128)(2,1)} %refs_7_.1), channel_id=1, source_target_pairs={{0,4},{4,8},{8,12},{12,0},{1,5},{5,9},{9,13},{13,1},{2,6},{6,10},{... | collective-permute-start | bytes 147464 | tf_op jit(solution)/shard_map/ppermute | solution.py:24
  2.6 0.0 collective-permute-start.2
  2.6 0.1 collective-permute-start.1
  2.7 0.1 pad_add_fusion.here_ref
  2.8 3.2 %shard_map.145 = (bf16[16,64,256]{2,1,0:T(8,128)(2,1)S(1)}, bf16[8,32,256]{2,1,0:T(8,128)(2,1)S(1)}, bf16[128,256]{1,0:T(8,128)(2,1)S(1)}, bf16[128,256]{1,0:T(8...) custom-call(s32[2]{0:T(128)S(1)} %pad_add_fusion.here_ref, ...), custom_call_target="tpu_custom_call" | custom-call | flops 300000000 | bytes 8000000 | tf_op jit(solution)/shard_map/pallas_call | solution.py:576
  6.0 0.0 collective-permute-done.refs_1_
  6.0 0.3 collective-permute-done.2.refs_3_
  6.3 0.0 collective-permute-done.1.refs_2_
  6.3 1.1 %shard_map.147 = (bf16[144,256]{1,0:T(8,128)(2,1)S(1)}, bf16[192,256]{1,0:T(8,128)(2,1)S(1)}, bf16[144,256]{1,0:T(8,128)(2,1)S(1)}, bf16[192,256]{1,0:T(8,128)(2,1)S(1)}) custom-call(s32[2]{0:T(128)S(1)} %pad_add_fusion.here_ref, f32[64,16]{1,0:T(8,128)S(1)} %get-tuple-element.29.table_ref, bf16[4,384,256]{2,1,0:T(8,128)(2,1)S(1)} %get-tuple-element.35.weight_ref, ...), custom_call_target="tpu_custom_call" | custom-call | flops 100000000 | bytes 1000000 | tf_op jit(solution)/shard_map/pallas_call | solution.py:597
  7.4 1.3 %collective-permute-start.3 = (bf16[192,256]{1,0:T(8,128)(2,1)S(1)}, bf16[192,256]{1,0:T(8,128)(2,1)S(1)}, u32[]{:S(2)}, u32[]{:S(2)}) collective-permute-start(bf16[192,256]{1,0:T(8,128)(2,1)S(1)} %get-tuple-element.41), channel_id=1, source_target_pairs={{0,1},{1,2},{2,3},{3,0},{4,5},{5,6},{6,7},{7,4},{8,9},{9,10},{10,1... | collective-permute-start | bytes 294920 | tf_op jit(solution)/shard_map/ppermute | solution.py:24
  8.7 2.1 %collective-permute-start.5 = (bf16[192,256]{1,0:T(8,128)(2,1)S(1)}, bf16[192,256]{1,0:T(8,128)(2,1)S(1)}, u32[]{:S(2)}, u32[]{:S(2)}) collective-permute-start(bf16[192,256]{1,0:T(8,128)(2,1)S(1)} %get-tuple-element.43), channel_id=1, source_target_pairs={{0,3},{1,0},{2,1},{3,2},{4,7},{5,4},{6,5},{7,6},{8,11},{9,8},{10,9... | collective-permute-start | bytes 294920 | tf_op jit(solution)/shard_map/ppermute | solution.py:24
  10.8 0.4 collective-permute-start.4
  11.2 5.9 %collective-permute-done.4.refs_2_ = bf16[144,256]{1,0:T(8,128)(2,1)S(1)} collective-permute-done((bf16[144,256]{1,0:T(8,128)(2,1)S(1)}, bf16[144,256]{1,0:T(8,128)(2,1)S(1)}, u32[]{:S(2)}, u32[]{:S(2)}) %collective-permute-start.4) | collective-permute-done | bytes 73760 | tf_op jit(solution)/shard_map/ppermute | solution.py:24
  17.2 0.0 collective-permute-done.3.refs_1_.refs_9_
  17.2 0.0 collective-permute-done.5.refs_3_.refs_10_
  17.2 0.6 %shard_map.149 = (bf16[4,20,256]{2,1,0:T(8,128)(2,1)S(1)}, bf16[248,256]{1,0:T(8,128)(2,1)S(1)}, bf16[248,256]{1,0:T(8,128)(2,1)S(1)}) custom-call(s32[2]{0:T(128)S(1)} %pad_add_fusion.here_ref, f32[12,256]{1,0:T(8,128)S(1)} %get-tuple-element.32.bias_ref.refs_11_, bf16[16,64,256]{2,1,0:T(8,128)(2,1)S(1)} %get-tuple-element.48.lat1_ref.refs_4_, ...), custom_call_target="tpu_custom_call" | custom-call | flops 1000000 | bytes 1000000 | tf_op jit(solution)/shard_map/pallas_call | solution.py:638
  17.8 5.5 %collective-permute-start.9 = (bf16[248,256]{1,0:T(8,128)(2,1)S(1)}, bf16[248,256]{1,0:T(8,128)(2,1)S(1)}, u32[]{:S(2)}, u32[]{:S(2)}) collective-permute-start(bf16[248,256]{1,0:T(8,128)(2,1)S(1)} %get-tuple-element.51), channel_id=1, source_target_pairs={{0,4},{4,8},{8,12},{1,5},{5,9},{9,13},{2,6},{6,10},{10,14},{3,7},{... | collective-permute-start | bytes 380936 | tf_op jit(solution)/shard_map/ppermute | solution.py:31
  23.3 1.9 %collective-permute-start.10 = (bf16[248,256]{1,0:T(8,128)(2,1)S(1)}, bf16[248,256]{1,0:T(8,128)(2,1)S(1)}, u32[]{:S(2)}, u32[]{:S(2)}) collective-permute-start(bf16[248,256]{1,0:T(8,128)(2,1)S(1)} %get-tuple-element.52), channel_id=1, source_target_pairs={{4,0},{8,4},{12,8},{5,1},{9,5},{13,9},{6,2},{10,6},{14,10},{7,3},{... | collective-permute-start | bytes 380936 | tf_op jit(solution)/shard_map/ppermute | solution.py:31
  25.2 1.2 %shard_map.146.taps_ref = f32[3,192,256]{2,1,0:T(8,128)S(1)} custom-call(s32[2]{0:T(128)S(1)} %pad_add_fusion.here_ref, bf16[3,3,384,256]{3,2,1,0:T(8,128)(2,1)S(1)} %get-tuple-element.33.weight_ref, bf16[2,32,384]{2,1,0:T(8,128)(2,1)S(1)} %get-tuple-element.34.refs_0_, bf16[2,32,384]{2,1,0:T(8,128)(2,1)S(1)} %collective-permute-done.refs_1_, ...), custom_call_target="tpu_custom_call" | custom-call | flops 700000000 | bytes 3000000 | tf_op jit(solution)/shard_map/pallas_call | solution.py:613
  26.4 1.8 %shard_map.148 = (bf16[6,12,256]{2,1,0:T(8,128)(2,1)S(1)}, bf16[6,12,256]{2,1,0:T(8,128)(2,1)S(1)}, bf16[6,12,256]{2,1,0:T(8,128)(2,1)S(1)}, bf16[6,12,256]{2,1,0:T(8,128)(2,1)S(1)}) custom-call(s32[2]{0:T(128)S(1)} %pad_add_fusion.here_ref, f32[64,16]{1,0:T(8,128)S(1)} %get-tuple-element.29.table_ref, f32[16,64]{1,0:T(8,128)S(1)} %get-tuple-element.30.turned_ref, ...), custom_call_target="tpu_custom_call" | custom-call | flops 300000000 | bytes 3000000 | tf_op jit(solution)/shard_map/pallas_call | solution.py:622
  28.2 0.1 collective-permute-start.6
  28.3 2.4 %collective-permute-start.7 = (bf16[6,12,256]{2,1,0:T(8,128)(2,1)S(1)}, bf16[6,12,256]{2,1,0:T(8,128)(2,1)S(1)}, u32[]{:S(2)}, u32[]{:S(2)}) collective-permute-start(bf16[6,12,256]{2,1,0:T(8,128)(2,1)S(1)} %get-tuple-element.46), channel_id=1, source_target_pairs={{0,2},{1,3},{2,0},{3,1},{4,6},{5,7},{6,4},{7,5},{8,10},{9,11},{10,... | collective-permute-start | bytes 110600 | tf_op jit(solution)/shard_map/ppermute | solution.py:24
  30.7 0.9 %collective-permute-start.8 = (bf16[6,12,256]{2,1,0:T(8,128)(2,1)S(1)}, bf16[6,12,256]{2,1,0:T(8,128)(2,1)S(1)}, u32[]{:S(2)}, u32[]{:S(2)}) collective-permute-start(bf16[6,12,256]{2,1,0:T(8,128)(2,1)S(1)} %get-tuple-element.47), channel_id=1, source_target_pairs={{0,3},{1,0},{2,1},{3,2},{4,7},{5,4},{6,5},{7,6},{8,11},{9,8},{10,9... | collective-permute-start | bytes 110600 | tf_op jit(solution)/shard_map/ppermute | solution.py:24
  31.5 1.6 %collective-permute-done.6.refs_1_ = bf16[6,12,256]{2,1,0:T(8,128)(2,1)S(1)} collective-permute-done((bf16[6,12,256]{2,1,0:T(8,128)(2,1)S(1)}, bf16[6,12,256]{2,1,0:T(8,128)(2,1)S(1)}, u32[]{:S(2)}, u32[]{:S(2)}) %collective-permute-start.6) | collective-permute-done | bytes 36896 | tf_op jit(solution)/shard_map/ppermute | solution.py:24
  33.1 0.0 collective-permute-done.7.refs_2_
  33.1 1.2 %collective-permute-done.8.refs_3_ = bf16[6,12,256]{2,1,0:T(8,128)(2,1)S(1)} collective-permute-done((bf16[6,12,256]{2,1,0:T(8,128)(2,1)S(1)}, bf16[6,12,256]{2,1,0:T(8,128)(2,1)S(1)}, u32[]{:S(2)}, u32[]{:S(2)}) %collective-permute-start.8) | collective-permute-done | bytes 36896 | tf_op jit(solution)/shard_map/ppermute | solution.py:24
  34.3 0.0 collective-permute-done.9.refs_7_
  34.3 0.0 collective-permute-done.10.refs_8_
  34.3 18.9 %shard_map.150 = bf16[16,64,256]{2,1,0:T(8,128)(2,1)} custom-call(s32[2]{0:T(128)S(1)} %pad_add_fusion.here_ref, bf16[6,12,256]{2,1,0:T(8,128)(2,1)S(1)} %get-tuple-element.44.refs_0_, bf16[6,12,256]{2,1,0:T(8,128)(2,1)S(1)} %collective-permute-done.6.refs_1_, bf16[6,12,256]{2,1,0:T(8,128)(2,1)S(1)} %collective-permute-done.7.refs_2_, ...), custom_call_target="tpu_custom_call" | custom-call | flops 10000000000 | bytes 12000000 | tf_op jit(solution)/shard_map/pallas_call | solution.py:498
Async XLA Ops:
  0.0 6.0 %collective-permute-start = (bf16[2,32,384]{2,1,0:T(8,128)(2,1)}, bf16[2,32,384]{2,1,0:T(8,128)(2,1)S(1)}, u32[]{:S(2)}, u32[]{:S(2)}) collective-permute-start(bf16[2,32,384]{2,1,0:T(8,128)(2,1)} %refs_7_.1), channel_id=1, source_target_pairs={{0,4},{4,8},{8,12},{12,0},{1,5},{5,9},{9,13},{13,1},{2,6},{6,10},{... | collective-permute-start | bytes 147464 | tf_op jit(solution)/shard_map/ppermute | solution.py:24
  2.6 3.7 %collective-permute-start.2 = (bf16[2,32,384]{2,1,0:T(8,128)(2,1)}, bf16[2,32,384]{2,1,0:T(8,128)(2,1)S(1)}, u32[]{:S(2)}, u32[]{:S(2)}) collective-permute-start(bf16[2,32,384]{2,1,0:T(8,128)(2,1)} %refs_7_.1), channel_id=1, source_target_pairs={{0,12},{4,0},{8,4},{12,8},{1,13},{5,1},{9,5},{13,9},{2,14},{6,2},{... | collective-permute-start | bytes 147464 | tf_op jit(solution)/shard_map/ppermute | solution.py:24
  2.6 3.7 %collective-permute-start.1 = (bf16[2,32,384]{2,1,0:T(8,128)(2,1)}, bf16[2,32,384]{2,1,0:T(8,128)(2,1)S(1)}, u32[]{:S(2)}, u32[]{:S(2)}) collective-permute-start(bf16[2,32,384]{2,1,0:T(8,128)(2,1)} %refs_7_.1), channel_id=1, source_target_pairs={{0,8},{4,12},{8,0},{12,4},{1,9},{5,13},{9,1},{13,5},{2,10},{6,14},... | collective-permute-start | bytes 147464 | tf_op jit(solution)/shard_map/ppermute | solution.py:24
  7.4 9.8 %collective-permute-start.3 = (bf16[192,256]{1,0:T(8,128)(2,1)S(1)}, bf16[192,256]{1,0:T(8,128)(2,1)S(1)}, u32[]{:S(2)}, u32[]{:S(2)}) collective-permute-start(bf16[192,256]{1,0:T(8,128)(2,1)S(1)} %get-tuple-element.41), channel_id=1, source_target_pairs={{0,1},{1,2},{2,3},{3,0},{4,5},{5,6},{6,7},{7,4},{8,9},{9,10},{10,1... | collective-permute-start | bytes 294920 | tf_op jit(solution)/shard_map/ppermute | solution.py:24
  8.7 8.4 %collective-permute-start.5 = (bf16[192,256]{1,0:T(8,128)(2,1)S(1)}, bf16[192,256]{1,0:T(8,128)(2,1)S(1)}, u32[]{:S(2)}, u32[]{:S(2)}) collective-permute-start(bf16[192,256]{1,0:T(8,128)(2,1)S(1)} %get-tuple-element.43), channel_id=1, source_target_pairs={{0,3},{1,0},{2,1},{3,2},{4,7},{5,4},{6,5},{7,6},{8,11},{9,8},{10,9... | collective-permute-start | bytes 294920 | tf_op jit(solution)/shard_map/ppermute | solution.py:24
  10.8 6.3 %collective-permute-start.4 = (bf16[144,256]{1,0:T(8,128)(2,1)S(1)}, bf16[144,256]{1,0:T(8,128)(2,1)S(1)}, u32[]{:S(2)}, u32[]{:S(2)}) collective-permute-start(bf16[144,256]{1,0:T(8,128)(2,1)S(1)} %get-tuple-element.42), channel_id=1, source_target_pairs={{0,2},{1,3},{2,0},{3,1},{4,6},{5,7},{6,4},{7,5},{8,10},{9,11},{10,... | collective-permute-start | bytes 221192 | tf_op jit(solution)/shard_map/ppermute | solution.py:24
  17.8 16.5 %collective-permute-start.9 = (bf16[248,256]{1,0:T(8,128)(2,1)S(1)}, bf16[248,256]{1,0:T(8,128)(2,1)S(1)}, u32[]{:S(2)}, u32[]{:S(2)}) collective-permute-start(bf16[248,256]{1,0:T(8,128)(2,1)S(1)} %get-tuple-element.51), channel_id=1, source_target_pairs={{0,4},{4,8},{8,12},{1,5},{5,9},{9,13},{2,6},{6,10},{10,14},{3,7},{... | collective-permute-start | bytes 380936 | tf_op jit(solution)/shard_map/ppermute | solution.py:31
  23.3 11.0 %collective-permute-start.10 = (bf16[248,256]{1,0:T(8,128)(2,1)S(1)}, bf16[248,256]{1,0:T(8,128)(2,1)S(1)}, u32[]{:S(2)}, u32[]{:S(2)}) collective-permute-start(bf16[248,256]{1,0:T(8,128)(2,1)S(1)} %get-tuple-element.52), channel_id=1, source_target_pairs={{4,0},{8,4},{12,8},{5,1},{9,5},{13,9},{6,2},{10,6},{14,10},{7,3},{... | collective-permute-start | bytes 380936 | tf_op jit(solution)/shard_map/ppermute | solution.py:31
  28.2 4.9 %collective-permute-start.6 = (bf16[6,12,256]{2,1,0:T(8,128)(2,1)S(1)}, bf16[6,12,256]{2,1,0:T(8,128)(2,1)S(1)}, u32[]{:S(2)}, u32[]{:S(2)}) collective-permute-start(bf16[6,12,256]{2,1,0:T(8,128)(2,1)S(1)} %get-tuple-element.45), channel_id=1, source_target_pairs={{0,1},{1,2},{2,3},{3,0},{4,5},{5,6},{6,7},{7,4},{8,9},{9,10},{10,1... | collective-permute-start | bytes 110600 | tf_op jit(solution)/shard_map/ppermute | solution.py:24
  28.3 4.8 %collective-permute-start.7 = (bf16[6,12,256]{2,1,0:T(8,128)(2,1)S(1)}, bf16[6,12,256]{2,1,0:T(8,128)(2,1)S(1)}, u32[]{:S(2)}, u32[]{:S(2)}) collective-permute-start(bf16[6,12,256]{2,1,0:T(8,128)(2,1)S(1)} %get-tuple-element.46), channel_id=1, source_target_pairs={{0,2},{1,3},{2,0},{3,1},{4,6},{5,7},{6,4},{7,5},{8,10},{9,11},{10,... | collective-permute-start | bytes 110600 | tf_op jit(solution)/shard_map/ppermute | solution.py:24
  30.7 3.6 %collective-permute-start.8 = (bf16[6,12,256]{2,1,0:T(8,128)(2,1)S(1)}, bf16[6,12,256]{2,1,0:T(8,128)(2,1)S(1)}, u32[]{:S(2)}, u32[]{:S(2)}) collective-permute-start(bf16[6,12,256]{2,1,0:T(8,128)(2,1)S(1)} %get-tuple-element.47), channel_id=1, source_target_pairs={{0,3},{1,0},{2,1},{3,2},{4,7},{5,4},{6,5},{7,6},{8,11},{9,8},{10,9... | collective-permute-start | bytes 110600 | tf_op jit(solution)/shard_map/ppermute | solution.py:24

commit v5 on v4

--- a/solution.py
+++ b/solution.py
@@ -16,7 +16,7 @@
 vmem_spec = pl.BlockSpec(memory_space=pltpu.VMEM)
 hbm_spec = pl.BlockSpec(memory_space=pltpu.HBM)
 smem_spec = pl.BlockSpec(memory_space=pltpu.SMEM)
-params = pltpu.CompilerParams(vmem_limit_bytes=24 * 1024 * 1024)
+params = pltpu.CompilerParams(vmem_limit_bytes=30 * 1024 * 1024)
 
 
 def shifted(value, axis, shift):
@@ -74,6 +74,65 @@
 
 def floor_div(value, step):
     return jnp.floor((value + 0.5) / step)
+
+
+def stretch_matrix(here, out_shape, out_border, in_shape, in_border, factor, out_size, in_size, counts, lanes, taps=1):
+    out_rows, out_pitch = out_shape
+    lane = lax.broadcasted_iota(jnp.int32, (1, lanes * taps * taps), 1).astype(f32)
+    tap = floor_div(lane, lanes)
+    place = lane - tap * lanes
+    row_tap = floor_div(tap, taps)
+    col_tap = tap - row_tap * taps
+    place_row = floor_div(place, in_shape[1])
+    place_col = place - place_row * in_shape[1]
+
+    def weights(axis, length, targets, tap_here):
+        whole = float(in_size[axis] * counts[axis])
+        first_out = (here[axis] * out_size[axis] - out_border).astype(f32) - (taps // 2)
+        first_in = (here[axis] * in_size[axis] - in_border).astype(f32)
+        output = first_out + tap_here + lax.broadcasted_iota(jnp.int32, (length, 1), 0).astype(f32)
+        source = (output + 0.5) * (1.0 / factor) - 0.5
+        source = jnp.minimum(jnp.maximum(source, 0.0), whole - 1.0)
+        inside = jnp.where((output >= 0.0) & (output < whole * factor), 1.0, 0.0)
+        return jnp.maximum(0.0, 1.0 - jnp.abs(source - (first_in + targets))) * inside
+
+    down = weights(0, out_rows, place_row, row_tap)
+    across = weights(1, out_pitch, place_col, col_tap)
+    matrix = down[:, None, :] * across[None, :, :]
+    return matrix.astype(bf16).reshape(out_rows * out_pitch, -1)
+
+
+def pitch_of(width):
+    return (width + 15) // 16 * 16
+
+
+def window_shape(size, border):
+    return size[0] + 2 * border, pitch_of(size[1] + 2 * border)
+
+
+def compact_shape(size, border):
+    return size[0] + 2 * border, size[1] + 2 * border
+
+
+def stretches(sizes):
+    one, two, three, four, counts = sizes
+
+    def matrix(out, out_border, source, in_border, compact=False):
+        factor = out[0] // source[0]
+        if compact:
+            shape = compact_shape(source, in_border)
+            return (out, out_border, shape, in_border, factor, out, source, counts, pitch_of(shape[0] * shape[1]), 3)
+        shape = window_shape(source, in_border)
+        return (window_shape(out, out_border), out_border, shape, in_border, factor, out, source, counts, shape[0] * shape[1], 1)
+
+    return (
+        matrix(three, rim, four, rim),
+        matrix(two, rim, three, rim),
+        matrix(one, rim, two, rim),
+        matrix(one, 1, two, 1),
+        matrix(one, 0, three, 1, True),
+        matrix(one, 0, four, 1, True),
+    )
 
 
 def lateral_kernel(col_count, kept_count, here_ref, *refs):
@@ -166,8 +225,20 @@
             message[window_rows + cells :, :] = piece[window_rows:, :]
 
 
-def feature_kernel(row_count, here_ref, weight_ref, *refs):
-    blocks, (out_ref, grid_buf) = refs[:row_count], refs[row_count:]
+def feature_kernel(row_count, plans, here_ref, weight_hbm, *refs):
+    blocks, refs = refs[:row_count], refs[row_count:]
+    late, refs = refs[:3], refs[3:]
+    out_ref, kept, matrices = refs[0], refs[1:4], refs[4 : 4 + len(plans)]
+    weight_ref, grid_buf, sems = refs[4 + len(plans) :]
+    copies = [
+        pltpu.make_async_copy(source, target, sems.at[number])
+        for number, (source, target) in enumerate(zip((weight_hbm, *late), (weight_ref, *kept)))
+    ]
+    for copy in copies:
+        copy.start()
+    here = (here_ref[0], here_ref[1])
+    for plan, matrix in zip(plans, matrices):
+        matrix[...] = stretch_matrix(here, *plan)
     high, wide, depth = blocks[0].shape
     grid_buf[...] = jnp.zeros_like(grid_buf)
     for shift, block in enumerate(blocks):
@@ -175,6 +246,7 @@
         grid_buf[pl.ds(row, high)] = block[...]
     rows = out_ref.shape[1] // wide
     window = grid_buf[pl.ds(here_ref[0] * high, rows + 2)].reshape((rows + 2) * wide, depth)
+    copies[0].wait()
     for col_tap in range(3):
         total = dot(window[0 : rows * wide], weight_ref[0, col_tap])
         for row_tap in (1, 2):
@@ -182,6 +254,8 @@
                 window[row_tap * wide : (row_tap + rows) * wide], weight_ref[row_tap, col_tap]
             )
         out_ref[col_tap] = total
+    for copy in copies[1:]:
+        copy.wait()
 
 
 def neck_kernel(
@@ -284,26 +358,6 @@
         out[...] = pack_buf[...].astype(bf16)
 
 
-def stretch_matrix(out_shape, out_first, in_shape, in_first, factor, extent):
-    out_rows, out_pitch = out_shape
-    in_rows, in_pitch = in_shape
-    place = lax.broadcasted_iota(jnp.int32, (1, in_rows * in_pitch), 1).astype(f32)
-    place_row = floor_div(place, in_pitch)
-    place_col = place - place_row * in_pitch
-
-    def weights(length, first_out, first_in, targets, whole):
-        output = first_out + lax.broadcasted_iota(jnp.int32, (length, 1), 0).astype(f32)
-        source = (output + 0.5) * (1.0 / factor) - 0.5
-        source = jnp.minimum(jnp.maximum(source, 0.0), whole - 1.0)
-        inside = jnp.where((output >= 0.0) & (output < whole * factor), 1.0, 0.0)
-        return jnp.maximum(0.0, 1.0 - jnp.abs(source - (first_in + targets))) * inside
-
-    down = weights(out_rows, out_first[0], in_first[0], place_row, extent[0])
-    across = weights(out_pitch, out_first[1], in_first[1], place_col, extent[1])
-    matrix = down[:, None, :] * across[None, :, :]
-    return matrix.astype(bf16).reshape(out_rows * out_pitch, in_rows * in_pitch)
-
-
 def tail_kernel(
     sizes,
     top_count,
@@ -321,8 +375,14 @@
         before_ref,
         after_ref,
         bias_ref,
-        smooth_hbm,
-        join_hbm,
+        smooth_w,
+        join_w,
+        up3_ref,
+        up2_ref,
+        up1_ref,
+        raise2_ref,
+        spread3_ref,
+        spread4_ref,
         out_ref,
         top_buf,
         lat1_buf,
@@ -334,23 +394,12 @@
         acc_buf,
         sums_buf,
         stack_buf,
-        smooth_w,
-        join_w,
-        sems,
+        small3_buf,
+        small4_buf,
+        terms3_buf,
+        terms4_buf,
     ) = refs
-    smooth_copy = pltpu.make_async_copy(smooth_hbm, smooth_w, sems.at[0])
-    join_copy = pltpu.make_async_copy(join_hbm, join_w, sems.at[1])
-    smooth_copy.start()
-    join_copy.start()
-    row_here = here_ref[0].astype(f32)
-    col_here = here_ref[1].astype(f32)
     channels = bias_ref.shape[1]
-
-    def firsts(high, wide, border):
-        return row_here * high - border, col_here * wide - border
-
-    def extent(high, wide):
-        return float(high * row_count), float(wide * col_count)
 
     side_start = before_ref.shape[0] - rim * (high1 + high2)
     row_start = 0
@@ -390,117 +439,90 @@
     pitch4 = top_buf.shape[1]
     top = top_buf[...].astype(bf16).reshape(tall4 * pitch4, channels)
 
-    def pyramid(lat_buf, high, wide, source, source_shape, source_first, source_size):
-        rows, pitch = lat_buf.shape[:2]
-        matrix = stretch_matrix(
-            (rows, pitch), firsts(high, wide, rim), source_shape, source_first, 2, extent(*source_size)
-        )
-        total = lat_buf[...].reshape(rows * pitch, channels) + dot(matrix, source)
-        return total.astype(bf16)
-
-    first4 = firsts(high4, wide4, rim)
-    pyr3_buf[...] = pyramid(lat3_buf, high3, wide3, top, (tall4, pitch4), first4, (high4, wide4))
-    shape3 = lat3_buf.shape[:2]
-    pyr2_buf[...] = pyramid(
-        lat2_buf, high2, wide2, pyr3_buf[...], shape3, firsts(high3, wide3, rim), (high3, wide3)
-    )
-    shape2 = lat2_buf.shape[:2]
-    pyr1_buf[...] = pyramid(
-        lat1_buf, high1, wide1, pyr2_buf[...], shape2, firsts(high2, wide2, rim), (high2, wide2)
-    )
-    shape1 = lat1_buf.shape[:2]
-    smooth_copy.wait()
+    shape1, shape2, shape3 = lat1_buf.shape[:2], lat2_buf.shape[:2], lat3_buf.shape[:2]
+    for lat_buf, matrix, source, out in (
+        (lat3_buf, up3_ref, None, pyr3_buf),
+        (lat2_buf, up2_ref, pyr3_buf, pyr2_buf),
+        (lat1_buf, up1_ref, pyr2_buf, pyr1_buf),
+    ):
+        source = top if source is None else source[...]
+        total = lat_buf[...].reshape(-1, channels) + dot(matrix[...], source)
+        out[...] = total.astype(bf16)
 
     def conv(source, shape, weight_at, rows):
         pitch = shape[1]
         span = rows * pitch
+        stacked = jnp.concatenate(
+            [source[row_tap * pitch : row_tap * pitch + span, :] for row_tap in range(3)], axis=1
+        )
         for col_tap in range(3):
-            total = dot(source[0:span, :], weight_at(0, col_tap))
-            for row_tap in (1, 2):
-                total = total + dot(
-                    source[row_tap * pitch : row_tap * pitch + span, :], weight_at(row_tap, col_tap)
-                )
-            yield col_tap, total.reshape(rows, pitch, channels)
+            weight = weight_at(col_tap)
+            total = dot(stacked, weight.reshape(-1, channels))
+            acc_buf[col_tap, :rows, :pitch, :] = total.reshape(rows, pitch, channels)
+
+    def taps_total(rows, whole):
+        total = acc_buf[0, :rows, 0:whole, :]
+        for col_tap in (1, 2):
+            total = total + acc_buf[col_tap, :rows, col_tap : whole + col_tap, :]
+        return total
 
     def smooth(number, source, shape, wide):
-        rows, pitch = shape[0] - 2, shape[1]
-        for col_tap, total in conv(
-            source, shape, lambda i, j: smooth_w[number, i, j], rows
-        ):
-            acc_buf[col_tap, :rows, :pitch, :] = total
-        whole = wide + 2
-        total = (
-            acc_buf[0, :rows, 0:whole, :]
-            + acc_buf[1, :rows, 1 : whole + 1, :]
-            + acc_buf[2, :rows, 2 : whole + 2, :]
-        )
+        rows = shape[0] - 2
+        conv(source, shape, lambda j: smooth_w[number, :, j], rows)
+        total = taps_total(rows, wide + 2)
         return jnp.maximum(total + bias_ref[8 + number : 9 + number, :][None], 0.0)
 
-    def smooth_flat(number, source, shape, wide):
-        rows, pitch = shape[0] - 2, shape[1]
-        value = smooth(number, source, shape, wide)
-        sums_buf[:rows, :pitch, :] = jnp.zeros((rows, pitch, channels), f32)
-        sums_buf[:rows, : wide + 2, :] = value
-        return sums_buf[:rows, :pitch, :].astype(bf16).reshape(rows * pitch, channels)
-
-    rows1, pitch1 = shape1[0] - 2, shape1[1]
-    out_first = firsts(high1, wide1, 1)
-
-    def raise_to_one(source, source_shape, source_first, factor, source_size):
-        matrix = stretch_matrix(
-            (rows1, pitch1), out_first, source_shape, source_first, factor, extent(*source_size)
-        )
-        return dot(matrix, source).astype(bf16)
-
-    stack_buf[:, 3 * channels : 4 * channels] = raise_to_one(
-        top, (tall4, pitch4), first4, 8, (high4, wide4)
-    )
-    smooth3 = smooth_flat(2, pyr3_buf, shape3, wide3)
-    stack_buf[:, 2 * channels : 3 * channels] = raise_to_one(
-        smooth3, (shape3[0] - 2, shape3[1]), firsts(high3, wide3, 1), 4, (high3, wide3)
-    )
-    smooth2 = smooth_flat(1, pyr2_buf, shape2, wide2)
-    stack_buf[:, channels : 2 * channels] = raise_to_one(
-        smooth2, (shape2[0] - 2, shape2[1]), firsts(high2, wide2, 1), 2, (high2, wide2)
-    )
+    def tap_terms(source, first, buf):
+        lanes = source.shape[0]
+        small = source[...].astype(bf16)
+        for tap in range(9):
+            weight = join_w[tap // 3, tap % 3, first : first + channels, :]
+            buf[tap * lanes : (tap + 1) * lanes, :] = dot(small, weight).astype(bf16)
+
+    tall, broad = compact_shape((high4, wide4), 1)
+    small4_buf[...] = jnp.zeros_like(small4_buf)
+    for row in range(tall):
+        small4_buf[row * broad : (row + 1) * broad, :] = top_buf[row + rim - 1, rim - 1 : rim - 1 + broad, :]
+    tap_terms(small4_buf, 3 * channels, terms4_buf)
+    value = smooth(2, pyr3_buf, shape3, wide3)
+    tall, broad = compact_shape((high3, wide3), 1)
+    small3_buf[...] = jnp.zeros_like(small3_buf)
+    for row in range(tall):
+        small3_buf[row * broad : (row + 1) * broad, :] = value[row]
+    tap_terms(small3_buf, 2 * channels, terms3_buf)
+
+    rows2, pitch2 = window_shape((high2, wide2), 1)
+    value = smooth(1, pyr2_buf, shape2, wide2)
+    sums_buf[:rows2, :pitch2, :] = jnp.zeros((rows2, pitch2, channels), f32)
+    sums_buf[:rows2, : wide2 + 2, :] = value
+    smooth2 = sums_buf[:rows2, :pitch2, :].astype(bf16).reshape(rows2 * pitch2, channels)
+    stack_buf[:, channels : 2 * channels] = dot(raise2_ref[...], smooth2).astype(bf16)
+
+    rows1, pitch1 = window_shape((high1, wide1), 1)
     value = smooth(0, pyr1_buf, shape1, wide1)
-    down = out_first[0] + lax.broadcasted_iota(jnp.int32, (rows1, 1, 1), 0).astype(f32)
-    across = out_first[1] + lax.broadcasted_iota(jnp.int32, (1, wide1 + 2, 1), 1).astype(f32)
-    tall, broad = extent(high1, wide1)
-    inside = (down >= 0.0) & (down < tall) & (across >= 0.0) & (across < broad)
+    down = here_ref[0] * high1 - 1 + lax.broadcasted_iota(jnp.int32, (rows1, 1, 1), 0)
+    across = here_ref[1] * wide1 - 1 + lax.broadcasted_iota(jnp.int32, (1, wide1 + 2, 1), 1)
+    inside = (down >= 0) & (down < high1 * row_count) & (across >= 0) & (across < wide1 * col_count)
     sums_buf[:rows1, : wide1 + 2, :] = jnp.where(inside, value, 0.0)
     stack_buf[:, 0:channels] = sums_buf[...].astype(bf16).reshape(rows1 * pitch1, channels)
-    join_copy.wait()
-    shape_join = (rows1, pitch1)
-    for col_tap, total in conv(stack_buf, shape_join, lambda i, j: join_w[i, j], high1):
-        acc_buf[col_tap, :high1] = total
-    total = (
-        acc_buf[0, :high1, 0:wide1, :]
-        + acc_buf[1, :high1, 1 : wide1 + 1, :]
-        + acc_buf[2, :high1, 2 : wide1 + 2, :]
-    )
+    conv(stack_buf, (rows1, pitch1), lambda j: join_w[:, j, 0 : 2 * channels], high1)
+    total = taps_total(high1, wide1)
+    spread = dot(spread3_ref[...], terms3_buf[...]) + dot(spread4_ref[...], terms4_buf[...])
+    total = total + spread.reshape(high1, wide1, channels)
     out_ref[...] = jnp.maximum(total + bias_ref[11:12, :][None], 0.0).astype(bf16)
 
 
-def pitch_of(width):
-    return (width + 15) // 16 * 16
-
-
-def tail(here, tops, lats, above, below, before, after, biases, smooth_weight, join_weight, sizes):
-    (high1, wide1), (high2, wide2), (high3, wide3), (high4, wide4), _ = sizes
+def tail(here, tops, lats, above, below, before, after, biases, weights, matrices, sizes):
+    one, _, _, _, _ = sizes
     channels = biases.shape[1]
-
-    def window(high, wide):
-        return high + 2 * rim, pitch_of(wide + 2 * rim)
-
-    shapes = [window(high, wide) for high, wide in sizes[:4]]
+    shapes = [window_shape(size, rim) for size in sizes[:4]]
     (rows1, pitch1), (rows2, pitch2), (rows3, pitch3), (rows4, pitch4) = shapes
+    small3, small4 = (matrix.shape[1] // 9 for matrix in matrices[-2:])
+    inputs = (*tops, *lats, above, below, before, after, biases, *weights, *matrices)
     return pl.pallas_call(
         functools.partial(tail_kernel, sizes, len(tops)),
-        out_shape=jax.ShapeDtypeStruct((high1, wide1, channels), bf16),
-        in_specs=[smem_spec]
-        + [vmem_spec] * (len(tops) + 8)
-        + [hbm_spec] * 2,
+        out_shape=jax.ShapeDtypeStruct((*one, channels), bf16),
+        in_specs=[smem_spec] + [vmem_spec] * len(inputs),
         out_specs=vmem_spec,
         scratch_shapes=[
             pltpu.VMEM((rows4, pitch4, channels), f32),
@@ -512,27 +534,17 @@
             pltpu.VMEM((rows3 * pitch3, channels), bf16),
             pltpu.VMEM((3, rows1 - 2, pitch1, channels), f32),
             pltpu.VMEM((rows1 - 2, pitch1, channels), f32),
-            pltpu.VMEM(((rows1 - 2) * pitch1, 4 * channels), bf16),
-            pltpu.VMEM(smooth_weight.shape, bf16),
-            pltpu.VMEM(join_weight.shape, bf16),
-            pltpu.SemaphoreType.DMA((2,)),
+            pltpu.VMEM(((rows1 - 2) * pitch1, 2 * channels), bf16),
+            pltpu.VMEM((small3, channels), f32),
+            pltpu.VMEM((small4, channels), f32),
+            pltpu.VMEM((9 * small3, channels), bf16),
+            pltpu.VMEM((9 * small4, channels), bf16),
         ],
-        compiler_params=pltpu.CompilerParams(vmem_limit_bytes=44 * 1024 * 1024),
+        compiler_params=pltpu.CompilerParams(vmem_limit_bytes=32 * 1024 * 1024),
         cost_estimate=pl.CostEstimate(
             flops=10_000_000_000, bytes_accessed=12_000_000, transcendentals=0
         ),
-    )(
-        here,
-        *tops,
-        *lats,
-        above,
-        below,
-        before,
-        after,
-        biases,
-        in_hbm(smooth_weight),
-        in_hbm(join_weight),
-    )
+    )(here, *inputs)
 
 
 def local(
@@ -572,7 +584,7 @@
     window_rows = high3 * (wide3 + 2 * rim)
     side_rows = rim * (high1 + high2)
     used = (level_one, lateral_one, level_two, lateral_two, level_three, lateral_three)
-    kept = (biases, level_four, table, bin_weight, turned, neck_feature, neck_pooled)
+    kept = (biases, level_four, table, bin_weight, turned)
     lat1, lat2, *rest = call(
         functools.partial(lateral_kernel, col_count, len(kept)),
         [shape((high1, wide1, channels)), shape((high2, wide2, channels))]
@@ -588,10 +600,10 @@
             pltpu.SemaphoreType.DMA((len(used) + len(kept),)),
         ],
         300_000_000,
-        8_000_000,
+        4_000_000,
     )(here, *(in_hbm(value) for value in (*used, *kept)))
     pieces = rest[:col_count]
-    bias_table, level_four, table, bin_weight, turned, neck_feature, neck_pooled = rest[col_count:]
+    bias_table, level_four, table, bin_weight, turned = rest[col_count:]
     blocks = [level_four] + others
     near = (1, col_count - 1)
     messages = call(
@@ -610,14 +622,29 @@
         shifted(messages[shift], "col", shift) for shift in range(1, col_count)
     ]
     rows = high4 + 2 * rim
-    taps = call(
-        functools.partial(feature_kernel, row_count),
-        shape((3, rows * grid_cols, channels), f32),
-        [smem_spec] + [vmem_spec] * (1 + row_count),
-        [pltpu.VMEM((grid_rows + 2 * rim + 2, grid_cols, part_four), bf16)],
+    sizes = (
+        (high1, wide1),
+        (high2, wide2),
+        (high3, wide3),
+        (high4, wide4),
+        (row_count, col_count),
+    )
+    plans = stretches(sizes)
+    late = (neck_pooled, smooth_weight, join_weight)
+    taps, neck_pooled, smooth_weight, join_weight, *matrices = call(
+        functools.partial(feature_kernel, row_count, plans),
+        [shape((3, rows * grid_cols, channels), f32)]
+        + [shape(value.shape) for value in late]
+        + [shape((plan[0][0] * plan[0][1], plan[8] * plan[9] ** 2)) for plan in plans],
+        [smem_spec, hbm_spec] + [vmem_spec] * row_count + [hbm_spec] * len(late),
+        [
+            pltpu.VMEM(neck_feature.shape, bf16),
+            pltpu.VMEM((grid_rows + 2 * rim + 2, grid_cols, part_four), bf16),
+            pltpu.SemaphoreType.DMA((1 + len(late),)),
+        ],
         700_000_000,
-        3_000_000,
-    )(here, neck_feature, *blocks)
+        12_000_000,
+    )(here, in_hbm(neck_feature), *blocks, *(in_hbm(value) for value in late))
     span4 = wide4 + 2 * rim
     windows = call(
         functools.partial(neck_kernel, row_count, col_count, high4, window_rows),
@@ -647,13 +674,6 @@
         1_000_000,
     )(here, bias_table, lat1, lat2, *received)
     above, below = edge_swap(low_rows, high_rows, "row")
-    sizes = (
-        (high1, wide1),
-        (high2, wide2),
-        (high3, wide3),
-        (high4, wide4),
-        (row_count, col_count),
-    )
     return tail(
         here,
         tops,
@@ -663,8 +683,8 @@
         received[1],
         received[-1],
         bias_table,
-        smooth_weight,
-        join_weight,
+        (smooth_weight, join_weight),
+        matrices,
         sizes,
     )
 

time: 53.9 us -> 51.8 us (0.961)
  Pallas kernels: 26.8 us -> 24.7 us
    pallas_call x1, Pallas kernels: 18.9 us -> 13.5 us  [tail(): pl.pallas_call(functools.partial(tail_kernel, sizes, len(tops)), out_shap...]
    pallas_call x1, Pallas kernels: 1.19 us -> 4.84 us  [local(): call(functools.partial(feature_kernel, row_count, plans), [shape((3, rows...]
  transfers between devices with their start and end apart: 11 -> 11, of which waited for: 4 -> 4; matrix products, arithmetic and copies ran while one was open for 0% -> 0% of each run, Pallas kernels for 12% -> 18%
where the time goes in v5:
time: 51.8 us; the launch traced here: 51.3 us
  Pallas kernels  24.7 us (48%)
  starting transfers between devices  17 us (33%)
  waiting for transfers between devices  9.42 us (18%)
    pallas_call x1, Pallas kernels, tail(): pl.pallas_call(functools.partial(tail_kernel, sizes, len(tops)), out_shap...  13.5 us
    ppermute x9, starting transfers between devices, shifted(): lax.ppermute(value, axis, [(i, (i + shift) % count) for i in range(count)])  9.85 us
    ppermute x9, waiting for transfers between devices, shifted(): lax.ppermute(value, axis, [(i, (i + shift) % count) for i in range(count)])  9.42 us
    ppermute x1, starting transfers between devices, edge_swap(): lax.ppermute(high_out, axis, forward)  5.25 us
    pallas_call x1, Pallas kernels, local(): call(functools.partial(feature_kernel, row_count, plans), [shape((3, rows...  4.84 us
    pallas_call x1, Pallas kernels, local(): call(functools.partial(lateral_kernel, col_count, len(kept)), [shape((hig...  2.85 us
    ppermute x1, starting transfers between devices, edge_swap(): lax.ppermute(low_out, axis, backward)  1.92 us
    pallas_call x1, Pallas kernels, local(): call(functools.partial(neck_kernel, row_count, col_count, high4, window_r...  1.78 us
  transfers between devices with their start and end apart: 11, of which 4 were waited for; matrix products, arithmetic and copies ran while one was open for 0% of the time, Pallas kernels for 18%

profile of v5, /device:TPU:1, one launch (start us, length us, event | category | flops | bytes accessed | tf_op | source)
XLA Modules:
  0.0 51.3 jit_solution(8394970861247847362)
XLA Ops:
  0.0 2.6 %collective-permute-start = (bf16[2,32,384]{2,1,0:T(8,128)(2,1)}, bf16[2,32,384]{2,1,0:T(8,128)(2,1)S(1)}, u32[]{:S(2)}, u32[]{:S(2)}) collective-permute-start(bf16[2,32,384]{2,1,0:T(8,128)(2,1)} %refs_7_.1), channel_id=1, source_target_pairs={{0,4},{4,8},{8,12},{12,0},{1,5},{5,9},{9,13},{13,1},{2,6},{6,10},{... | collective-permute-start | bytes 147464 | tf_op jit(solution)/shard_map/ppermute | solution.py:24
  2.6 0.0 collective-permute-start.2
  2.6 0.1 collective-permute-start.1
  2.7 0.1 pad_add_fusion.here_ref
  2.8 2.8 %shard_map.145 = (bf16[16,64,256]{2,1,0:T(8,128)(2,1)S(1)}, bf16[8,32,256]{2,1,0:T(8,128)(2,1)S(1)}, bf16[128,256]{1,0:T(8,128)(2,1)S(1)}, bf16[128,256]{1,0:T(8...) custom-call(s32[2]{0:T(128)S(1)} %pad_add_fusion.here_ref, ...), custom_call_target="tpu_custom_call" | custom-call | flops 300000000 | bytes 4000000 | tf_op jit(solution)/shard_map/pallas_call | solution.py:588
  5.6 0.0 collective-permute-done.refs_1_
  5.7 0.7 %collective-permute-done.2.refs_3_ = bf16[2,32,384]{2,1,0:T(8,128)(2,1)S(1)} collective-permute-done((bf16[2,32,384]{2,1,0:T(8,128)(2,1)}, bf16[2,32,384]{2,1,0:T(8,128)(2,1)S(1)}, u32[]{:S(2)}, u32[]{:S(2)}) %collective-permute-start.2) | collective-permute-done | bytes 49184 | tf_op jit(solution)/shard_map/ppermute | solution.py:24
  6.3 0.0 collective-permute-done.1.refs_2_
  6.3 1.1 %shard_map.147 = (bf16[144,256]{1,0:T(8,128)(2,1)S(1)}, bf16[192,256]{1,0:T(8,128)(2,1)S(1)}, bf16[144,256]{1,0:T(8,128)(2,1)S(1)}, bf16[192,256]{1,0:T(8,128)(2,1)S(1)}) custom-call(s32[2]{0:T(128)S(1)} %pad_add_fusion.here_ref, f32[64,16]{1,0:T(8,128)S(1)} %get-tuple-element.37.table_ref, bf16[4,384,256]{2,1,0:T(8,128)(2,1)S(1)} %get-tuple-element.43.weight_ref, ...), custom_call_target="tpu_custom_call" | custom-call | flops 100000000 | bytes 1000000 | tf_op jit(solution)/shard_map/pallas_call | solution.py:609
  7.4 1.3 %collective-permute-start.3 = (bf16[192,256]{1,0:T(8,128)(2,1)S(1)}, bf16[192,256]{1,0:T(8,128)(2,1)S(1)}, u32[]{:S(2)}, u32[]{:S(2)}) collective-permute-start(bf16[192,256]{1,0:T(8,128)(2,1)S(1)} %get-tuple-element.49), channel_id=1, source_target_pairs={{0,1},{1,2},{2,3},{3,0},{4,5},{5,6},{6,7},{7,4},{8,9},{9,10},{10,1... | collective-permute-start | bytes 294920 | tf_op jit(solution)/shard_map/ppermute | solution.py:24
  8.7 2.1 %collective-permute-start.5 = (bf16[192,256]{1,0:T(8,128)(2,1)S(1)}, bf16[192,256]{1,0:T(8,128)(2,1)S(1)}, u32[]{:S(2)}, u32[]{:S(2)}) collective-permute-start(bf16[192,256]{1,0:T(8,128)(2,1)S(1)} %get-tuple-element.51), channel_id=1, source_target_pairs={{0,3},{1,0},{2,1},{3,2},{4,7},{5,4},{6,5},{7,6},{8,11},{9,8},{10,9... | collective-permute-start | bytes 294920 | tf_op jit(solution)/shard_map/ppermute | solution.py:24
  10.8 0.4 collective-permute-start.4
  11.2 6.0 %collective-permute-done.4.refs_2_ = bf16[144,256]{1,0:T(8,128)(2,1)S(1)} collective-permute-done((bf16[144,256]{1,0:T(8,128)(2,1)S(1)}, bf16[144,256]{1,0:T(8,128)(2,1)S(1)}, u32[]{:S(2)}, u32[]{:S(2)}) %collective-permute-start.4) | collective-permute-done | bytes 73760 | tf_op jit(solution)/shard_map/ppermute | solution.py:24
  17.2 0.0 collective-permute-done.3.refs_1_.refs_9_
  17.2 0.0 collective-permute-done.5.refs_3_.refs_10_
  17.2 0.6 %shard_map.149 = (bf16[4,20,256]{2,1,0:T(8,128)(2,1)S(1)}, bf16[248,256]{1,0:T(8,128)(2,1)S(1)}, bf16[248,256]{1,0:T(8,128)(2,1)S(1)}) custom-call(s32[2]{0:T(128)S(1)} %pad_add_fusion.here_ref, f32[12,256]{1,0:T(8,128)S(1)} %get-tuple-element.41.bias_ref.refs_11_, bf16[16,64,256]{2,1,0:T(8,128)(2,1)S(1)} %get-tuple-element.56.lat1_ref.refs_4_, ...), custom_call_target="tpu_custom_call" | custom-call | flops 1000000 | bytes 1000000 | tf_op jit(solution)/shard_map/pallas_call | solution.py:665
  17.9 5.3 %collective-permute-start.9 = (bf16[248,256]{1,0:T(8,128)(2,1)S(1)}, bf16[248,256]{1,0:T(8,128)(2,1)S(1)}, u32[]{:S(2)}, u32[]{:S(2)}) collective-permute-start(bf16[248,256]{1,0:T(8,128)(2,1)S(1)} %get-tuple-element.59), channel_id=1, source_target_pairs={{0,4},{4,8},{8,12},{1,5},{5,9},{9,13},{2,6},{6,10},{10,14},{3,7},{... | collective-permute-start | bytes 380936 | tf_op jit(solution)/shard_map/ppermute | solution.py:31
  23.1 1.9 %collective-permute-start.10 = (bf16[248,256]{1,0:T(8,128)(2,1)S(1)}, bf16[248,256]{1,0:T(8,128)(2,1)S(1)}, u32[]{:S(2)}, u32[]{:S(2)}) collective-permute-start(bf16[248,256]{1,0:T(8,128)(2,1)S(1)} %get-tuple-element.60), channel_id=1, source_target_pairs={{4,0},{8,4},{12,8},{5,1},{9,5},{13,9},{6,2},{10,6},{14,10},{7,3},{... | collective-permute-start | bytes 380936 | tf_op jit(solution)/shard_map/ppermute | solution.py:31
  25.0 4.8 %shard_map.146 = (f32[3,192,256]{2,1,0:T(8,128)S(1)}, bf16[3,3,256,256]{3,2,1,0:T(8,128)(2,1)S(1)}, bf16[3,3,3,256,256]{4,3,2,1,0:T(8,128)(2,1)S(1)}, bf16[3,3,1...) custom-call(s32[2]{0:T(128)S(1)} %pad_add_fusion.here_ref, ...), custom_call_target="tpu_custom_call" | custom-call | flops 700000000 | bytes 12000000 | tf_op jit(solution)/shard_map/pallas_call | solution.py:634
  29.9 1.8 %shard_map.148 = (bf16[6,12,256]{2,1,0:T(8,128)(2,1)S(1)}, bf16[6,12,256]{2,1,0:T(8,128)(2,1)S(1)}, bf16[6,12,256]{2,1,0:T(8,128)(2,1)S(1)}, bf16[6,12,256]{2,1,0:T(8,128)(2,1)S(1)}) custom-call(s32[2]{0:T(128)S(1)} %pad_add_fusion.here_ref, f32[64,16]{1,0:T(8,128)S(1)} %get-tuple-element.37.table_ref, f32[16,64]{1,0:T(8,128)S(1)} %get-tuple-element.38.turned_ref, ...), custom_call_target="tpu_custom_call" | custom-call | flops 300000000 | bytes 3000000 | tf_op jit(solution)/shard_map/pallas_call | solution.py:649
  31.7 0.1 collective-permute-start.6
  31.7 2.4 %collective-permute-start.7 = (bf16[6,12,256]{2,1,0:T(8,128)(2,1)S(1)}, bf16[6,12,256]{2,1,0:T(8,128)(2,1)S(1)}, u32[]{:S(2)}, u32[]{:S(2)}) collective-permute-start(bf16[6,12,256]{2,1,0:T(8,128)(2,1)S(1)} %get-tuple-element.54), channel_id=1, source_target_pairs={{0,2},{1,3},{2,0},{3,1},{4,6},{5,7},{6,4},{7,5},{8,10},{9,11},{10,... | collective-permute-start | bytes 110600 | tf_op jit(solution)/shard_map/ppermute | solution.py:24
  34.2 0.8 %collective-permute-start.8 = (bf16[6,12,256]{2,1,0:T(8,128)(2,1)S(1)}, bf16[6,12,256]{2,1,0:T(8,128)(2,1)S(1)}, u32[]{:S(2)}, u32[]{:S(2)}) collective-permute-start(bf16[6,12,256]{2,1,0:T(8,128)(2,1)S(1)} %get-tuple-element.55), channel_id=1, source_target_pairs={{0,3},{1,0},{2,1},{3,2},{4,7},{5,4},{6,5},{7,6},{8,11},{9,8},{10,9... | collective-permute-start | bytes 110600 | tf_op jit(solution)/shard_map/ppermute | solution.py:24
  35.0 1.6 %collective-permute-done.6.refs_1_ = bf16[6,12,256]{2,1,0:T(8,128)(2,1)S(1)} collective-permute-done((bf16[6,12,256]{2,1,0:T(8,128)(2,1)S(1)}, bf16[6,12,256]{2,1,0:T(8,128)(2,1)S(1)}, u32[]{:S(2)}, u32[]{:S(2)}) %collective-permute-start.6) | collective-permute-done | bytes 36896 | tf_op jit(solution)/shard_map/ppermute | solution.py:24
  36.6 0.0 collective-permute-done.7.refs_2_
  36.6 1.2 %collective-permute-done.8.refs_3_ = bf16[6,12,256]{2,1,0:T(8,128)(2,1)S(1)} collective-permute-done((bf16[6,12,256]{2,1,0:T(8,128)(2,1)S(1)}, bf16[6,12,256]{2,1,0:T(8,128)(2,1)S(1)}, u32[]{:S(2)}, u32[]{:S(2)}) %collective-permute-start.8) | collective-permute-done | bytes 36896 | tf_op jit(solution)/shard_map/ppermute | solution.py:24
  37.8 0.0 collective-permute-done.9.refs_7_
  37.8 0.0 collective-permute-done.10.refs_8_
  37.8 13.5 %shard_map.150 = bf16[16,64,256]{2,1,0:T(8,128)(2,1)} custom-call(s32[2]{0:T(128)S(1)} %pad_add_fusion.here_ref, bf16[6,12,256]{2,1,0:T(8,128)(2,1)S(1)} %get-tuple-element.52.refs_0_, bf16[6,12,256]{2,1,0:T(8,128)(2,1)S(1)} %collective-permute-done.6.refs_1_, bf16[6,12,256]{2,1,0:T(8,128)(2,1)S(1)} %collective-permute-done.7.refs_2_, ...), custom_call_target="tpu_custom_call" | custom-call | flops 10000000000 | bytes 12000000 | tf_op jit(solution)/shard_map/pallas_call | solution.py:522
Async XLA Ops:
  0.0 5.6 %collective-permute-start = (bf16[2,32,384]{2,1,0:T(8,128)(2,1)}, bf16[2,32,384]{2,1,0:T(8,128)(2,1)S(1)}, u32[]{:S(2)}, u32[]{:S(2)}) collective-permute-start(bf16[2,32,384]{2,1,0:T(8,128)(2,1)} %refs_7_.1), channel_id=1, source_target_pairs={{0,4},{4,8},{8,12},{12,0},{1,5},{5,9},{9,13},{13,1},{2,6},{6,10},{... | collective-permute-start | bytes 147464 | tf_op jit(solution)/shard_map/ppermute | solution.py:24
  2.6 3.7 %collective-permute-start.2 = (bf16[2,32,384]{2,1,0:T(8,128)(2,1)}, bf16[2,32,384]{2,1,0:T(8,128)(2,1)S(1)}, u32[]{:S(2)}, u32[]{:S(2)}) collective-permute-start(bf16[2,32,384]{2,1,0:T(8,128)(2,1)} %refs_7_.1), channel_id=1, source_target_pairs={{0,12},{4,0},{8,4},{12,8},{1,13},{5,1},{9,5},{13,9},{2,14},{6,2},{... | collective-permute-start | bytes 147464 | tf_op jit(solution)/shard_map/ppermute | solution.py:24
  2.6 3.7 %collective-permute-start.1 = (bf16[2,32,384]{2,1,0:T(8,128)(2,1)}, bf16[2,32,384]{2,1,0:T(8,128)(2,1)S(1)}, u32[]{:S(2)}, u32[]{:S(2)}) collective-permute-start(bf16[2,32,384]{2,1,0:T(8,128)(2,1)} %refs_7_.1), channel_id=1, source_target_pairs={{0,8},{4,12},{8,0},{12,4},{1,9},{5,13},{9,1},{13,5},{2,10},{6,14},... | collective-permute-start | bytes 147464 | tf_op jit(solution)/shard_map/ppermute | solution.py:24
  7.4 9.8 %collective-permute-start.3 = (bf16[192,256]{1,0:T(8,128)(2,1)S(1)}, bf16[192,256]{1,0:T(8,128)(2,1)S(1)}, u32[]{:S(2)}, u32[]{:S(2)}) collective-permute-start(bf16[192,256]{1,0:T(8,128)(2,1)S(1)} %get-tuple-element.49), channel_id=1, source_target_pairs={{0,1},{1,2},{2,3},{3,0},{4,5},{5,6},{6,7},{7,4},{8,9},{9,10},{10,1... | collective-permute-start | bytes 294920 | tf_op jit(solution)/shard_map/ppermute | solution.py:24
  8.7 8.5 %collective-permute-start.5 = (bf16[192,256]{1,0:T(8,128)(2,1)S(1)}, bf16[192,256]{1,0:T(8,128)(2,1)S(1)}, u32[]{:S(2)}, u32[]{:S(2)}) collective-permute-start(bf16[192,256]{1,0:T(8,128)(2,1)S(1)} %get-tuple-element.51), channel_id=1, source_target_pairs={{0,3},{1,0},{2,1},{3,2},{4,7},{5,4},{6,5},{7,6},{8,11},{9,8},{10,9... | collective-permute-start | bytes 294920 | tf_op jit(solution)/shard_map/ppermute | solution.py:24
  10.8 6.4 %collective-permute-start.4 = (bf16[144,256]{1,0:T(8,128)(2,1)S(1)}, bf16[144,256]{1,0:T(8,128)(2,1)S(1)}, u32[]{:S(2)}, u32[]{:S(2)}) collective-permute-start(bf16[144,256]{1,0:T(8,128)(2,1)S(1)} %get-tuple-element.50), channel_id=1, source_target_pairs={{0,2},{1,3},{2,0},{3,1},{4,6},{5,7},{6,4},{7,5},{8,10},{9,11},{10,... | collective-permute-start | bytes 221192 | tf_op jit(solution)/shard_map/ppermute | solution.py:24
  17.9 19.9 %collective-permute-start.9 = (bf16[248,256]{1,0:T(8,128)(2,1)S(1)}, bf16[248,256]{1,0:T(8,128)(2,1)S(1)}, u32[]{:S(2)}, u32[]{:S(2)}) collective-permute-start(bf16[248,256]{1,0:T(8,128)(2,1)S(1)} %get-tuple-element.59), channel_id=1, source_target_pairs={{0,4},{4,8},{8,12},{1,5},{5,9},{9,13},{2,6},{6,10},{10,14},{3,7},{... | collective-permute-start | bytes 380936 | tf_op jit(solution)/shard_map/ppermute | solution.py:31
  23.1 14.7 %collective-permute-start.10 = (bf16[248,256]{1,0:T(8,128)(2,1)S(1)}, bf16[248,256]{1,0:T(8,128)(2,1)S(1)}, u32[]{:S(2)}, u32[]{:S(2)}) collective-permute-start(bf16[248,256]{1,0:T(8,128)(2,1)S(1)} %get-tuple-element.60), channel_id=1, source_target_pairs={{4,0},{8,4},{12,8},{5,1},{9,5},{13,9},{6,2},{10,6},{14,10},{7,3},{... | collective-permute-start | bytes 380936 | tf_op jit(solution)/shard_map/ppermute | solution.py:31
  31.7 4.9 %collective-permute-start.6 = (bf16[6,12,256]{2,1,0:T(8,128)(2,1)S(1)}, bf16[6,12,256]{2,1,0:T(8,128)(2,1)S(1)}, u32[]{:S(2)}, u32[]{:S(2)}) collective-permute-start(bf16[6,12,256]{2,1,0:T(8,128)(2,1)S(1)} %get-tuple-element.53), channel_id=1, source_target_pairs={{0,1},{1,2},{2,3},{3,0},{4,5},{5,6},{6,7},{7,4},{8,9},{9,10},{10,1... | collective-permute-start | bytes 110600 | tf_op jit(solution)/shard_map/ppermute | solution.py:24
  31.7 4.9 %collective-permute-start.7 = (bf16[6,12,256]{2,1,0:T(8,128)(2,1)S(1)}, bf16[6,12,256]{2,1,0:T(8,128)(2,1)S(1)}, u32[]{:S(2)}, u32[]{:S(2)}) collective-permute-start(bf16[6,12,256]{2,1,0:T(8,128)(2,1)S(1)} %get-tuple-element.54), channel_id=1, source_target_pairs={{0,2},{1,3},{2,0},{3,1},{4,6},{5,7},{6,4},{7,5},{8,10},{9,11},{10,... | collective-permute-start | bytes 110600 | tf_op jit(solution)/shard_map/ppermute | solution.py:24
  34.2 3.6 %collective-permute-start.8 = (bf16[6,12,256]{2,1,0:T(8,128)(2,1)S(1)}, bf16[6,12,256]{2,1,0:T(8,128)(2,1)S(1)}, u32[]{:S(2)}, u32[]{:S(2)}) collective-permute-start(bf16[6,12,256]{2,1,0:T(8,128)(2,1)S(1)} %get-tuple-element.55), channel_id=1, source_target_pairs={{0,3},{1,0},{2,1},{3,2},{4,7},{5,4},{6,5},{7,6},{8,11},{9,8},{10,9... | collective-permute-start | bytes 110600 | tf_op jit(solution)/shard_map/ppermute | solution.py:24

commit v6 on v5

--- a/solution.py
+++ b/solution.py
@@ -11,6 +11,7 @@
 highest = lax.Precision.HIGHEST
 bin_sides = (1, 2, 3, 6)
 rim = 2
+cuts2 = 2
 f32 = jnp.float32
 bf16 = jnp.bfloat16
 vmem_spec = pl.BlockSpec(memory_space=pltpu.VMEM)
@@ -24,11 +25,17 @@
     return lax.ppermute(value, axis, [(i, (i + shift) % count) for i in range(count)])
 
 
-def edge_swap(low_out, high_out, axis):
+def pair_swap(first, second, axis):
     count = lax.axis_size(axis)
-    forward = [(i, i + 1) for i in range(count - 1)]
-    backward = [(target, source) for source, target in forward]
-    return lax.ppermute(high_out, axis, forward), lax.ppermute(low_out, axis, backward)
+
+    def pairs(start):
+        return [
+            edge
+            for i in range(start, count - 1, 2)
+            for edge in ((i, i + 1), (i + 1, i))
+        ]
+
+    return lax.ppermute(first, axis, pairs(0)), lax.ppermute(second, axis, pairs(1))
 
 
 def cell_table(extent_rows, extent_cols):
@@ -88,8 +95,8 @@
 
     def weights(axis, length, targets, tap_here):
         whole = float(in_size[axis] * counts[axis])
-        first_out = (here[axis] * out_size[axis] - out_border).astype(f32) - (taps // 2)
-        first_in = (here[axis] * in_size[axis] - in_border).astype(f32)
+        first_out = (here[axis] * out_size[axis] - out_border[axis]).astype(f32) - (taps // 2)
+        first_in = (here[axis] * in_size[axis] - in_border[axis]).astype(f32)
         output = first_out + tap_here + lax.broadcasted_iota(jnp.int32, (length, 1), 0).astype(f32)
         source = (output + 0.5) * (1.0 / factor) - 0.5
         source = jnp.minimum(jnp.maximum(source, 0.0), whole - 1.0)
@@ -117,22 +124,33 @@
 def stretches(sizes):
     one, two, three, four, counts = sizes
 
-    def matrix(out, out_border, source, in_border, compact=False):
+    def pyramid(out, source):
+        shape = window_shape(source, rim)
+        borders = (rim, rim)
         factor = out[0] // source[0]
-        if compact:
-            shape = compact_shape(source, in_border)
-            return (out, out_border, shape, in_border, factor, out, source, counts, pitch_of(shape[0] * shape[1]), 3)
-        shape = window_shape(source, in_border)
-        return (window_shape(out, out_border), out_border, shape, in_border, factor, out, source, counts, shape[0] * shape[1], 1)
-
+        return (
+            window_shape(out, rim), borders, shape, borders, factor, out, source, counts, shape[0] * shape[1]
+        )
+
+    def join(source, cuts, part):
+        tile = (one[0] // cuts, one[1] // cuts)
+        small = (source[0] // cuts, source[1] // cuts)
+        shape = compact_shape(small, 1)
+        out_border = (-part[0] * tile[0], -part[1] * tile[1])
+        in_border = (1 - part[0] * small[0], 1 - part[1] * small[1])
+        factor = one[0] // source[0]
+        lanes = pitch_of(shape[0] * shape[1])
+        return tile, out_border, shape, in_border, factor, one, source, counts, lanes, 3
+
+    parts = [(i, j) for i in range(cuts2) for j in range(cuts2)]
     return (
-        matrix(three, rim, four, rim),
-        matrix(two, rim, three, rim),
-        matrix(one, rim, two, rim),
-        matrix(one, 1, two, 1),
-        matrix(one, 0, three, 1, True),
-        matrix(one, 0, four, 1, True),
-    )
+        (pyramid(three, four), pyramid(two, three), pyramid(one, two), join(three, 1, (0, 0))),
+        (join(four, 1, (0, 0)), *(join(two, cuts2, part) for part in parts)),
+    )
+
+
+def matrix_shape(plan):
+    return plan[0][0] * plan[0][1], plan[8] * (plan[9] if len(plan) > 9 else 1) ** 2
 
 
 def lateral_kernel(col_count, kept_count, here_ref, *refs):
@@ -320,7 +338,10 @@
 
 
 def rows_kernel(col_count, high3, wide3, here_ref, bias_ref, lat1_ref, lat2_ref, *refs):
-    messages, (lat3_ref, low_ref, high_ref, three_buf, pack_buf) = refs[:col_count], refs[col_count:]
+    messages, (lat3_ref, first_ref, second_ref, three_buf, low_buf, high_buf) = (
+        refs[:col_count],
+        refs[col_count:],
+    )
     span = wide3 + 2 * rim
     total = messages[0][0 : high3 * span, :].astype(f32)
     for message in messages[1:]:
@@ -336,7 +357,7 @@
     high2, wide2 = lat2_ref.shape[:2]
     before, after = messages[1], messages[col_count - 1]
     sides_at = before.shape[0] - rim * (high1 + high2)
-    for out, last in ((low_ref, False), (high_ref, True)):
+    for pack_buf, last in ((low_buf, False), (high_buf, True)):
         start, at = 0, sides_at
         for lat, high, wide in ((lat1_ref, high1, wide1), (lat2_ref, high2, wide2)):
             whole = wide + 2 * rim
@@ -355,23 +376,59 @@
             row = high3 - rim + step if last else step
             pack_buf[start : start + span, :] = three_buf[row, :span, :]
             start += span
-        out[...] = pack_buf[...].astype(bf16)
-
-
-def tail_kernel(
-    sizes,
-    top_count,
-    here_ref,
-    *refs,
-):
-    (high1, wide1), (high2, wide2), (high3, wide3), (high4, wide4), (row_count, col_count) = sizes
-    top_refs, refs = refs[:top_count], refs[top_count:]
+    even = lax.rem(here_ref[0], 2) == 0
+    low, high = low_buf[...], high_buf[...]
+    first_ref[...] = jnp.where(even, high, low).astype(bf16)
+    second_ref[...] = jnp.where(even, low, high).astype(bf16)
+
+
+def tap_terms(small, weight_ref, first, store):
+    channels = weight_ref.shape[3]
+    for tap in range(9):
+        weight = weight_ref[tap // 3, tap % 3, first : first + channels, :]
+        store(tap, dot(small, weight).astype(bf16))
+
+
+def late_kernel(sizes, plans, top_count, here_ref, bias_ref, join_ref, *refs):
+    tops, refs = refs[:top_count], refs[top_count:]
+    top_ref, base_ref, matrices, refs = refs[0], refs[1], refs[2 : 1 + len(plans)], refs[1 + len(plans) :]
+    top_buf, small_buf, terms_buf = refs
+    high4, wide4 = sizes[3]
+    here = (here_ref[0], here_ref[1])
+    total = tops[0][...].astype(f32)
+    for ref in tops[1:]:
+        total = total + ref[...].astype(f32)
+    top_buf[...] = jnp.zeros_like(top_buf)
+    top_buf[:, : wide4 + 2 * rim, :] = jnp.maximum(total + bias_ref[4:5, :][None], 0.0)
+    top_ref[...] = top_buf[...].astype(bf16).reshape(top_ref.shape)
+    tall, broad = compact_shape((high4, wide4), 1)
+    small_buf[...] = jnp.zeros_like(small_buf)
+    for row in range(tall):
+        small_buf[row * broad : (row + 1) * broad, :] = top_buf[
+            row + rim - 1, rim - 1 : rim - 1 + broad, :
+        ]
+    lanes, channels = small_buf.shape
+
+    def store(tap, value):
+        terms_buf[tap * lanes : (tap + 1) * lanes, :] = value
+
+    tap_terms(small_buf[...].astype(bf16), join_ref, 3 * channels, store)
+    base_ref[...] = dot(stretch_matrix(here, *plans[0]), terms_buf[...])
+    for plan, matrix in zip(plans[1:], matrices):
+        matrix[...] = stretch_matrix(here, *plan)
+
+
+def tail_kernel(sizes, part_count, here_ref, *refs):
+    (high1, wide1), (high2, wide2), (high3, wide3), _, (row_count, col_count) = sizes
+    quarters, refs = refs[:part_count], refs[part_count:]
     (
+        top_ref,
+        base_ref,
         lat1_ref,
         lat2_ref,
         lat3_ref,
-        above_ref,
-        below_ref,
+        first_ref,
+        second_ref,
         before_ref,
         after_ref,
         bias_ref,
@@ -380,11 +437,8 @@
         up3_ref,
         up2_ref,
         up1_ref,
-        raise2_ref,
         spread3_ref,
-        spread4_ref,
         out_ref,
-        top_buf,
         lat1_buf,
         lat2_buf,
         lat3_buf,
@@ -395,12 +449,18 @@
         sums_buf,
         stack_buf,
         small3_buf,
-        small4_buf,
+        small2_buf,
         terms3_buf,
-        terms4_buf,
+        terms2_buf,
+        above_buf,
+        below_buf,
     ) = refs
     channels = bias_ref.shape[1]
 
+    even = lax.rem(here_ref[0], 2) == 0
+    first, second = first_ref[...].astype(f32), second_ref[...].astype(f32)
+    above_buf[...] = jnp.where(even, second, first)
+    below_buf[...] = jnp.where(even, first, second)
     side_start = before_ref.shape[0] - rim * (high1 + high2)
     row_start = 0
     for ref, buf, high, wide in (
@@ -424,20 +484,11 @@
                 for row in range(high):
                     buf[rim + row, col : col + rim, :] = sides[rim * row : rim * row + rim]
             side_start += rim * high
-        for source, row in ((above_ref, 0), (below_ref, rim + high)):
-            both = source[row_start : row_start + rim * whole, :].astype(f32)
+        for source, row in ((above_buf, 0), (below_buf, rim + high)):
+            both = source[row_start : row_start + rim * whole, :]
             for step in range(rim):
                 buf[row + step, :whole, :] = both[step * whole : (step + 1) * whole]
         row_start += rim * whole
-
-    tall4, whole4 = high4 + 2 * rim, wide4 + 2 * rim
-    top_sum = top_refs[0][...].astype(f32)
-    for ref in top_refs[1:]:
-        top_sum = top_sum + ref[...].astype(f32)
-    top_buf[...] = jnp.zeros_like(top_buf)
-    top_buf[:, :whole4, :] = jnp.maximum(top_sum + bias_ref[4:5, :][None], 0.0)
-    pitch4 = top_buf.shape[1]
-    top = top_buf[...].astype(bf16).reshape(tall4 * pitch4, channels)
 
     shape1, shape2, shape3 = lat1_buf.shape[:2], lat2_buf.shape[:2], lat3_buf.shape[:2]
     for lat_buf, matrix, source, out in (
@@ -445,7 +496,7 @@
         (lat2_buf, up2_ref, pyr3_buf, pyr2_buf),
         (lat1_buf, up1_ref, pyr2_buf, pyr1_buf),
     ):
-        source = top if source is None else source[...]
+        source = top_ref[...] if source is None else source[...]
         total = lat_buf[...].reshape(-1, channels) + dot(matrix[...], source)
         out[...] = total.astype(bf16)
 
@@ -472,31 +523,36 @@
         total = taps_total(rows, wide + 2)
         return jnp.maximum(total + bias_ref[8 + number : 9 + number, :][None], 0.0)
 
-    def tap_terms(source, first, buf):
-        lanes = source.shape[0]
-        small = source[...].astype(bf16)
-        for tap in range(9):
-            weight = join_w[tap // 3, tap % 3, first : first + channels, :]
-            buf[tap * lanes : (tap + 1) * lanes, :] = dot(small, weight).astype(bf16)
-
-    tall, broad = compact_shape((high4, wide4), 1)
-    small4_buf[...] = jnp.zeros_like(small4_buf)
-    for row in range(tall):
-        small4_buf[row * broad : (row + 1) * broad, :] = top_buf[row + rim - 1, rim - 1 : rim - 1 + broad, :]
-    tap_terms(small4_buf, 3 * channels, terms4_buf)
     value = smooth(2, pyr3_buf, shape3, wide3)
     tall, broad = compact_shape((high3, wide3), 1)
     small3_buf[...] = jnp.zeros_like(small3_buf)
     for row in range(tall):
         small3_buf[row * broad : (row + 1) * broad, :] = value[row]
-    tap_terms(small3_buf, 2 * channels, terms3_buf)
-
-    rows2, pitch2 = window_shape((high2, wide2), 1)
-    value = smooth(1, pyr2_buf, shape2, wide2)
-    sums_buf[:rows2, :pitch2, :] = jnp.zeros((rows2, pitch2, channels), f32)
-    sums_buf[:rows2, : wide2 + 2, :] = value
-    smooth2 = sums_buf[:rows2, :pitch2, :].astype(bf16).reshape(rows2 * pitch2, channels)
-    stack_buf[:, channels : 2 * channels] = dot(raise2_ref[...], smooth2).astype(bf16)
+    lanes3 = small3_buf.shape[0]
+
+    def store3(tap, value):
+        terms3_buf[tap * lanes3 : (tap + 1) * lanes3, :] = value
+
+    tap_terms(small3_buf[...].astype(bf16), join_w, 2 * channels, store3)
+
+    rows2, whole2 = compact_shape((high2, wide2), 1)
+    sums_buf[:rows2, :whole2, :] = smooth(1, pyr2_buf, shape2, wide2)
+    half = (high2 // cuts2, wide2 // cuts2)
+    tall, broad = compact_shape(half, 1)
+    lanes2 = small2_buf.shape[0] // part_count
+    small2_buf[...] = jnp.zeros_like(small2_buf)
+    for part in range(part_count):
+        row0, col0 = part // cuts2 * half[0], part % cuts2 * half[1]
+        for row in range(tall):
+            start = part * lanes2 + row * broad
+            small2_buf[start : start + broad, :] = sums_buf[row0 + row, col0 : col0 + broad, :]
+
+    def store2(tap, value):
+        for part in range(part_count):
+            start = (part * 9 + tap) * lanes2
+            terms2_buf[start : start + lanes2, :] = value[part * lanes2 : (part + 1) * lanes2]
+
+    tap_terms(small2_buf[...].astype(bf16), join_w, channels, store2)
 
     rows1, pitch1 = window_shape((high1, wide1), 1)
     value = smooth(0, pyr1_buf, shape1, wide1)
@@ -504,28 +560,34 @@
     across = here_ref[1] * wide1 - 1 + lax.broadcasted_iota(jnp.int32, (1, wide1 + 2, 1), 1)
     inside = (down >= 0) & (down < high1 * row_count) & (across >= 0) & (across < wide1 * col_count)
     sums_buf[:rows1, : wide1 + 2, :] = jnp.where(inside, value, 0.0)
-    stack_buf[:, 0:channels] = sums_buf[...].astype(bf16).reshape(rows1 * pitch1, channels)
-    conv(stack_buf, (rows1, pitch1), lambda j: join_w[:, j, 0 : 2 * channels], high1)
+    stack_buf[...] = sums_buf[...].astype(bf16).reshape(rows1 * pitch1, channels)
+    conv(stack_buf, (rows1, pitch1), lambda j: join_w[:, j, 0:channels], high1)
     total = taps_total(high1, wide1)
-    spread = dot(spread3_ref[...], terms3_buf[...]) + dot(spread4_ref[...], terms4_buf[...])
-    total = total + spread.reshape(high1, wide1, channels)
-    out_ref[...] = jnp.maximum(total + bias_ref[11:12, :][None], 0.0).astype(bf16)
-
-
-def tail(here, tops, lats, above, below, before, after, biases, weights, matrices, sizes):
+    spread = base_ref[...] + dot(spread3_ref[...], terms3_buf[...])
+    sums_buf[:high1, :wide1, :] = total + spread.reshape(high1, wide1, channels)
+    tall, broad = high1 // cuts2, wide1 // cuts2
+    for part, matrix in enumerate(quarters):
+        terms = terms2_buf[part * 9 * lanes2 : (part + 1) * 9 * lanes2, :]
+        value = dot(matrix[...], terms).reshape(tall, broad, channels)
+        row0, col0 = part // cuts2 * tall, part % cuts2 * broad
+        value = value + sums_buf[row0 : row0 + tall, col0 : col0 + broad, :]
+        value = jnp.maximum(value + bias_ref[11:12, :][None], 0.0)
+        out_ref[row0 : row0 + tall, col0 : col0 + broad, :] = value.astype(bf16)
+
+
+def tail(here, top, base, lats, swapped, before, after, biases, weights, matrices, quarters, sizes):
     one, _, _, _, _ = sizes
     channels = biases.shape[1]
-    shapes = [window_shape(size, rim) for size in sizes[:4]]
-    (rows1, pitch1), (rows2, pitch2), (rows3, pitch3), (rows4, pitch4) = shapes
-    small3, small4 = (matrix.shape[1] // 9 for matrix in matrices[-2:])
-    inputs = (*tops, *lats, above, below, before, after, biases, *weights, *matrices)
+    shapes = [window_shape(size, rim) for size in sizes[:3]]
+    (rows1, pitch1), (rows2, pitch2), (rows3, pitch3) = shapes
+    small3, small2 = matrices[-1].shape[1] // 9, quarters[0].shape[1] // 9 * len(quarters)
+    inputs = (*quarters, top, base, *lats, *swapped, before, after, biases, *weights, *matrices)
     return pl.pallas_call(
-        functools.partial(tail_kernel, sizes, len(tops)),
+        functools.partial(tail_kernel, sizes, len(quarters)),
         out_shape=jax.ShapeDtypeStruct((*one, channels), bf16),
         in_specs=[smem_spec] + [vmem_spec] * len(inputs),
         out_specs=vmem_spec,
         scratch_shapes=[
-            pltpu.VMEM((rows4, pitch4, channels), f32),
             pltpu.VMEM((rows1, pitch1, channels), f32),
             pltpu.VMEM((rows2, pitch2, channels), f32),
             pltpu.VMEM((rows3, pitch3, channels), f32),
@@ -534,15 +596,17 @@
             pltpu.VMEM((rows3 * pitch3, channels), bf16),
             pltpu.VMEM((3, rows1 - 2, pitch1, channels), f32),
             pltpu.VMEM((rows1 - 2, pitch1, channels), f32),
-            pltpu.VMEM(((rows1 - 2) * pitch1, 2 * channels), bf16),
+            pltpu.VMEM(((rows1 - 2) * pitch1, channels), bf16),
             pltpu.VMEM((small3, channels), f32),
-            pltpu.VMEM((small4, channels), f32),
+            pltpu.VMEM((small2, channels), f32),
             pltpu.VMEM((9 * small3, channels), bf16),
-            pltpu.VMEM((9 * small4, channels), bf16),
+            pltpu.VMEM((9 * small2, channels), bf16),
+            pltpu.VMEM(swapped[0].shape, f32),
+            pltpu.VMEM(swapped[0].shape, f32),
         ],
-        compiler_params=pltpu.CompilerParams(vmem_limit_bytes=32 * 1024 * 1024),
+        compiler_params=pltpu.CompilerParams(vmem_limit_bytes=30 * 1024 * 1024),
         cost_estimate=pl.CostEstimate(
-            flops=10_000_000_000, bytes_accessed=12_000_000, transcendentals=0
+            flops=8_000_000_000, bytes_accessed=12_000_000, transcendentals=0
         ),
     )(here, *inputs)
 
@@ -629,13 +693,13 @@
         (high4, wide4),
         (row_count, col_count),
     )
-    plans = stretches(sizes)
+    plans, late_plans = stretches(sizes)
     late = (neck_pooled, smooth_weight, join_weight)
     taps, neck_pooled, smooth_weight, join_weight, *matrices = call(
         functools.partial(feature_kernel, row_count, plans),
         [shape((3, rows * grid_cols, channels), f32)]
         + [shape(value.shape) for value in late]
-        + [shape((plan[0][0] * plan[0][1], plan[8] * plan[9] ** 2)) for plan in plans],
+        + [shape(matrix_shape(plan)) for plan in plans],
         [smem_spec, hbm_spec] + [vmem_spec] * row_count + [hbm_spec] * len(late),
         [
             pltpu.VMEM(neck_feature.shape, bf16),
@@ -662,29 +726,48 @@
     tops = [windows[0]] + [shifted(windows[shift], "col", shift) for shift in range(1, col_count)]
     span3 = wide3 + 2 * rim
     packed = rim * (wide1 + wide2 + wide3 + 6 * rim)
-    lat3, low_rows, high_rows = call(
+    lat3, first_rows, second_rows = call(
         functools.partial(rows_kernel, col_count, high3, wide3),
         [shape((high3, span3, channels))] + [shape((packed, channels))] * 2,
         [smem_spec] + [vmem_spec] * (3 + col_count),
         [
             pltpu.VMEM((high3, (span3 + 7) // 8 * 8, channels), f32),
             pltpu.VMEM((packed, channels), f32),
+            pltpu.VMEM((packed, channels), f32),
         ],
         1_000_000,
         1_000_000,
     )(here, bias_table, lat1, lat2, *received)
-    above, below = edge_swap(low_rows, high_rows, "row")
+    swapped = pair_swap(first_rows, second_rows, "row")
+    small = late_plans[0][8]
+    top, base, *quarters = call(
+        functools.partial(late_kernel, sizes, late_plans, col_count),
+        [
+            shape((rows * pitch_of(span4), channels)),
+            shape((high1 * wide1, channels), f32),
+        ]
+        + [shape(matrix_shape(plan)) for plan in late_plans[1:]],
+        [smem_spec] + [vmem_spec] * (2 + col_count),
+        [
+            pltpu.VMEM((rows, pitch_of(span4), channels), f32),
+            pltpu.VMEM((small, channels), f32),
+            pltpu.VMEM((9 * small, channels), bf16),
+        ],
+        700_000_000,
+        5_000_000,
+    )(here, bias_table, join_weight, *tops)
     return tail(
         here,
-        tops,
+        top,
+        base,
         (lat1, lat2, lat3),
-        above,
-        below,
+        swapped,
         received[1],
         received[-1],
         bias_table,
         (smooth_weight, join_weight),
         matrices,
+        quarters,
         sizes,
     )
 

time: 51.8 us -> 45.5 us (0.88)
  waiting for transfers between devices: 9.42 us -> 4.58 us
  starting transfers between devices: 17 us -> 15.2 us
    ppermute x9, waiting for transfers between devices: 9.42 us -> 4.58 us  [shifted(): lax.ppermute(value, axis, [(i, (i + shift) % count) for i in range(count)])]
    ppermute x2, starting transfers between devices: 7.18 us -> 5.33 us  [the longest x1 2.68 us: pair_swap(): lax.ppermute(second, axis, pairs(1))]
    pallas_call x1 -> x2, Pallas kernels: 13.5 us -> 13.9 us  [the longest x1 11.9 us: tail(): pl.pallas_call(functools.partial(tail_kernel, sizes, len(quarters)), out_...]
  transfers between devices with their start and end apart: 11 -> 11, of which waited for: 4 -> 4; matrix products, arithmetic and copies ran while one was open for 0% -> 0% of each run, Pallas kernels for 18% -> 25%
where the time goes in v6:
time: 45.5 us; the launch traced here: 45 us
  Pallas kernels  25.1 us (55%)
  starting transfers between devices  15.2 us (33%)
  waiting for transfers between devices  4.58 us (10%)
    pallas_call x1, Pallas kernels, tail(): pl.pallas_call(functools.partial(tail_kernel, sizes, len(quarters)), out_...  11.9 us
    ppermute x9, starting transfers between devices, shifted(): lax.ppermute(value, axis, [(i, (i + shift) % count) for i in range(count)])  9.85 us
    pallas_call x1, Pallas kernels, local(): call(functools.partial(feature_kernel, row_count, plans), [shape((3, rows...  4.83 us
    ppermute x9, waiting for transfers between devices, shifted(): lax.ppermute(value, axis, [(i, (i + shift) % count) for i in range(count)])  4.58 us
    pallas_call x1, Pallas kernels, local(): call(functools.partial(lateral_kernel, col_count, len(kept)), [shape((hig...  2.85 us
    ppermute x1, starting transfers between devices, pair_swap(): lax.ppermute(second, axis, pairs(1))  2.68 us
    ppermute x1, starting transfers between devices, pair_swap(): lax.ppermute(first, axis, pairs(0))  2.65 us
    pallas_call x1, Pallas kernels, local(): call(functools.partial(late_kernel, sizes, late_plans, col_count), [shape...  1.91 us
  transfers between devices with their start and end apart: 11, of which 4 were waited for; matrix products, arithmetic and copies ran while one was open for 0% of the time, Pallas kernels for 25%

profile of v6, /device:TPU:1, one launch (start us, length us, event | category | flops | bytes accessed | tf_op | source)
XLA Modules:
  0.0 45.0 jit_solution(15977472219490397406)
XLA Ops:
  0.0 2.6 %collective-permute-start = (bf16[2,32,384]{2,1,0:T(8,128)(2,1)}, bf16[2,32,384]{2,1,0:T(8,128)(2,1)S(1)}, u32[]{:S(2)}, u32[]{:S(2)}) collective-permute-start(bf16[2,32,384]{2,1,0:T(8,128)(2,1)} %refs_7_.1), channel_id=1, source_target_pairs={{0,4},{4,8},{8,12},{12,0},{1,5},{5,9},{9,13},{13,1},{2,6},{6,10},{... | collective-permute-start | bytes 147464 | tf_op jit(solution)/shard_map/ppermute | solution.py:25
  2.6 0.0 collective-permute-start.2
  2.6 0.1 collective-permute-start.1
  2.7 0.1 pad_add_fusion.here_ref
  2.8 2.8 %shard_map.145 = (bf16[16,64,256]{2,1,0:T(8,128)(2,1)S(1)}, bf16[8,32,256]{2,1,0:T(8,128)(2,1)S(1)}, bf16[128,256]{1,0:T(8,128)(2,1)S(1)}, bf16[128,256]{1,0:T(8...) custom-call(s32[2]{0:T(128)S(1)} %pad_add_fusion.here_ref, ...), custom_call_target="tpu_custom_call" | custom-call | flops 300000000 | bytes 4000000 | tf_op jit(solution)/shard_map/pallas_call | solution.py:652
  5.6 0.0 collective-permute-done.refs_1_
  5.7 0.7 %collective-permute-done.2.refs_3_ = bf16[2,32,384]{2,1,0:T(8,128)(2,1)S(1)} collective-permute-done((bf16[2,32,384]{2,1,0:T(8,128)(2,1)}, bf16[2,32,384]{2,1,0:T(8,128)(2,1)S(1)}, u32[]{:S(2)}, u32[]{:S(2)}) %collective-permute-start.2) | collective-permute-done | bytes 49184 | tf_op jit(solution)/shard_map/ppermute | solution.py:25
  6.3 0.0 collective-permute-done.1.refs_2_
  6.3 1.1 %shard_map.147 = (bf16[144,256]{1,0:T(8,128)(2,1)S(1)}, bf16[192,256]{1,0:T(8,128)(2,1)S(1)}, bf16[144,256]{1,0:T(8,128)(2,1)S(1)}, bf16[192,256]{1,0:T(8,128)(2,1)S(1)}) custom-call(s32[2]{0:T(128)S(1)} %pad_add_fusion.here_ref, f32[64,16]{1,0:T(8,128)S(1)} %get-tuple-element.44.table_ref, bf16[4,384,256]{2,1,0:T(8,128)(2,1)S(1)} %get-tuple-element.48.weight_ref, ...), custom_call_target="tpu_custom_call" | custom-call | flops 100000000 | bytes 1000000 | tf_op jit(solution)/shard_map/pallas_call | solution.py:673
  7.4 1.3 %collective-permute-start.3 = (bf16[192,256]{1,0:T(8,128)(2,1)S(1)}, bf16[192,256]{1,0:T(8,128)(2,1)S(1)}, u32[]{:S(2)}, u32[]{:S(2)}) collective-permute-start(bf16[192,256]{1,0:T(8,128)(2,1)S(1)} %get-tuple-element.54), channel_id=1, source_target_pairs={{0,1},{1,2},{2,3},{3,0},{4,5},{5,6},{6,7},{7,4},{8,9},{9,10},{10,1... | collective-permute-start | bytes 294920 | tf_op jit(solution)/shard_map/ppermute | solution.py:25
  8.7 2.1 %collective-permute-start.5 = (bf16[192,256]{1,0:T(8,128)(2,1)S(1)}, bf16[192,256]{1,0:T(8,128)(2,1)S(1)}, u32[]{:S(2)}, u32[]{:S(2)}) collective-permute-start(bf16[192,256]{1,0:T(8,128)(2,1)S(1)} %get-tuple-element.56), channel_id=1, source_target_pairs={{0,3},{1,0},{2,1},{3,2},{4,7},{5,4},{6,5},{7,6},{8,11},{9,8},{10,9... | collective-permute-start | bytes 294920 | tf_op jit(solution)/shard_map/ppermute | solution.py:25
  10.8 0.4 collective-permute-start.4
  11.2 4.8 %shard_map.146 = (f32[3,192,256]{2,1,0:T(8,128)S(1)}, bf16[3,3,256,256]{3,2,1,0:T(8,128)(2,1)S(1)}, bf16[3,3,3,256,256]{4,3,2,1,0:T(8,128)(2,1)S(1)}, bf16[3,3,1...) custom-call(s32[2]{0:T(128)S(1)} %pad_add_fusion.here_ref, ...), custom_call_target="tpu_custom_call" | custom-call | flops 700000000 | bytes 12000000 | tf_op jit(solution)/shard_map/pallas_call | solution.py:698
  16.1 1.1 %collective-permute-done.4.refs_2_ = bf16[144,256]{1,0:T(8,128)(2,1)S(1)} collective-permute-done((bf16[144,256]{1,0:T(8,128)(2,1)S(1)}, bf16[144,256]{1,0:T(8,128)(2,1)S(1)}, u32[]{:S(2)}, u32[]{:S(2)}) %collective-permute-start.4) | collective-permute-done | bytes 73760 | tf_op jit(solution)/shard_map/ppermute | solution.py:25
  17.2 0.0 collective-permute-done.3.refs_1_.refs_11_
  17.2 0.0 collective-permute-done.5.refs_3_.refs_12_
  17.2 0.7 %shard_map.150 = (bf16[4,20,256]{2,1,0:T(8,128)(2,1)S(1)}, bf16[248,256]{1,0:T(8,128)(2,1)S(1)}, bf16[248,256]{1,0:T(8,128)(2,1)S(1)}) custom-call(s32[2]{0:T(128)S(1)} %pad_add_fusion.here_ref, f32[12,256]{1,0:T(8,128)S(1)} %get-tuple-element.41.bias_ref.refs_13_, bf16[16,64,256]{2,1,0:T(8,128)(2,1)S(1)} %get-tuple-element.67.lat1_ref.refs_6_, ...), custom_call_target="tpu_custom_call" | custom-call | flops 1000000 | bytes 1000000 | tf_op jit(solution)/shard_map/pallas_call | solution.py:729
  17.9 2.7 %collective-permute-start.9 = (bf16[248,256]{1,0:T(8,128)(2,1)S(1)}, bf16[248,256]{1,0:T(8,128)(2,1)S(1)}, u32[]{:S(2)}, u32[]{:S(2)}) collective-permute-start(bf16[248,256]{1,0:T(8,128)(2,1)S(1)} %get-tuple-element.70), channel_id=1, source_target_pairs={{0,4},{4,0},{8,12},{12,8},{1,5},{5,1},{9,13},{13,9},{2,6},{6,2},{1... | collective-permute-start | bytes 380936 | tf_op jit(solution)/shard_map/ppermute | solution.py:38
  20.6 2.7 %collective-permute-start.10 = (bf16[248,256]{1,0:T(8,128)(2,1)S(1)}, bf16[248,256]{1,0:T(8,128)(2,1)S(1)}, u32[]{:S(2)}, u32[]{:S(2)}) collective-permute-start(bf16[248,256]{1,0:T(8,128)(2,1)S(1)} %get-tuple-element.71), channel_id=1, source_target_pairs={{4,8},{8,4},{5,9},{9,5},{6,10},{10,6},{7,11},{11,7},{20,24},{24,20... | collective-permute-start | bytes 380936 | tf_op jit(solution)/shard_map/ppermute | solution.py:38
  23.2 1.8 %shard_map.148 = (bf16[6,12,256]{2,1,0:T(8,128)(2,1)S(1)}, bf16[6,12,256]{2,1,0:T(8,128)(2,1)S(1)}, bf16[6,12,256]{2,1,0:T(8,128)(2,1)S(1)}, bf16[6,12,256]{2,1,0:T(8,128)(2,1)S(1)}) custom-call(s32[2]{0:T(128)S(1)} %pad_add_fusion.here_ref, f32[64,16]{1,0:T(8,128)S(1)} %get-tuple-element.44.table_ref, f32[16,64]{1,0:T(8,128)S(1)} %get-tuple-element.45.turned_ref, ...), custom_call_target="tpu_custom_call" | custom-call | flops 300000000 | bytes 3000000 | tf_op jit(solution)/shard_map/pallas_call | solution.py:713
  25.0 0.1 collective-permute-start.6
  25.1 2.4 %collective-permute-start.7 = (bf16[6,12,256]{2,1,0:T(8,128)(2,1)S(1)}, bf16[6,12,256]{2,1,0:T(8,128)(2,1)S(1)}, u32[]{:S(2)}, u32[]{:S(2)}) collective-permute-start(bf16[6,12,256]{2,1,0:T(8,128)(2,1)S(1)} %get-tuple-element.59), channel_id=1, source_target_pairs={{0,2},{1,3},{2,0},{3,1},{4,6},{5,7},{6,4},{7,5},{8,10},{9,11},{10,... | collective-permute-start | bytes 110600 | tf_op jit(solution)/shard_map/ppermute | solution.py:25
  27.5 0.8 %collective-permute-start.8 = (bf16[6,12,256]{2,1,0:T(8,128)(2,1)S(1)}, bf16[6,12,256]{2,1,0:T(8,128)(2,1)S(1)}, u32[]{:S(2)}, u32[]{:S(2)}) collective-permute-start(bf16[6,12,256]{2,1,0:T(8,128)(2,1)S(1)} %get-tuple-element.60), channel_id=1, source_target_pairs={{0,3},{1,0},{2,1},{3,2},{4,7},{5,4},{6,5},{7,6},{8,11},{9,8},{10,9... | collective-permute-start | bytes 110600 | tf_op jit(solution)/shard_map/ppermute | solution.py:25
  28.3 1.6 %collective-permute-done.6.refs_1_ = bf16[6,12,256]{2,1,0:T(8,128)(2,1)S(1)} collective-permute-done((bf16[6,12,256]{2,1,0:T(8,128)(2,1)S(1)}, bf16[6,12,256]{2,1,0:T(8,128)(2,1)S(1)}, u32[]{:S(2)}, u32[]{:S(2)}) %collective-permute-start.6) | collective-permute-done | bytes 36896 | tf_op jit(solution)/shard_map/ppermute | solution.py:25
  30.0 0.0 collective-permute-done.7.refs_2_
  30.0 1.1 %collective-permute-done.8.refs_3_ = bf16[6,12,256]{2,1,0:T(8,128)(2,1)S(1)} collective-permute-done((bf16[6,12,256]{2,1,0:T(8,128)(2,1)S(1)}, bf16[6,12,256]{2,1,0:T(8,128)(2,1)S(1)}, u32[]{:S(2)}, u32[]{:S(2)}) %collective-permute-start.8) | collective-permute-done | bytes 36896 | tf_op jit(solution)/shard_map/ppermute | solution.py:25
  31.1 1.9 %shard_map.149 = (bf16[96,256]{1,0:T(8,128)(2,1)S(1)}, f32[1024,256]{1,0:T(8,128)S(1)}, bf16[256,1008]{1,0:T(8,128)(2,1)S(1)}, bf16[256,1008]{1,0:T(8,128)(2,1)S...) custom-call(s32[2]{0:T(128)S(1)} %pad_add_fusion.here_ref, ...), custom_call_target="tpu_custom_call" | custom-call | flops 700000000 | bytes 5000000 | tf_op jit(solution)/shard_map/pallas_call | solution.py:743
  33.0 0.0 collective-permute-done.9.refs_9_
  33.0 0.0 collective-permute-done.10.refs_10_
  33.0 11.9 %shard_map.151 = bf16[16,64,256]{2,1,0:T(8,128)(2,1)} custom-call(s32[2]{0:T(128)S(1)} %pad_add_fusion.here_ref, bf16[256,1008]{1,0:T(8,128)(2,1)S(1)} %get-tuple-element.61.refs_0_, bf16[256,1008]{1,0:T(8,128)(2,1)S(1)} %get-tuple-element.62.refs_1_, bf16[256,1008]{1,0:T(8,128)(2,1)S(1)} %get-tuple-element.63.refs_2_, ...), custom_call_target="tpu_custom_call" | custom-call | flops 8000000000 | bytes 12000000 | tf_op jit(solution)/shard_map/pallas_call | solution.py:585
Async XLA Ops:
  0.0 5.6 %collective-permute-start = (bf16[2,32,384]{2,1,0:T(8,128)(2,1)}, bf16[2,32,384]{2,1,0:T(8,128)(2,1)S(1)}, u32[]{:S(2)}, u32[]{:S(2)}) collective-permute-start(bf16[2,32,384]{2,1,0:T(8,128)(2,1)} %refs_7_.1), channel_id=1, source_target_pairs={{0,4},{4,8},{8,12},{12,0},{1,5},{5,9},{9,13},{13,1},{2,6},{6,10},{... | collective-permute-start | bytes 147464 | tf_op jit(solution)/shard_map/ppermute | solution.py:25
  2.6 3.7 %collective-permute-start.2 = (bf16[2,32,384]{2,1,0:T(8,128)(2,1)}, bf16[2,32,384]{2,1,0:T(8,128)(2,1)S(1)}, u32[]{:S(2)}, u32[]{:S(2)}) collective-permute-start(bf16[2,32,384]{2,1,0:T(8,128)(2,1)} %refs_7_.1), channel_id=1, source_target_pairs={{0,12},{4,0},{8,4},{12,8},{1,13},{5,1},{9,5},{13,9},{2,14},{6,2},{... | collective-permute-start | bytes 147464 | tf_op jit(solution)/shard_map/ppermute | solution.py:25
  2.6 3.7 %collective-permute-start.1 = (bf16[2,32,384]{2,1,0:T(8,128)(2,1)}, bf16[2,32,384]{2,1,0:T(8,128)(2,1)S(1)}, u32[]{:S(2)}, u32[]{:S(2)}) collective-permute-start(bf16[2,32,384]{2,1,0:T(8,128)(2,1)} %refs_7_.1), channel_id=1, source_target_pairs={{0,8},{4,12},{8,0},{12,4},{1,9},{5,13},{9,1},{13,5},{2,10},{6,14},... | collective-permute-start | bytes 147464 | tf_op jit(solution)/shard_map/ppermute | solution.py:25
  7.4 9.8 %collective-permute-start.3 = (bf16[192,256]{1,0:T(8,128)(2,1)S(1)}, bf16[192,256]{1,0:T(8,128)(2,1)S(1)}, u32[]{:S(2)}, u32[]{:S(2)}) collective-permute-start(bf16[192,256]{1,0:T(8,128)(2,1)S(1)} %get-tuple-element.54), channel_id=1, source_target_pairs={{0,1},{1,2},{2,3},{3,0},{4,5},{5,6},{6,7},{7,4},{8,9},{9,10},{10,1... | collective-permute-start | bytes 294920 | tf_op jit(solution)/shard_map/ppermute | solution.py:25
  8.7 8.5 %collective-permute-start.5 = (bf16[192,256]{1,0:T(8,128)(2,1)S(1)}, bf16[192,256]{1,0:T(8,128)(2,1)S(1)}, u32[]{:S(2)}, u32[]{:S(2)}) collective-permute-start(bf16[192,256]{1,0:T(8,128)(2,1)S(1)} %get-tuple-element.56), channel_id=1, source_target_pairs={{0,3},{1,0},{2,1},{3,2},{4,7},{5,4},{6,5},{7,6},{8,11},{9,8},{10,9... | collective-permute-start | bytes 294920 | tf_op jit(solution)/shard_map/ppermute | solution.py:25
  10.8 6.4 %collective-permute-start.4 = (bf16[144,256]{1,0:T(8,128)(2,1)S(1)}, bf16[144,256]{1,0:T(8,128)(2,1)S(1)}, u32[]{:S(2)}, u32[]{:S(2)}) collective-permute-start(bf16[144,256]{1,0:T(8,128)(2,1)S(1)} %get-tuple-element.55), channel_id=1, source_target_pairs={{0,2},{1,3},{2,0},{3,1},{4,6},{5,7},{6,4},{7,5},{8,10},{9,11},{10,... | collective-permute-start | bytes 221192 | tf_op jit(solution)/shard_map/ppermute | solution.py:25
  17.9 15.1 %collective-permute-start.9 = (bf16[248,256]{1,0:T(8,128)(2,1)S(1)}, bf16[248,256]{1,0:T(8,128)(2,1)S(1)}, u32[]{:S(2)}, u32[]{:S(2)}) collective-permute-start(bf16[248,256]{1,0:T(8,128)(2,1)S(1)} %get-tuple-element.70), channel_id=1, source_target_pairs={{0,4},{4,0},{8,12},{12,8},{1,5},{5,1},{9,13},{13,9},{2,6},{6,2},{1... | collective-permute-start | bytes 380936 | tf_op jit(solution)/shard_map/ppermute | solution.py:38
  20.6 12.5 %collective-permute-start.10 = (bf16[248,256]{1,0:T(8,128)(2,1)S(1)}, bf16[248,256]{1,0:T(8,128)(2,1)S(1)}, u32[]{:S(2)}, u32[]{:S(2)}) collective-permute-start(bf16[248,256]{1,0:T(8,128)(2,1)S(1)} %get-tuple-element.71), channel_id=1, source_target_pairs={{4,8},{8,4},{5,9},{9,5},{6,10},{10,6},{7,11},{11,7},{20,24},{24,20... | collective-permute-start | bytes 380936 | tf_op jit(solution)/shard_map/ppermute | solution.py:38
  25.0 4.9 %collective-permute-start.6 = (bf16[6,12,256]{2,1,0:T(8,128)(2,1)S(1)}, bf16[6,12,256]{2,1,0:T(8,128)(2,1)S(1)}, u32[]{:S(2)}, u32[]{:S(2)}) collective-permute-start(bf16[6,12,256]{2,1,0:T(8,128)(2,1)S(1)} %get-tuple-element.58), channel_id=1, source_target_pairs={{0,1},{1,2},{2,3},{3,0},{4,5},{5,6},{6,7},{7,4},{8,9},{9,10},{10,1... | collective-permute-start | bytes 110600 | tf_op jit(solution)/shard_map/ppermute | solution.py:25
  25.1 4.9 %collective-permute-start.7 = (bf16[6,12,256]{2,1,0:T(8,128)(2,1)S(1)}, bf16[6,12,256]{2,1,0:T(8,128)(2,1)S(1)}, u32[]{:S(2)}, u32[]{:S(2)}) collective-permute-start(bf16[6,12,256]{2,1,0:T(8,128)(2,1)S(1)} %get-tuple-element.59), channel_id=1, source_target_pairs={{0,2},{1,3},{2,0},{3,1},{4,6},{5,7},{6,4},{7,5},{8,10},{9,11},{10,... | collective-permute-start | bytes 110600 | tf_op jit(solution)/shard_map/ppermute | solution.py:25
  27.5 3.6 %collective-permute-start.8 = (bf16[6,12,256]{2,1,0:T(8,128)(2,1)S(1)}, bf16[6,12,256]{2,1,0:T(8,128)(2,1)S(1)}, u32[]{:S(2)}, u32[]{:S(2)}) collective-permute-start(bf16[6,12,256]{2,1,0:T(8,128)(2,1)S(1)} %get-tuple-element.60), channel_id=1, source_target_pairs={{0,3},{1,0},{2,1},{3,2},{4,7},{5,4},{6,5},{7,6},{8,11},{9,8},{10,9... | collective-permute-start | bytes 110600 | tf_op jit(solution)/shard_map/ppermute | solution.py:25

commit v7 on v6

--- a/solution.py
+++ b/solution.py
@@ -114,7 +114,7 @@
 
 
 def window_shape(size, border):
-    return size[0] + 2 * border, pitch_of(size[1] + 2 * border)
+    return size[0] + 2 * border, (size[1] + 2 * border + 7) // 8 * 8
 
 
 def compact_shape(size, border):
@@ -400,7 +400,7 @@
         total = total + ref[...].astype(f32)
     top_buf[...] = jnp.zeros_like(top_buf)
     top_buf[:, : wide4 + 2 * rim, :] = jnp.maximum(total + bias_ref[4:5, :][None], 0.0)
-    top_ref[...] = top_buf[...].astype(bf16).reshape(top_ref.shape)
+    top_ref[...] = top_buf[...].reshape(top_ref.shape).astype(bf16)
     tall, broad = compact_shape((high4, wide4), 1)
     small_buf[...] = jnp.zeros_like(small_buf)
     for row in range(tall):
@@ -445,6 +445,9 @@
         pyr1_buf,
         pyr2_buf,
         pyr3_buf,
+        moved1_buf,
+        moved2_buf,
+        moved3_buf,
         acc_buf,
         sums_buf,
         stack_buf,
@@ -454,6 +457,8 @@
         terms2_buf,
         above_buf,
         below_buf,
+        result_buf,
+        sems,
     ) = refs
     channels = bias_ref.shape[1]
 
@@ -491,20 +496,33 @@
         row_start += rim * whole
 
     shape1, shape2, shape3 = lat1_buf.shape[:2], lat2_buf.shape[:2], lat3_buf.shape[:2]
+
+    def put(value, plain, moved):
+        plain[0 : value.shape[0], :] = value.astype(bf16)
+        later = jnp.concatenate([jnp.zeros((8, channels), f32), value, jnp.zeros((8, channels), f32)])
+        moved[0 : later.shape[0], :] = later.astype(bf16)
+
     for lat_buf, matrix, source, out in (
-        (lat3_buf, up3_ref, None, pyr3_buf),
-        (lat2_buf, up2_ref, pyr3_buf, pyr2_buf),
-        (lat1_buf, up1_ref, pyr2_buf, pyr1_buf),
+        (lat3_buf, up3_ref, top_ref, (pyr3_buf, moved3_buf)),
+        (lat2_buf, up2_ref, pyr3_buf, (pyr2_buf, moved2_buf)),
+        (lat1_buf, up1_ref, pyr2_buf, (pyr1_buf, moved1_buf)),
     ):
-        source = top_ref[...] if source is None else source[...]
+        source = source[...]
         total = lat_buf[...].reshape(-1, channels) + dot(matrix[...], source)
-        out[...] = total.astype(bf16)
+        put(total, *out)
 
     def conv(source, shape, weight_at, rows):
         pitch = shape[1]
         span = rows * pitch
+        plain, moved = source
+        shift = pitch % 16
         stacked = jnp.concatenate(
-            [source[row_tap * pitch : row_tap * pitch + span, :] for row_tap in range(3)], axis=1
+            [
+                plain[0:span, :],
+                (moved if shift else plain)[pitch + shift : pitch + shift + span, :],
+                plain[2 * pitch : 2 * pitch + span, :],
+            ],
+            axis=1,
         )
         for col_tap in range(3):
             weight = weight_at(col_tap)
@@ -523,7 +541,7 @@
         total = taps_total(rows, wide + 2)
         return jnp.maximum(total + bias_ref[8 + number : 9 + number, :][None], 0.0)
 
-    value = smooth(2, pyr3_buf, shape3, wide3)
+    value = smooth(2, (pyr3_buf, moved3_buf), shape3, wide3)
     tall, broad = compact_shape((high3, wide3), 1)
     small3_buf[...] = jnp.zeros_like(small3_buf)
     for row in range(tall):
@@ -536,7 +554,7 @@
     tap_terms(small3_buf[...].astype(bf16), join_w, 2 * channels, store3)
 
     rows2, whole2 = compact_shape((high2, wide2), 1)
-    sums_buf[:rows2, :whole2, :] = smooth(1, pyr2_buf, shape2, wide2)
+    sums_buf[:rows2, :whole2, :] = smooth(1, (pyr2_buf, moved2_buf), shape2, wide2)
     half = (high2 // cuts2, wide2 // cuts2)
     tall, broad = compact_shape(half, 1)
     lanes2 = small2_buf.shape[0] // part_count
@@ -555,24 +573,30 @@
     tap_terms(small2_buf[...].astype(bf16), join_w, channels, store2)
 
     rows1, pitch1 = window_shape((high1, wide1), 1)
-    value = smooth(0, pyr1_buf, shape1, wide1)
+    value = smooth(0, (pyr1_buf, moved1_buf), shape1, wide1)
     down = here_ref[0] * high1 - 1 + lax.broadcasted_iota(jnp.int32, (rows1, 1, 1), 0)
     across = here_ref[1] * wide1 - 1 + lax.broadcasted_iota(jnp.int32, (1, wide1 + 2, 1), 1)
     inside = (down >= 0) & (down < high1 * row_count) & (across >= 0) & (across < wide1 * col_count)
     sums_buf[:rows1, : wide1 + 2, :] = jnp.where(inside, value, 0.0)
-    stack_buf[...] = sums_buf[...].astype(bf16).reshape(rows1 * pitch1, channels)
-    conv(stack_buf, (rows1, pitch1), lambda j: join_w[:, j, 0:channels], high1)
+    put(sums_buf[...].reshape(rows1 * pitch1, channels), stack_buf, moved1_buf)
+    conv((stack_buf, moved1_buf), (rows1, pitch1), lambda j: join_w[:, j, 0:channels], high1)
     total = taps_total(high1, wide1)
     spread = base_ref[...] + dot(spread3_ref[...], terms3_buf[...])
     sums_buf[:high1, :wide1, :] = total + spread.reshape(high1, wide1, channels)
     tall, broad = high1 // cuts2, wide1 // cuts2
+    copies = []
     for part, matrix in enumerate(quarters):
         terms = terms2_buf[part * 9 * lanes2 : (part + 1) * 9 * lanes2, :]
         value = dot(matrix[...], terms).reshape(tall, broad, channels)
         row0, col0 = part // cuts2 * tall, part % cuts2 * broad
         value = value + sums_buf[row0 : row0 + tall, col0 : col0 + broad, :]
         value = jnp.maximum(value + bias_ref[11:12, :][None], 0.0)
-        out_ref[row0 : row0 + tall, col0 : col0 + broad, :] = value.astype(bf16)
+        result_buf[part] = value.astype(bf16)
+        target = out_ref.at[pl.ds(row0, tall), pl.ds(col0, broad), :]
+        copies.append(pltpu.make_async_copy(result_buf.at[part], target, sems.at[part]))
+        copies[-1].start()
+    for copy in copies:
+        copy.wait()
 
 
 def tail(here, top, base, lats, swapped, before, after, biases, weights, matrices, quarters, sizes):
@@ -586,7 +610,7 @@
         functools.partial(tail_kernel, sizes, len(quarters)),
         out_shape=jax.ShapeDtypeStruct((*one, channels), bf16),
         in_specs=[smem_spec] + [vmem_spec] * len(inputs),
-        out_specs=vmem_spec,
+        out_specs=hbm_spec,
         scratch_shapes=[
             pltpu.VMEM((rows1, pitch1, channels), f32),
             pltpu.VMEM((rows2, pitch2, channels), f32),
@@ -594,6 +618,9 @@
             pltpu.VMEM((rows1 * pitch1, channels), bf16),
             pltpu.VMEM((rows2 * pitch2, channels), bf16),
             pltpu.VMEM((rows3 * pitch3, channels), bf16),
+            pltpu.VMEM((rows1 * pitch1 + 16, channels), bf16),
+            pltpu.VMEM((rows2 * pitch2 + 16, channels), bf16),
+            pltpu.VMEM((rows3 * pitch3 + 16, channels), bf16),
             pltpu.VMEM((3, rows1 - 2, pitch1, channels), f32),
             pltpu.VMEM((rows1 - 2, pitch1, channels), f32),
             pltpu.VMEM(((rows1 - 2) * pitch1, channels), bf16),
@@ -603,6 +630,8 @@
             pltpu.VMEM((9 * small2, channels), bf16),
             pltpu.VMEM(swapped[0].shape, f32),
             pltpu.VMEM(swapped[0].shape, f32),
+            pltpu.VMEM((len(quarters), one[0] // cuts2, one[1] // cuts2, channels), bf16),
+            pltpu.SemaphoreType.DMA((len(quarters),)),
         ],
         compiler_params=pltpu.CompilerParams(vmem_limit_bytes=30 * 1024 * 1024),
         cost_estimate=pl.CostEstimate(
@@ -740,16 +769,17 @@
     )(here, bias_table, lat1, lat2, *received)
     swapped = pair_swap(first_rows, second_rows, "row")
     small = late_plans[0][8]
+    top_pitch = window_shape((high4, wide4), rim)[1]
     top, base, *quarters = call(
         functools.partial(late_kernel, sizes, late_plans, col_count),
         [
-            shape((rows * pitch_of(span4), channels)),
+            shape((rows * top_pitch, channels)),
             shape((high1 * wide1, channels), f32),
         ]
         + [shape(matrix_shape(plan)) for plan in late_plans[1:]],
         [smem_spec] + [vmem_spec] * (2 + col_count),
         [
-            pltpu.VMEM((rows, pitch_of(span4), channels), f32),
+            pltpu.VMEM((rows, top_pitch, channels), f32),
             pltpu.VMEM((small, channels), f32),
             pltpu.VMEM((9 * small, channels), bf16),
         ],

time: 45.5 us -> 44.6 us (0.980)
  Pallas kernels: 25.1 us -> 24 us
    pallas_call x1, Pallas kernels: 11.9 us -> 10.9 us  [tail(): pl.pallas_call(functools.partial(tail_kernel, sizes, len(quarters)), out_...]
  transfers between devices with their start and end apart: 11 -> 11, of which waited for: 4 -> 4; matrix products, arithmetic and copies ran while one was open for 0% -> 0% of each run, Pallas kernels for 25% -> 26%
where the time goes in v7:
time: 44.6 us; the launch traced here: 44.1 us
  Pallas kernels  24 us (54%)
  starting transfers between devices  15.2 us (34%)
  waiting for transfers between devices  4.58 us (10%)
    pallas_call x1, Pallas kernels, tail(): pl.pallas_call(functools.partial(tail_kernel, sizes, len(quarters)), out_...  10.9 us
    ppermute x9, starting transfers between devices, shifted(): lax.ppermute(value, axis, [(i, (i + shift) % count) for i in range(count)])  9.85 us
    pallas_call x1, Pallas kernels, local(): call(functools.partial(feature_kernel, row_count, plans), [shape((3, rows...  4.83 us
    ppermute x9, waiting for transfers between devices, shifted(): lax.ppermute(value, axis, [(i, (i + shift) % count) for i in range(count)])  4.58 us
    pallas_call x1, Pallas kernels, local(): call(functools.partial(lateral_kernel, col_count, len(kept)), [shape((hig...  2.85 us
    ppermute x1, starting transfers between devices, pair_swap(): lax.ppermute(second, axis, pairs(1))  2.68 us
    ppermute x1, starting transfers between devices, pair_swap(): lax.ppermute(first, axis, pairs(0))  2.65 us
    pallas_call x1, Pallas kernels, local(): call(functools.partial(late_kernel, sizes, late_plans, col_count), [shape...  1.92 us
  transfers between devices with their start and end apart: 11, of which 4 were waited for; matrix products, arithmetic and copies ran while one was open for 0% of the time, Pallas kernels for 26%

profile of v7, /device:TPU:1, one launch (start us, length us, event | category | flops | bytes accessed | tf_op | source)
XLA Modules:
  0.0 44.1 jit_solution(4349645002048739522)
XLA Ops:
  0.0 2.6 %collective-permute-start = (bf16[2,32,384]{2,1,0:T(8,128)(2,1)}, bf16[2,32,384]{2,1,0:T(8,128)(2,1)S(1)}, u32[]{:S(2)}, u32[]{:S(2)}) collective-permute-start(bf16[2,32,384]{2,1,0:T(8,128)(2,1)} %refs_7_.1), channel_id=1, source_target_pairs={{0,4},{4,8},{8,12},{12,0},{1,5},{5,9},{9,13},{13,1},{2,6},{6,10},{... | collective-permute-start | bytes 147464 | tf_op jit(solution)/shard_map/ppermute | solution.py:25
  2.6 0.0 collective-permute-start.2
  2.6 0.1 collective-permute-start.1
  2.7 0.1 pad_add_fusion.here_ref
  2.8 2.8 %shard_map.145 = (bf16[16,64,256]{2,1,0:T(8,128)(2,1)S(1)}, bf16[8,32,256]{2,1,0:T(8,128)(2,1)S(1)}, bf16[128,256]{1,0:T(8,128)(2,1)S(1)}, bf16[128,256]{1,0:T(8...) custom-call(s32[2]{0:T(128)S(1)} %pad_add_fusion.here_ref, ...), custom_call_target="tpu_custom_call" | custom-call | flops 300000000 | bytes 4000000 | tf_op jit(solution)/shard_map/pallas_call | solution.py:681
  5.6 0.0 collective-permute-done.refs_1_
  5.7 0.7 %collective-permute-done.2.refs_3_ = bf16[2,32,384]{2,1,0:T(8,128)(2,1)S(1)} collective-permute-done((bf16[2,32,384]{2,1,0:T(8,128)(2,1)}, bf16[2,32,384]{2,1,0:T(8,128)(2,1)S(1)}, u32[]{:S(2)}, u32[]{:S(2)}) %collective-permute-start.2) | collective-permute-done | bytes 49184 | tf_op jit(solution)/shard_map/ppermute | solution.py:25
  6.3 0.0 collective-permute-done.1.refs_2_
  6.3 1.1 %shard_map.147 = (bf16[144,256]{1,0:T(8,128)(2,1)S(1)}, bf16[192,256]{1,0:T(8,128)(2,1)S(1)}, bf16[144,256]{1,0:T(8,128)(2,1)S(1)}, bf16[192,256]{1,0:T(8,128)(2,1)S(1)}) custom-call(s32[2]{0:T(128)S(1)} %pad_add_fusion.here_ref, f32[64,16]{1,0:T(8,128)S(1)} %get-tuple-element.44.table_ref, bf16[4,384,256]{2,1,0:T(8,128)(2,1)S(1)} %get-tuple-element.48.weight_ref, ...), custom_call_target="tpu_custom_call" | custom-call | flops 100000000 | bytes 1000000 | tf_op jit(solution)/shard_map/pallas_call | solution.py:702
  7.4 1.3 %collective-permute-start.3 = (bf16[192,256]{1,0:T(8,128)(2,1)S(1)}, bf16[192,256]{1,0:T(8,128)(2,1)S(1)}, u32[]{:S(2)}, u32[]{:S(2)}) collective-permute-start(bf16[192,256]{1,0:T(8,128)(2,1)S(1)} %get-tuple-element.54), channel_id=1, source_target_pairs={{0,1},{1,2},{2,3},{3,0},{4,5},{5,6},{6,7},{7,4},{8,9},{9,10},{10,1... | collective-permute-start | bytes 294920 | tf_op jit(solution)/shard_map/ppermute | solution.py:25
  8.7 2.1 %collective-permute-start.5 = (bf16[192,256]{1,0:T(8,128)(2,1)S(1)}, bf16[192,256]{1,0:T(8,128)(2,1)S(1)}, u32[]{:S(2)}, u32[]{:S(2)}) collective-permute-start(bf16[192,256]{1,0:T(8,128)(2,1)S(1)} %get-tuple-element.56), channel_id=1, source_target_pairs={{0,3},{1,0},{2,1},{3,2},{4,7},{5,4},{6,5},{7,6},{8,11},{9,8},{10,9... | collective-permute-start | bytes 294920 | tf_op jit(solution)/shard_map/ppermute | solution.py:25
  10.8 0.4 collective-permute-start.4
  11.2 4.8 %shard_map.146 = (f32[3,192,256]{2,1,0:T(8,128)S(1)}, bf16[3,3,256,256]{3,2,1,0:T(8,128)(2,1)S(1)}, bf16[3,3,3,256,256]{4,3,2,1,0:T(8,128)(2,1)S(1)}, bf16[3,3,1...) custom-call(s32[2]{0:T(128)S(1)} %pad_add_fusion.here_ref, ...), custom_call_target="tpu_custom_call" | custom-call | flops 700000000 | bytes 12000000 | tf_op jit(solution)/shard_map/pallas_call | solution.py:727
  16.1 1.1 %collective-permute-done.4.refs_2_ = bf16[144,256]{1,0:T(8,128)(2,1)S(1)} collective-permute-done((bf16[144,256]{1,0:T(8,128)(2,1)S(1)}, bf16[144,256]{1,0:T(8,128)(2,1)S(1)}, u32[]{:S(2)}, u32[]{:S(2)}) %collective-permute-start.4) | collective-permute-done | bytes 73760 | tf_op jit(solution)/shard_map/ppermute | solution.py:25
  17.2 0.0 collective-permute-done.3.refs_1_.refs_11_
  17.2 0.0 collective-permute-done.5.refs_3_.refs_12_
  17.2 0.7 %shard_map.150 = (bf16[4,20,256]{2,1,0:T(8,128)(2,1)S(1)}, bf16[248,256]{1,0:T(8,128)(2,1)S(1)}, bf16[248,256]{1,0:T(8,128)(2,1)S(1)}) custom-call(s32[2]{0:T(128)S(1)} %pad_add_fusion.here_ref, f32[12,256]{1,0:T(8,128)S(1)} %get-tuple-element.41.bias_ref.refs_13_, bf16[16,64,256]{2,1,0:T(8,128)(2,1)S(1)} %get-tuple-element.67.lat1_ref.refs_6_, ...), custom_call_target="tpu_custom_call" | custom-call | flops 1000000 | bytes 1000000 | tf_op jit(solution)/shard_map/pallas_call | solution.py:758
  17.9 2.7 %collective-permute-start.9 = (bf16[248,256]{1,0:T(8,128)(2,1)S(1)}, bf16[248,256]{1,0:T(8,128)(2,1)S(1)}, u32[]{:S(2)}, u32[]{:S(2)}) collective-permute-start(bf16[248,256]{1,0:T(8,128)(2,1)S(1)} %get-tuple-element.70), channel_id=1, source_target_pairs={{0,4},{4,0},{8,12},{12,8},{1,5},{5,1},{9,13},{13,9},{2,6},{6,2},{1... | collective-permute-start | bytes 380936 | tf_op jit(solution)/shard_map/ppermute | solution.py:38
  20.6 2.7 %collective-permute-start.10 = (bf16[248,256]{1,0:T(8,128)(2,1)S(1)}, bf16[248,256]{1,0:T(8,128)(2,1)S(1)}, u32[]{:S(2)}, u32[]{:S(2)}) collective-permute-start(bf16[248,256]{1,0:T(8,128)(2,1)S(1)} %get-tuple-element.71), channel_id=1, source_target_pairs={{4,8},{8,4},{5,9},{9,5},{6,10},{10,6},{7,11},{11,7},{20,24},{24,20... | collective-permute-start | bytes 380936 | tf_op jit(solution)/shard_map/ppermute | solution.py:38
  23.2 1.8 %shard_map.148 = (bf16[6,12,256]{2,1,0:T(8,128)(2,1)S(1)}, bf16[6,12,256]{2,1,0:T(8,128)(2,1)S(1)}, bf16[6,12,256]{2,1,0:T(8,128)(2,1)S(1)}, bf16[6,12,256]{2,1,0:T(8,128)(2,1)S(1)}) custom-call(s32[2]{0:T(128)S(1)} %pad_add_fusion.here_ref, f32[64,16]{1,0:T(8,128)S(1)} %get-tuple-element.44.table_ref, f32[16,64]{1,0:T(8,128)S(1)} %get-tuple-element.45.turned_ref, ...), custom_call_target="tpu_custom_call" | custom-call | flops 300000000 | bytes 3000000 | tf_op jit(solution)/shard_map/pallas_call | solution.py:742
  25.0 0.1 collective-permute-start.6
  25.1 2.4 %collective-permute-start.7 = (bf16[6,12,256]{2,1,0:T(8,128)(2,1)S(1)}, bf16[6,12,256]{2,1,0:T(8,128)(2,1)S(1)}, u32[]{:S(2)}, u32[]{:S(2)}) collective-permute-start(bf16[6,12,256]{2,1,0:T(8,128)(2,1)S(1)} %get-tuple-element.59), channel_id=1, source_target_pairs={{0,2},{1,3},{2,0},{3,1},{4,6},{5,7},{6,4},{7,5},{8,10},{9,11},{10,... | collective-permute-start | bytes 110600 | tf_op jit(solution)/shard_map/ppermute | solution.py:25
  27.5 0.8 %collective-permute-start.8 = (bf16[6,12,256]{2,1,0:T(8,128)(2,1)S(1)}, bf16[6,12,256]{2,1,0:T(8,128)(2,1)S(1)}, u32[]{:S(2)}, u32[]{:S(2)}) collective-permute-start(bf16[6,12,256]{2,1,0:T(8,128)(2,1)S(1)} %get-tuple-element.60), channel_id=1, source_target_pairs={{0,3},{1,0},{2,1},{3,2},{4,7},{5,4},{6,5},{7,6},{8,11},{9,8},{10,9... | collective-permute-start | bytes 110600 | tf_op jit(solution)/shard_map/ppermute | solution.py:25
  28.3 1.6 %collective-permute-done.6.refs_1_ = bf16[6,12,256]{2,1,0:T(8,128)(2,1)S(1)} collective-permute-done((bf16[6,12,256]{2,1,0:T(8,128)(2,1)S(1)}, bf16[6,12,256]{2,1,0:T(8,128)(2,1)S(1)}, u32[]{:S(2)}, u32[]{:S(2)}) %collective-permute-start.6) | collective-permute-done | bytes 36896 | tf_op jit(solution)/shard_map/ppermute | solution.py:25
  30.0 0.0 collective-permute-done.7.refs_2_
  30.0 1.1 %collective-permute-done.8.refs_3_ = bf16[6,12,256]{2,1,0:T(8,128)(2,1)S(1)} collective-permute-done((bf16[6,12,256]{2,1,0:T(8,128)(2,1)S(1)}, bf16[6,12,256]{2,1,0:T(8,128)(2,1)S(1)}, u32[]{:S(2)}, u32[]{:S(2)}) %collective-permute-start.8) | collective-permute-done | bytes 36896 | tf_op jit(solution)/shard_map/ppermute | solution.py:25
  31.1 1.9 %shard_map.149 = (bf16[96,256]{1,0:T(8,128)(2,1)S(1)}, f32[1024,256]{1,0:T(8,128)S(1)}, bf16[256,1008]{1,0:T(8,128)(2,1)S(1)}, bf16[256,1008]{1,0:T(8,128)(2,1)S...) custom-call(s32[2]{0:T(128)S(1)} %pad_add_fusion.here_ref, ...), custom_call_target="tpu_custom_call" | custom-call | flops 700000000 | bytes 5000000 | tf_op jit(solution)/shard_map/pallas_call | solution.py:773
  33.0 0.0 collective-permute-done.9.refs_9_
  33.0 0.0 collective-permute-done.10.refs_10_
  33.1 10.9 %shard_map.151 = bf16[16,64,256]{2,1,0:T(8,128)(2,1)} custom-call(s32[2]{0:T(128)S(1)} %pad_add_fusion.here_ref, bf16[256,1008]{1,0:T(8,128)(2,1)S(1)} %get-tuple-element.61.refs_0_, bf16[256,1008]{1,0:T(8,128)(2,1)S(1)} %get-tuple-element.62.refs_1_, bf16[256,1008]{1,0:T(8,128)(2,1)S(1)} %get-tuple-element.63.refs_2_, ...), custom_call_target="tpu_custom_call" | custom-call | flops 8000000000 | bytes 12000000 | tf_op jit(solution)/shard_map/pallas_call | solution.py:609
Async XLA Ops:
  0.0 5.6 %collective-permute-start = (bf16[2,32,384]{2,1,0:T(8,128)(2,1)}, bf16[2,32,384]{2,1,0:T(8,128)(2,1)S(1)}, u32[]{:S(2)}, u32[]{:S(2)}) collective-permute-start(bf16[2,32,384]{2,1,0:T(8,128)(2,1)} %refs_7_.1), channel_id=1, source_target_pairs={{0,4},{4,8},{8,12},{12,0},{1,5},{5,9},{9,13},{13,1},{2,6},{6,10},{... | collective-permute-start | bytes 147464 | tf_op jit(solution)/shard_map/ppermute | solution.py:25
  2.6 3.7 %collective-permute-start.2 = (bf16[2,32,384]{2,1,0:T(8,128)(2,1)}, bf16[2,32,384]{2,1,0:T(8,128)(2,1)S(1)}, u32[]{:S(2)}, u32[]{:S(2)}) collective-permute-start(bf16[2,32,384]{2,1,0:T(8,128)(2,1)} %refs_7_.1), channel_id=1, source_target_pairs={{0,12},{4,0},{8,4},{12,8},{1,13},{5,1},{9,5},{13,9},{2,14},{6,2},{... | collective-permute-start | bytes 147464 | tf_op jit(solution)/shard_map/ppermute | solution.py:25
  2.6 3.7 %collective-permute-start.1 = (bf16[2,32,384]{2,1,0:T(8,128)(2,1)}, bf16[2,32,384]{2,1,0:T(8,128)(2,1)S(1)}, u32[]{:S(2)}, u32[]{:S(2)}) collective-permute-start(bf16[2,32,384]{2,1,0:T(8,128)(2,1)} %refs_7_.1), channel_id=1, source_target_pairs={{0,8},{4,12},{8,0},{12,4},{1,9},{5,13},{9,1},{13,5},{2,10},{6,14},... | collective-permute-start | bytes 147464 | tf_op jit(solution)/shard_map/ppermute | solution.py:25
  7.4 9.8 %collective-permute-start.3 = (bf16[192,256]{1,0:T(8,128)(2,1)S(1)}, bf16[192,256]{1,0:T(8,128)(2,1)S(1)}, u32[]{:S(2)}, u32[]{:S(2)}) collective-permute-start(bf16[192,256]{1,0:T(8,128)(2,1)S(1)} %get-tuple-element.54), channel_id=1, source_target_pairs={{0,1},{1,2},{2,3},{3,0},{4,5},{5,6},{6,7},{7,4},{8,9},{9,10},{10,1... | collective-permute-start | bytes 294920 | tf_op jit(solution)/shard_map/ppermute | solution.py:25
  8.7 8.5 %collective-permute-start.5 = (bf16[192,256]{1,0:T(8,128)(2,1)S(1)}, bf16[192,256]{1,0:T(8,128)(2,1)S(1)}, u32[]{:S(2)}, u32[]{:S(2)}) collective-permute-start(bf16[192,256]{1,0:T(8,128)(2,1)S(1)} %get-tuple-element.56), channel_id=1, source_target_pairs={{0,3},{1,0},{2,1},{3,2},{4,7},{5,4},{6,5},{7,6},{8,11},{9,8},{10,9... | collective-permute-start | bytes 294920 | tf_op jit(solution)/shard_map/ppermute | solution.py:25
  10.8 6.4 %collective-permute-start.4 = (bf16[144,256]{1,0:T(8,128)(2,1)S(1)}, bf16[144,256]{1,0:T(8,128)(2,1)S(1)}, u32[]{:S(2)}, u32[]{:S(2)}) collective-permute-start(bf16[144,256]{1,0:T(8,128)(2,1)S(1)} %get-tuple-element.55), channel_id=1, source_target_pairs={{0,2},{1,3},{2,0},{3,1},{4,6},{5,7},{6,4},{7,5},{8,10},{9,11},{10,... | collective-permute-start | bytes 221192 | tf_op jit(solution)/shard_map/ppermute | solution.py:25
  17.9 15.1 %collective-permute-start.9 = (bf16[248,256]{1,0:T(8,128)(2,1)S(1)}, bf16[248,256]{1,0:T(8,128)(2,1)S(1)}, u32[]{:S(2)}, u32[]{:S(2)}) collective-permute-start(bf16[248,256]{1,0:T(8,128)(2,1)S(1)} %get-tuple-element.70), channel_id=1, source_target_pairs={{0,4},{4,0},{8,12},{12,8},{1,5},{5,1},{9,13},{13,9},{2,6},{6,2},{1... | collective-permute-start | bytes 380936 | tf_op jit(solution)/shard_map/ppermute | solution.py:38
  20.6 12.5 %collective-permute-start.10 = (bf16[248,256]{1,0:T(8,128)(2,1)S(1)}, bf16[248,256]{1,0:T(8,128)(2,1)S(1)}, u32[]{:S(2)}, u32[]{:S(2)}) collective-permute-start(bf16[248,256]{1,0:T(8,128)(2,1)S(1)} %get-tuple-element.71), channel_id=1, source_target_pairs={{4,8},{8,4},{5,9},{9,5},{6,10},{10,6},{7,11},{11,7},{20,24},{24,20... | collective-permute-start | bytes 380936 | tf_op jit(solution)/shard_map/ppermute | solution.py:38
  25.0 4.9 %collective-permute-start.6 = (bf16[6,12,256]{2,1,0:T(8,128)(2,1)S(1)}, bf16[6,12,256]{2,1,0:T(8,128)(2,1)S(1)}, u32[]{:S(2)}, u32[]{:S(2)}) collective-permute-start(bf16[6,12,256]{2,1,0:T(8,128)(2,1)S(1)} %get-tuple-element.58), channel_id=1, source_target_pairs={{0,1},{1,2},{2,3},{3,0},{4,5},{5,6},{6,7},{7,4},{8,9},{9,10},{10,1... | collective-permute-start | bytes 110600 | tf_op jit(solution)/shard_map/ppermute | solution.py:25
  25.1 4.9 %collective-permute-start.7 = (bf16[6,12,256]{2,1,0:T(8,128)(2,1)S(1)}, bf16[6,12,256]{2,1,0:T(8,128)(2,1)S(1)}, u32[]{:S(2)}, u32[]{:S(2)}) collective-permute-start(bf16[6,12,256]{2,1,0:T(8,128)(2,1)S(1)} %get-tuple-element.59), channel_id=1, source_target_pairs={{0,2},{1,3},{2,0},{3,1},{4,6},{5,7},{6,4},{7,5},{8,10},{9,11},{10,... | collective-permute-start | bytes 110600 | tf_op jit(solution)/shard_map/ppermute | solution.py:25
  27.5 3.6 %collective-permute-start.8 = (bf16[6,12,256]{2,1,0:T(8,128)(2,1)S(1)}, bf16[6,12,256]{2,1,0:T(8,128)(2,1)S(1)}, u32[]{:S(2)}, u32[]{:S(2)}) collective-permute-start(bf16[6,12,256]{2,1,0:T(8,128)(2,1)S(1)} %get-tuple-element.60), channel_id=1, source_target_pairs={{0,3},{1,0},{2,1},{3,2},{4,7},{5,4},{6,5},{7,6},{8,11},{9,8},{10,9... | collective-permute-start | bytes 110600 | tf_op jit(solution)/shard_map/ppermute | solution.py:25

commit v8 on v7

--- a/solution.py
+++ b/solution.py
@@ -56,7 +56,17 @@
 
 
 def dot(a, b):
-    return jnp.dot(a, b, preferred_element_type=f32)
+    rows = a.shape[0]
+    half = (rows // 2 + 15) // 16 * 16
+    if half >= rows:
+        return jnp.dot(a, b, preferred_element_type=f32)
+    return jnp.concatenate(
+        [
+            jnp.dot(a[:half], b, preferred_element_type=f32),
+            jnp.dot(a[half:], b, preferred_element_type=f32),
+        ],
+        axis=0,
+    )
 
 
 def in_hbm(value):
@@ -83,7 +93,7 @@
     return jnp.floor((value + 0.5) / step)
 
 
-def stretch_matrix(here, out_shape, out_border, in_shape, in_border, factor, out_size, in_size, counts, lanes, taps=1):
+def stretch_matrix(out_ref, here, out_shape, out_border, in_shape, in_border, factor, out_size, in_size, counts, lanes, taps=1):
     out_rows, out_pitch = out_shape
     lane = lax.broadcasted_iota(jnp.int32, (1, lanes * taps * taps), 1).astype(f32)
     tap = floor_div(lane, lanes)
@@ -105,8 +115,11 @@
 
     down = weights(0, out_rows, place_row, row_tap)
     across = weights(1, out_pitch, place_col, col_tap)
-    matrix = down[:, None, :] * across[None, :, :]
-    return matrix.astype(bf16).reshape(out_rows * out_pitch, -1)
+    for row in range(0, out_rows, 2):
+        pair = [down[step : step + 1, :] * across for step in range(row, min(row + 2, out_rows))]
+        start = row * out_pitch
+        value = jnp.concatenate(pair, axis=0)
+        out_ref[start : start + value.shape[0], :] = value.astype(bf16)
 
 
 def pitch_of(width):
@@ -245,9 +258,9 @@
 
 def feature_kernel(row_count, plans, here_ref, weight_hbm, *refs):
     blocks, refs = refs[:row_count], refs[row_count:]
-    late, refs = refs[:3], refs[3:]
-    out_ref, kept, matrices = refs[0], refs[1:4], refs[4 : 4 + len(plans)]
-    weight_ref, grid_buf, sems = refs[4 + len(plans) :]
+    late, refs = refs[:1], refs[1:]
+    out_ref, kept, matrices = refs[0], refs[1:2], refs[2 : 2 + len(plans)]
+    weight_ref, grid_buf, sems = refs[2 + len(plans) :]
     copies = [
         pltpu.make_async_copy(source, target, sems.at[number])
         for number, (source, target) in enumerate(zip((weight_hbm, *late), (weight_ref, *kept)))
@@ -256,7 +269,7 @@
         copy.start()
     here = (here_ref[0], here_ref[1])
     for plan, matrix in zip(plans, matrices):
-        matrix[...] = stretch_matrix(here, *plan)
+        stretch_matrix(matrix, here, *plan)
     high, wide, depth = blocks[0].shape
     grid_buf[...] = jnp.zeros_like(grid_buf)
     for shift, block in enumerate(blocks):
@@ -392,7 +405,7 @@
 def late_kernel(sizes, plans, top_count, here_ref, bias_ref, join_ref, *refs):
     tops, refs = refs[:top_count], refs[top_count:]
     top_ref, base_ref, matrices, refs = refs[0], refs[1], refs[2 : 1 + len(plans)], refs[1 + len(plans) :]
-    top_buf, small_buf, terms_buf = refs
+    top_buf, small_buf, terms_buf, matrix_buf = refs
     high4, wide4 = sizes[3]
     here = (here_ref[0], here_ref[1])
     total = tops[0][...].astype(f32)
@@ -413,9 +426,9 @@
         terms_buf[tap * lanes : (tap + 1) * lanes, :] = value
 
     tap_terms(small_buf[...].astype(bf16), join_ref, 3 * channels, store)
-    base_ref[...] = dot(stretch_matrix(here, *plans[0]), terms_buf[...])
-    for plan, matrix in zip(plans[1:], matrices):
-        matrix[...] = stretch_matrix(here, *plan)
+    for plan, matrix in zip(plans, (matrix_buf, *matrices)):
+        stretch_matrix(matrix, here, *plan)
+    base_ref[...] = dot(matrix_buf[...], terms_buf[...])
 
 
 def tail_kernel(sizes, part_count, here_ref, *refs):
@@ -723,8 +736,8 @@
         (row_count, col_count),
     )
     plans, late_plans = stretches(sizes)
-    late = (neck_pooled, smooth_weight, join_weight)
-    taps, neck_pooled, smooth_weight, join_weight, *matrices = call(
+    late = (neck_pooled,)
+    taps, neck_pooled, *matrices = call(
         functools.partial(feature_kernel, row_count, plans),
         [shape((3, rows * grid_cols, channels), f32)]
         + [shape(value.shape) for value in late]
@@ -782,6 +795,7 @@
             pltpu.VMEM((rows, top_pitch, channels), f32),
             pltpu.VMEM((small, channels), f32),
             pltpu.VMEM((9 * small, channels), bf16),
+            pltpu.VMEM(matrix_shape(late_plans[0]), bf16),
         ],
         700_000_000,
         5_000_000,

time: 44.6 us -> 42.7 us (0.957)
  Pallas kernels: 24 us -> 20 us
  waiting for transfers between devices: 4.58 us -> 7.43 us
  starting transfers between devices: 15.2 us -> 14.2 us
    ppermute x9, waiting for transfers between devices: 4.58 us -> 7.43 us  [shifted(): lax.ppermute(value, axis, [(i, (i + shift) % count) for i in range(count)])]
    pallas_call x1, Pallas kernels: 10.9 us -> 8.85 us  [tail(): pl.pallas_call(functools.partial(tail_kernel, sizes, len(quarters)), out_...]
    pallas_call x1, Pallas kernels: 4.83 us -> 3.06 us  [local(): call(functools.partial(feature_kernel, row_count, plans), [shape((3, rows...]
    ppermute x1, starting transfers between devices: 2.65 us -> 1.71 us  [pair_swap(): lax.ppermute(first, axis, pairs(0))]
  transfers between devices with their start and end apart: 11 -> 11, of which waited for: 4 -> 4; matrix products, arithmetic and copies ran while one was open for 0% -> 0% of each run, Pallas kernels for 26% -> 22%
where the time goes in v8:
time: 42.7 us; the launch traced here: 42.1 us
  Pallas kernels  20 us (47%)
  starting transfers between devices  14.2 us (33%)
  waiting for transfers between devices  7.43 us (17%)
    ppermute x9, starting transfers between devices, shifted(): lax.ppermute(value, axis, [(i, (i + shift) % count) for i in range(count)])  9.85 us
    pallas_call x1, Pallas kernels, tail(): pl.pallas_call(functools.partial(tail_kernel, sizes, len(quarters)), out_...  8.85 us
    ppermute x9, waiting for transfers between devices, shifted(): lax.ppermute(value, axis, [(i, (i + shift) % count) for i in range(count)])  7.43 us
    pallas_call x1, Pallas kernels, local(): call(functools.partial(feature_kernel, row_count, plans), [shape((3, rows...  3.06 us
    pallas_call x1, Pallas kernels, local(): call(functools.partial(lateral_kernel, col_count, len(kept)), [shape((hig...  2.65 us
    ppermute x1, starting transfers between devices, pair_swap(): lax.ppermute(second, axis, pairs(1))  2.59 us
    pallas_call x1, Pallas kernels, local(): call(functools.partial(neck_kernel, row_count, col_count, high4, window_r...  1.87 us
    pallas_call x1, Pallas kernels, local(): call(functools.partial(late_kernel, sizes, late_plans, col_count), [shape...  1.75 us
  transfers between devices with their start and end apart: 11, of which 4 were waited for; matrix products, arithmetic and copies ran while one was open for 0% of the time, Pallas kernels for 22%

profile of v8, /device:TPU:1, one launch (start us, length us, event | category | flops | bytes accessed | tf_op | source)
XLA Modules:
  0.0 42.1 jit_solution(18409224544736345758)
XLA Ops:
  0.0 2.6 %collective-permute-start = (bf16[2,32,384]{2,1,0:T(8,128)(2,1)}, bf16[2,32,384]{2,1,0:T(8,128)(2,1)S(1)}, u32[]{:S(2)}, u32[]{:S(2)}) collective-permute-start(bf16[2,32,384]{2,1,0:T(8,128)(2,1)} %refs_7_.1), channel_id=1, source_target_pairs={{0,4},{4,8},{8,12},{12,0},{1,5},{5,9},{9,13},{13,1},{2,6},{6,10},{... | collective-permute-start | bytes 147464 | tf_op jit(solution)/shard_map/ppermute | solution.py:25
  2.6 0.0 collective-permute-start.2
  2.6 0.1 collective-permute-start.1
  2.7 0.1 pad_add_fusion.here_ref
  2.8 2.6 %shard_map.145 = (bf16[16,64,256]{2,1,0:T(8,128)(2,1)S(1)}, bf16[8,32,256]{2,1,0:T(8,128)(2,1)S(1)}, bf16[128,256]{1,0:T(8,128)(2,1)S(1)}, bf16[128,256]{1,0:T(8...) custom-call(s32[2]{0:T(128)S(1)} %pad_add_fusion.here_ref, ...), custom_call_target="tpu_custom_call" | custom-call | flops 300000000 | bytes 4000000 | tf_op jit(solution)/shard_map/pallas_call | solution.py:694
  5.4 0.0 collective-permute-done.refs_1_
  5.5 0.9 %collective-permute-done.2.refs_3_ = bf16[2,32,384]{2,1,0:T(8,128)(2,1)S(1)} collective-permute-done((bf16[2,32,384]{2,1,0:T(8,128)(2,1)}, bf16[2,32,384]{2,1,0:T(8,128)(2,1)S(1)}, u32[]{:S(2)}, u32[]{:S(2)}) %collective-permute-start.2) | collective-permute-done | bytes 49184 | tf_op jit(solution)/shard_map/ppermute | solution.py:25
  6.3 0.0 collective-permute-done.1.refs_2_
  6.3 1.1 %shard_map.147 = (bf16[144,256]{1,0:T(8,128)(2,1)S(1)}, bf16[192,256]{1,0:T(8,128)(2,1)S(1)}, bf16[144,256]{1,0:T(8,128)(2,1)S(1)}, bf16[192,256]{1,0:T(8,128)(2,1)S(1)}) custom-call(s32[2]{0:T(128)S(1)} %pad_add_fusion.here_ref, f32[64,16]{1,0:T(8,128)S(1)} %get-tuple-element.40.table_ref, bf16[4,384,256]{2,1,0:T(8,128)(2,1)S(1)} %get-tuple-element.45.weight_ref, ...), custom_call_target="tpu_custom_call" | custom-call | flops 100000000 | bytes 1000000 | tf_op jit(solution)/shard_map/pallas_call | solution.py:715
  7.5 1.3 %collective-permute-start.3 = (bf16[192,256]{1,0:T(8,128)(2,1)S(1)}, bf16[192,256]{1,0:T(8,128)(2,1)S(1)}, u32[]{:S(2)}, u32[]{:S(2)}) collective-permute-start(bf16[192,256]{1,0:T(8,128)(2,1)S(1)} %get-tuple-element.51), channel_id=1, source_target_pairs={{0,1},{1,2},{2,3},{3,0},{4,5},{5,6},{6,7},{7,4},{8,9},{9,10},{10,1... | collective-permute-start | bytes 294920 | tf_op jit(solution)/shard_map/ppermute | solution.py:25
  8.8 2.1 %collective-permute-start.5 = (bf16[192,256]{1,0:T(8,128)(2,1)S(1)}, bf16[192,256]{1,0:T(8,128)(2,1)S(1)}, u32[]{:S(2)}, u32[]{:S(2)}) collective-permute-start(bf16[192,256]{1,0:T(8,128)(2,1)S(1)} %get-tuple-element.53), channel_id=1, source_target_pairs={{0,3},{1,0},{2,1},{3,2},{4,7},{5,4},{6,5},{7,6},{8,11},{9,8},{10,9... | collective-permute-start | bytes 294920 | tf_op jit(solution)/shard_map/ppermute | solution.py:25
  10.9 0.4 collective-permute-start.4
  11.3 0.0 copy-start
  11.3 3.1 %shard_map.146 = (f32[3,192,256]{2,1,0:T(8,128)S(1)}, bf16[3,3,256,256]{3,2,1,0:T(8,128)(2,1)S(1)}, bf16[192,96]{1,0:T(8,128)(2,1)S(1)}, bf16[480,192]{1,0:T(8,1...) custom-call(s32[2]{0:T(128)S(1)} %pad_add_fusion.here_ref, ...), custom_call_target="tpu_custom_call" | custom-call | flops 700000000 | bytes 12000000 | tf_op jit(solution)/shard_map/pallas_call | solution.py:740
  14.4 3.8 %collective-permute-done.4.refs_2_ = bf16[144,256]{1,0:T(8,128)(2,1)S(1)} collective-permute-done((bf16[144,256]{1,0:T(8,128)(2,1)S(1)}, bf16[144,256]{1,0:T(8,128)(2,1)S(1)}, u32[]{:S(2)}, u32[]{:S(2)}) %collective-permute-start.4) | collective-permute-done | bytes 73760 | tf_op jit(solution)/shard_map/ppermute | solution.py:25
  18.2 0.0 collective-permute-done.3.refs_1_.refs_11_
  18.2 0.0 collective-permute-done.5.refs_3_.refs_12_
  18.2 0.7 %shard_map.150 = (bf16[4,20,256]{2,1,0:T(8,128)(2,1)S(1)}, bf16[248,256]{1,0:T(8,128)(2,1)S(1)}, bf16[248,256]{1,0:T(8,128)(2,1)S(1)}) custom-call(s32[2]{0:T(128)S(1)} %pad_add_fusion.here_ref, f32[12,256]{1,0:T(8,128)S(1)} %get-tuple-element.39.bias_ref.refs_13_, bf16[16,64,256]{2,1,0:T(8,128)(2,1)S(1)} %get-tuple-element.64.lat1_ref.refs_6_, ...), custom_call_target="tpu_custom_call" | custom-call | flops 1000000 | bytes 1000000 | tf_op jit(solution)/shard_map/pallas_call | solution.py:771
  18.9 1.7 %collective-permute-start.9 = (bf16[248,256]{1,0:T(8,128)(2,1)S(1)}, bf16[248,256]{1,0:T(8,128)(2,1)S(1)}, u32[]{:S(2)}, u32[]{:S(2)}) collective-permute-start(bf16[248,256]{1,0:T(8,128)(2,1)S(1)} %get-tuple-element.67), channel_id=1, source_target_pairs={{0,4},{4,0},{8,12},{12,8},{1,5},{5,1},{9,13},{13,9},{2,6},{6,2},{1... | collective-permute-start | bytes 380936 | tf_op jit(solution)/shard_map/ppermute | solution.py:38
  20.6 2.6 %collective-permute-start.10 = (bf16[248,256]{1,0:T(8,128)(2,1)S(1)}, bf16[248,256]{1,0:T(8,128)(2,1)S(1)}, u32[]{:S(2)}, u32[]{:S(2)}) collective-permute-start(bf16[248,256]{1,0:T(8,128)(2,1)S(1)} %get-tuple-element.68), channel_id=1, source_target_pairs={{4,8},{8,4},{5,9},{9,5},{6,10},{10,6},{7,11},{11,7},{20,24},{24,20... | collective-permute-start | bytes 380936 | tf_op jit(solution)/shard_map/ppermute | solution.py:38
  23.2 1.9 %shard_map.148 = (bf16[6,12,256]{2,1,0:T(8,128)(2,1)S(1)}, bf16[6,12,256]{2,1,0:T(8,128)(2,1)S(1)}, bf16[6,12,256]{2,1,0:T(8,128)(2,1)S(1)}, bf16[6,12,256]{2,1,0:T(8,128)(2,1)S(1)}) custom-call(s32[2]{0:T(128)S(1)} %pad_add_fusion.here_ref, f32[64,16]{1,0:T(8,128)S(1)} %get-tuple-element.40.table_ref, f32[16,64]{1,0:T(8,128)S(1)} %get-tuple-element.41.turned_ref, ...), custom_call_target="tpu_custom_call" | custom-call | flops 300000000 | bytes 3000000 | tf_op jit(solution)/shard_map/pallas_call | solution.py:755
  25.1 0.1 collective-permute-start.6
  25.2 2.3 %collective-permute-start.7 = (bf16[6,12,256]{2,1,0:T(8,128)(2,1)S(1)}, bf16[6,12,256]{2,1,0:T(8,128)(2,1)S(1)}, u32[]{:S(2)}, u32[]{:S(2)}) collective-permute-start(bf16[6,12,256]{2,1,0:T(8,128)(2,1)S(1)} %get-tuple-element.56), channel_id=1, source_target_pairs={{0,2},{1,3},{2,0},{3,1},{4,6},{5,7},{6,4},{7,5},{8,10},{9,11},{10,... | collective-permute-start | bytes 110600 | tf_op jit(solution)/shard_map/ppermute | solution.py:25
  27.5 0.9 %collective-permute-start.8 = (bf16[6,12,256]{2,1,0:T(8,128)(2,1)S(1)}, bf16[6,12,256]{2,1,0:T(8,128)(2,1)S(1)}, u32[]{:S(2)}, u32[]{:S(2)}) collective-permute-start(bf16[6,12,256]{2,1,0:T(8,128)(2,1)S(1)} %get-tuple-element.57), channel_id=1, source_target_pairs={{0,3},{1,0},{2,1},{3,2},{4,7},{5,4},{6,5},{7,6},{8,11},{9,8},{10,9... | collective-permute-start | bytes 110600 | tf_op jit(solution)/shard_map/ppermute | solution.py:25
  28.4 1.7 %collective-permute-done.6.refs_1_ = bf16[6,12,256]{2,1,0:T(8,128)(2,1)S(1)} collective-permute-done((bf16[6,12,256]{2,1,0:T(8,128)(2,1)S(1)}, bf16[6,12,256]{2,1,0:T(8,128)(2,1)S(1)}, u32[]{:S(2)}, u32[]{:S(2)}) %collective-permute-start.6) | collective-permute-done | bytes 36896 | tf_op jit(solution)/shard_map/ppermute | solution.py:25
  30.1 0.0 collective-permute-done.7.refs_2_
  30.1 1.0 %collective-permute-done.8.refs_3_ = bf16[6,12,256]{2,1,0:T(8,128)(2,1)S(1)} collective-permute-done((bf16[6,12,256]{2,1,0:T(8,128)(2,1)S(1)}, bf16[6,12,256]{2,1,0:T(8,128)(2,1)S(1)}, u32[]{:S(2)}, u32[]{:S(2)}) %collective-permute-start.8) | collective-permute-done | bytes 36896 | tf_op jit(solution)/shard_map/ppermute | solution.py:25
  31.1 0.0 copy-done
  31.1 0.0 copy-start.1
  31.1 1.7 %shard_map.149 = (bf16[96,256]{1,0:T(8,128)(2,1)S(1)}, f32[1024,256]{1,0:T(8,128)S(1)}, bf16[256,1008]{1,0:T(8,128)(2,1)S(1)}, bf16[256,1008]{1,0:T(8,128)(2,1)S...) custom-call(s32[2]{0:T(128)S(1)} %pad_add_fusion.here_ref, ...), custom_call_target="tpu_custom_call" | custom-call | flops 700000000 | bytes 5000000 | tf_op jit(solution)/shard_map/pallas_call | solution.py:786
  32.9 0.0 collective-permute-done.9.refs_9_
  32.9 0.0 collective-permute-done.10.refs_10_
  32.9 0.2 copy-done.1
  33.1 8.8 %shard_map.151 = bf16[16,64,256]{2,1,0:T(8,128)(2,1)} custom-call(s32[2]{0:T(128)S(1)} %pad_add_fusion.here_ref, bf16[256,1008]{1,0:T(8,128)(2,1)S(1)} %get-tuple-element.58.refs_0_, bf16[256,1008]{1,0:T(8,128)(2,1)S(1)} %get-tuple-element.59.refs_1_, bf16[256,1008]{1,0:T(8,128)(2,1)S(1)} %get-tuple-element.60.refs_2_, ...), custom_call_target="tpu_custom_call" | custom-call | flops 8000000000 | bytes 12000000 | tf_op jit(solution)/shard_map/pallas_call | solution.py:622
Async XLA Ops:
  0.0 5.4 %collective-permute-start = (bf16[2,32,384]{2,1,0:T(8,128)(2,1)}, bf16[2,32,384]{2,1,0:T(8,128)(2,1)S(1)}, u32[]{:S(2)}, u32[]{:S(2)}) collective-permute-start(bf16[2,32,384]{2,1,0:T(8,128)(2,1)} %refs_7_.1), channel_id=1, source_target_pairs={{0,4},{4,8},{8,12},{12,0},{1,5},{5,9},{9,13},{13,1},{2,6},{6,10},{... | collective-permute-start | bytes 147464 | tf_op jit(solution)/shard_map/ppermute | solution.py:25
  2.6 3.7 %collective-permute-start.2 = (bf16[2,32,384]{2,1,0:T(8,128)(2,1)}, bf16[2,32,384]{2,1,0:T(8,128)(2,1)S(1)}, u32[]{:S(2)}, u32[]{:S(2)}) collective-permute-start(bf16[2,32,384]{2,1,0:T(8,128)(2,1)} %refs_7_.1), channel_id=1, source_target_pairs={{0,12},{4,0},{8,4},{12,8},{1,13},{5,1},{9,5},{13,9},{2,14},{6,2},{... | collective-permute-start | bytes 147464 | tf_op jit(solution)/shard_map/ppermute | solution.py:25
  2.6 3.7 %collective-permute-start.1 = (bf16[2,32,384]{2,1,0:T(8,128)(2,1)}, bf16[2,32,384]{2,1,0:T(8,128)(2,1)S(1)}, u32[]{:S(2)}, u32[]{:S(2)}) collective-permute-start(bf16[2,32,384]{2,1,0:T(8,128)(2,1)} %refs_7_.1), channel_id=1, source_target_pairs={{0,8},{4,12},{8,0},{12,4},{1,9},{5,13},{9,1},{13,5},{2,10},{6,14},... | collective-permute-start | bytes 147464 | tf_op jit(solution)/shard_map/ppermute | solution.py:25
  7.5 10.7 %collective-permute-start.3 = (bf16[192,256]{1,0:T(8,128)(2,1)S(1)}, bf16[192,256]{1,0:T(8,128)(2,1)S(1)}, u32[]{:S(2)}, u32[]{:S(2)}) collective-permute-start(bf16[192,256]{1,0:T(8,128)(2,1)S(1)} %get-tuple-element.51), channel_id=1, source_target_pairs={{0,1},{1,2},{2,3},{3,0},{4,5},{5,6},{6,7},{7,4},{8,9},{9,10},{10,1... | collective-permute-start | bytes 294920 | tf_op jit(solution)/shard_map/ppermute | solution.py:25
  8.8 9.4 %collective-permute-start.5 = (bf16[192,256]{1,0:T(8,128)(2,1)S(1)}, bf16[192,256]{1,0:T(8,128)(2,1)S(1)}, u32[]{:S(2)}, u32[]{:S(2)}) collective-permute-start(bf16[192,256]{1,0:T(8,128)(2,1)S(1)} %get-tuple-element.53), channel_id=1, source_target_pairs={{0,3},{1,0},{2,1},{3,2},{4,7},{5,4},{6,5},{7,6},{8,11},{9,8},{10,9... | collective-permute-start | bytes 294920 | tf_op jit(solution)/shard_map/ppermute | solution.py:25
  10.9 7.3 %collective-permute-start.4 = (bf16[144,256]{1,0:T(8,128)(2,1)S(1)}, bf16[144,256]{1,0:T(8,128)(2,1)S(1)}, u32[]{:S(2)}, u32[]{:S(2)}) collective-permute-start(bf16[144,256]{1,0:T(8,128)(2,1)S(1)} %get-tuple-element.52), channel_id=1, source_target_pairs={{0,2},{1,3},{2,0},{3,1},{4,6},{5,7},{6,4},{7,5},{8,10},{9,11},{10,... | collective-permute-start | bytes 221192 | tf_op jit(solution)/shard_map/ppermute | solution.py:25
  11.3 19.8 %copy-start = (bf16[3,3,1024,256]{3,2,1,0:T(8,128)(2,1)S(1)}, bf16[3,3,1024,256]{3,2,1,0:T(8,128)(2,1)}, u32[]{:S(2)}) copy-start(bf16[3,3,1024,256]{3,2,1,0:T(8,128)(2,1)} %refs_15_.1) | copy-start | bytes 14155780
  18.9 14.0 %collective-permute-start.9 = (bf16[248,256]{1,0:T(8,128)(2,1)S(1)}, bf16[248,256]{1,0:T(8,128)(2,1)S(1)}, u32[]{:S(2)}, u32[]{:S(2)}) collective-permute-start(bf16[248,256]{1,0:T(8,128)(2,1)S(1)} %get-tuple-element.67), channel_id=1, source_target_pairs={{0,4},{4,0},{8,12},{12,8},{1,5},{5,1},{9,13},{13,9},{2,6},{6,2},{1... | collective-permute-start | bytes 380936 | tf_op jit(solution)/shard_map/ppermute | solution.py:38
  20.6 12.3 %collective-permute-start.10 = (bf16[248,256]{1,0:T(8,128)(2,1)S(1)}, bf16[248,256]{1,0:T(8,128)(2,1)S(1)}, u32[]{:S(2)}, u32[]{:S(2)}) collective-permute-start(bf16[248,256]{1,0:T(8,128)(2,1)S(1)} %get-tuple-element.68), channel_id=1, source_target_pairs={{4,8},{8,4},{5,9},{9,5},{6,10},{10,6},{7,11},{11,7},{20,24},{24,20... | collective-permute-start | bytes 380936 | tf_op jit(solution)/shard_map/ppermute | solution.py:38
  25.1 5.0 %collective-permute-start.6 = (bf16[6,12,256]{2,1,0:T(8,128)(2,1)S(1)}, bf16[6,12,256]{2,1,0:T(8,128)(2,1)S(1)}, u32[]{:S(2)}, u32[]{:S(2)}) collective-permute-start(bf16[6,12,256]{2,1,0:T(8,128)(2,1)S(1)} %get-tuple-element.55), channel_id=1, source_target_pairs={{0,1},{1,2},{2,3},{3,0},{4,5},{5,6},{6,7},{7,4},{8,9},{9,10},{10,1... | collective-permute-start | bytes 110600 | tf_op jit(solution)/shard_map/ppermute | solution.py:25
  25.2 5.0 %collective-permute-start.7 = (bf16[6,12,256]{2,1,0:T(8,128)(2,1)S(1)}, bf16[6,12,256]{2,1,0:T(8,128)(2,1)S(1)}, u32[]{:S(2)}, u32[]{:S(2)}) collective-permute-start(bf16[6,12,256]{2,1,0:T(8,128)(2,1)S(1)} %get-tuple-element.56), channel_id=1, source_target_pairs={{0,2},{1,3},{2,0},{3,1},{4,6},{5,7},{6,4},{7,5},{8,10},{9,11},{10,... | collective-permute-start | bytes 110600 | tf_op jit(solution)/shard_map/ppermute | solution.py:25
  27.5 3.6 %collective-permute-start.8 = (bf16[6,12,256]{2,1,0:T(8,128)(2,1)S(1)}, bf16[6,12,256]{2,1,0:T(8,128)(2,1)S(1)}, u32[]{:S(2)}, u32[]{:S(2)}) collective-permute-start(bf16[6,12,256]{2,1,0:T(8,128)(2,1)S(1)} %get-tuple-element.57), channel_id=1, source_target_pairs={{0,3},{1,0},{2,1},{3,2},{4,7},{5,4},{6,5},{7,6},{8,11},{9,8},{10,9... | collective-permute-start | bytes 110600 | tf_op jit(solution)/shard_map/ppermute | solution.py:25
  31.1 2.0 %copy-start.1 = (bf16[3,3,3,256,256]{4,3,2,1,0:T(8,128)(2,1)S(1)}, bf16[3,3,3,256,256]{4,3,2,1,0:T(8,128)(2,1)}, u32[]{:S(2)}) copy-start(bf16[3,3,3,256,256]{4,3,2,1,0:T(8,128)(2,1)} %refs_14_.1) | copy-start | bytes 10616836

commit v9 on v8

--- a/solution.py
+++ b/solution.py
@@ -38,21 +38,29 @@
     return lax.ppermute(first, axis, pairs(0)), lax.ppermute(second, axis, pairs(1))
 
 
+cell_rows = max(bin_sides) ** 2 + 4
+cell_starts = tuple(sum((side * side + 7) // 8 * 8 for side in bin_sides[:k]) for k in range(len(bin_sides)))
+
+
 def cell_table(extent_rows, extent_cols):
-    rows = []
+    table = np.zeros((cell_starts[-1] + cell_rows, 8), np.float32)
+    table[:, 0] = -1.0
+    table[:, 5] = 1.0
     for number, side in enumerate(bin_sides):
         for i in range(side):
             for j in range(side):
                 top, low = i * extent_rows // side, -(-(i + 1) * extent_rows // side)
                 left, right = j * extent_cols // side, -(-(j + 1) * extent_cols // side)
-                rows.append([number, side, i, j, top, low, left, right, (low - top) * (right - left)])
-    padded = (len(rows) + 15) // 16 * 16
-    table = np.zeros((padded, 16), np.float32)
-    table[:, 0] = -1.0
-    table[:, 1] = 1.0
-    table[:, 8] = 1.0
-    table[: len(rows), :9] = np.array(rows, np.float32)
+                size = (low - top) * (right - left)
+                table[cell_starts[number] + i * side + j, :6] = (number, top, low, left, right, size)
     return table
+
+
+def pick(number, values):
+    result = values[0]
+    for step, value in enumerate(values[1:], 1):
+        result = jnp.where(number == step, value, result)
+    return result
 
 
 def dot(a, b):
@@ -223,44 +231,66 @@
         copy.wait()
 
 
-def bins_kernel(row_count, col_count, window_rows, here_ref, table_ref, weight_ref, *refs):
-    blocks, pieces, messages = (
+def bins_kernel(row_count, col_count, share, here_ref, table_ref, weight_ref, *refs):
+    blocks, pieces, messages, (bins_buf,) = (
         refs[:row_count],
         refs[row_count : row_count + col_count],
-        refs[row_count + col_count :],
+        refs[row_count + col_count : row_count + 2 * col_count],
+        refs[row_count + 2 * col_count :],
     )
     table = table_ref[...]
     high, wide, depth = blocks[0].shape
     place = lax.broadcasted_iota(jnp.int32, (1, high * wide), 1).astype(f32)
     place_row = floor_div(place, wide)
     place_col = place - place_row * wide
-    in_cols = (place_col >= table[:, 6:7]) & (place_col < table[:, 7:8])
+    in_cols = (place_col >= table[:, 3:4]) & (place_col < table[:, 4:5])
     pooled = None
     for shift, block in enumerate(blocks):
         row = place_row + (wrap(here_ref[0] - shift, row_count) * high).astype(f32)
-        inside = in_cols & (row >= table[:, 4:5]) & (row < table[:, 5:6])
+        inside = in_cols & (row >= table[:, 1:2]) & (row < table[:, 2:3])
         inside = jnp.where(inside, 1.0, 0.0).astype(bf16)
         term = dot(inside, block[...].reshape(high * wide, depth))
         pooled = term if pooled is None else pooled + term
-    pooled = (pooled / table[:, 8:9]).astype(bf16)
+    pooled = (pooled / table[:, 5:6]).astype(bf16)
     bins = None
     for number in range(len(bin_sides)):
         term = jnp.where(table[:, 0:1] == number, dot(pooled, weight_ref[number]), 0.0)
         bins = term if bins is None else bins + term
-    bins = bins.astype(bf16)
-    cells = bins.shape[0]
-    for piece, message in zip(pieces, messages):
-        message[0:window_rows, :] = piece[0:window_rows, :]
-        message[window_rows : window_rows + cells, :] = bins
-        if message.shape[0] > window_rows + cells:
-            message[window_rows + cells :, :] = piece[window_rows:, :]
-
-
-def feature_kernel(row_count, plans, here_ref, weight_hbm, *refs):
+    bins_buf[...] = bins
+    channels = bins.shape[1]
+    for shift, (piece, message) in enumerate(zip(pieces, messages)):
+        kept = message.shape[0] - cell_rows
+        message[0:kept, :] = piece[0:kept, :]
+        target = wrap(here_ref[1] + shift, col_count)
+        start = pl.multiple_of(pick(target * share // channels, cell_starts), 8)
+        message[kept:, :] = bins_buf[pl.ds(start, cell_rows), :].astype(bf16)
+
+
+def spread_weights(here, high, wide, rows, row_count, share, channels):
+    side = pick(here[1] * share // channels, bin_sides).astype(f32)
+    lane = lax.broadcasted_iota(jnp.int32, (1, cell_rows), 1).astype(f32)
+    cell_row = floor_div(lane, side)
+    cell_col = lane - cell_row * side
+    place = lax.broadcasted_iota(jnp.int32, (rows * wide, 1), 0).astype(f32)
+    place_row = floor_div(place, wide)
+    place_col = place - place_row * wide
+    place_row = place_row + (here[0] * high - rim - 1).astype(f32)
+    grid_rows = float(high * row_count)
+
+    def weights(position, extent, index):
+        source = (position + 0.5) * side / extent - 0.5
+        source = jnp.minimum(jnp.maximum(source, 0.0), side - 1.0)
+        return jnp.maximum(0.0, 1.0 - jnp.abs(source - index))
+
+    spread = weights(place_row, grid_rows, cell_row) * weights(place_col, float(wide), cell_col)
+    return jnp.where((place_row >= 0.0) & (place_row < grid_rows), spread, 0.0)
+
+
+def feature_kernel(row_count, share, channels, plans, here_ref, weight_hbm, *refs):
     blocks, refs = refs[:row_count], refs[row_count:]
     late, refs = refs[:1], refs[1:]
-    out_ref, kept, matrices = refs[0], refs[1:2], refs[2 : 2 + len(plans)]
-    weight_ref, grid_buf, sems = refs[2 + len(plans) :]
+    (out_ref, spread_ref), kept, matrices = refs[:2], refs[2:3], refs[3 : 3 + len(plans)]
+    weight_ref, grid_buf, sems = refs[3 + len(plans) :]
     copies = [
         pltpu.make_async_copy(source, target, sems.at[number])
         for number, (source, target) in enumerate(zip((weight_hbm, *late), (weight_ref, *kept)))
@@ -271,11 +301,12 @@
     for plan, matrix in zip(plans, matrices):
         stretch_matrix(matrix, here, *plan)
     high, wide, depth = blocks[0].shape
+    rows = out_ref.shape[1] // wide
+    spread_ref[...] = spread_weights(here, high, wide, rows + 2, row_count, share, channels)
     grid_buf[...] = jnp.zeros_like(grid_buf)
     for shift, block in enumerate(blocks):
         row = wrap(here_ref[0] - shift, row_count) * high + rim + 1
         grid_buf[pl.ds(row, high)] = block[...]
-    rows = out_ref.shape[1] // wide
     window = grid_buf[pl.ds(here_ref[0] * high, rows + 2)].reshape((rows + 2) * wide, depth)
     copies[0].wait()
     for col_tap in range(3):
@@ -289,55 +320,32 @@
         copy.wait()
 
 
-def neck_kernel(
-    row_count, col_count, high, window_rows, here_ref, table_ref, turned_ref, weight_ref, bias_ref, taps_ref, *refs
-):
+def neck_kernel(col_count, here_ref, weight_ref, bias_ref, taps_ref, spread_ref, *refs):
     messages, refs = refs[:col_count], refs[col_count:]
     windows, (bins_buf, acc_buf, term_buf) = refs[:col_count], refs[col_count:]
     rows, span, channels = windows[0].shape
     wide = taps_ref.shape[1] // rows
     width4 = span - 2 * rim
-    table = table_ref[...]
-    cells = table.shape[0]
-    bins = messages[0][window_rows : window_rows + cells, :].astype(f32)
+    bins = messages[0][messages[0].shape[0] - cell_rows :, :].astype(f32)
     for message in messages[1:]:
-        bins = bins + message[window_rows : window_rows + cells, :].astype(f32)
-    bias = jnp.zeros((cells, channels), f32)
-    for number in range(len(bin_sides)):
-        bias = jnp.where(table[:, 0:1] == number, bias_ref[number : number + 1, :], bias)
+        bins = bins + message[message.shape[0] - cell_rows :, :].astype(f32)
     share = weight_ref.shape[2]
     first = here_ref[1] * share
-    mine = table[:, 0:1] == (first // channels).astype(f32)
-    bins_buf[...] = jnp.where(mine, jnp.maximum(bins + bias, 0.0), 0.0)
-    if share == channels:
-        binned = bins_buf[...]
-    else:
-        binned = bins_buf[:, pl.ds(pl.multiple_of(lax.rem(first, channels), 128), share)]
-    place = lax.broadcasted_iota(jnp.int32, ((rows + 2) * wide, 1), 0).astype(f32)
-    place_row = floor_div(place, wide)
-    place_col = place - place_row * wide
-    place_row = place_row + (here_ref[0] * high - rim - 1).astype(f32)
-    grid_rows = float(high * row_count)
-    sides = turned_ref[1:2, :]
-
-    def weights(position, extent, index):
-        source = (position + 0.5) * sides / extent - 0.5
-        source = jnp.minimum(jnp.maximum(source, 0.0), sides - 1.0)
-        return jnp.maximum(0.0, 1.0 - jnp.abs(source - index))
-
-    spread = weights(place_row, grid_rows, turned_ref[2:3, :])
-    spread = spread * weights(place_col, float(wide), turned_ref[3:4, :])
-    spread = jnp.where((place_row >= 0.0) & (place_row < grid_rows), spread, 0.0)
-    ppm = jnp.dot(spread, binned, precision=highest, preferred_element_type=f32).astype(bf16)
+    branch = first // channels
+    side = pick(branch, bin_sides)
+    used = lax.broadcasted_iota(jnp.int32, (cell_rows, 1), 0) < side * side
+    bins = jnp.where(used, jnp.maximum(bins + bias_ref[pl.ds(branch, 1), :], 0.0), 0.0)
+    if share != channels:
+        bins_buf[...] = bins
+        bins = bins_buf[:, pl.ds(pl.multiple_of(lax.rem(first, channels), 128), share)]
+    ppm = jnp.dot(spread_ref[...], bins, precision=highest, preferred_element_type=f32).astype(bf16)
     size = rows * wide
+    stacked = jnp.concatenate([ppm[tap * wide : tap * wide + size] for tap in range(3)], axis=1)
     for col_tap in range(3):
-        total = taps_ref[col_tap]
-        for row_tap in range(3):
-            total = total + dot(
-                ppm[row_tap * wide : row_tap * wide + size], weight_ref[row_tap, col_tap]
-            )
-        acc_buf[col_tap, 8 : 8 + size, :] = total
-    col = place_col[0:size]
+        total = dot(stacked, weight_ref[:, col_tap].reshape(3 * share, channels))
+        acc_buf[col_tap, 8 : 8 + size, :] = total + taps_ref[col_tap]
+    place = lax.broadcasted_iota(jnp.int32, (size, 1), 0).astype(f32)
+    col = place - floor_div(place, wide) * wide
     total = (
         acc_buf[1, 8 : 8 + size, :]
         + jnp.where(col > 0.0, acc_buf[0, 7 : 7 + size, :], 0.0)
@@ -369,7 +377,7 @@
     high1, wide1 = lat1_ref.shape[:2]
     high2, wide2 = lat2_ref.shape[:2]
     before, after = messages[1], messages[col_count - 1]
-    sides_at = before.shape[0] - rim * (high1 + high2)
+    sides_at = high3 * span
     for pack_buf, last in ((low_buf, False), (high_buf, True)):
         start, at = 0, sides_at
         for lat, high, wide in ((lat1_ref, high1, wide1), (lat2_ref, high2, wide2)):
@@ -479,7 +487,7 @@
     first, second = first_ref[...].astype(f32), second_ref[...].astype(f32)
     above_buf[...] = jnp.where(even, second, first)
     below_buf[...] = jnp.where(even, first, second)
-    side_start = before_ref.shape[0] - rim * (high1 + high2)
+    side_start = high3 * (wide3 + 2 * rim)
     row_start = 0
     for ref, buf, high, wide in (
         (lat1_ref, lat1_buf, high1, wide1),
@@ -679,9 +687,8 @@
     channels = bin_weight.shape[2]
     grid_rows = high4 * row_count
     table = cell_table(grid_rows, grid_cols)
-    cells = table.shape[0]
-    turned = jnp.asarray(np.ascontiguousarray(table.T))
     table = jnp.asarray(table)
+    share_ppm = neck_pooled.shape[2]
 
     def shape(dims, kind=bf16):
         return jax.ShapeDtypeStruct(dims, kind)
@@ -690,7 +697,7 @@
     window_rows = high3 * (wide3 + 2 * rim)
     side_rows = rim * (high1 + high2)
     used = (level_one, lateral_one, level_two, lateral_two, level_three, lateral_three)
-    kept = (biases, level_four, table, bin_weight, turned)
+    kept = (biases, level_four, table, bin_weight)
     lat1, lat2, *rest = call(
         functools.partial(lateral_kernel, col_count, len(kept)),
         [shape((high1, wide1, channels)), shape((high2, wide2, channels))]
@@ -709,17 +716,17 @@
         4_000_000,
     )(here, *(in_hbm(value) for value in (*used, *kept)))
     pieces = rest[:col_count]
-    bias_table, level_four, table, bin_weight, turned = rest[col_count:]
+    bias_table, level_four, table, bin_weight = rest[col_count:]
     blocks = [level_four] + others
     near = (1, col_count - 1)
     messages = call(
-        functools.partial(bins_kernel, row_count, col_count, window_rows),
+        functools.partial(bins_kernel, row_count, col_count, share_ppm),
         [
-            shape((window_rows + cells + (side_rows if shift in near else 0), channels))
+            shape((window_rows + cell_rows + (side_rows if shift in near else 0), channels))
             for shift in range(col_count)
         ],
         [smem_spec] + [vmem_spec] * (2 + row_count + col_count),
-        [],
+        [pltpu.VMEM((table.shape[0], channels), f32)],
         100_000_000,
         1_000_000,
     )(here, table, bin_weight, *blocks, *pieces)
@@ -737,9 +744,12 @@
     )
     plans, late_plans = stretches(sizes)
     late = (neck_pooled,)
-    taps, neck_pooled, *matrices = call(
-        functools.partial(feature_kernel, row_count, plans),
-        [shape((3, rows * grid_cols, channels), f32)]
+    taps, spread, neck_pooled, *matrices = call(
+        functools.partial(feature_kernel, row_count, share_ppm, channels, plans),
+        [
+            shape((3, rows * grid_cols, channels), f32),
+            shape(((rows + 2) * grid_cols, cell_rows), f32),
+        ]
         + [shape(value.shape) for value in late]
         + [shape(matrix_shape(plan)) for plan in plans],
         [smem_spec, hbm_spec] + [vmem_spec] * row_count + [hbm_spec] * len(late),
@@ -753,17 +763,17 @@
     )(here, in_hbm(neck_feature), *blocks, *(in_hbm(value) for value in late))
     span4 = wide4 + 2 * rim
     windows = call(
-        functools.partial(neck_kernel, row_count, col_count, high4, window_rows),
+        functools.partial(neck_kernel, col_count),
         [shape((rows, span4, channels))] * col_count,
-        [smem_spec] + [vmem_spec] * (5 + col_count),
+        [smem_spec] + [vmem_spec] * (4 + col_count),
         [
-            pltpu.VMEM((cells, channels), f32),
+            pltpu.VMEM((cell_rows, channels), f32),
             pltpu.VMEM((3, rows * grid_cols + 16, channels), f32),
             pltpu.VMEM((rows, grid_cols + 16, channels), f32),
         ],
         300_000_000,
         3_000_000,
-    )(here, table, turned, neck_pooled, bias_table, taps, *received)
+    )(here, neck_pooled, bias_table, taps, spread, *received)
 
     tops = [windows[0]] + [shifted(windows[shift], "col", shift) for shift in range(1, col_count)]
     span3 = wide3 + 2 * rim

time: 42.7 us -> 41.7 us (0.977)
  waiting for transfers between devices: 7.43 us -> 6.47 us
    ppermute x9, waiting for transfers between devices: 7.43 us -> 6.46 us  [shifted(): lax.ppermute(value, axis, [(i, (i + shift) % count) for i in range(count)])]
where the time goes in v9:
time: 41.7 us; the launch traced here: 41.1 us
  Pallas kernels  19.9 us (48%)
  starting transfers between devices  14.2 us (34%)
  waiting for transfers between devices  6.47 us (16%)
    ppermute x9, starting transfers between devices, shifted(): lax.ppermute(value, axis, [(i, (i + shift) % count) for i in range(count)])  9.85 us
    pallas_call x1, Pallas kernels, tail(): pl.pallas_call(functools.partial(tail_kernel, sizes, len(quarters)), out_...  8.87 us
    ppermute x9, waiting for transfers between devices, shifted(): lax.ppermute(value, axis, [(i, (i + shift) % count) for i in range(count)])  6.46 us
    pallas_call x1, Pallas kernels, local(): call(functools.partial(feature_kernel, row_count, share_ppm, channels, pl...  3.06 us
    ppermute x1, starting transfers between devices, pair_swap(): lax.ppermute(second, axis, pairs(1))  2.68 us
    pallas_call x1, Pallas kernels, local(): call(functools.partial(lateral_kernel, col_count, len(kept)), [shape((hig...  2.64 us
    pallas_call x1, Pallas kernels, local(): call(functools.partial(late_kernel, sizes, late_plans, col_count), [shape...  1.75 us
    pallas_call x1, Pallas kernels, local(): call(functools.partial(neck_kernel, col_count), [shape((rows, span4, chan...  1.71 us
  transfers between devices with their start and end apart: 11, of which 4 were waited for; matrix products, arithmetic and copies ran while one was open for 0% of the time, Pallas kernels for 22%

profile of v9, /device:TPU:1, one launch (start us, length us, event | category | flops | bytes accessed | tf_op | source)
XLA Modules:
  0.0 41.1 jit_solution(3625449516508423779)
XLA Ops:
  0.0 2.6 %collective-permute-start = (bf16[2,32,384]{2,1,0:T(8,128)(2,1)}, bf16[2,32,384]{2,1,0:T(8,128)(2,1)S(1)}, u32[]{:S(2)}, u32[]{:S(2)}) collective-permute-start(bf16[2,32,384]{2,1,0:T(8,128)(2,1)} %refs_7_.1), channel_id=1, source_target_pairs={{0,4},{4,8},{8,12},{12,0},{1,5},{5,9},{9,13},{13,1},{2,6},{6,10},{... | collective-permute-start | bytes 147464 | tf_op jit(solution)/shard_map/ppermute | solution.py:25
  2.6 0.0 collective-permute-start.2
  2.6 0.1 collective-permute-start.1
  2.7 0.1 pad_add_fusion.here_ref
  2.8 2.6 %shard_map.136 = (bf16[16,64,256]{2,1,0:T(8,128)(2,1)S(1)}, bf16[8,32,256]{2,1,0:T(8,128)(2,1)S(1)}, bf16[128,256]{1,0:T(8,128)(2,1)S(1)}, bf16[128,256]{1,0:T(8...) custom-call(s32[2]{0:T(128)S(1)} %pad_add_fusion.here_ref, ...), custom_call_target="tpu_custom_call" | custom-call | flops 300000000 | bytes 4000000 | tf_op jit(solution)/shard_map/pallas_call | solution.py:701
  5.4 0.0 collective-permute-done.refs_1_
  5.4 0.9 %collective-permute-done.2.refs_3_ = bf16[2,32,384]{2,1,0:T(8,128)(2,1)S(1)} collective-permute-done((bf16[2,32,384]{2,1,0:T(8,128)(2,1)}, bf16[2,32,384]{2,1,0:T(8,128)(2,1)S(1)}, u32[]{:S(2)}, u32[]{:S(2)}) %collective-permute-start.2) | collective-permute-done | bytes 49184 | tf_op jit(solution)/shard_map/ppermute | solution.py:25
  6.3 0.0 collective-permute-done.1.refs_2_
  6.3 1.2 %shard_map.138 = (bf16[120,256]{1,0:T(8,128)(2,1)S(1)}, bf16[168,256]{1,0:T(8,128)(2,1)S(1)}, bf16[120,256]{1,0:T(8,128)(2,1)S(1)}, bf16[168,256]{1,0:T(8,128)(2,1)S(1)}) custom-call(s32[2]{0:T(128)S(1)} %pad_add_fusion.here_ref, f32[72,8]{1,0:T(8,128)S(1)} %get-tuple-element.44.table_ref, bf16[4,384,256]{2,1,0:T(8,128)(2,1)S(1)} %get-tuple-element.45.weight_ref, ...), custom_call_target="tpu_custom_call" | custom-call | flops 100000000 | bytes 1000000 | tf_op jit(solution)/shard_map/pallas_call | solution.py:722
  7.5 1.3 %collective-permute-start.3 = (bf16[168,256]{1,0:T(8,128)(2,1)S(1)}, bf16[168,256]{1,0:T(8,128)(2,1)S(1)}, u32[]{:S(2)}, u32[]{:S(2)}) collective-permute-start(bf16[168,256]{1,0:T(8,128)(2,1)S(1)} %get-tuple-element.51), channel_id=1, source_target_pairs={{0,1},{1,2},{2,3},{3,0},{4,5},{5,6},{6,7},{7,4},{8,9},{9,10},{10,1... | collective-permute-start | bytes 258056 | tf_op jit(solution)/shard_map/ppermute | solution.py:25
  8.9 2.1 %collective-permute-start.5 = (bf16[168,256]{1,0:T(8,128)(2,1)S(1)}, bf16[168,256]{1,0:T(8,128)(2,1)S(1)}, u32[]{:S(2)}, u32[]{:S(2)}) collective-permute-start(bf16[168,256]{1,0:T(8,128)(2,1)S(1)} %get-tuple-element.53), channel_id=1, source_target_pairs={{0,3},{1,0},{2,1},{3,2},{4,7},{5,4},{6,5},{7,6},{8,11},{9,8},{10,9... | collective-permute-start | bytes 258056 | tf_op jit(solution)/shard_map/ppermute | solution.py:25
  11.0 0.4 collective-permute-start.4
  11.3 0.0 copy-start
  11.3 3.1 %shard_map.137 = (f32[3,192,256]{2,1,0:T(8,128)S(1)}, f32[256,40]{1,0:T(8,128)S(1)}, bf16[3,3,256,256]{3,2,1,0:T(8,128)(2,1)S(1)}, bf16[192,96]{1,0:T(8,128)(2,1...) custom-call(s32[2]{0:T(128)S(1)} %pad_add_fusion.here_ref, ...), custom_call_target="tpu_custom_call" | custom-call | flops 700000000 | bytes 12000000 | tf_op jit(solution)/shard_map/pallas_call | solution.py:747
  14.4 3.0 %collective-permute-done.4.refs_2_ = bf16[120,256]{1,0:T(8,128)(2,1)S(1)} collective-permute-done((bf16[120,256]{1,0:T(8,128)(2,1)S(1)}, bf16[120,256]{1,0:T(8,128)(2,1)S(1)}, u32[]{:S(2)}, u32[]{:S(2)}) %collective-permute-start.4) | collective-permute-done | bytes 61472 | tf_op jit(solution)/shard_map/ppermute | solution.py:25
  17.4 0.0 collective-permute-done.3.refs_1_.refs_11_
  17.4 0.0 collective-permute-done.5.refs_3_.refs_12_
  17.4 0.7 %shard_map.141 = (bf16[4,20,256]{2,1,0:T(8,128)(2,1)S(1)}, bf16[248,256]{1,0:T(8,128)(2,1)S(1)}, bf16[248,256]{1,0:T(8,128)(2,1)S(1)}) custom-call(s32[2]{0:T(128)S(1)} %pad_add_fusion.here_ref, f32[12,256]{1,0:T(8,128)S(1)} %get-tuple-element.39.bias_ref.refs_13_, bf16[16,64,256]{2,1,0:T(8,128)(2,1)S(1)} %get-tuple-element.64.lat1_ref.refs_6_, ...), custom_call_target="tpu_custom_call" | custom-call | flops 1000000 | bytes 1000000 | tf_op jit(solution)/shard_map/pallas_call | solution.py:781
  18.1 1.7 %collective-permute-start.9 = (bf16[248,256]{1,0:T(8,128)(2,1)S(1)}, bf16[248,256]{1,0:T(8,128)(2,1)S(1)}, u32[]{:S(2)}, u32[]{:S(2)}) collective-permute-start(bf16[248,256]{1,0:T(8,128)(2,1)S(1)} %get-tuple-element.67), channel_id=1, source_target_pairs={{0,4},{4,0},{8,12},{12,8},{1,5},{5,1},{9,13},{13,9},{2,6},{6,2},{1... | collective-permute-start | bytes 380936 | tf_op jit(solution)/shard_map/ppermute | solution.py:38
  19.8 2.7 %collective-permute-start.10 = (bf16[248,256]{1,0:T(8,128)(2,1)S(1)}, bf16[248,256]{1,0:T(8,128)(2,1)S(1)}, u32[]{:S(2)}, u32[]{:S(2)}) collective-permute-start(bf16[248,256]{1,0:T(8,128)(2,1)S(1)} %get-tuple-element.68), channel_id=1, source_target_pairs={{4,8},{8,4},{5,9},{9,5},{6,10},{10,6},{7,11},{11,7},{20,24},{24,20... | collective-permute-start | bytes 380936 | tf_op jit(solution)/shard_map/ppermute | solution.py:38
  22.5 1.7 %shard_map.139 = (bf16[6,12,256]{2,1,0:T(8,128)(2,1)S(1)}, bf16[6,12,256]{2,1,0:T(8,128)(2,1)S(1)}, bf16[6,12,256]{2,1,0:T(8,128)(2,1)S(1)}, bf16[6,12,256]{2,1,0:T(8,128)(2,1)S(1)}) custom-call(s32[2]{0:T(128)S(1)} %pad_add_fusion.here_ref, bf16[3,3,256,256]{3,2,1,0:T(8,128)(2,1)S(1)} %get-tuple-element.41.weight_ref, ...), custom_call_target="tpu_custom_call" | custom-call | flops 300000000 | bytes 3000000 | tf_op jit(solution)/shard_map/pallas_call | solution.py:765
  24.2 0.1 collective-permute-start.6
  24.3 2.2 %collective-permute-start.7 = (bf16[6,12,256]{2,1,0:T(8,128)(2,1)S(1)}, bf16[6,12,256]{2,1,0:T(8,128)(2,1)S(1)}, u32[]{:S(2)}, u32[]{:S(2)}) collective-permute-start(bf16[6,12,256]{2,1,0:T(8,128)(2,1)S(1)} %get-tuple-element.56), channel_id=1, source_target_pairs={{0,2},{1,3},{2,0},{3,1},{4,6},{5,7},{6,4},{7,5},{8,10},{9,11},{10,... | collective-permute-start | bytes 110600 | tf_op jit(solution)/shard_map/ppermute | solution.py:25
  26.5 1.0 %collective-permute-start.8 = (bf16[6,12,256]{2,1,0:T(8,128)(2,1)S(1)}, bf16[6,12,256]{2,1,0:T(8,128)(2,1)S(1)}, u32[]{:S(2)}, u32[]{:S(2)}) collective-permute-start(bf16[6,12,256]{2,1,0:T(8,128)(2,1)S(1)} %get-tuple-element.57), channel_id=1, source_target_pairs={{0,3},{1,0},{2,1},{3,2},{4,7},{5,4},{6,5},{7,6},{8,11},{9,8},{10,9... | collective-permute-start | bytes 110600 | tf_op jit(solution)/shard_map/ppermute | solution.py:25
  27.5 1.6 %collective-permute-done.6.refs_1_ = bf16[6,12,256]{2,1,0:T(8,128)(2,1)S(1)} collective-permute-done((bf16[6,12,256]{2,1,0:T(8,128)(2,1)S(1)}, bf16[6,12,256]{2,1,0:T(8,128)(2,1)S(1)}, u32[]{:S(2)}, u32[]{:S(2)}) %collective-permute-start.6) | collective-permute-done | bytes 36896 | tf_op jit(solution)/shard_map/ppermute | solution.py:25
  29.1 0.0 collective-permute-done.7.refs_2_
  29.1 1.0 %collective-permute-done.8.refs_3_ = bf16[6,12,256]{2,1,0:T(8,128)(2,1)S(1)} collective-permute-done((bf16[6,12,256]{2,1,0:T(8,128)(2,1)S(1)}, bf16[6,12,256]{2,1,0:T(8,128)(2,1)S(1)}, u32[]{:S(2)}, u32[]{:S(2)}) %collective-permute-start.8) | collective-permute-done | bytes 36896 | tf_op jit(solution)/shard_map/ppermute | solution.py:25
  30.1 0.0 copy-done
  30.1 0.0 copy-start.1
  30.1 1.7 %shard_map.140 = (bf16[96,256]{1,0:T(8,128)(2,1)S(1)}, f32[1024,256]{1,0:T(8,128)S(1)}, bf16[256,1008]{1,0:T(8,128)(2,1)S(1)}, bf16[256,1008]{1,0:T(8,128)(2,1)S...) custom-call(s32[2]{0:T(128)S(1)} %pad_add_fusion.here_ref, ...), custom_call_target="tpu_custom_call" | custom-call | flops 700000000 | bytes 5000000 | tf_op jit(solution)/shard_map/pallas_call | solution.py:796
  31.8 0.0 collective-permute-done.9.refs_9_
  31.9 0.0 collective-permute-done.10.refs_10_
  31.9 0.2 copy-done.1
  32.1 8.9 %shard_map.142 = bf16[16,64,256]{2,1,0:T(8,128)(2,1)} custom-call(s32[2]{0:T(128)S(1)} %pad_add_fusion.here_ref, bf16[256,1008]{1,0:T(8,128)(2,1)S(1)} %get-tuple-element.58.refs_0_, bf16[256,1008]{1,0:T(8,128)(2,1)S(1)} %get-tuple-element.59.refs_1_, bf16[256,1008]{1,0:T(8,128)(2,1)S(1)} %get-tuple-element.60.refs_2_, ...), custom_call_target="tpu_custom_call" | custom-call | flops 8000000000 | bytes 12000000 | tf_op jit(solution)/shard_map/pallas_call | solution.py:630
Async XLA Ops:
  0.0 5.4 %collective-permute-start = (bf16[2,32,384]{2,1,0:T(8,128)(2,1)}, bf16[2,32,384]{2,1,0:T(8,128)(2,1)S(1)}, u32[]{:S(2)}, u32[]{:S(2)}) collective-permute-start(bf16[2,32,384]{2,1,0:T(8,128)(2,1)} %refs_7_.1), channel_id=1, source_target_pairs={{0,4},{4,8},{8,12},{12,0},{1,5},{5,9},{9,13},{13,1},{2,6},{6,10},{... | collective-permute-start | bytes 147464 | tf_op jit(solution)/shard_map/ppermute | solution.py:25
  2.6 3.7 %collective-permute-start.2 = (bf16[2,32,384]{2,1,0:T(8,128)(2,1)}, bf16[2,32,384]{2,1,0:T(8,128)(2,1)S(1)}, u32[]{:S(2)}, u32[]{:S(2)}) collective-permute-start(bf16[2,32,384]{2,1,0:T(8,128)(2,1)} %refs_7_.1), channel_id=1, source_target_pairs={{0,12},{4,0},{8,4},{12,8},{1,13},{5,1},{9,5},{13,9},{2,14},{6,2},{... | collective-permute-start | bytes 147464 | tf_op jit(solution)/shard_map/ppermute | solution.py:25
  2.6 3.7 %collective-permute-start.1 = (bf16[2,32,384]{2,1,0:T(8,128)(2,1)}, bf16[2,32,384]{2,1,0:T(8,128)(2,1)S(1)}, u32[]{:S(2)}, u32[]{:S(2)}) collective-permute-start(bf16[2,32,384]{2,1,0:T(8,128)(2,1)} %refs_7_.1), channel_id=1, source_target_pairs={{0,8},{4,12},{8,0},{12,4},{1,9},{5,13},{9,1},{13,5},{2,10},{6,14},... | collective-permute-start | bytes 147464 | tf_op jit(solution)/shard_map/ppermute | solution.py:25
  7.5 9.9 %collective-permute-start.3 = (bf16[168,256]{1,0:T(8,128)(2,1)S(1)}, bf16[168,256]{1,0:T(8,128)(2,1)S(1)}, u32[]{:S(2)}, u32[]{:S(2)}) collective-permute-start(bf16[168,256]{1,0:T(8,128)(2,1)S(1)} %get-tuple-element.51), channel_id=1, source_target_pairs={{0,1},{1,2},{2,3},{3,0},{4,5},{5,6},{6,7},{7,4},{8,9},{9,10},{10,1... | collective-permute-start | bytes 258056 | tf_op jit(solution)/shard_map/ppermute | solution.py:25
  8.9 8.6 %collective-permute-start.5 = (bf16[168,256]{1,0:T(8,128)(2,1)S(1)}, bf16[168,256]{1,0:T(8,128)(2,1)S(1)}, u32[]{:S(2)}, u32[]{:S(2)}) collective-permute-start(bf16[168,256]{1,0:T(8,128)(2,1)S(1)} %get-tuple-element.53), channel_id=1, source_target_pairs={{0,3},{1,0},{2,1},{3,2},{4,7},{5,4},{6,5},{7,6},{8,11},{9,8},{10,9... | collective-permute-start | bytes 258056 | tf_op jit(solution)/shard_map/ppermute | solution.py:25
  11.0 6.5 %collective-permute-start.4 = (bf16[120,256]{1,0:T(8,128)(2,1)S(1)}, bf16[120,256]{1,0:T(8,128)(2,1)S(1)}, u32[]{:S(2)}, u32[]{:S(2)}) collective-permute-start(bf16[120,256]{1,0:T(8,128)(2,1)S(1)} %get-tuple-element.52), channel_id=1, source_target_pairs={{0,2},{1,3},{2,0},{3,1},{4,6},{5,7},{6,4},{7,5},{8,10},{9,11},{10,... | collective-permute-start | bytes 184328 | tf_op jit(solution)/shard_map/ppermute | solution.py:25
  11.3 18.8 %copy-start = (bf16[3,3,1024,256]{3,2,1,0:T(8,128)(2,1)S(1)}, bf16[3,3,1024,256]{3,2,1,0:T(8,128)(2,1)}, u32[]{:S(2)}) copy-start(bf16[3,3,1024,256]{3,2,1,0:T(8,128)(2,1)} %refs_15_.1) | copy-start | bytes 14155780
  18.1 13.7 %collective-permute-start.9 = (bf16[248,256]{1,0:T(8,128)(2,1)S(1)}, bf16[248,256]{1,0:T(8,128)(2,1)S(1)}, u32[]{:S(2)}, u32[]{:S(2)}) collective-permute-start(bf16[248,256]{1,0:T(8,128)(2,1)S(1)} %get-tuple-element.67), channel_id=1, source_target_pairs={{0,4},{4,0},{8,12},{12,8},{1,5},{5,1},{9,13},{13,9},{2,6},{6,2},{1... | collective-permute-start | bytes 380936 | tf_op jit(solution)/shard_map/ppermute | solution.py:38
  19.8 12.1 %collective-permute-start.10 = (bf16[248,256]{1,0:T(8,128)(2,1)S(1)}, bf16[248,256]{1,0:T(8,128)(2,1)S(1)}, u32[]{:S(2)}, u32[]{:S(2)}) collective-permute-start(bf16[248,256]{1,0:T(8,128)(2,1)S(1)} %get-tuple-element.68), channel_id=1, source_target_pairs={{4,8},{8,4},{5,9},{9,5},{6,10},{10,6},{7,11},{11,7},{20,24},{24,20... | collective-permute-start | bytes 380936 | tf_op jit(solution)/shard_map/ppermute | solution.py:38
  24.2 4.9 %collective-permute-start.6 = (bf16[6,12,256]{2,1,0:T(8,128)(2,1)S(1)}, bf16[6,12,256]{2,1,0:T(8,128)(2,1)S(1)}, u32[]{:S(2)}, u32[]{:S(2)}) collective-permute-start(bf16[6,12,256]{2,1,0:T(8,128)(2,1)S(1)} %get-tuple-element.55), channel_id=1, source_target_pairs={{0,1},{1,2},{2,3},{3,0},{4,5},{5,6},{6,7},{7,4},{8,9},{9,10},{10,1... | collective-permute-start | bytes 110600 | tf_op jit(solution)/shard_map/ppermute | solution.py:25
  24.3 4.9 %collective-permute-start.7 = (bf16[6,12,256]{2,1,0:T(8,128)(2,1)S(1)}, bf16[6,12,256]{2,1,0:T(8,128)(2,1)S(1)}, u32[]{:S(2)}, u32[]{:S(2)}) collective-permute-start(bf16[6,12,256]{2,1,0:T(8,128)(2,1)S(1)} %get-tuple-element.56), channel_id=1, source_target_pairs={{0,2},{1,3},{2,0},{3,1},{4,6},{5,7},{6,4},{7,5},{8,10},{9,11},{10,... | collective-permute-start | bytes 110600 | tf_op jit(solution)/shard_map/ppermute | solution.py:25
  26.5 3.6 %collective-permute-start.8 = (bf16[6,12,256]{2,1,0:T(8,128)(2,1)S(1)}, bf16[6,12,256]{2,1,0:T(8,128)(2,1)S(1)}, u32[]{:S(2)}, u32[]{:S(2)}) collective-permute-start(bf16[6,12,256]{2,1,0:T(8,128)(2,1)S(1)} %get-tuple-element.57), channel_id=1, source_target_pairs={{0,3},{1,0},{2,1},{3,2},{4,7},{5,4},{6,5},{7,6},{8,11},{9,8},{10,9... | collective-permute-start | bytes 110600 | tf_op jit(solution)/shard_map/ppermute | solution.py:25
  30.1 2.0 %copy-start.1 = (bf16[3,3,3,256,256]{4,3,2,1,0:T(8,128)(2,1)S(1)}, bf16[3,3,3,256,256]{4,3,2,1,0:T(8,128)(2,1)}, u32[]{:S(2)}) copy-start(bf16[3,3,3,256,256]{4,3,2,1,0:T(8,128)(2,1)} %refs_14_.1) | copy-start | bytes 10616836

commit v10 on v9

--- a/solution.py
+++ b/solution.py
@@ -16,13 +16,16 @@
 bf16 = jnp.bfloat16
 vmem_spec = pl.BlockSpec(memory_space=pltpu.VMEM)
 hbm_spec = pl.BlockSpec(memory_space=pltpu.HBM)
-smem_spec = pl.BlockSpec(memory_space=pltpu.SMEM)
 params = pltpu.CompilerParams(vmem_limit_bytes=30 * 1024 * 1024)
 
 
 def shifted(value, axis, shift):
     count = lax.axis_size(axis)
     return lax.ppermute(value, axis, [(i, (i + shift) % count) for i in range(count)])
+
+
+def place_here():
+    return lax.axis_index("row").astype(jnp.int32), lax.axis_index("col").astype(jnp.int32)
 
 
 def pair_swap(first, second, axis):
@@ -174,7 +177,8 @@
     return plan[0][0] * plan[0][1], plan[8] * (plan[9] if len(plan) > 9 else 1) ** 2
 
 
-def lateral_kernel(col_count, kept_count, here_ref, *refs):
+def lateral_kernel(col_count, kept_count, *refs):
+    here_ref = place_here()
     sources, refs = refs[: 6 + kept_count], refs[6 + kept_count :]
     (lat1_ref, lat2_ref), refs = refs[:2], refs[2:]
     pieces, refs = refs[:col_count], refs[col_count:]
@@ -231,7 +235,8 @@
         copy.wait()
 
 
-def bins_kernel(row_count, col_count, share, here_ref, table_ref, weight_ref, *refs):
+def bins_kernel(row_count, col_count, share, table_ref, weight_ref, *refs):
+    here_ref = place_here()
     blocks, pieces, messages, (bins_buf,) = (
         refs[:row_count],
         refs[row_count : row_count + col_count],
@@ -286,11 +291,12 @@
     return jnp.where((place_row >= 0.0) & (place_row < grid_rows), spread, 0.0)
 
 
-def feature_kernel(row_count, share, channels, plans, here_ref, weight_hbm, *refs):
+def feature_kernel(row_count, share, channels, plans, weight_hbm, *refs):
+    here_ref = place_here()
     blocks, refs = refs[:row_count], refs[row_count:]
-    late, refs = refs[:1], refs[1:]
-    (out_ref, spread_ref), kept, matrices = refs[:2], refs[2:3], refs[3 : 3 + len(plans)]
-    weight_ref, grid_buf, sems = refs[3 + len(plans) :]
+    late, refs = refs[:2], refs[2:]
+    (out_ref, spread_ref), kept, matrices = refs[:2], refs[2:4], refs[4 : 4 + len(plans)]
+    weight_ref, grid_buf, sems = refs[4 + len(plans) :]
     copies = [
         pltpu.make_async_copy(source, target, sems.at[number])
         for number, (source, target) in enumerate(zip((weight_hbm, *late), (weight_ref, *kept)))
@@ -320,7 +326,8 @@
         copy.wait()
 
 
-def neck_kernel(col_count, here_ref, weight_ref, bias_ref, taps_ref, spread_ref, *refs):
+def neck_kernel(col_count, weight_ref, bias_ref, taps_ref, spread_ref, *refs):
+    here_ref = place_here()
     messages, refs = refs[:col_count], refs[col_count:]
     windows, (bins_buf, acc_buf, term_buf) = refs[:col_count], refs[col_count:]
     rows, span, channels = windows[0].shape
@@ -358,7 +365,8 @@
         window[...] = term_buf[:, pl.ds(pl.multiple_of(target * width4, 8), span), :].astype(bf16)
 
 
-def rows_kernel(col_count, high3, wide3, here_ref, bias_ref, lat1_ref, lat2_ref, *refs):
+def rows_kernel(col_count, high3, wide3, bias_ref, lat1_ref, lat2_ref, *refs):
+    here_ref = place_here()
     messages, (lat3_ref, first_ref, second_ref, three_buf, low_buf, high_buf) = (
         refs[:col_count],
         refs[col_count:],
@@ -410,7 +418,8 @@
         store(tap, dot(small, weight).astype(bf16))
 
 
-def late_kernel(sizes, plans, top_count, here_ref, bias_ref, join_ref, *refs):
+def late_kernel(sizes, plans, top_count, bias_ref, join_ref, *refs):
+    here_ref = place_here()
     tops, refs = refs[:top_count], refs[top_count:]
     top_ref, base_ref, matrices, refs = refs[0], refs[1], refs[2 : 1 + len(plans)], refs[1 + len(plans) :]
     top_buf, small_buf, terms_buf, matrix_buf = refs
@@ -439,7 +448,8 @@
     base_ref[...] = dot(matrix_buf[...], terms_buf[...])
 
 
-def tail_kernel(sizes, part_count, here_ref, *refs):
+def tail_kernel(sizes, part_count, *refs):
+    here_ref = place_here()
     (high1, wide1), (high2, wide2), (high3, wide3), _, (row_count, col_count) = sizes
     quarters, refs = refs[:part_count], refs[part_count:]
     (
@@ -620,7 +630,7 @@
         copy.wait()
 
 
-def tail(here, top, base, lats, swapped, before, after, biases, weights, matrices, quarters, sizes):
+def tail(top, base, lats, swapped, before, after, biases, weights, matrices, quarters, sizes):
     one, _, _, _, _ = sizes
     channels = biases.shape[1]
     shapes = [window_shape(size, rim) for size in sizes[:3]]
@@ -630,7 +640,7 @@
     return pl.pallas_call(
         functools.partial(tail_kernel, sizes, len(quarters)),
         out_shape=jax.ShapeDtypeStruct((*one, channels), bf16),
-        in_specs=[smem_spec] + [vmem_spec] * len(inputs),
+        in_specs=[vmem_spec] * len(inputs),
         out_specs=hbm_spec,
         scratch_shapes=[
             pltpu.VMEM((rows1, pitch1, channels), f32),
@@ -658,7 +668,7 @@
         cost_estimate=pl.CostEstimate(
             flops=8_000_000_000, bytes_accessed=12_000_000, transcendentals=0
         ),
-    )(here, *inputs)
+    )(*inputs)
 
 
 def local(
@@ -678,7 +688,6 @@
 ):
     row_count = lax.axis_size("row")
     col_count = lax.axis_size("col")
-    here = jnp.stack([lax.axis_index("row"), lax.axis_index("col")]).astype(jnp.int32)
     high1, wide1 = level_one.shape[:2]
     high2, wide2 = level_two.shape[:2]
     high3, wide3 = level_three.shape[0], level_three.shape[1] // col_count
@@ -703,7 +712,7 @@
         [shape((high1, wide1, channels)), shape((high2, wide2, channels))]
         + [shape((window_rows + side_rows, channels))] * col_count
         + [shape(value.shape, value.dtype) for value in kept],
-        [smem_spec] + [hbm_spec] * (len(used) + len(kept)),
+        [hbm_spec] * (len(used) + len(kept)),
         [pltpu.VMEM(value.shape, value.dtype) for value in used]
         + [
             pltpu.VMEM((high3, level_three.shape[1] + 8, channels), f32),
@@ -714,7 +723,7 @@
         ],
         300_000_000,
         4_000_000,
-    )(here, *(in_hbm(value) for value in (*used, *kept)))
+    )(*(in_hbm(value) for value in (*used, *kept)))
     pieces = rest[:col_count]
     bias_table, level_four, table, bin_weight = rest[col_count:]
     blocks = [level_four] + others
@@ -725,11 +734,11 @@
             shape((window_rows + cell_rows + (side_rows if shift in near else 0), channels))
             for shift in range(col_count)
         ],
-        [smem_spec] + [vmem_spec] * (2 + row_count + col_count),
+        [vmem_spec] * (2 + row_count + col_count),
         [pltpu.VMEM((table.shape[0], channels), f32)],
         100_000_000,
         1_000_000,
-    )(here, table, bin_weight, *blocks, *pieces)
+    )(table, bin_weight, *blocks, *pieces)
 
     received = [messages[0]] + [
         shifted(messages[shift], "col", shift) for shift in range(1, col_count)
@@ -743,8 +752,8 @@
         (row_count, col_count),
     )
     plans, late_plans = stretches(sizes)
-    late = (neck_pooled,)
-    taps, spread, neck_pooled, *matrices = call(
+    late = (neck_pooled, smooth_weight)
+    taps, spread, neck_pooled, smooth_weight, *matrices = call(
         functools.partial(feature_kernel, row_count, share_ppm, channels, plans),
         [
             shape((3, rows * grid_cols, channels), f32),
@@ -752,7 +761,7 @@
         ]
         + [shape(value.shape) for value in late]
         + [shape(matrix_shape(plan)) for plan in plans],
-        [smem_spec, hbm_spec] + [vmem_spec] * row_count + [hbm_spec] * len(late),
+        [hbm_spec] + [vmem_spec] * row_count + [hbm_spec] * len(late),
         [
             pltpu.VMEM(neck_feature.shape, bf16),
             pltpu.VMEM((grid_rows + 2 * rim + 2, grid_cols, part_four), bf16),
@@ -760,12 +769,12 @@
         ],
         700_000_000,
         12_000_000,
-    )(here, in_hbm(neck_feature), *blocks, *(in_hbm(value) for value in late))
+    )(in_hbm(neck_feature), *blocks, *(in_hbm(value) for value in late))
     span4 = wide4 + 2 * rim
     windows = call(
         functools.partial(neck_kernel, col_count),
         [shape((rows, span4, channels))] * col_count,
-        [smem_spec] + [vmem_spec] * (4 + col_count),
+        [vmem_spec] * (4 + col_count),
         [
             pltpu.VMEM((cell_rows, channels), f32),
             pltpu.VMEM((3, rows * grid_cols + 16, channels), f32),
@@ -773,7 +782,7 @@
         ],
         300_000_000,
         3_000_000,
-    )(here, neck_pooled, bias_table, taps, spread, *received)
+    )(neck_pooled, bias_table, taps, spread, *received)
 
     tops = [windows[0]] + [shifted(windows[shift], "col", shift) for shift in range(1, col_count)]
     span3 = wide3 + 2 * rim
@@ -781,7 +790,7 @@
     lat3, first_rows, second_rows = call(
         functools.partial(rows_kernel, col_count, high3, wide3),
         [shape((high3, span3, channels))] + [shape((packed, channels))] * 2,
-        [smem_spec] + [vmem_spec] * (3 + col_count),
+        [vmem_spec] * (3 + col_count),
         [
             pltpu.VMEM((high3, (span3 + 7) // 8 * 8, channels), f32),
             pltpu.VMEM((packed, channels), f32),
@@ -789,7 +798,7 @@
         ],
         1_000_000,
         1_000_000,
-    )(here, bias_table, lat1, lat2, *received)
+    )(bias_table, lat1, lat2, *received)
     swapped = pair_swap(first_rows, second_rows, "row")
     small = late_plans[0][8]
     top_pitch = window_shape((high4, wide4), rim)[1]
@@ -800,7 +809,7 @@
             shape((high1 * wide1, channels), f32),
         ]
         + [shape(matrix_shape(plan)) for plan in late_plans[1:]],
-        [smem_spec] + [vmem_spec] * (2 + col_count),
+        [vmem_spec] * (2 + col_count),
         [
             pltpu.VMEM((rows, top_pitch, channels), f32),
             pltpu.VMEM((small, channels), f32),
@@ -809,9 +818,8 @@
         ],
         700_000_000,
         5_000_000,
-    )(here, bias_table, join_weight, *tops)
+    )(bias_table, join_weight, *tops)
     return tail(
-        here,
         top,
         base,
         (lat1, lat2, lat3),

time: 41.7 us -> 38.5 us (0.923)
  Pallas kernels: 19.9 us -> 16.5 us
  waiting for transfers between devices: 6.47 us -> 7.04 us
    pallas_call x1, Pallas kernels: 8.87 us -> 8.1 us  [tail(): pl.pallas_call(functools.partial(tail_kernel, sizes, len(quarters)), out_...]
    ppermute x9, waiting for transfers between devices: 6.46 us -> 7.03 us  [shifted(): lax.ppermute(value, axis, [(i, (i + shift) % count) for i in range(count)])]
    pallas_call x1, Pallas kernels: 1.75 us -> 1.2 us  [local(): call(functools.partial(late_kernel, sizes, late_plans, col_count), [shape...]
    pallas_call x1, Pallas kernels: 1.19 us -> 0.65 us  [local(): call(functools.partial(bins_kernel, row_count, col_count, share_ppm), [sh...]
    pallas_call x1, Pallas kernels: 1.71 us -> 1.17 us  [local(): call(functools.partial(neck_kernel, col_count), [shape((rows, span4, chan...]
    pallas_call x1, Pallas kernels: 0.69 us -> 0.15 us  [local(): call(functools.partial(rows_kernel, col_count, high3, wide3), [shape((hig...]
    pallas_call x1, Pallas kernels: 2.64 us -> 2.11 us  [local(): call(functools.partial(lateral_kernel, col_count, len(kept)), [shape((hig...]
  transfers between devices with their start and end apart: 11 -> 11, of which waited for: 4 -> 4; matrix products, arithmetic and copies ran while one was open for 0% -> 0% of each run, Pallas kernels for 22% -> 20%
where the time goes in v10:
time: 38.5 us; the launch traced here: 38 us
  Pallas kernels  16.5 us (43%)
  starting transfers between devices  14.2 us (37%)
  waiting for transfers between devices  7.04 us (18%)
    ppermute x9, starting transfers between devices, shifted(): lax.ppermute(value, axis, [(i, (i + shift) % count) for i in range(count)])  9.84 us
    pallas_call x1, Pallas kernels, tail(): pl.pallas_call(functools.partial(tail_kernel, sizes, len(quarters)), out_...  8.1 us
    ppermute x9, waiting for transfers between devices, shifted(): lax.ppermute(value, axis, [(i, (i + shift) % count) for i in range(count)])  7.03 us
    pallas_call x1, Pallas kernels, local(): call(functools.partial(feature_kernel, row_count, share_ppm, channels, pl...  3.1 us
    ppermute x1, starting transfers between devices, pair_swap(): lax.ppermute(second, axis, pairs(1))  2.66 us
    pallas_call x1, Pallas kernels, local(): call(functools.partial(lateral_kernel, col_count, len(kept)), [shape((hig...  2.11 us
    ppermute x1, starting transfers between devices, pair_swap(): lax.ppermute(first, axis, pairs(0))  1.67 us
    pallas_call x1, Pallas kernels, local(): call(functools.partial(late_kernel, sizes, late_plans, col_count), [shape...  1.2 us
  transfers between devices with their start and end apart: 11, of which 4 were waited for; matrix products, arithmetic and copies ran while one was open for 0% of the time, Pallas kernels for 20%

profile of v10, /device:TPU:1, one launch (start us, length us, event | category | flops | bytes accessed | tf_op | source)
XLA Modules:
  0.0 38.0 jit_solution(9131697263085987964)
XLA Ops:
  0.0 2.6 %collective-permute-start = (bf16[2,32,384]{2,1,0:T(8,128)(2,1)}, bf16[2,32,384]{2,1,0:T(8,128)(2,1)S(1)}, u32[]{:S(2)}, u32[]{:S(2)}) collective-permute-start(bf16[2,32,384]{2,1,0:T(8,128)(2,1)} %refs_7_.1), channel_id=1, source_target_pairs={{0,4},{4,8},{8,12},{12,0},{1,5},{5,9},{9,13},{13,1},{2,6},{6,10},{... | collective-permute-start | bytes 147464 | tf_op jit(solution)/shard_map/ppermute | solution.py:24
  2.6 0.0 collective-permute-start.2
  2.6 0.1 collective-permute-start.1
  2.7 2.1 %shard_map.136 = (bf16[16,64,256]{2,1,0:T(8,128)(2,1)S(1)}, bf16[8,32,256]{2,1,0:T(8,128)(2,1)S(1)}, bf16[128,256]{1,0:T(8,128)(2,1)S(1)}, bf16[128,256]{1,0:T(8...) custom-call(bf16[16,64,192]{2,1,0:T(8,128)(2,1)} %refs_0_.1, ...), custom_call_target="tpu_custom_call" | custom-call | flops 300000000 | bytes 4000000 | tf_op jit(solution)/shard_map/pallas_call | solution.py:710
  4.8 0.0 collective-permute-done.refs_1_
  4.8 1.5 %collective-permute-done.2.refs_3_ = bf16[2,32,384]{2,1,0:T(8,128)(2,1)S(1)} collective-permute-done((bf16[2,32,384]{2,1,0:T(8,128)(2,1)}, bf16[2,32,384]{2,1,0:T(8,128)(2,1)S(1)}, u32[]{:S(2)}, u32[]{:S(2)}) %collective-permute-start.2) | collective-permute-done | bytes 49184 | tf_op jit(solution)/shard_map/ppermute | solution.py:24
  6.3 0.0 collective-permute-done.1.refs_2_
  6.3 0.6 %shard_map.138 = (bf16[120,256]{1,0:T(8,128)(2,1)S(1)}, bf16[168,256]{1,0:T(8,128)(2,1)S(1)}, bf16[120,256]{1,0:T(8,128)(2,1)S(1)}, bf16[168,256]{1,0:T(8,128)(2,1)S(1)}) custom-call(f32[72,8]{1,0:T(8,128)S(1)} %get-tuple-element.45.table_ref, bf16[4,384,256]{2,1,0:T(8,128)(2,1)S(1)} %get-tuple-element.46.weight_ref, ...), custom_call_target="tpu_custom_call" | custom-call | flops 100000000 | bytes 1000000 | tf_op jit(solution)/shard_map/pallas_call | solution.py:731
  7.0 1.3 %collective-permute-start.3 = (bf16[168,256]{1,0:T(8,128)(2,1)S(1)}, bf16[168,256]{1,0:T(8,128)(2,1)S(1)}, u32[]{:S(2)}, u32[]{:S(2)}) collective-permute-start(bf16[168,256]{1,0:T(8,128)(2,1)S(1)} %get-tuple-element.52), channel_id=1, source_target_pairs={{0,1},{1,2},{2,3},{3,0},{4,5},{5,6},{6,7},{7,4},{8,9},{9,10},{10,1... | collective-permute-start | bytes 258056 | tf_op jit(solution)/shard_map/ppermute | solution.py:24
  8.3 2.1 %collective-permute-start.5 = (bf16[168,256]{1,0:T(8,128)(2,1)S(1)}, bf16[168,256]{1,0:T(8,128)(2,1)S(1)}, u32[]{:S(2)}, u32[]{:S(2)}) collective-permute-start(bf16[168,256]{1,0:T(8,128)(2,1)S(1)} %get-tuple-element.54), channel_id=1, source_target_pairs={{0,3},{1,0},{2,1},{3,2},{4,7},{5,4},{6,5},{7,6},{8,11},{9,8},{10,9... | collective-permute-start | bytes 258056 | tf_op jit(solution)/shard_map/ppermute | solution.py:24
  10.4 0.0 slice-start
  10.4 0.0 slice-start.1
  10.4 0.4 %collective-permute-start.4 = (bf16[120,256]{1,0:T(8,128)(2,1)S(1)}, bf16[120,256]{1,0:T(8,128)(2,1)S(1)}, u32[]{:S(2)}, u32[]{:S(2)}) collective-permute-start(bf16[120,256]{1,0:T(8,128)(2,1)S(1)} %get-tuple-element.53), channel_id=1, source_target_pairs={{0,2},{1,3},{2,0},{3,1},{4,6},{5,7},{6,4},{7,5},{8,10},{9,11},{10,... | collective-permute-start | bytes 184328 | tf_op jit(solution)/shard_map/ppermute | solution.py:24
  10.8 3.1 %shard_map.137 = (f32[3,192,256]{2,1,0:T(8,128)S(1)}, f32[256,40]{1,0:T(8,128)S(1)}, bf16[3,3,256,256]{3,2,1,0:T(8,128)(2,1)S(1)}, bf16[3,3,3,256,256]{4,3,2,1,0...) custom-call(bf16[3,3,384,256]{3,2,1,0:T(8,128)(2,1)} %weight_hbm.1, ...), custom_call_target="tpu_custom_call" | custom-call | flops 700000000 | bytes 12000000 | tf_op jit(solution)/shard_map/pallas_call | solution.py:756
  13.9 3.0 %collective-permute-done.4.refs_2_ = bf16[120,256]{1,0:T(8,128)(2,1)S(1)} collective-permute-done((bf16[120,256]{1,0:T(8,128)(2,1)S(1)}, bf16[120,256]{1,0:T(8,128)(2,1)S(1)}, u32[]{:S(2)}, u32[]{:S(2)}) %collective-permute-start.4) | collective-permute-done | bytes 61472 | tf_op jit(solution)/shard_map/ppermute | solution.py:24
  16.9 0.0 collective-permute-done.3.refs_1_.refs_11_
  16.9 0.0 collective-permute-done.5.refs_3_.refs_12_
  16.9 0.2 shard_map.141
  17.0 1.7 %collective-permute-start.9 = (bf16[248,256]{1,0:T(8,128)(2,1)S(1)}, bf16[248,256]{1,0:T(8,128)(2,1)S(1)}, u32[]{:S(2)}, u32[]{:S(2)}) collective-permute-start(bf16[248,256]{1,0:T(8,128)(2,1)S(1)} %get-tuple-element.68), channel_id=1, source_target_pairs={{0,4},{4,0},{8,12},{12,8},{1,5},{5,1},{9,13},{13,9},{2,6},{6,2},{1... | collective-permute-start | bytes 380936 | tf_op jit(solution)/shard_map/ppermute | solution.py:41
  18.7 2.7 %collective-permute-start.10 = (bf16[248,256]{1,0:T(8,128)(2,1)S(1)}, bf16[248,256]{1,0:T(8,128)(2,1)S(1)}, u32[]{:S(2)}, u32[]{:S(2)}) collective-permute-start(bf16[248,256]{1,0:T(8,128)(2,1)S(1)} %get-tuple-element.69), channel_id=1, source_target_pairs={{4,8},{8,4},{5,9},{9,5},{6,10},{10,6},{7,11},{11,7},{20,24},{24,20... | collective-permute-start | bytes 380936 | tf_op jit(solution)/shard_map/ppermute | solution.py:41
  21.4 1.2 %shard_map.139 = (bf16[6,12,256]{2,1,0:T(8,128)(2,1)S(1)}, bf16[6,12,256]{2,1,0:T(8,128)(2,1)S(1)}, bf16[6,12,256]{2,1,0:T(8,128)(2,1)S(1)}, bf16[6,12,256]{2,1,0:T(8,128)(2,1)S(1)}) custom-call(bf16[3,3,256,256]{3,2,1,0:T(8,128)(2,1)S(1)} %get-tuple-element.42.weight_ref, f32[12,256]{1,0:T(8,128)S(1)} %get-tuple-element.40.bias_ref.refs_13_, ...), custom_call_target="tpu_custom_call" | custom-call | flops 300000000 | bytes 3000000 | tf_op jit(solution)/shard_map/pallas_call | solution.py:774
  22.5 0.1 collective-permute-start.6
  22.6 2.2 %collective-permute-start.7 = (bf16[6,12,256]{2,1,0:T(8,128)(2,1)S(1)}, bf16[6,12,256]{2,1,0:T(8,128)(2,1)S(1)}, u32[]{:S(2)}, u32[]{:S(2)}) collective-permute-start(bf16[6,12,256]{2,1,0:T(8,128)(2,1)S(1)} %get-tuple-element.57), channel_id=1, source_target_pairs={{0,2},{1,3},{2,0},{3,1},{4,6},{5,7},{6,4},{7,5},{8,10},{9,11},{10,... | collective-permute-start | bytes 110600 | tf_op jit(solution)/shard_map/ppermute | solution.py:24
  24.8 1.1 %collective-permute-start.8 = (bf16[6,12,256]{2,1,0:T(8,128)(2,1)S(1)}, bf16[6,12,256]{2,1,0:T(8,128)(2,1)S(1)}, u32[]{:S(2)}, u32[]{:S(2)}) collective-permute-start(bf16[6,12,256]{2,1,0:T(8,128)(2,1)S(1)} %get-tuple-element.58), channel_id=1, source_target_pairs={{0,3},{1,0},{2,1},{3,2},{4,7},{5,4},{6,5},{7,6},{8,11},{9,8},{10,9... | collective-permute-start | bytes 110600 | tf_op jit(solution)/shard_map/ppermute | solution.py:24
  25.9 1.6 %collective-permute-done.6.refs_1_ = bf16[6,12,256]{2,1,0:T(8,128)(2,1)S(1)} collective-permute-done((bf16[6,12,256]{2,1,0:T(8,128)(2,1)S(1)}, bf16[6,12,256]{2,1,0:T(8,128)(2,1)S(1)}, u32[]{:S(2)}, u32[]{:S(2)}) %collective-permute-start.6) | collective-permute-done | bytes 36896 | tf_op jit(solution)/shard_map/ppermute | solution.py:24
  27.5 0.0 collective-permute-done.7.refs_2_
  27.5 1.0 %collective-permute-done.8.refs_3_ = bf16[6,12,256]{2,1,0:T(8,128)(2,1)S(1)} collective-permute-done((bf16[6,12,256]{2,1,0:T(8,128)(2,1)S(1)}, bf16[6,12,256]{2,1,0:T(8,128)(2,1)S(1)}, u32[]{:S(2)}, u32[]{:S(2)}) %collective-permute-start.8) | collective-permute-done | bytes 36896 | tf_op jit(solution)/shard_map/ppermute | solution.py:24
  28.5 0.0 slice-done
  28.5 0.0 slice-done.1
  28.5 1.2 %shard_map.140 = (bf16[96,256]{1,0:T(8,128)(2,1)S(1)}, f32[1024,256]{1,0:T(8,128)S(1)}, bf16[256,1008]{1,0:T(8,128)(2,1)S(1)}, bf16[256,1008]{1,0:T(8,128)(2,1)S...) custom-call(f32[12,256]{1,0:T(8,128)S(1)} %get-tuple-element.40.bias_ref.refs_13_, ...), custom_call_target="tpu_custom_call" | custom-call | flops 700000000 | bytes 5000000 | tf_op jit(solution)/shard_map/pallas_call | solution.py:805
  29.7 0.0 collective-permute-done.9.refs_9_
  29.7 0.0 collective-permute-done.10.refs_10_
  29.7 8.1 %shard_map.142 = bf16[16,64,256]{2,1,0:T(8,128)(2,1)} custom-call(bf16[256,1008]{1,0:T(8,128)(2,1)S(1)} %get-tuple-element.59.refs_0_, bf16[256,1008]{1,0:T(8,128)(2,1)S(1)} %get-tuple-element.60.refs_1_, bf16[256,1008]{1,0:T(8,128)(2,1)S(1)} %get-tuple-element.61.refs_2_, bf16[256,1008]{1,0:T(8,128)(2,1)S(1)} %get-tuple-element.62.refs_3_, ...), custom_call_target="tpu_custom_call" | custom-call | flops 8000000000 | bytes 12000000 | tf_op jit(solution)/shard_map/pallas_call | solution.py:640
  (1 shorter events, 0.0 us)
Async XLA Ops:
  0.0 4.8 %collective-permute-start = (bf16[2,32,384]{2,1,0:T(8,128)(2,1)}, bf16[2,32,384]{2,1,0:T(8,128)(2,1)S(1)}, u32[]{:S(2)}, u32[]{:S(2)}) collective-permute-start(bf16[2,32,384]{2,1,0:T(8,128)(2,1)} %refs_7_.1), channel_id=1, source_target_pairs={{0,4},{4,8},{8,12},{12,0},{1,5},{5,9},{9,13},{13,1},{2,6},{6,10},{... | collective-permute-start | bytes 147464 | tf_op jit(solution)/shard_map/ppermute | solution.py:24
  2.6 3.7 %collective-permute-start.2 = (bf16[2,32,384]{2,1,0:T(8,128)(2,1)}, bf16[2,32,384]{2,1,0:T(8,128)(2,1)S(1)}, u32[]{:S(2)}, u32[]{:S(2)}) collective-permute-start(bf16[2,32,384]{2,1,0:T(8,128)(2,1)} %refs_7_.1), channel_id=1, source_target_pairs={{0,12},{4,0},{8,4},{12,8},{1,13},{5,1},{9,5},{13,9},{2,14},{6,2},{... | collective-permute-start | bytes 147464 | tf_op jit(solution)/shard_map/ppermute | solution.py:24
  2.6 3.7 %collective-permute-start.1 = (bf16[2,32,384]{2,1,0:T(8,128)(2,1)}, bf16[2,32,384]{2,1,0:T(8,128)(2,1)S(1)}, u32[]{:S(2)}, u32[]{:S(2)}) collective-permute-start(bf16[2,32,384]{2,1,0:T(8,128)(2,1)} %refs_7_.1), channel_id=1, source_target_pairs={{0,8},{4,12},{8,0},{12,4},{1,9},{5,13},{9,1},{13,5},{2,10},{6,14},... | collective-permute-start | bytes 147464 | tf_op jit(solution)/shard_map/ppermute | solution.py:24
  7.0 9.9 %collective-permute-start.3 = (bf16[168,256]{1,0:T(8,128)(2,1)S(1)}, bf16[168,256]{1,0:T(8,128)(2,1)S(1)}, u32[]{:S(2)}, u32[]{:S(2)}) collective-permute-start(bf16[168,256]{1,0:T(8,128)(2,1)S(1)} %get-tuple-element.52), channel_id=1, source_target_pairs={{0,1},{1,2},{2,3},{3,0},{4,5},{5,6},{6,7},{7,4},{8,9},{9,10},{10,1... | collective-permute-start | bytes 258056 | tf_op jit(solution)/shard_map/ppermute | solution.py:24
  8.3 8.6 %collective-permute-start.5 = (bf16[168,256]{1,0:T(8,128)(2,1)S(1)}, bf16[168,256]{1,0:T(8,128)(2,1)S(1)}, u32[]{:S(2)}, u32[]{:S(2)}) collective-permute-start(bf16[168,256]{1,0:T(8,128)(2,1)S(1)} %get-tuple-element.54), channel_id=1, source_target_pairs={{0,3},{1,0},{2,1},{3,2},{4,7},{5,4},{6,5},{7,6},{8,11},{9,8},{10,9... | collective-permute-start | bytes 258056 | tf_op jit(solution)/shard_map/ppermute | solution.py:24
  10.4 18.1 %slice-start = ((s8[4718592]{0:T(1024)(128)(4,1)}), s8[4194304]{0:T(1024)(128)(4,1)S(1)}, s32[]{:S(2)}) async-start(s8[4718592]{0:T(1024)(128)(4,1)} %bitcast), calls=%async_computation | async-start | bytes 8388608
  10.4 18.1 %slice-start.1 = ((s8[4718592]{0:T(1024)(128)(4,1)}), s8[524288]{0:T(1024)(128)(4,1)S(1)}, s32[]{:S(2)}) async-start(s8[4718592]{0:T(1024)(128)(4,1)} %bitcast), calls=%async_computation.1 | async-start | bytes 1048576
  10.4 6.5 %collective-permute-start.4 = (bf16[120,256]{1,0:T(8,128)(2,1)S(1)}, bf16[120,256]{1,0:T(8,128)(2,1)S(1)}, u32[]{:S(2)}, u32[]{:S(2)}) collective-permute-start(bf16[120,256]{1,0:T(8,128)(2,1)S(1)} %get-tuple-element.53), channel_id=1, source_target_pairs={{0,2},{1,3},{2,0},{3,1},{4,6},{5,7},{6,4},{7,5},{8,10},{9,11},{10,... | collective-permute-start | bytes 184328 | tf_op jit(solution)/shard_map/ppermute | solution.py:24
  17.0 12.6 %collective-permute-start.9 = (bf16[248,256]{1,0:T(8,128)(2,1)S(1)}, bf16[248,256]{1,0:T(8,128)(2,1)S(1)}, u32[]{:S(2)}, u32[]{:S(2)}) collective-permute-start(bf16[248,256]{1,0:T(8,128)(2,1)S(1)} %get-tuple-element.68), channel_id=1, source_target_pairs={{0,4},{4,0},{8,12},{12,8},{1,5},{5,1},{9,13},{13,9},{2,6},{6,2},{1... | collective-permute-start | bytes 380936 | tf_op jit(solution)/shard_map/ppermute | solution.py:41
  18.7 11.0 %collective-permute-start.10 = (bf16[248,256]{1,0:T(8,128)(2,1)S(1)}, bf16[248,256]{1,0:T(8,128)(2,1)S(1)}, u32[]{:S(2)}, u32[]{:S(2)}) collective-permute-start(bf16[248,256]{1,0:T(8,128)(2,1)S(1)} %get-tuple-element.69), channel_id=1, source_target_pairs={{4,8},{8,4},{5,9},{9,5},{6,10},{10,6},{7,11},{11,7},{20,24},{24,20... | collective-permute-start | bytes 380936 | tf_op jit(solution)/shard_map/ppermute | solution.py:41
  22.5 5.0 %collective-permute-start.6 = (bf16[6,12,256]{2,1,0:T(8,128)(2,1)S(1)}, bf16[6,12,256]{2,1,0:T(8,128)(2,1)S(1)}, u32[]{:S(2)}, u32[]{:S(2)}) collective-permute-start(bf16[6,12,256]{2,1,0:T(8,128)(2,1)S(1)} %get-tuple-element.56), channel_id=1, source_target_pairs={{0,1},{1,2},{2,3},{3,0},{4,5},{5,6},{6,7},{7,4},{8,9},{9,10},{10,1... | collective-permute-start | bytes 110600 | tf_op jit(solution)/shard_map/ppermute | solution.py:24
  22.6 4.9 %collective-permute-start.7 = (bf16[6,12,256]{2,1,0:T(8,128)(2,1)S(1)}, bf16[6,12,256]{2,1,0:T(8,128)(2,1)S(1)}, u32[]{:S(2)}, u32[]{:S(2)}) collective-permute-start(bf16[6,12,256]{2,1,0:T(8,128)(2,1)S(1)} %get-tuple-element.57), channel_id=1, source_target_pairs={{0,2},{1,3},{2,0},{3,1},{4,6},{5,7},{6,4},{7,5},{8,10},{9,11},{10,... | collective-permute-start | bytes 110600 | tf_op jit(solution)/shard_map/ppermute | solution.py:24
  24.8 3.7 %collective-permute-start.8 = (bf16[6,12,256]{2,1,0:T(8,128)(2,1)S(1)}, bf16[6,12,256]{2,1,0:T(8,128)(2,1)S(1)}, u32[]{:S(2)}, u32[]{:S(2)}) collective-permute-start(bf16[6,12,256]{2,1,0:T(8,128)(2,1)S(1)} %get-tuple-element.58), channel_id=1, source_target_pairs={{0,3},{1,0},{2,1},{3,2},{4,7},{5,4},{6,5},{7,6},{8,11},{9,8},{10,9... | collective-permute-start | bytes 110600 | tf_op jit(solution)/shard_map/ppermute | solution.py:24

commit v11 on v10

--- a/solution.py
+++ b/solution.py
@@ -26,19 +26,6 @@
 
 def place_here():
     return lax.axis_index("row").astype(jnp.int32), lax.axis_index("col").astype(jnp.int32)
-
-
-def pair_swap(first, second, axis):
-    count = lax.axis_size(axis)
-
-    def pairs(start):
-        return [
-            edge
-            for i in range(start, count - 1, 2)
-            for edge in ((i, i + 1), (i + 1, i))
-        ]
-
-    return lax.ppermute(first, axis, pairs(0)), lax.ppermute(second, axis, pairs(1))
 
 
 cell_rows = max(bin_sides) ** 2 + 4
@@ -405,10 +392,8 @@
             row = high3 - rim + step if last else step
             pack_buf[start : start + span, :] = three_buf[row, :span, :]
             start += span
-    even = lax.rem(here_ref[0], 2) == 0
-    low, high = low_buf[...], high_buf[...]
-    first_ref[...] = jnp.where(even, high, low).astype(bf16)
-    second_ref[...] = jnp.where(even, low, high).astype(bf16)
+    first_ref[...] = high_buf[...].astype(bf16)
+    second_ref[...] = low_buf[...].astype(bf16)
 
 
 def tap_terms(small, weight_ref, first, store):
@@ -493,10 +478,8 @@
     ) = refs
     channels = bias_ref.shape[1]
 
-    even = lax.rem(here_ref[0], 2) == 0
-    first, second = first_ref[...].astype(f32), second_ref[...].astype(f32)
-    above_buf[...] = jnp.where(even, second, first)
-    below_buf[...] = jnp.where(even, first, second)
+    above_buf[...] = jnp.where(here_ref[0] > 0, first_ref[...].astype(f32), 0.0)
+    below_buf[...] = jnp.where(here_ref[0] < row_count - 1, second_ref[...].astype(f32), 0.0)
     side_start = high3 * (wide3 + 2 * rim)
     row_start = 0
     for ref, buf, high, wide in (
@@ -799,7 +782,7 @@
         1_000_000,
         1_000_000,
     )(bias_table, lat1, lat2, *received)
-    swapped = pair_swap(first_rows, second_rows, "row")
+    swapped = shifted(first_rows, "row", 1), shifted(second_rows, "row", row_count - 1)
     small = late_plans[0][8]
     top_pitch = window_shape((high4, wide4), rim)[1]
     top, base, *quarters = call(

time: 38.5 us -> 38.2 us (level)
  the two profiles are of different devices: /device:TPU:1 before, /device:TPU:0 now
where the time goes in v11:
time: 38.2 us; the launch traced here: 38 us
  Pallas kernels  16.6 us (43%)
  starting transfers between devices  15 us (39%)
  waiting for transfers between devices  6.08 us (16%)
    ppermute x11, starting transfers between devices, shifted(): lax.ppermute(value, axis, [(i, (i + shift) % count) for i in range(count)])  15 us
    pallas_call x1, Pallas kernels, tail(): pl.pallas_call(functools.partial(tail_kernel, sizes, len(quarters)), out_...  8.12 us
    ppermute x11, waiting for transfers between devices, shifted(): lax.ppermute(value, axis, [(i, (i + shift) % count) for i in range(count)])  6.08 us
    pallas_call x1, Pallas kernels, local(): call(functools.partial(feature_kernel, row_count, share_ppm, channels, pl...  3.3 us
    pallas_call x1, Pallas kernels, local(): call(functools.partial(lateral_kernel, col_count, len(kept)), [shape((hig...  2.1 us
    pallas_call x1, Pallas kernels, local(): call(functools.partial(late_kernel, sizes, late_plans, col_count), [shape...  1.2 us
    pallas_call x1, Pallas kernels, local(): call(functools.partial(neck_kernel, col_count), [shape((rows, span4, chan...  1.17 us
  transfers between devices with their start and end apart: 11, of which 5 were waited for; matrix products, arithmetic and copies ran while one was open for 0% of the time, Pallas kernels for 20%

profile of v11, /device:TPU:0, one launch (start us, length us, event | category | flops | bytes accessed | tf_op | source)
XLA Modules:
  0.0 38.0 jit_solution(15210410150064502413)
XLA Ops:
  0.0 0.5 %collective-permute-start = (bf16[2,32,384]{2,1,0:T(8,128)(2,1)}, bf16[2,32,384]{2,1,0:T(8,128)(2,1)S(1)}, u32[]{:S(2)}, u32[]{:S(2)}) collective-permute-start(bf16[2,32,384]{2,1,0:T(8,128)(2,1)} %refs_7_.1), channel_id=1, source_target_pairs={{0,4},{4,8},{8,12},{12,0},{1,5},{5,9},{9,13},{13,1},{2,6},{6,10},{... | collective-permute-start | bytes 147464 | tf_op jit(solution)/shard_map/ppermute | solution.py:24
  0.5 1.9 %collective-permute-start.2 = (bf16[2,32,384]{2,1,0:T(8,128)(2,1)}, bf16[2,32,384]{2,1,0:T(8,128)(2,1)S(1)}, u32[]{:S(2)}, u32[]{:S(2)}) collective-permute-start(bf16[2,32,384]{2,1,0:T(8,128)(2,1)} %refs_7_.1), channel_id=1, source_target_pairs={{0,12},{4,0},{8,4},{12,8},{1,13},{5,1},{9,5},{13,9},{2,14},{6,2},{... | collective-permute-start | bytes 147464 | tf_op jit(solution)/shard_map/ppermute | solution.py:24
  2.4 2.3 %collective-permute-start.1 = (bf16[2,32,384]{2,1,0:T(8,128)(2,1)}, bf16[2,32,384]{2,1,0:T(8,128)(2,1)S(1)}, u32[]{:S(2)}, u32[]{:S(2)}) collective-permute-start(bf16[2,32,384]{2,1,0:T(8,128)(2,1)} %refs_7_.1), channel_id=1, source_target_pairs={{0,8},{4,12},{8,0},{12,4},{1,9},{5,13},{9,1},{13,5},{2,10},{6,14},... | collective-permute-start | bytes 147464 | tf_op jit(solution)/shard_map/ppermute | solution.py:24
  4.7 2.1 %shard_map.136 = (bf16[16,64,256]{2,1,0:T(8,128)(2,1)S(1)}, bf16[8,32,256]{2,1,0:T(8,128)(2,1)S(1)}, bf16[128,256]{1,0:T(8,128)(2,1)S(1)}, bf16[128,256]{1,0:T(8...) custom-call(bf16[16,64,192]{2,1,0:T(8,128)(2,1)} %refs_0_.1, ...), custom_call_target="tpu_custom_call" | custom-call | flops 300000000 | bytes 4000000 | tf_op jit(solution)/shard_map/pallas_call | solution.py:693
  6.8 0.0 collective-permute-done.refs_1_
  6.8 0.0 collective-permute-done.2.refs_3_
  6.8 0.7 %collective-permute-done.1.refs_2_ = bf16[2,32,384]{2,1,0:T(8,128)(2,1)S(1)} collective-permute-done((bf16[2,32,384]{2,1,0:T(8,128)(2,1)}, bf16[2,32,384]{2,1,0:T(8,128)(2,1)S(1)}, u32[]{:S(2)}, u32[]{:S(2)}) %collective-permute-start.1) | collective-permute-done | bytes 49184 | tf_op jit(solution)/shard_map/ppermute | solution.py:24
  7.5 0.6 %shard_map.138 = (bf16[120,256]{1,0:T(8,128)(2,1)S(1)}, bf16[168,256]{1,0:T(8,128)(2,1)S(1)}, bf16[120,256]{1,0:T(8,128)(2,1)S(1)}, bf16[168,256]{1,0:T(8,128)(2,1)S(1)}) custom-call(f32[72,8]{1,0:T(8,128)S(1)} %get-tuple-element.45.table_ref, bf16[4,384,256]{2,1,0:T(8,128)(2,1)S(1)} %get-tuple-element.46.weight_ref, ...), custom_call_target="tpu_custom_call" | custom-call | flops 100000000 | bytes 1000000 | tf_op jit(solution)/shard_map/pallas_call | solution.py:714
  8.2 1.6 %collective-permute-start.3 = (bf16[168,256]{1,0:T(8,128)(2,1)S(1)}, bf16[168,256]{1,0:T(8,128)(2,1)S(1)}, u32[]{:S(2)}, u32[]{:S(2)}) collective-permute-start(bf16[168,256]{1,0:T(8,128)(2,1)S(1)} %get-tuple-element.52), channel_id=1, source_target_pairs={{0,1},{1,2},{2,3},{3,0},{4,5},{5,6},{6,7},{7,4},{8,9},{9,10},{10,1... | collective-permute-start | bytes 258056 | tf_op jit(solution)/shard_map/ppermute | solution.py:24
  9.8 2.2 %collective-permute-start.5 = (bf16[168,256]{1,0:T(8,128)(2,1)S(1)}, bf16[168,256]{1,0:T(8,128)(2,1)S(1)}, u32[]{:S(2)}, u32[]{:S(2)}) collective-permute-start(bf16[168,256]{1,0:T(8,128)(2,1)S(1)} %get-tuple-element.54), channel_id=1, source_target_pairs={{0,3},{1,0},{2,1},{3,2},{4,7},{5,4},{6,5},{7,6},{8,11},{9,8},{10,9... | collective-permute-start | bytes 258056 | tf_op jit(solution)/shard_map/ppermute | solution.py:24
  12.0 0.0 slice-start
  12.0 0.0 slice-start.1
  12.0 0.8 %collective-permute-start.4 = (bf16[120,256]{1,0:T(8,128)(2,1)S(1)}, bf16[120,256]{1,0:T(8,128)(2,1)S(1)}, u32[]{:S(2)}, u32[]{:S(2)}) collective-permute-start(bf16[120,256]{1,0:T(8,128)(2,1)S(1)} %get-tuple-element.53), channel_id=1, source_target_pairs={{0,2},{1,3},{2,0},{3,1},{4,6},{5,7},{6,4},{7,5},{8,10},{9,11},{10,... | collective-permute-start | bytes 184328 | tf_op jit(solution)/shard_map/ppermute | solution.py:24
  12.8 3.3 %shard_map.137 = (f32[3,192,256]{2,1,0:T(8,128)S(1)}, f32[256,40]{1,0:T(8,128)S(1)}, bf16[3,3,256,256]{3,2,1,0:T(8,128)(2,1)S(1)}, bf16[3,3,3,256,256]{4,3,2,1,0...) custom-call(bf16[3,3,384,256]{3,2,1,0:T(8,128)(2,1)} %weight_hbm.1, ...), custom_call_target="tpu_custom_call" | custom-call | flops 700000000 | bytes 12000000 | tf_op jit(solution)/shard_map/pallas_call | solution.py:739
  16.2 2.3 %collective-permute-done.4.refs_2_ = bf16[120,256]{1,0:T(8,128)(2,1)S(1)} collective-permute-done((bf16[120,256]{1,0:T(8,128)(2,1)S(1)}, bf16[120,256]{1,0:T(8,128)(2,1)S(1)}, u32[]{:S(2)}, u32[]{:S(2)}) %collective-permute-start.4) | collective-permute-done | bytes 61472 | tf_op jit(solution)/shard_map/ppermute | solution.py:24
  18.5 0.0 collective-permute-done.3.refs_1_.refs_11_
  18.5 0.0 collective-permute-done.5.refs_3_.refs_12_
  18.5 0.1 shard_map.141
  18.6 0.1 collective-permute-start.9
  18.6 1.7 %collective-permute-start.10 = (bf16[248,256]{1,0:T(8,128)(2,1)S(1)}, bf16[248,256]{1,0:T(8,128)(2,1)S(1)}, u32[]{:S(2)}, u32[]{:S(2)}) collective-permute-start(bf16[248,256]{1,0:T(8,128)(2,1)S(1)} %get-tuple-element.69), channel_id=1, source_target_pairs={{0,12},{4,0},{8,4},{12,8},{1,13},{5,1},{9,5},{13,9},{2,14},{6,2},{... | collective-permute-start | bytes 380936 | tf_op jit(solution)/shard_map/ppermute | solution.py:24
  20.4 1.2 %shard_map.139 = (bf16[6,12,256]{2,1,0:T(8,128)(2,1)S(1)}, bf16[6,12,256]{2,1,0:T(8,128)(2,1)S(1)}, bf16[6,12,256]{2,1,0:T(8,128)(2,1)S(1)}, bf16[6,12,256]{2,1,0:T(8,128)(2,1)S(1)}) custom-call(bf16[3,3,256,256]{3,2,1,0:T(8,128)(2,1)S(1)} %get-tuple-element.42.weight_ref, f32[12,256]{1,0:T(8,128)S(1)} %get-tuple-element.40.bias_ref.refs_13_, ...), custom_call_target="tpu_custom_call" | custom-call | flops 300000000 | bytes 3000000 | tf_op jit(solution)/shard_map/pallas_call | solution.py:757
  21.5 0.1 collective-permute-start.6
  21.6 2.8 %collective-permute-start.7 = (bf16[6,12,256]{2,1,0:T(8,128)(2,1)S(1)}, bf16[6,12,256]{2,1,0:T(8,128)(2,1)S(1)}, u32[]{:S(2)}, u32[]{:S(2)}) collective-permute-start(bf16[6,12,256]{2,1,0:T(8,128)(2,1)S(1)} %get-tuple-element.57), channel_id=1, source_target_pairs={{0,2},{1,3},{2,0},{3,1},{4,6},{5,7},{6,4},{7,5},{8,10},{9,11},{10,... | collective-permute-start | bytes 110600 | tf_op jit(solution)/shard_map/ppermute | solution.py:24
  24.4 1.0 %collective-permute-start.8 = (bf16[6,12,256]{2,1,0:T(8,128)(2,1)S(1)}, bf16[6,12,256]{2,1,0:T(8,128)(2,1)S(1)}, u32[]{:S(2)}, u32[]{:S(2)}) collective-permute-start(bf16[6,12,256]{2,1,0:T(8,128)(2,1)S(1)} %get-tuple-element.58), channel_id=1, source_target_pairs={{0,3},{1,0},{2,1},{3,2},{4,7},{5,4},{6,5},{7,6},{8,11},{9,8},{10,9... | collective-permute-start | bytes 110600 | tf_op jit(solution)/shard_map/ppermute | solution.py:24
  25.4 2.2 %collective-permute-done.6.refs_1_ = bf16[6,12,256]{2,1,0:T(8,128)(2,1)S(1)} collective-permute-done((bf16[6,12,256]{2,1,0:T(8,128)(2,1)S(1)}, bf16[6,12,256]{2,1,0:T(8,128)(2,1)S(1)}, u32[]{:S(2)}, u32[]{:S(2)}) %collective-permute-start.6) | collective-permute-done | bytes 36896 | tf_op jit(solution)/shard_map/ppermute | solution.py:24
  27.6 0.6 %collective-permute-done.7.refs_2_ = bf16[6,12,256]{2,1,0:T(8,128)(2,1)S(1)} collective-permute-done((bf16[6,12,256]{2,1,0:T(8,128)(2,1)S(1)}, bf16[6,12,256]{2,1,0:T(8,128)(2,1)S(1)}, u32[]{:S(2)}, u32[]{:S(2)}) %collective-permute-start.7) | collective-permute-done | bytes 36896 | tf_op jit(solution)/shard_map/ppermute | solution.py:24
  28.2 0.3 collective-permute-done.8.refs_3_
  28.5 0.0 slice-done
  28.5 0.0 slice-done.1
  28.5 1.2 %shard_map.140 = (bf16[96,256]{1,0:T(8,128)(2,1)S(1)}, f32[1024,256]{1,0:T(8,128)S(1)}, bf16[256,1008]{1,0:T(8,128)(2,1)S(1)}, bf16[256,1008]{1,0:T(8,128)(2,1)S...) custom-call(f32[12,256]{1,0:T(8,128)S(1)} %get-tuple-element.40.bias_ref.refs_13_, ...), custom_call_target="tpu_custom_call" | custom-call | flops 700000000 | bytes 5000000 | tf_op jit(solution)/shard_map/pallas_call | solution.py:788
  29.7 0.0 collective-permute-done.9.refs_9_
  29.7 0.0 collective-permute-done.10.refs_10_
  29.8 8.1 %shard_map.142 = bf16[16,64,256]{2,1,0:T(8,128)(2,1)} custom-call(bf16[256,1008]{1,0:T(8,128)(2,1)S(1)} %get-tuple-element.59.refs_0_, bf16[256,1008]{1,0:T(8,128)(2,1)S(1)} %get-tuple-element.60.refs_1_, bf16[256,1008]{1,0:T(8,128)(2,1)S(1)} %get-tuple-element.61.refs_2_, bf16[256,1008]{1,0:T(8,128)(2,1)S(1)} %get-tuple-element.62.refs_3_, ...), custom_call_target="tpu_custom_call" | custom-call | flops 8000000000 | bytes 12000000 | tf_op jit(solution)/shard_map/pallas_call | solution.py:623
  (1 shorter events, 0.0 us)
Async XLA Ops:
  0.0 6.8 %collective-permute-start = (bf16[2,32,384]{2,1,0:T(8,128)(2,1)}, bf16[2,32,384]{2,1,0:T(8,128)(2,1)S(1)}, u32[]{:S(2)}, u32[]{:S(2)}) collective-permute-start(bf16[2,32,384]{2,1,0:T(8,128)(2,1)} %refs_7_.1), channel_id=1, source_target_pairs={{0,4},{4,8},{8,12},{12,0},{1,5},{5,9},{9,13},{13,1},{2,6},{6,10},{... | collective-permute-start | bytes 147464 | tf_op jit(solution)/shard_map/ppermute | solution.py:24
  0.5 6.3 %collective-permute-start.2 = (bf16[2,32,384]{2,1,0:T(8,128)(2,1)}, bf16[2,32,384]{2,1,0:T(8,128)(2,1)S(1)}, u32[]{:S(2)}, u32[]{:S(2)}) collective-permute-start(bf16[2,32,384]{2,1,0:T(8,128)(2,1)} %refs_7_.1), channel_id=1, source_target_pairs={{0,12},{4,0},{8,4},{12,8},{1,13},{5,1},{9,5},{13,9},{2,14},{6,2},{... | collective-permute-start | bytes 147464 | tf_op jit(solution)/shard_map/ppermute | solution.py:24
  2.4 5.1 %collective-permute-start.1 = (bf16[2,32,384]{2,1,0:T(8,128)(2,1)}, bf16[2,32,384]{2,1,0:T(8,128)(2,1)S(1)}, u32[]{:S(2)}, u32[]{:S(2)}) collective-permute-start(bf16[2,32,384]{2,1,0:T(8,128)(2,1)} %refs_7_.1), channel_id=1, source_target_pairs={{0,8},{4,12},{8,0},{12,4},{1,9},{5,13},{9,1},{13,5},{2,10},{6,14},... | collective-permute-start | bytes 147464 | tf_op jit(solution)/shard_map/ppermute | solution.py:24
  8.2 10.3 %collective-permute-start.3 = (bf16[168,256]{1,0:T(8,128)(2,1)S(1)}, bf16[168,256]{1,0:T(8,128)(2,1)S(1)}, u32[]{:S(2)}, u32[]{:S(2)}) collective-permute-start(bf16[168,256]{1,0:T(8,128)(2,1)S(1)} %get-tuple-element.52), channel_id=1, source_target_pairs={{0,1},{1,2},{2,3},{3,0},{4,5},{5,6},{6,7},{7,4},{8,9},{9,10},{10,1... | collective-permute-start | bytes 258056 | tf_op jit(solution)/shard_map/ppermute | solution.py:24
  9.8 8.7 %collective-permute-start.5 = (bf16[168,256]{1,0:T(8,128)(2,1)S(1)}, bf16[168,256]{1,0:T(8,128)(2,1)S(1)}, u32[]{:S(2)}, u32[]{:S(2)}) collective-permute-start(bf16[168,256]{1,0:T(8,128)(2,1)S(1)} %get-tuple-element.54), channel_id=1, source_target_pairs={{0,3},{1,0},{2,1},{3,2},{4,7},{5,4},{6,5},{7,6},{8,11},{9,8},{10,9... | collective-permute-start | bytes 258056 | tf_op jit(solution)/shard_map/ppermute | solution.py:24
  12.0 16.5 %slice-start = ((s8[4718592]{0:T(1024)(128)(4,1)}), s8[4194304]{0:T(1024)(128)(4,1)S(1)}, s32[]{:S(2)}) async-start(s8[4718592]{0:T(1024)(128)(4,1)} %bitcast), calls=%async_computation | async-start | bytes 8388608
  12.0 16.5 %slice-start.1 = ((s8[4718592]{0:T(1024)(128)(4,1)}), s8[524288]{0:T(1024)(128)(4,1)S(1)}, s32[]{:S(2)}) async-start(s8[4718592]{0:T(1024)(128)(4,1)} %bitcast), calls=%async_computation.1 | async-start | bytes 1048576
  12.0 6.4 %collective-permute-start.4 = (bf16[120,256]{1,0:T(8,128)(2,1)S(1)}, bf16[120,256]{1,0:T(8,128)(2,1)S(1)}, u32[]{:S(2)}, u32[]{:S(2)}) collective-permute-start(bf16[120,256]{1,0:T(8,128)(2,1)S(1)} %get-tuple-element.53), channel_id=1, source_target_pairs={{0,2},{1,3},{2,0},{3,1},{4,6},{5,7},{6,4},{7,5},{8,10},{9,11},{10,... | collective-permute-start | bytes 184328 | tf_op jit(solution)/shard_map/ppermute | solution.py:24
  18.6 11.2 %collective-permute-start.9 = (bf16[248,256]{1,0:T(8,128)(2,1)S(1)}, bf16[248,256]{1,0:T(8,128)(2,1)S(1)}, u32[]{:S(2)}, u32[]{:S(2)}) collective-permute-start(bf16[248,256]{1,0:T(8,128)(2,1)S(1)} %get-tuple-element.68), channel_id=1, source_target_pairs={{0,4},{4,8},{8,12},{12,0},{1,5},{5,9},{9,13},{13,1},{2,6},{6,10},{... | collective-permute-start | bytes 380936 | tf_op jit(solution)/shard_map/ppermute | solution.py:24
  18.6 11.1 %collective-permute-start.10 = (bf16[248,256]{1,0:T(8,128)(2,1)S(1)}, bf16[248,256]{1,0:T(8,128)(2,1)S(1)}, u32[]{:S(2)}, u32[]{:S(2)}) collective-permute-start(bf16[248,256]{1,0:T(8,128)(2,1)S(1)} %get-tuple-element.69), channel_id=1, source_target_pairs={{0,12},{4,0},{8,4},{12,8},{1,13},{5,1},{9,5},{13,9},{2,14},{6,2},{... | collective-permute-start | bytes 380936 | tf_op jit(solution)/shard_map/ppermute | solution.py:24
  21.5 6.1 %collective-permute-start.6 = (bf16[6,12,256]{2,1,0:T(8,128)(2,1)S(1)}, bf16[6,12,256]{2,1,0:T(8,128)(2,1)S(1)}, u32[]{:S(2)}, u32[]{:S(2)}) collective-permute-start(bf16[6,12,256]{2,1,0:T(8,128)(2,1)S(1)} %get-tuple-element.56), channel_id=1, source_target_pairs={{0,1},{1,2},{2,3},{3,0},{4,5},{5,6},{6,7},{7,4},{8,9},{9,10},{10,1... | collective-permute-start | bytes 110600 | tf_op jit(solution)/shard_map/ppermute | solution.py:24
  21.6 6.6 %collective-permute-start.7 = (bf16[6,12,256]{2,1,0:T(8,128)(2,1)S(1)}, bf16[6,12,256]{2,1,0:T(8,128)(2,1)S(1)}, u32[]{:S(2)}, u32[]{:S(2)}) collective-permute-start(bf16[6,12,256]{2,1,0:T(8,128)(2,1)S(1)} %get-tuple-element.57), channel_id=1, source_target_pairs={{0,2},{1,3},{2,0},{3,1},{4,6},{5,7},{6,4},{7,5},{8,10},{9,11},{10,... | collective-permute-start | bytes 110600 | tf_op jit(solution)/shard_map/ppermute | solution.py:24
  24.4 4.1 %collective-permute-start.8 = (bf16[6,12,256]{2,1,0:T(8,128)(2,1)S(1)}, bf16[6,12,256]{2,1,0:T(8,128)(2,1)S(1)}, u32[]{:S(2)}, u32[]{:S(2)}) collective-permute-start(bf16[6,12,256]{2,1,0:T(8,128)(2,1)S(1)} %get-tuple-element.58), channel_id=1, source_target_pairs={{0,3},{1,0},{2,1},{3,2},{4,7},{5,4},{6,5},{7,6},{8,11},{9,8},{10,9... | collective-permute-start | bytes 110600 | tf_op jit(solution)/shard_map/ppermute | solution.py:24
